TPU v7x, 128 devices: a whole 4x4x4 slice. The times are simulated.
128 devices in a mesh: pipe: 2 (over x_lo), dp: 64 (over z, x_hi, y, core).
Axes of the slice: x: 4 (x_hi: 2, x_lo: 2; x = x_hi * 2 + x_lo), y: 4, z: 4, core: 2. Of those that a mesh axis runs over, the one named last changes fastest.
Arguments:
- segment_input: bfloat16 [2, 512, 12288], P('pipe', 'dp'), may hold values from -3000 to 3000, as said below
- norm_gain: float32 [2, 12288], P('pipe'), may hold values from 0.5 to 2
- head_weights: bfloat16 [2, 12288, 64, 384], P('pipe', None, 'dp'), may hold values from -0.04818163 to 0.04818163
- output_weights: bfloat16 [2, 8192, 12288], P('pipe', 'dp'), may hold values from -0.25 to 0.25
Outputs:
- section_outputs: bfloat16 [2, 512, 12288], P('pipe', 'dp')
Inputs may be any that keep to these rules, and one draw needn't show every extreme that they name: `segment_input`: activations of order one to some thousands, rows and features of unlike scales.
All inputs are finite; a program needn't handle non-finite values.
Results may differ from a plain program's by a relative error of at most 0.0083.
Values may be sent and summed in bfloat16 or wider, within the bound.
No kernel may reach another device: no remote copies, remote signals or barrier semaphores. Data moves between devices by JAX's collectives and lax.ppermute only.
A program may use at most 128 MiB of HBM per device.

v0:
```python
import math

import jax
import jax.numpy as jnp
from jax import lax
from jax.sharding import PartitionSpec as P


def from_behind(value, axis, steps):
    count = lax.axis_size(axis)
    pairs = [(source, (source + steps) % count) for source in range(count)]
    return lax.ppermute(value, axis, pairs)


def normalize(section_rows, gain_vector):
    values = section_rows.astype(jnp.float32)
    centre = jnp.mean(values, axis=-1, keepdims=True)
    shifted = values - centre
    spread = jnp.mean(shifted * shifted, axis=-1, keepdims=True)
    return (shifted * lax.rsqrt(spread + 1e-05) * gain_vector).astype(jnp.bfloat16)


def attend(projected, head_size):
    queries = projected[:, :head_size]
    keys_part = projected[:, head_size : 2 * head_size]
    values_part = projected[:, 2 * head_size :].astype(jnp.bfloat16)
    scores = jnp.einsum(
        "qd,kd->qk", queries, keys_part, precision=lax.Precision.HIGHEST
    ) / math.sqrt(head_size)
    length = projected.shape[0]
    causal = jnp.arange(length)[:, None] >= jnp.arange(length)[None, :]
    scores = jnp.where(causal, scores, -1e30)
    largest = jnp.max(scores, axis=-1, keepdims=True)
    weights = jnp.where(causal, jnp.exp(scores - largest), 0.0)
    totals = jnp.sum(weights, axis=-1, keepdims=True)
    probabilities = (weights / totals).astype(jnp.bfloat16)
    return jnp.dot(probabilities, values_part, preferred_element_type=jnp.float32).astype(
        jnp.bfloat16
    )


def shards(segment_input, norm_gain, head_weights, output_weights):
    head_size = output_weights.shape[1]
    normed = normalize(segment_input[0], norm_gain[0])
    head_block = head_weights[0, :, 0, :]
    projected = jnp.dot(
        lax.all_gather(normed, "dp", axis=0, tiled=True),
        head_block,
        preferred_element_type=jnp.float32,
    )
    attended = attend(projected, head_size)
    out_rows = output_weights[0]
    finished = lax.psum_scatter(
        jnp.dot(attended, out_rows, preferred_element_type=jnp.float32),
        "dp",
        scatter_dimension=0,
        tiled=True,
    ).astype(jnp.bfloat16)
    handed = from_behind(finished, "pipe", 1)
    return handed[None]


def solution(mesh):
    placed = (
        P("pipe", "dp", None),
        P("pipe", None),
        P("pipe", None, "dp", None),
        P("pipe", "dp", None),
    )
    return jax.shard_map(
        shards, mesh=mesh, in_specs=placed, out_specs=P("pipe", "dp", None), check_vma=False
    )
```

profile of v0, /device:TPU:0, one launch (start us, length us, event | category | flops | bytes accessed | tf_op | source)
XLA Modules:
  0.0 382.8 jit_solution(5650053508658786681)
XLA Ops:
  6.5 0.0 copy-start
  6.5 0.0 all-gather.2.cloned.1.call-start
  6.5 1.3 convert_reduce_fusion
  7.8 1.2 fusion.15
  9.1 1.7 fusion.17
  10.8 0.0 all-gather.2.cloned.1.call-update
  10.8 0.0 reduce-scatter.2.cloned.1.call-start
  10.9 95.6 %all-gather.2.cloned.1.call-done = bf16[512,12288]{1,0:T(8,128)(2,1)} async-done(((bf16[8,12288]{1,0:T(8,128)(2,1)}), bf16[512,12288]{1,0:T(8,128)(2,1)}) %all-gather.2.cloned.1.call-update) | async-done | bytes 12582928 | tf_op jit(solution)/shard_map/all_gather | solution.py:47
  106.5 12.7 %fusion = f32[512,384]{1,0:T(8,128)S(1)} fusion(bf16[512,12288]{1,0:T(8,128)(2,1)} %all-gather.2.cloned.1.call-done, bf16[1,12288,1,384]{3,1,2,0:T(8,128)(2,1)} %param.6), kind=kOutput, calls=%fused_computation | convolution fusion | flops 4831838208 | bytes 22806528 | tf_op jit(solution)/shard_map/dot_general | solution.py:46
  119.2 0.0 copy-start.2
  119.2 0.9 copy-done.2
  120.1 1.0 fusion.22
  121.1 0.0 copy-start.1
  121.1 1.1 copy-done.1
  122.2 0.2 fusion.5
  122.3 0.0 copy-done
  122.3 11.8 %fusion.2 = f32[512,12288]{1,0:T(8,128)} fusion(bf16[1,128,12288]{2,1,0:T(8,128)(2,1)S(1)} %copy-done, f32[512,512]{0,1:T(8,128)} %copy-done.1, f32[512]{0:T(512)S(1)} %fusion.5, f32[512]{0:T(512)S(1)} %get-tuple-element.5, f32[512,384]{1,0:T(8,128)} %copy-done.2), kind=kOutput, calls=%fused_computation.2 | convolution fusion | flops 1679097856 | bytes 29495296 | tf_op jit(solution)/shard_map/dot_general | solution.py:54
  134.1 0.0 reduce-scatter.2.cloned.1.call-update
  134.1 234.4 %reduce-scatter.2.cloned.1.call-done = f32[8,12288]{1,0:T(8,128)} async-done(((f32[512,12288]{1,0:T(8,128)}), f32[8,12288]{1,0:T(8,128)}) %reduce-scatter.2.cloned.1.call-update) | async-done | bytes 393232 | tf_op jit(solution)/shard_map/reduce_scatter | solution.py:53
  368.5 1.0 convert_element_type.24
  369.6 0.6 collective-permute-start
  370.2 5.1 %collective-permute-done = bf16[8,12288]{1,0:T(8,128)(2,1)S(1)} collective-permute-done((bf16[8,12288]{1,0:T(8,128)(2,1)S(1)}, bf16[8,12288]{1,0:T(8,128)(2,1)S(1)}, u32[]{:S(2)}, u32[]{:S(2)}) %collective-permute-start) | collective-permute-done | bytes 196640 | tf_op jit(solution)/shard_map/ppermute | solution.py:12
  375.3 0.7 copy.6
  (2 shorter events, 0.0 us)
Async XLA Ops:
  6.5 115.8 %copy-start = (bf16[1,128,12288]{2,1,0:T(8,128)(2,1)S(1)}, bf16[1,128,12288]{2,1,0:T(8,128)(2,1)}, u32[]{:S(2)}) copy-start(bf16[1,128,12288]{2,1,0:T(8,128)(2,1)} %param.7) | copy-start | bytes 9437188
  6.5 100.0 %all-gather.2.cloned.1.call-start = ((), (), s32[]{:S(2)}) async-start(), calls=%async_computation.1 | async-start | bytes 12779520 | tf_op jit(solution)/shard_map/all_gather | solution.py:47
  10.8 357.7 %reduce-scatter.2.cloned.1.call-start = ((), (), s32[]{:S(2)}) async-start(), calls=%async_computation.2 | async-start | bytes 25559040 | tf_op jit(solution)/shard_map/reduce_scatter | solution.py:53
  119.2 0.9 copy-start.2
  121.1 1.1 copy-start.1
  369.6 5.7 %collective-permute-start = (bf16[8,12288]{1,0:T(8,128)(2,1)S(1)}, bf16[8,12288]{1,0:T(8,128)(2,1)S(1)}, u32[]{:S(2)}, u32[]{:S(2)}) collective-permute-start(bf16[8,12288]{1,0:T(8,128)(2,1)S(1)} %convert_element_type.24), channel_id=1, source_target_pairs={{0,64},{64,0},{1,65},{65,1},{2,66},{66,2},{3,67},{67,3},{4,68},{68... | collective-permute-start | bytes 589832 | tf_op jit(solution)/shard_map/ppermute | solution.py:12
Sparse Core Ops, SparseCore 0:
  10.9 95.5 all-gather.1
  134.2 234.2 reduce-scatter.1
where the time goes:
time: 383 us
  waiting for transfers between devices  335 us (87%)
  matrix products  25.5 us (7%)
  between operations  13.4 us (3%)
  other arithmetic  5.42 us (1%)
    reduce_scatter x1, waiting for transfers between devices, shards(): lax.psum_scatter(jnp.dot(attended, out_rows, preferred_element_type=jnp.f...  234 us
    all_gather x1, waiting for transfers between devices, shards(): lax.all_gather(normed, 'dp', axis=0, tiled=True)  95.6 us
    dot_general x1, matrix products, shards(): jnp.dot(lax.all_gather(normed, 'dp', axis=0, tiled=True), head_block, pre...  12.7 us
    dot_general x1, matrix products, shards(): jnp.dot(attended, out_rows, preferred_element_type=jnp.float32)  11.8 us
  transfers between devices with their start and end apart: 3, of which 3 were waited for; matrix products, arithmetic and copies ran while one was open for 0% of the time, Pallas kernels for 0%

commit v1 on v0

v1 whole, which is shorter than its diff:
```python
import math

import jax
import jax.numpy as jnp
import numpy as np
from jax import lax
from jax.sharding import PartitionSpec as P

RING = 4
AXES = ("pipe", "dp")


def split_place(index):
    core = index % 2
    y = index // 2 % 4
    half_x = index // 8 % 2
    z = index // 16 % 4
    pipe = index // 64
    return pipe, z, half_x, y, core


def join_place(pipe, z, half_x, y, core):
    return (((pipe * 4 + z) * 2 + half_x) * 4 + y) * 2 + core


def send(value, pipe=0, z=0, x=0, y=0, core=0):
    pairs = []
    for source in range(128):
        p0, z0, x0, y0, c0 = split_place(source)
        target = join_place(p0 ^ pipe, (z0 + z) % 4, x0 ^ x, (y0 + y) % 4, c0 ^ core)
        pairs.append((source, target))
    return lax.ppermute(value, AXES, pairs)


def normalize(section_rows, gain_vector):
    values = section_rows.astype(jnp.float32)
    centre = jnp.mean(values, axis=-1, keepdims=True)
    shifted = values - centre
    spread = jnp.mean(shifted * shifted, axis=-1, keepdims=True)
    return (shifted * lax.rsqrt(spread + 1e-05) * gain_vector).astype(jnp.bfloat16)


def ring_gather(block, axis):
    half = block.shape[0] // 2
    top, bottom = block[:half], block[half:]
    top_before = send(top, **{axis: 1})
    bottom_after = send(bottom, **{axis: -1})
    bottom_before = send(bottom, **{axis: 1})
    top_after = send(top, **{axis: -1})
    top_far = send(top_before, **{axis: 1})
    bottom_far = send(bottom_after, **{axis: -1})
    return (
        (top, bottom),
        (top_after, bottom_after),
        (top_before, bottom_before),
        (top_far, bottom_far),
    )


def rows_of(*pairs):
    return jnp.concatenate([piece for pair in pairs for piece in pair], axis=0)


def ring_scatter(far, after, before, own, axis):
    half = far.shape[0] // 2
    from_before = send(far[:half], **{axis: 1})
    from_after = send(far[half:], **{axis: -1})
    to_after = jnp.concatenate(
        [after[:half] + from_before.astype(jnp.float32), after[half:]], axis=0
    ).astype(jnp.bfloat16)
    to_before = jnp.concatenate(
        [before[:half], before[half:] + from_after.astype(jnp.float32)], axis=0
    ).astype(jnp.bfloat16)
    got_before = send(to_after, **{axis: 1})
    got_after = send(to_before, **{axis: -1})
    return own + got_before.astype(jnp.float32) + got_after.astype(jnp.float32)


def small_scatter(chunks, axis):
    size = chunks.shape[0] // 4
    parts = [chunks[k * size : (k + 1) * size] for k in range(4)]
    total = parts[0]
    for part, step in ((parts[1], 1), (parts[2], -1), (parts[3], 2)):
        total = total + send(part.astype(jnp.bfloat16), **{axis: step}).astype(jnp.float32)
    return total


def token_positions(z, y):
    steps = (0, 1, -1, 2)
    dz, dy, xs, low = [], [], [], []
    for side, far_step in (
        (0, 2), (1, 2), (0, 1), (0, -1), (1, 1), (1, -1), (0, 0), (1, 0),
    ):
        for near in steps:
            for r in range(16):
                dz.append(far_step if side == 0 else near)
                dy.append(near if side == 0 else far_step)
                xs.append(side)
                low.append(r)
    dz, dy, xs, low = (np.asarray(v, np.int32) for v in (dz, dy, xs, low))
    return ((((z + dz) % 4) * 2 + xs) * 4 + (y + dy) % 4) * 16 + low


def attend(projected, position, head_size):
    queries = projected[:, :head_size]
    keys_part = projected[:, head_size : 2 * head_size]
    values_part = projected[:, 2 * head_size :].astype(jnp.bfloat16)
    scores = jnp.einsum(
        "qd,kd->qk", queries, keys_part, precision=lax.Precision.HIGHEST
    ) / math.sqrt(head_size)
    causal = position[:, None] >= position[None, :]
    scores = jnp.where(causal, scores, -1e30)
    largest = jnp.max(scores, axis=-1, keepdims=True)
    weights = jnp.where(causal, jnp.exp(scores - largest), 0.0)
    totals = jnp.sum(weights, axis=-1, keepdims=True)
    probabilities = (weights / totals).astype(jnp.bfloat16)
    return jnp.dot(probabilities, values_part, preferred_element_type=jnp.float32).astype(
        jnp.bfloat16
    )


def shards(segment_input, norm_gain, head_weights, output_weights):
    head_size = output_weights.shape[1]
    width = segment_input.shape[2]
    half, quarter = width // 2, width // 4
    _, z, half_x, y, core = split_place(lax.axis_index("dp"))

    normed = normalize(segment_input[0], norm_gain[0])
    left, right = normed[:, :half], normed[:, half:]
    kept = jnp.where(core == 0, left, right)
    given = send(jnp.where(core == 0, right, left), core=1)
    block = jnp.where(
        core == 0, jnp.concatenate([kept, given]), jnp.concatenate([given, kept])
    )
    other = send(block, x=1)
    first = jnp.where(half_x == 0, block, other)
    second = jnp.where(half_x == 0, other, block)

    head_block = head_weights[0, :, 0, :]
    own_weights = lax.dynamic_slice_in_dim(head_block, core * half, half, 0)
    swapped_weights = send(
        lax.dynamic_slice_in_dim(head_block, (1 - core) * half, half, 0), core=1
    )
    out_rows = output_weights[0]
    out_parts = []
    for dx, dc in ((0, 0), (0, 1), (1, 0), (1, 1)):
        start = ((half_x ^ dx) * 2 + (core ^ dc)) * quarter
        part = lax.dynamic_slice_in_dim(out_rows, start, quarter, 1)
        out_parts.append(send(part, x=dx, core=dc) if dx or dc else part)
    out_block = jnp.concatenate(out_parts, axis=0)

    first_near = rows_of(*ring_gather(first, "y"))
    second_near = rows_of(*ring_gather(second, "z"))
    first_all = ring_gather(first_near, "z")
    second_all = ring_gather(second_near, "y")

    def project(rows):
        mine = jnp.dot(rows, own_weights, preferred_element_type=jnp.float32)
        theirs = jnp.dot(rows, swapped_weights, preferred_element_type=jnp.float32)
        return mine + send(theirs, core=1)

    near = project(jnp.concatenate([first_near, second_near]))
    middle = project(
        rows_of(first_all[1], first_all[2], second_all[1], second_all[2])
    )
    far = project(rows_of(first_all[3], second_all[3]))
    projected = jnp.concatenate([far, middle, near], axis=0)

    attended = attend(projected, token_positions(z, y), head_size)
    across_x = send(attended, x=1)
    across_core = send(attended, core=1)
    across_both = send(across_x, core=1)
    heads = jnp.concatenate([attended, across_core, across_x, across_both], axis=1)

    edge = jnp.dot(heads[:128], out_block, preferred_element_type=jnp.float32).astype(
        jnp.bfloat16
    )
    rest = jnp.dot(heads[128:], out_block, preferred_element_type=jnp.float32)
    first_sum = ring_scatter(
        edge[:64], rest[:64], rest[64:128], rest[256:320], "z"
    )
    second_sum = ring_scatter(
        edge[64:], rest[128:192], rest[192:256], rest[320:384], "y"
    )
    first_rows = small_scatter(first_sum, "y").astype(jnp.bfloat16)
    second_rows = small_scatter(second_sum, "z").astype(jnp.bfloat16)

    owners = jnp.stack([first_rows, second_rows]).reshape(2, 2, 8, quarter)
    by_x = jnp.where(half_x == 0, owners, owners[::-1])
    by_place = jnp.where(core == 0, by_x, by_x[:, ::-1])
    got = jnp.stack(
        [
            jnp.stack([send(by_place[dx, dc], pipe=1, x=dx, core=dc) for dc in (0, 1)])
            for dx in (0, 1)
        ]
    )
    got = jnp.where(core == 0, got, got[:, ::-1])
    got = jnp.where(half_x == 0, got, got[::-1])
    return jnp.concatenate([got[0, 0], got[0, 1], got[1, 0], got[1, 1]], axis=1)[None]


def solution(mesh):
    placed = (
        P("pipe", "dp", None),
        P("pipe", None),
        P("pipe", None, "dp", None),
        P("pipe", "dp", None),
    )
    return jax.shard_map(
        shards, mesh=mesh, in_specs=placed, out_specs=P("pipe", "dp", None), check_vma=False
    )
```

time: 383 us -> 263 us (0.69)
  waiting for transfers between devices: 335 us -> 165 us
  starting transfers between devices: 0.69 us -> 59.5 us
  between operations: 13.4 us -> 0.64 us
  local copies, waits for them, and re-layouts: 2.63 us -> 7.58 us
  matrix products: 25.5 us -> 21.3 us
    reduce_scatter x1 -> x0, waiting for transfers between devices: 234 us -> none  [shards(): lax.psum_scatter(jnp.dot(attended, out_rows, preferred_element_type=jnp.f...]
    ppermute x1 -> x54, waiting for transfers between devices: 5.1 us -> 165 us  [send(): return lax.ppermute(value, AXES, pairs)]
    all_gather x1 -> x0, waiting for transfers between devices: 95.6 us -> none  [shards(): lax.all_gather(normed, 'dp', axis=0, tiled=True)]
    ppermute x1 -> x54, starting transfers between devices: 0.65 us -> 59.5 us  [send(): return lax.ppermute(value, AXES, pairs)]
    dynamic_slice x0 -> x2, local copies, waits for them, and re-layouts: none -> 6.86 us  [the longest x1 5.15 us: shards(): lax.dynamic_slice_in_dim(head_block, (1 - core) * half, half, 0)]
    dot_general x2 -> x9, matrix products: 24.4 us -> 20.3 us  [the longest x3 11.2 us: project(): theirs = jnp.dot(rows, swapped_weights, preferred_element_type=jnp.float32)]
  transfers between devices with their start and end apart: 3 -> 54, of which waited for: 3 -> 33; matrix products, arithmetic and copies ran while one was open for 0% -> 11% of each run, Pallas kernels for 0% -> 0%
where the time goes in v1:
time: 263 us; the launch traced here: 261 us
  waiting for transfers between devices  165 us (63%)
  starting transfers between devices  59.5 us (23%)
  matrix products  21.3 us (8%)
  local copies, waits for them, and re-layouts  7.58 us (3%)
  other arithmetic  6.28 us (2%)
    ppermute x54, waiting for transfers between devices, send(): return lax.ppermute(value, AXES, pairs)  165 us
    ppermute x54, starting transfers between devices, send(): return lax.ppermute(value, AXES, pairs)  59.5 us
    dot_general x3, matrix products, project(): theirs = jnp.dot(rows, swapped_weights, preferred_element_type=jnp.float32)  11.2 us
  transfers between devices with their start and end apart: 54, of which 33 were waited for; matrix products, arithmetic and copies ran while one was open for 11% of the time, Pallas kernels for 0%

profile of v1, /device:TPU:0, one launch (start us, length us, event | category | flops | bytes accessed | tf_op | source)
XLA Modules:
  0.0 260.7 jit_solution(251313766851400524)
XLA Ops:
  3.6 5.1 %dynamic-slice_bitcast_fusion = bf16[6144,384]{1,0:T(8,128)(2,1)} fusion(bf16[1,12288,1,384]{3,1,2,0:T(8,128)(2,1)} %param.10, s32[]{:T(128)S(6)} %select_n.136), kind=kLoop, calls=%fused_computation.6 | loop fusion | bytes 9437188 | tf_op jit(solution)/shard_map/dynamic_slice | solution.py:142
  23.2 3.6 %collective-permute-start.3 = (bf16[8,6144]{1,0:T(8,128)(2,1)S(1)}, bf16[8,6144]{1,0:T(8,128)(2,1)S(1)}, u32[]{:S(2)}, u32[]{:S(2)}) collective-permute-start(bf16[8,6144]{1,0:T(8,128)(2,1)S(1)} %get-tuple-element.47), channel_id=1, source_target_pairs={{0,6},{1,7},{2,0},{3,1},{4,2},{5,3},{6,4},{7,5},{8,14},{9,15},{10,... | collective-permute-start | bytes 294920 | tf_op jit(solution)/shard_map/ppermute | solution.py:32
  30.8 4.4 %collective-permute-done.7 = bf16[8,6144]{1,0:T(8,128)(2,1)S(1)} collective-permute-done((bf16[8,6144]{1,0:T(8,128)(2,1)S(1)}, bf16[8,6144]{1,0:T(8,128)(2,1)S(1)}, u32[]{:S(2)}, u32[]{:S(2)}) %collective-permute-start.7) | collective-permute-done | bytes 98336 | tf_op jit(solution)/shard_map/ppermute | solution.py:32
  39.9 4.1 %collective-permute-start.12 = (bf16[8,6144]{1,0:T(8,128)(2,1)S(1)}, bf16[8,6144]{1,0:T(8,128)(2,1)S(1)}, u32[]{:S(2)}, u32[]{:S(2)}) collective-permute-start(bf16[8,6144]{1,0:T(8,128)(2,1)S(1)} %get-tuple-element.46), channel_id=1, source_target_pairs={{0,48},{1,49},{2,50},{3,51},{4,52},{5,53},{6,54},{7,55},{8,56},{9,... | collective-permute-start | bytes 294920 | tf_op jit(solution)/shard_map/ppermute | solution.py:32
  48.7 5.8 %collective-permute-done.16 = bf16[8,6144]{1,0:T(8,128)(2,1)S(1)} collective-permute-done((bf16[8,6144]{1,0:T(8,128)(2,1)S(1)}, bf16[8,6144]{1,0:T(8,128)(2,1)S(1)}, u32[]{:S(2)}, u32[]{:S(2)}) %collective-permute-start.16) | collective-permute-done | bytes 98336 | tf_op jit(solution)/shard_map/ppermute | solution.py:32
  54.5 6.4 %collective-permute-done.17 = bf16[8,6144]{1,0:T(8,128)(2,1)S(1)} collective-permute-done((bf16[8,6144]{1,0:T(8,128)(2,1)S(1)}, bf16[8,6144]{1,0:T(8,128)(2,1)S(1)}, u32[]{:S(2)}, u32[]{:S(2)}) %collective-permute-start.17) | collective-permute-done | bytes 98336 | tf_op jit(solution)/shard_map/ppermute | solution.py:32
  60.9 6.4 %collective-permute-done.18 = bf16[8,6144]{1,0:T(8,128)(2,1)S(1)} collective-permute-done((bf16[8,6144]{1,0:T(8,128)(2,1)S(1)}, bf16[8,6144]{1,0:T(8,128)(2,1)S(1)}, u32[]{:S(2)}, u32[]{:S(2)}) %collective-permute-start.18) | collective-permute-done | bytes 98336 | tf_op jit(solution)/shard_map/ppermute | solution.py:32
  67.4 4.6 %collective-permute-done.19 = bf16[8,6144]{1,0:T(8,128)(2,1)S(1)} collective-permute-done((bf16[8,6144]{1,0:T(8,128)(2,1)S(1)}, bf16[8,6144]{1,0:T(8,128)(2,1)S(1)}, u32[]{:S(2)}, u32[]{:S(2)}) %collective-permute-start.19) | collective-permute-done | bytes 98336 | tf_op jit(solution)/shard_map/ppermute | solution.py:32
  73.3 8.3 %collective-permute-done.24 = bf16[32,6144]{1,0:T(8,128)(2,1)S(1)} collective-permute-done((bf16[32,6144]{1,0:T(8,128)(2,1)S(1)}, bf16[32,6144]{1,0:T(8,128)(2,1)S(1)}, u32[]{:S(2)}, u32[]{:S(2)}) %collective-permute-start.24) | collective-permute-done | bytes 393248 | tf_op jit(solution)/shard_map/ppermute | solution.py:32
  84.8 6.8 %collective-permute-done.10 = bf16[32,6144]{1,0:T(8,128)(2,1)S(1)} collective-permute-done((bf16[32,6144]{1,0:T(8,128)(2,1)S(1)}, bf16[32,6144]{1,0:T(8,128)(2,1)S(1)}, u32[]{:S(2)}, u32[]{:S(2)}) %collective-permute-start.10) | collective-permute-done | bytes 393248 | tf_op jit(solution)/shard_map/ppermute | solution.py:32
  91.6 10.3 %collective-permute-done.4 = bf16[32,6144]{1,0:T(8,128)(2,1)S(1)} collective-permute-done((bf16[32,6144]{1,0:T(8,128)(2,1)S(1)}, bf16[32,6144]{1,0:T(8,128)(2,1)S(1)}, u32[]{:S(2)}, u32[]{:S(2)}) %collective-permute-start.4) | collective-permute-done | bytes 393248 | tf_op jit(solution)/shard_map/ppermute | solution.py:32
  102.0 9.0 %collective-permute-done.25 = bf16[32,6144]{1,0:T(8,128)(2,1)S(1)} collective-permute-done((bf16[32,6144]{1,0:T(8,128)(2,1)S(1)}, bf16[32,6144]{1,0:T(8,128)(2,1)S(1)}, u32[]{:S(2)}, u32[]{:S(2)}) %collective-permute-start.25) | collective-permute-done | bytes 393248 | tf_op jit(solution)/shard_map/ppermute | solution.py:32
  114.2 7.0 %collective-permute-done.26 = bf16[32,6144]{1,0:T(8,128)(2,1)S(1)} collective-permute-done((bf16[32,6144]{1,0:T(8,128)(2,1)S(1)}, bf16[32,6144]{1,0:T(8,128)(2,1)S(1)}, u32[]{:S(2)}, u32[]{:S(2)}) %collective-permute-start.26) | collective-permute-done | bytes 393248 | tf_op jit(solution)/shard_map/ppermute | solution.py:32
  121.1 3.7 %collective-permute-start.20 = (bf16[32,6144]{1,0:T(8,128)(2,1)S(1)}, bf16[32,6144]{1,0:T(8,128)(2,1)S(1)}, u32[]{:S(2)}, u32[]{:S(2)}) collective-permute-start(bf16[32,6144]{1,0:T(8,128)(2,1)S(1)} %get-tuple-element.51), channel_id=1, source_target_pairs={{0,6},{1,7},{2,0},{3,1},{4,2},{5,3},{6,4},{7,5},{8,14},{9,15},{10,... | collective-permute-start | bytes 1179656 | tf_op jit(solution)/shard_map/ppermute | solution.py:32
  124.9 5.3 %collective-permute-done.20 = bf16[32,6144]{1,0:T(8,128)(2,1)S(1)} collective-permute-done((bf16[32,6144]{1,0:T(8,128)(2,1)S(1)}, bf16[32,6144]{1,0:T(8,128)(2,1)S(1)}, u32[]{:S(2)}, u32[]{:S(2)}) %collective-permute-start.20) | collective-permute-done | bytes 393248 | tf_op jit(solution)/shard_map/ppermute | solution.py:32
  130.2 13.2 %collective-permute-done.14 = bf16[32,6144]{1,0:T(8,128)(2,1)S(1)} collective-permute-done((bf16[32,6144]{1,0:T(8,128)(2,1)S(1)}, bf16[32,6144]{1,0:T(8,128)(2,1)S(1)}, u32[]{:S(2)}, u32[]{:S(2)}) %collective-permute-start.14) | collective-permute-done | bytes 393248 | tf_op jit(solution)/shard_map/ppermute | solution.py:32
  143.4 9.0 %collective-permute-done.27 = bf16[32,6144]{1,0:T(8,128)(2,1)S(1)} collective-permute-done((bf16[32,6144]{1,0:T(8,128)(2,1)S(1)}, bf16[32,6144]{1,0:T(8,128)(2,1)S(1)}, u32[]{:S(2)}, u32[]{:S(2)}) %collective-permute-start.27) | collective-permute-done | bytes 393248 | tf_op jit(solution)/shard_map/ppermute | solution.py:32
  152.4 9.0 %collective-permute-done.5 = bf16[32,6144]{1,0:T(8,128)(2,1)S(1)} collective-permute-done((bf16[32,6144]{1,0:T(8,128)(2,1)S(1)}, bf16[32,6144]{1,0:T(8,128)(2,1)S(1)}, u32[]{:S(2)}, u32[]{:S(2)}) %collective-permute-start.5) | collective-permute-done | bytes 393248 | tf_op jit(solution)/shard_map/ppermute | solution.py:32
  162.0 7.2 %collective-permute-done.11 = bf16[32,6144]{1,0:T(8,128)(2,1)S(1)} collective-permute-done((bf16[32,6144]{1,0:T(8,128)(2,1)S(1)}, bf16[32,6144]{1,0:T(8,128)(2,1)S(1)}, u32[]{:S(2)}, u32[]{:S(2)}) %collective-permute-start.11) | collective-permute-done | bytes 393248 | tf_op jit(solution)/shard_map/ppermute | solution.py:32
  169.2 9.0 %collective-permute-done.15 = bf16[32,6144]{1,0:T(8,128)(2,1)S(1)} collective-permute-done((bf16[32,6144]{1,0:T(8,128)(2,1)S(1)}, bf16[32,6144]{1,0:T(8,128)(2,1)S(1)}, u32[]{:S(2)}, u32[]{:S(2)}) %collective-permute-start.15) | collective-permute-done | bytes 393248 | tf_op jit(solution)/shard_map/ppermute | solution.py:32
  178.1 7.7 %collective-permute-done.21 = bf16[32,6144]{1,0:T(8,128)(2,1)S(1)} collective-permute-done((bf16[32,6144]{1,0:T(8,128)(2,1)S(1)}, bf16[32,6144]{1,0:T(8,128)(2,1)S(1)}, u32[]{:S(2)}, u32[]{:S(2)}) %collective-permute-start.21) | collective-permute-done | bytes 393248 | tf_op jit(solution)/shard_map/ppermute | solution.py:32
  189.6 4.4 %fusion.78 = f32[256,384]{1,0:T(8,128)S(1)} fusion(bf16[256,6144]{1,0:T(8,128)(2,1)S(1)} %constant_dynamic-update-slice_fusion.12, bf16[6144,384]{1,0:T(8,128)(2,1)} %collective-permute-done.22), kind=kOutput, calls=%fused_computation.168 | convolution fusion | flops 1207959552 | bytes 8257536 | tf_op jit(solution)/shard_map/dot_general | solution.py:159
  205.3 5.7 %collective-permute-done.31 = bf16[512,128]{0,1:T(8,128)(2,1)S(1)} collective-permute-done((bf16[512,128]{0,1:T(8,128)(2,1)S(1)}, bf16[512,128]{0,1:T(8,128)(2,1)S(1)}, u32[]{:S(2)}, u32[]{:S(2)}) %collective-permute-start.31) | collective-permute-done | bytes 131104 | tf_op jit(solution)/shard_map/ppermute | solution.py:32
  232.4 4.1 %collective-permute-done.44 = bf16[64,3072]{1,0:T(8,128)(2,1)S(1)} collective-permute-done((bf16[64,3072]{1,0:T(8,128)(2,1)S(1)}, bf16[64,3072]{1,0:T(8,128)(2,1)S(1)}, u32[]{:S(2)}, u32[]{:S(2)}) %collective-permute-start.44) | collective-permute-done | bytes 393248 | tf_op jit(solution)/shard_map/ppermute | solution.py:32
  (179 shorter events, 100.2 us)
Async XLA Ops:
  8.7 177.2 %collective-permute-start.22 = (bf16[6144,384]{1,0:T(8,128)(2,1)}, bf16[6144,384]{1,0:T(8,128)(2,1)}, u32[]{:S(2)}, u32[]{:S(2)}) collective-permute-start(bf16[6144,384]{1,0:T(8,128)(2,1)} %dynamic-slice_bitcast_fusion), channel_id=1, source_target_pairs={{0,1},{1,0},{2,3},{3,2},{4,5},{5,4},{6,7},{7,6},{8,9},{9,8},{10,11... | collective-permute-start | bytes 14155784 | tf_op jit(solution)/shard_map/ppermute | solution.py:32
  9.3 8.5 %collective-permute-start.1 = (bf16[16,6144]{1,0:T(8,128)(2,1)S(1)}, bf16[16,6144]{1,0:T(8,128)(2,1)S(1)}, u32[]{:S(2)}, u32[]{:S(2)}) collective-permute-start(bf16[16,6144]{1,0:T(8,128)(2,1)S(1)} %maximum_select_fusion), channel_id=1, source_target_pairs={{0,8},{1,9},{2,10},{3,11},{4,12},{5,13},{6,14},{7,15},{8,0},{9,1},... | collective-permute-start | bytes 589832 | tf_op jit(solution)/shard_map/ppermute | solution.py:32
  14.2 196.9 %collective-permute-start.33 = (bf16[128,3072]{1,0:T(8,128)(2,1)}, bf16[128,3072]{1,0:T(8,128)(2,1)}, u32[]{:S(2)}, u32[]{:S(2)}) collective-permute-start(bf16[128,3072]{1,0:T(8,128)(2,1)} %get-tuple-element.20), channel_id=1, source_target_pairs={{0,1},{1,0},{2,3},{3,2},{4,5},{5,4},{6,7},{7,6},{8,9},{9,8},{10,11... | collective-permute-start | bytes 2359304 | tf_op jit(solution)/shard_map/ppermute | solution.py:32
  14.2 196.9 %collective-permute-start.34 = (bf16[128,3072]{1,0:T(8,128)(2,1)}, bf16[128,3072]{1,0:T(8,128)(2,1)}, u32[]{:S(2)}, u32[]{:S(2)}) collective-permute-start(bf16[128,3072]{1,0:T(8,128)(2,1)} %get-tuple-element.22), channel_id=1, source_target_pairs={{0,8},{1,9},{2,10},{3,11},{4,12},{5,13},{6,14},{7,15},{8,0},{9,1},... | collective-permute-start | bytes 2359304 | tf_op jit(solution)/shard_map/ppermute | solution.py:32
  29.0 8.2 %collective-permute-start.8 = (bf16[8,6144]{1,0:T(8,128)(2,1)S(1)}, bf16[8,6144]{1,0:T(8,128)(2,1)S(1)}, u32[]{:S(2)}, u32[]{:S(2)}) collective-permute-start(bf16[8,6144]{1,0:T(8,128)(2,1)S(1)} %collective-permute-done.6), channel_id=1, source_target_pairs={{0,2},{1,3},{2,4},{3,5},{4,6},{5,7},{6,0},{7,1},{8,10},{9,11},{10,... | collective-permute-start | bytes 294920 | tf_op jit(solution)/shard_map/ppermute | solution.py:32
  46.2 164.8 %collective-permute-start.35 = (bf16[128,3072]{1,0:T(8,128)(2,1)S(1)}, bf16[128,3072]{1,0:T(8,128)(2,1)S(1)}, u32[]{:S(2)}, u32[]{:S(2)}) collective-permute-start(bf16[128,3072]{1,0:T(8,128)(2,1)S(1)} %copy-done.2), channel_id=1, source_target_pairs={{0,9},{1,8},{2,11},{3,10},{4,13},{5,12},{6,15},{7,14},{8,1},{9,0},... | collective-permute-start | bytes 2359304 | tf_op jit(solution)/shard_map/ppermute | solution.py:32
  72.0 9.6 %collective-permute-start.24 = (bf16[32,6144]{1,0:T(8,128)(2,1)S(1)}, bf16[32,6144]{1,0:T(8,128)(2,1)S(1)}, u32[]{:S(2)}, u32[]{:S(2)}) collective-permute-start(bf16[32,6144]{1,0:T(8,128)(2,1)S(1)} %pad_maximum_fusion.5), channel_id=1, source_target_pairs={{0,48},{1,49},{2,50},{3,51},{4,52},{5,53},{6,54},{7,55},{8,56},{9,... | collective-permute-start | bytes 1179656 | tf_op jit(solution)/shard_map/ppermute | solution.py:32
  81.6 10.0 %collective-permute-start.10 = (bf16[32,6144]{1,0:T(8,128)(2,1)S(1)}, bf16[32,6144]{1,0:T(8,128)(2,1)S(1)}, u32[]{:S(2)}, u32[]{:S(2)}) collective-permute-start(bf16[32,6144]{1,0:T(8,128)(2,1)S(1)} %get-tuple-element.59), channel_id=1, source_target_pairs={{0,48},{1,49},{2,50},{3,51},{4,52},{5,53},{6,54},{7,55},{8,56},{9,... | collective-permute-start | bytes 1179656 | tf_op jit(solution)/shard_map/ppermute | solution.py:32
  91.6 10.3 %collective-permute-start.4 = (bf16[32,6144]{1,0:T(8,128)(2,1)S(1)}, bf16[32,6144]{1,0:T(8,128)(2,1)S(1)}, u32[]{:S(2)}, u32[]{:S(2)}) collective-permute-start(bf16[32,6144]{1,0:T(8,128)(2,1)S(1)} %pad_maximum_fusion.5), channel_id=1, source_target_pairs={{0,16},{1,17},{2,18},{3,19},{4,20},{5,21},{6,22},{7,23},{8,24},{9,... | collective-permute-start | bytes 1179656 | tf_op jit(solution)/shard_map/ppermute | solution.py:32
  101.9 9.0 %collective-permute-start.25 = (bf16[32,6144]{1,0:T(8,128)(2,1)S(1)}, bf16[32,6144]{1,0:T(8,128)(2,1)S(1)}, u32[]{:S(2)}, u32[]{:S(2)}) collective-permute-start(bf16[32,6144]{1,0:T(8,128)(2,1)S(1)} %get-tuple-element.59), channel_id=1, source_target_pairs={{0,16},{1,17},{2,18},{3,19},{4,20},{5,21},{6,22},{7,23},{8,24},{9,... | collective-permute-start | bytes 1179656 | tf_op jit(solution)/shard_map/ppermute | solution.py:32
  110.9 10.2 %collective-permute-start.26 = (bf16[32,6144]{1,0:T(8,128)(2,1)S(1)}, bf16[32,6144]{1,0:T(8,128)(2,1)S(1)}, u32[]{:S(2)}, u32[]{:S(2)}) collective-permute-start(bf16[32,6144]{1,0:T(8,128)(2,1)S(1)} %pad_maximum_fusion.6), channel_id=1, source_target_pairs={{0,6},{1,7},{2,0},{3,1},{4,2},{5,3},{6,4},{7,5},{8,14},{9,15},{10,... | collective-permute-start | bytes 1179656 | tf_op jit(solution)/shard_map/ppermute | solution.py:32
  121.1 9.0 %collective-permute-start.20 = (bf16[32,6144]{1,0:T(8,128)(2,1)S(1)}, bf16[32,6144]{1,0:T(8,128)(2,1)S(1)}, u32[]{:S(2)}, u32[]{:S(2)}) collective-permute-start(bf16[32,6144]{1,0:T(8,128)(2,1)S(1)} %get-tuple-element.51), channel_id=1, source_target_pairs={{0,6},{1,7},{2,0},{3,1},{4,2},{5,3},{6,4},{7,5},{8,14},{9,15},{10,... | collective-permute-start | bytes 1179656 | tf_op jit(solution)/shard_map/ppermute | solution.py:32
  130.1 13.2 %collective-permute-start.14 = (bf16[32,6144]{1,0:T(8,128)(2,1)S(1)}, bf16[32,6144]{1,0:T(8,128)(2,1)S(1)}, u32[]{:S(2)}, u32[]{:S(2)}) collective-permute-start(bf16[32,6144]{1,0:T(8,128)(2,1)S(1)} %pad_maximum_fusion.6), channel_id=1, source_target_pairs={{0,2},{1,3},{2,4},{3,5},{4,6},{5,7},{6,0},{7,1},{8,10},{9,11},{10,... | collective-permute-start | bytes 1179656 | tf_op jit(solution)/shard_map/ppermute | solution.py:32
  143.4 9.0 %collective-permute-start.27 = (bf16[32,6144]{1,0:T(8,128)(2,1)S(1)}, bf16[32,6144]{1,0:T(8,128)(2,1)S(1)}, u32[]{:S(2)}, u32[]{:S(2)}) collective-permute-start(bf16[32,6144]{1,0:T(8,128)(2,1)S(1)} %get-tuple-element.51), channel_id=1, source_target_pairs={{0,2},{1,3},{2,4},{3,5},{4,6},{5,7},{6,0},{7,1},{8,10},{9,11},{10,... | collective-permute-start | bytes 1179656 | tf_op jit(solution)/shard_map/ppermute | solution.py:32
  152.4 9.0 %collective-permute-start.5 = (bf16[32,6144]{1,0:T(8,128)(2,1)S(1)}, bf16[32,6144]{1,0:T(8,128)(2,1)S(1)}, u32[]{:S(2)}, u32[]{:S(2)}) collective-permute-start(bf16[32,6144]{1,0:T(8,128)(2,1)S(1)} %collective-permute-done.4), channel_id=1, source_target_pairs={{0,16},{1,17},{2,18},{3,19},{4,20},{5,21},{6,22},{7,23},{8,24},{9,... | collective-permute-start | bytes 1179656 | tf_op jit(solution)/shard_map/ppermute | solution.py:32
  169.1 9.0 %collective-permute-start.15 = (bf16[32,6144]{1,0:T(8,128)(2,1)S(1)}, bf16[32,6144]{1,0:T(8,128)(2,1)S(1)}, u32[]{:S(2)}, u32[]{:S(2)}) collective-permute-start(bf16[32,6144]{1,0:T(8,128)(2,1)S(1)} %collective-permute-done.14), channel_id=1, source_target_pairs={{0,2},{1,3},{2,4},{3,5},{4,6},{5,7},{6,0},{7,1},{8,10},{9,11},{10,... | collective-permute-start | bytes 1179656 | tf_op jit(solution)/shard_map/ppermute | solution.py:32
  189.5 8.2 %collective-permute-start.23 = (f32[128,384]{1,0:T(8,128)S(1)}, f32[128,384]{1,0:T(8,128)S(1)}, u32[]{:S(2)}, u32[]{:S(2)}) collective-permute-start(f32[128,384]{1,0:T(8,128)S(1)} %fusion.77), channel_id=1, source_target_pairs={{0,1},{1,0},{2,3},{3,2},{4,5},{5,4},{6,7},{7,6},{8,9},{9,8},{10,11... | collective-permute-start | bytes 589832 | tf_op jit(solution)/shard_map/ppermute | solution.py:32
  214.4 9.4 %collective-permute-start.36 = (bf16[32,3072]{1,0:T(8,128)(2,1)S(1)}, bf16[32,3072]{1,0:T(8,128)(2,1)S(1)}, u32[]{:S(2)}, u32[]{:S(2)}) collective-permute-start(bf16[32,3072]{1,0:T(8,128)(2,1)S(1)} %get-tuple-element.27), channel_id=1, source_target_pairs={{0,16},{1,17},{2,18},{3,19},{4,20},{5,21},{6,22},{7,23},{8,24},{9,... | collective-permute-start | bytes 589832 | tf_op jit(solution)/shard_map/ppermute | solution.py:32
  214.5 9.4 %collective-permute-start.38 = (bf16[32,3072]{1,0:T(8,128)(2,1)S(1)}, bf16[32,3072]{1,0:T(8,128)(2,1)S(1)}, u32[]{:S(2)}, u32[]{:S(2)}) collective-permute-start(bf16[32,3072]{1,0:T(8,128)(2,1)S(1)} %get-tuple-element.30), channel_id=1, source_target_pairs={{0,48},{1,49},{2,50},{3,51},{4,52},{5,53},{6,54},{7,55},{8,56},{9,... | collective-permute-start | bytes 589832 | tf_op jit(solution)/shard_map/ppermute | solution.py:32
  225.6 11.0 %collective-permute-start.44 = (bf16[64,3072]{1,0:T(8,128)(2,1)S(1)}, bf16[64,3072]{1,0:T(8,128)(2,1)S(1)}, u32[]{:S(2)}, u32[]{:S(2)}) collective-permute-start(bf16[64,3072]{1,0:T(8,128)(2,1)S(1)} %pad_maximum_fusion.9), channel_id=1, source_target_pairs={{0,2},{1,3},{2,4},{3,5},{4,6},{5,7},{6,0},{7,1},{8,10},{9,11},{10,... | collective-permute-start | bytes 1179656 | tf_op jit(solution)/shard_map/ppermute | solution.py:32
  225.7 10.9 %collective-permute-start.46 = (bf16[64,3072]{1,0:T(8,128)(2,1)S(1)}, bf16[64,3072]{1,0:T(8,128)(2,1)S(1)}, u32[]{:S(2)}, u32[]{:S(2)}) collective-permute-start(bf16[64,3072]{1,0:T(8,128)(2,1)S(1)} %pad_maximum_fusion.10), channel_id=1, source_target_pairs={{0,6},{1,7},{2,0},{3,1},{4,2},{5,3},{6,4},{7,5},{8,14},{9,15},{10,... | collective-permute-start | bytes 1179656 | tf_op jit(solution)/shard_map/ppermute | solution.py:32
  229.0 10.4 %collective-permute-start.37 = (bf16[64,3072]{1,0:T(8,128)(2,1)S(1)}, bf16[64,3072]{1,0:T(8,128)(2,1)S(1)}, u32[]{:S(2)}, u32[]{:S(2)}) collective-permute-start(bf16[64,3072]{1,0:T(8,128)(2,1)S(1)} %pad_maximum_fusion.7), channel_id=1, source_target_pairs={{0,16},{1,17},{2,18},{3,19},{4,20},{5,21},{6,22},{7,23},{8,24},{9,... | collective-permute-start | bytes 1179656 | tf_op jit(solution)/shard_map/ppermute | solution.py:32
  229.1 10.3 %collective-permute-start.39 = (bf16[64,3072]{1,0:T(8,128)(2,1)S(1)}, bf16[64,3072]{1,0:T(8,128)(2,1)S(1)}, u32[]{:S(2)}, u32[]{:S(2)}) collective-permute-start(bf16[64,3072]{1,0:T(8,128)(2,1)S(1)} %pad_maximum_fusion.8), channel_id=1, source_target_pairs={{0,48},{1,49},{2,50},{3,51},{4,52},{5,53},{6,54},{7,55},{8,56},{9,... | collective-permute-start | bytes 1179656 | tf_op jit(solution)/shard_map/ppermute | solution.py:32
  239.9 7.8 %collective-permute-start.41 = (bf16[16,3072]{1,0:T(8,128)(2,1)S(1)}, bf16[16,3072]{1,0:T(8,128)(2,1)S(1)}, u32[]{:S(2)}, u32[]{:S(2)}) collective-permute-start(bf16[16,3072]{1,0:T(8,128)(2,1)S(1)} %get-tuple-element.33), channel_id=1, source_target_pairs={{0,6},{1,7},{2,0},{3,1},{4,2},{5,3},{6,4},{7,5},{8,14},{9,15},{10,... | collective-permute-start | bytes 294920 | tf_op jit(solution)/shard_map/ppermute | solution.py:32
  (39 other events, 286.8 us)

commit v2 on v1

v2 whole, which is shorter than its diff:
```python
import math

import jax
import jax.numpy as jnp
import numpy as np
from jax import lax
from jax.sharding import PartitionSpec as P

RING = 4
AXES = ("pipe", "dp")


def split_place(index):
    core = index % 2
    y = index // 2 % 4
    half_x = index // 8 % 2
    z = index // 16 % 4
    pipe = index // 64
    return pipe, z, half_x, y, core


def join_place(pipe, z, half_x, y, core):
    return (((pipe * 4 + z) * 2 + half_x) * 4 + y) * 2 + core


def send(value, pipe=0, z=0, x=0, y=0, core=0):
    pairs = []
    for source in range(128):
        p0, z0, x0, y0, c0 = split_place(source)
        target = join_place(p0 ^ pipe, (z0 + z) % 4, x0 ^ x, (y0 + y) % 4, c0 ^ core)
        pairs.append((source, target))
    return lax.ppermute(value, AXES, pairs)


def normalize(section_rows, gain_vector):
    values = section_rows.astype(jnp.float32)
    centre = jnp.mean(values, axis=-1, keepdims=True)
    shifted = values - centre
    spread = jnp.mean(shifted * shifted, axis=-1, keepdims=True)
    return (shifted * lax.rsqrt(spread + 1e-05) * gain_vector).astype(jnp.bfloat16)


def onward(value, axis):
    pairs = []
    for source in range(128):
        pipe, z, half_x, y, core = split_place(source)
        step = 1 - 2 * core
        if axis == "z":
            z = (z + step) % RING
        else:
            y = (y + step) % RING
        pairs.append((source, join_place(pipe, z, half_x, y, core)))
    return lax.ppermute(value, AXES, pairs)


def both_onward(first, first_axis, second, second_axis, *beside):
    first, second = lax.optimization_barrier((first, second))
    first, second = onward(first, first_axis), onward(second, second_axis)
    return lax.optimization_barrier((first, second, *beside))


def both_scatter(first, first_axis, second, second_axis):
    narrow = jnp.bfloat16
    first_sum, second_sum = first[1].astype(narrow), second[1].astype(narrow)
    for k in (2, 3, 0):
        first_got, second_got = both_onward(
            first_sum, first_axis, second_sum, second_axis
        )
        first_sum = first[k] + first_got.astype(jnp.float32)
        second_sum = second[k] + second_got.astype(jnp.float32)
        if k:
            first_sum, second_sum = first_sum.astype(narrow), second_sum.astype(narrow)
    return first_sum, second_sum


def mirrored(value):
    blocks = value.reshape(4, 2, 4, 16, value.shape[1])
    blocks = jnp.stack([blocks[2], blocks[1], blocks[0], blocks[3]])
    blocks = jnp.stack(
        [blocks[:, :, 0], blocks[:, :, 3], blocks[:, :, 2], blocks[:, :, 1]], axis=2
    )
    return blocks.reshape(value.shape)


def token_positions(z, y, core):
    far = np.repeat(np.asarray([1, 2, 3, 0], np.int32), 128)
    side = np.tile(np.repeat(np.asarray([0, 1], np.int32), 64), 4)
    near = np.tile(np.repeat(np.arange(4, dtype=np.int32), 16), 8)
    low = np.tile(np.arange(16, dtype=np.int32), 32)
    step = 1 - 2 * core
    dz = np.where(side == 0, far, near)
    dy = np.where(side == 0, near, far)
    return (((z - step * dz) % 4 * 2 + side) * 4 + (y - step * dy) % 4) * 16 + low


def attend(projected, position, head_size):
    queries = projected[:, :head_size]
    keys_part = projected[:, head_size : 2 * head_size]
    values_part = projected[:, 2 * head_size :].astype(jnp.bfloat16)
    scores = jnp.einsum(
        "qd,kd->qk", queries, keys_part, precision=lax.Precision.HIGHEST
    ) / math.sqrt(head_size)
    causal = position[:, None] >= position[None, :]
    scores = jnp.where(causal, scores, -1e30)
    largest = jnp.max(scores, axis=-1, keepdims=True)
    weights = jnp.where(causal, jnp.exp(scores - largest), 0.0)
    totals = jnp.sum(weights, axis=-1, keepdims=True)
    probabilities = (weights / totals).astype(jnp.bfloat16)
    return jnp.dot(probabilities, values_part, preferred_element_type=jnp.float32).astype(
        jnp.bfloat16
    )


def shards(segment_input, norm_gain, head_weights, output_weights):
    head_size = output_weights.shape[1]
    width = segment_input.shape[2]
    half, quarter = width // 2, width // 4
    _, z, half_x, y, core = split_place(lax.axis_index("dp"))

    normed = normalize(segment_input[0], norm_gain[0])
    left, right = normed[:, :half], normed[:, half:]
    kept = jnp.where(core == 0, left, right)
    given = send(jnp.where(core == 0, right, left), core=1)
    block = jnp.where(
        core == 0, jnp.concatenate([kept, given]), jnp.concatenate([given, kept])
    )
    head_block, out_rows, block = lax.optimization_barrier(
        (head_weights[0, :, 0, :], output_weights[0], block)
    )
    other = send(block, x=1)
    first = jnp.where(half_x == 0, block, other)
    second = jnp.where(half_x == 0, other, block)
    own_weights = lax.dynamic_slice_in_dim(head_block, core * half, half, 0)
    swapped_weights = send(
        lax.dynamic_slice_in_dim(head_block, (1 - core) * half, half, 0), core=1
    )
    out_parts = []
    for dx, dc in ((0, 0), (0, 1), (1, 0), (1, 1)):
        start = ((half_x ^ dx) * 2 + (core ^ dc)) * quarter
        part = lax.dynamic_slice_in_dim(out_rows, start, quarter, 1)
        out_parts.append(send(part, x=dx, core=dc) if dx or dc else part)
    out_block = jnp.concatenate(out_parts, axis=0)

    first_near, second_near = [first], [second]
    for _ in range(3):
        got = both_onward(first_near[-1], "y", second_near[-1], "z")
        first_near.append(got[0])
        second_near.append(got[1])
    first_far = [jnp.concatenate(first_near)]
    second_far = [jnp.concatenate(second_near)]

    def project(rows):
        mine = jnp.dot(rows, own_weights, preferred_element_type=jnp.float32)
        theirs = jnp.dot(rows, swapped_weights, preferred_element_type=jnp.float32)
        return mine, theirs

    mine, theirs = [], []
    for k in range(4):
        here = project(jnp.concatenate([first_far[k], second_far[k]]))
        if k < 3:
            got = both_onward(first_far[k], "z", second_far[k], "y", *here)
            first_far.append(got[0])
            second_far.append(got[1])
            here = got[2:]
        mine.append(here[0])
        theirs.append(send(here[1], core=1))
    projected = []
    for k in (1, 2, 3, 0):
        back = theirs[-k % 4].reshape(2, 4, 16, -1)
        back = jnp.stack([back[:, 0], back[:, 3], back[:, 2], back[:, 1]], axis=1)
        projected.append(mine[k] + back.reshape(mine[k].shape))
    projected = jnp.concatenate(projected)

    attended = attend(projected, token_positions(z, y, core), head_size)
    across_x = send(attended, x=1)
    across_core = send(mirrored(attended), core=1)
    across_both = send(mirrored(across_x), core=1)
    heads = jnp.concatenate([attended, across_core, across_x, across_both], axis=1)

    edge = jnp.dot(heads[:128], out_block, preferred_element_type=jnp.float32)
    rest = jnp.dot(heads[128:], out_block, preferred_element_type=jnp.float32)
    first_sum, second_sum = both_scatter(
        (rest[256:320], edge[:64], rest[:64], rest[128:192]),
        "z",
        (rest[320:384], edge[64:], rest[64:128], rest[192:256]),
        "y",
    )
    first_rows, second_rows = both_scatter(
        first_sum.reshape(4, 16, quarter), "y", second_sum.reshape(4, 16, quarter), "z"
    )
    first_rows = first_rows.astype(jnp.bfloat16)
    second_rows = second_rows.astype(jnp.bfloat16)

    owners = jnp.stack([first_rows, second_rows]).reshape(2, 2, 8, quarter)
    by_x = jnp.where(half_x == 0, owners, owners[::-1])
    by_place = jnp.where(core == 0, by_x, by_x[:, ::-1])
    got = jnp.stack(
        [
            jnp.stack([send(by_place[dx, dc], pipe=1, x=dx, core=dc) for dc in (0, 1)])
            for dx in (0, 1)
        ]
    )
    got = jnp.where(core == 0, got, got[:, ::-1])
    got = jnp.where(half_x == 0, got, got[::-1])
    return jnp.concatenate([got[0, 0], got[0, 1], got[1, 0], got[1, 1]], axis=1)[None]


def solution(mesh):
    placed = (
        P("pipe", "dp", None),
        P("pipe", None),
        P("pipe", None, "dp", None),
        P("pipe", "dp", None),
    )
    return jax.shard_map(
        shards, mesh=mesh, in_specs=placed, out_specs=P("pipe", "dp", None), check_vma=False
    )
```

time: 263 us -> 160 us (0.61)
  waiting for transfers between devices: 165 us -> 98.2 us
  starting transfers between devices: 59.5 us -> 36.8 us
  matrix products: 21.3 us -> 12.2 us
  local copies, waits for them, and re-layouts: 7.58 us -> 3.86 us
    ppermute x54 -> x17, waiting for transfers between devices: 165 us -> 12.6 us  [send(): return lax.ppermute(value, AXES, pairs)]
    ppermute x0 -> x24, waiting for transfers between devices: none -> 85.6 us  [onward(): return lax.ppermute(value, AXES, pairs)]
    ppermute x54 -> x17, starting transfers between devices: 59.5 us -> 20.6 us  [send(): return lax.ppermute(value, AXES, pairs)]
    ppermute x0 -> x24, starting transfers between devices: none -> 16.2 us  [onward(): return lax.ppermute(value, AXES, pairs)]
    dot_general x3 -> x4, matrix products: 11.2 us -> 4.17 us  [project(): theirs = jnp.dot(rows, swapped_weights, preferred_element_type=jnp.float32)]
  transfers between devices with their start and end apart: 54 -> 41, of which waited for: 33 -> 31; matrix products, arithmetic and copies ran while one was open for 11% -> 10% of each run, Pallas kernels for 0% -> 0%
where the time goes in v2:
time: 160 us; the launch traced here: 158 us
  waiting for transfers between devices  98.2 us (61%)
  starting transfers between devices  36.8 us (23%)
  matrix products  12.2 us (8%)
  other arithmetic  6.55 us (4%)
  local copies, waits for them, and re-layouts  3.86 us (2%)
    ppermute x24, waiting for transfers between devices, onward(): return lax.ppermute(value, AXES, pairs)  85.6 us
    ppermute x17, starting transfers between devices, send(): return lax.ppermute(value, AXES, pairs)  20.6 us
    ppermute x24, starting transfers between devices, onward(): return lax.ppermute(value, AXES, pairs)  16.2 us
    ppermute x17, waiting for transfers between devices, send(): return lax.ppermute(value, AXES, pairs)  12.6 us
    dot_general x4, matrix products, project(): theirs = jnp.dot(rows, swapped_weights, preferred_element_type=jnp.float32)  4.17 us
    dot_general x4, matrix products, project(): mine = jnp.dot(rows, own_weights, preferred_element_type=jnp.float32)  4.16 us
  transfers between devices with their start and end apart: 41, of which 31 were waited for; matrix products, arithmetic and copies ran while one was open for 10% of the time, Pallas kernels for 0%

profile of v2, /device:TPU:0, one launch (start us, length us, event | category | flops | bytes accessed | tf_op | source)
XLA Modules:
  0.0 158.4 jit_solution(3866160060869818711)
XLA Ops:
  4.9 3.2 %collective-permute-start.1 = (bf16[16,6144]{1,0:T(8,128)(2,1)S(1)}, bf16[16,6144]{1,0:T(8,128)(2,1)S(1)}, u32[]{:S(2)}, u32[]{:S(2)}) collective-permute-start(bf16[16,6144]{1,0:T(8,128)(2,1)S(1)} %maximum_select_fusion), channel_id=1, source_target_pairs={{0,8},{1,9},{2,10},{3,11},{4,12},{5,13},{6,14},{7,15},{8,0},{9,1},... | collective-permute-start | bytes 589832 | tf_op jit(solution)/shard_map/ppermute | solution.py:32
  8.1 3.0 %constant_dynamic-slice_fusion.4 = bf16[6144,384]{1,0:T(8,128)(2,1)S(1)} fusion(bf16[12288,384]{1,0:T(8,128)(2,1)} %bitcast.80, s32[]{:T(128)S(6)} %select_n.136), kind=kLoop, calls=%fused_computation.135 | loop fusion | bytes 9437188 | tf_op jit(solution)/shard_map/dynamic_slice | solution.py:135
  11.1 2.3 %collective-permute-done.1 = bf16[16,6144]{1,0:T(8,128)(2,1)S(1)} collective-permute-done((bf16[16,6144]{1,0:T(8,128)(2,1)S(1)}, bf16[16,6144]{1,0:T(8,128)(2,1)S(1)}, u32[]{:S(2)}, u32[]{:S(2)}) %collective-permute-start.1) | collective-permute-done | bytes 196640 | tf_op jit(solution)/shard_map/ppermute | solution.py:32
  17.4 2.4 %collective-permute-start.22 = (bf16[128,3072]{1,0:T(8,128)(2,1)S(1)}, bf16[128,3072]{1,0:T(8,128)(2,1)S(1)}, u32[]{:S(2)}, u32[]{:S(2)}) collective-permute-start(bf16[128,3072]{1,0:T(8,128)(2,1)S(1)} %get-tuple-element.130), channel_id=1, source_target_pairs={{0,1},{1,0},{2,3},{3,2},{4,5},{5,4},{6,7},{7,6},{8,9},{9,8},{10,11... | collective-permute-start | bytes 2359304 | tf_op jit(solution)/shard_map/ppermute | solution.py:32
  19.8 3.0 %collective-permute-start.23 = (bf16[128,3072]{1,0:T(8,128)(2,1)S(1)}, bf16[128,3072]{1,0:T(8,128)(2,1)S(1)}, u32[]{:S(2)}, u32[]{:S(2)}) collective-permute-start(bf16[128,3072]{1,0:T(8,128)(2,1)S(1)} %get-tuple-element.129), channel_id=1, source_target_pairs={{0,8},{1,9},{2,10},{3,11},{4,12},{5,13},{6,14},{7,15},{8,0},{9,1},... | collective-permute-start | bytes 2359304 | tf_op jit(solution)/shard_map/ppermute | solution.py:32
  24.5 5.3 %collective-permute-done.4 = bf16[16,6144]{1,0:T(8,128)(2,1)S(1)} collective-permute-done((bf16[16,6144]{1,0:T(8,128)(2,1)S(1)}, bf16[16,6144]{1,0:T(8,128)(2,1)S(1)}, u32[]{:S(2)}, u32[]{:S(2)}) %collective-permute-start.4) | collective-permute-done | bytes 196640 | tf_op jit(solution)/shard_map/ppermute | solution.py:53
  32.7 5.6 %collective-permute-done.6 = bf16[16,6144]{1,0:T(8,128)(2,1)S(1)} collective-permute-done((bf16[16,6144]{1,0:T(8,128)(2,1)S(1)}, bf16[16,6144]{1,0:T(8,128)(2,1)S(1)}, u32[]{:S(2)}, u32[]{:S(2)}) %collective-permute-start.6) | collective-permute-done | bytes 196640 | tf_op jit(solution)/shard_map/ppermute | solution.py:53
  42.2 10.7 %collective-permute-done.8 = bf16[64,6144]{1,0:T(8,128)(2,1)S(1)} collective-permute-done((bf16[64,6144]{1,0:T(8,128)(2,1)S(1)}, bf16[64,6144]{1,0:T(8,128)(2,1)S(1)}, u32[]{:S(2)}, u32[]{:S(2)}) %collective-permute-start.8) | collective-permute-done | bytes 786464 | tf_op jit(solution)/shard_map/ppermute | solution.py:53
  55.6 10.8 %collective-permute-done.11 = bf16[64,6144]{1,0:T(8,128)(2,1)S(1)} collective-permute-done((bf16[64,6144]{1,0:T(8,128)(2,1)S(1)}, bf16[64,6144]{1,0:T(8,128)(2,1)S(1)}, u32[]{:S(2)}, u32[]{:S(2)}) %collective-permute-start.11) | collective-permute-done | bytes 786464 | tf_op jit(solution)/shard_map/ppermute | solution.py:53
  69.7 3.2 %collective-permute-start.24 = (bf16[128,3072]{1,0:T(8,128)(2,1)S(1)}, bf16[128,3072]{1,0:T(8,128)(2,1)S(1)}, u32[]{:S(2)}, u32[]{:S(2)}) collective-permute-start(bf16[128,3072]{1,0:T(8,128)(2,1)S(1)} %get-tuple-element.128), channel_id=1, source_target_pairs={{0,9},{1,8},{2,11},{3,10},{4,13},{5,12},{6,15},{7,14},{8,1},{9,0},... | collective-permute-start | bytes 2359304 | tf_op jit(solution)/shard_map/ppermute | solution.py:32
  72.9 7.0 %collective-permute-done.13 = bf16[64,6144]{1,0:T(8,128)(2,1)S(1)} collective-permute-done((bf16[64,6144]{1,0:T(8,128)(2,1)S(1)}, bf16[64,6144]{1,0:T(8,128)(2,1)S(1)}, u32[]{:S(2)}, u32[]{:S(2)}) %collective-permute-start.13) | collective-permute-done | bytes 786464 | tf_op jit(solution)/shard_map/ppermute | solution.py:53
  85.7 3.1 %collective-permute-start.20 = (bf16[512,128]{1,0:T(8,128)(2,1)S(1)}, bf16[512,128]{1,0:T(8,128)(2,1)S(1)}, u32[]{:S(2)}, u32[]{:S(2)}) collective-permute-start(bf16[512,128]{1,0:T(8,128)(2,1)S(1)} %convolution_convert_fusion.1), channel_id=1, source_target_pairs={{0,8},{1,9},{2,10},{3,11},{4,12},{5,13},{6,14},{7,15},{8,0},{9,1},... | collective-permute-start | bytes 393224 | tf_op jit(solution)/shard_map/ppermute | solution.py:32
  89.0 4.9 %collective-permute-done.20 = bf16[512,128]{1,0:T(8,128)(2,1)S(1)} collective-permute-done((bf16[512,128]{1,0:T(8,128)(2,1)S(1)}, bf16[512,128]{1,0:T(8,128)(2,1)S(1)}, u32[]{:S(2)}, u32[]{:S(2)}) %collective-permute-start.20) | collective-permute-done | bytes 131104 | tf_op jit(solution)/shard_map/ppermute | solution.py:32
  96.3 3.7 %collective-permute-start.25 = (bf16[64,3072]{1,0:T(8,128)(2,1)S(1)}, bf16[64,3072]{1,0:T(8,128)(2,1)S(1)}, u32[]{:S(2)}, u32[]{:S(2)}) collective-permute-start(bf16[64,3072]{1,0:T(8,128)(2,1)S(1)} %get-tuple-element.95), channel_id=1, source_target_pairs={{0,16},{1,49},{2,18},{3,51},{4,20},{5,53},{6,22},{7,55},{8,24},{9,... | collective-permute-start | bytes 1179656 | tf_op jit(solution)/shard_map/ppermute | solution.py:53
  101.5 3.8 %collective-permute-done.25 = bf16[64,3072]{1,0:T(8,128)(2,1)S(1)} collective-permute-done((bf16[64,3072]{1,0:T(8,128)(2,1)S(1)}, bf16[64,3072]{1,0:T(8,128)(2,1)S(1)}, u32[]{:S(2)}, u32[]{:S(2)}) %collective-permute-start.25) | collective-permute-done | bytes 393248 | tf_op jit(solution)/shard_map/ppermute | solution.py:53
  105.3 3.6 %collective-permute-done.26 = bf16[64,3072]{1,0:T(8,128)(2,1)S(1)} collective-permute-done((bf16[64,3072]{1,0:T(8,128)(2,1)S(1)}, bf16[64,3072]{1,0:T(8,128)(2,1)S(1)}, u32[]{:S(2)}, u32[]{:S(2)}) %collective-permute-start.26) | collective-permute-done | bytes 393248 | tf_op jit(solution)/shard_map/ppermute | solution.py:53
  109.5 8.6 %collective-permute-done.27 = bf16[64,3072]{1,0:T(8,128)(2,1)S(1)} collective-permute-done((bf16[64,3072]{1,0:T(8,128)(2,1)S(1)}, bf16[64,3072]{1,0:T(8,128)(2,1)S(1)}, u32[]{:S(2)}, u32[]{:S(2)}) %collective-permute-start.27) | collective-permute-done | bytes 393248 | tf_op jit(solution)/shard_map/ppermute | solution.py:53
  119.1 8.7 %collective-permute-done.29 = bf16[64,3072]{1,0:T(8,128)(2,1)S(1)} collective-permute-done((bf16[64,3072]{1,0:T(8,128)(2,1)S(1)}, bf16[64,3072]{1,0:T(8,128)(2,1)S(1)}, u32[]{:S(2)}, u32[]{:S(2)}) %collective-permute-start.29) | collective-permute-done | bytes 393248 | tf_op jit(solution)/shard_map/ppermute | solution.py:53
  128.8 5.4 %collective-permute-done.31 = bf16[16,3072]{1,0:T(8,128)(2,1)S(1)} collective-permute-done((bf16[16,3072]{1,0:T(8,128)(2,1)S(1)}, bf16[16,3072]{1,0:T(8,128)(2,1)S(1)}, u32[]{:S(2)}, u32[]{:S(2)}) %collective-permute-start.31) | collective-permute-done | bytes 98336 | tf_op jit(solution)/shard_map/ppermute | solution.py:53
  134.9 5.4 %collective-permute-done.33 = bf16[16,3072]{1,0:T(8,128)(2,1)S(1)} collective-permute-done((bf16[16,3072]{1,0:T(8,128)(2,1)S(1)}, bf16[16,3072]{1,0:T(8,128)(2,1)S(1)}, u32[]{:S(2)}, u32[]{:S(2)}) %collective-permute-start.33) | collective-permute-done | bytes 98336 | tf_op jit(solution)/shard_map/ppermute | solution.py:53
  140.5 2.6 %collective-permute-start.35 = (bf16[16,3072]{1,0:T(8,128)(2,1)S(1)}, bf16[16,3072]{1,0:T(8,128)(2,1)S(1)}, u32[]{:S(2)}, u32[]{:S(2)}) collective-permute-start(bf16[16,3072]{1,0:T(8,128)(2,1)S(1)} %fusion.31), channel_id=1, source_target_pairs={{0,2},{1,7},{2,4},{3,1},{4,6},{5,3},{6,0},{7,5},{8,10},{9,15},{10,... | collective-permute-start | bytes 294920 | tf_op jit(solution)/shard_map/ppermute | solution.py:53
  143.1 3.3 %collective-permute-done.35 = bf16[16,3072]{1,0:T(8,128)(2,1)S(1)} collective-permute-done((bf16[16,3072]{1,0:T(8,128)(2,1)S(1)}, bf16[16,3072]{1,0:T(8,128)(2,1)S(1)}, u32[]{:S(2)}, u32[]{:S(2)}) %collective-permute-start.35) | collective-permute-done | bytes 98336 | tf_op jit(solution)/shard_map/ppermute | solution.py:53
  146.4 2.5 %collective-permute-done.36 = bf16[16,3072]{1,0:T(8,128)(2,1)S(1)} collective-permute-done((bf16[16,3072]{1,0:T(8,128)(2,1)S(1)}, bf16[16,3072]{1,0:T(8,128)(2,1)S(1)}, u32[]{:S(2)}, u32[]{:S(2)}) %collective-permute-start.36) | collective-permute-done | bytes 98336 | tf_op jit(solution)/shard_map/ppermute | solution.py:53
  150.7 2.1 %collective-permute-start.39 = (bf16[8,3072]{1,0:T(8,128)(2,1)S(1)}, bf16[8,3072]{1,0:T(8,128)(2,1)S(1)}, u32[]{:S(2)}, u32[]{:S(2)}) collective-permute-start(bf16[8,3072]{1,0:T(8,128)(2,1)S(1)} %get-tuple-element.140), channel_id=1, source_target_pairs={{0,72},{1,73},{2,74},{3,75},{4,76},{5,77},{6,78},{7,79},{8,64},{9,... | collective-permute-start | bytes 147464 | tf_op jit(solution)/shard_map/ppermute | solution.py:32
  (149 shorter events, 43.5 us)
Async XLA Ops:
  4.9 8.5 %collective-permute-start.1 = (bf16[16,6144]{1,0:T(8,128)(2,1)S(1)}, bf16[16,6144]{1,0:T(8,128)(2,1)S(1)}, u32[]{:S(2)}, u32[]{:S(2)}) collective-permute-start(bf16[16,6144]{1,0:T(8,128)(2,1)S(1)} %maximum_select_fusion), channel_id=1, source_target_pairs={{0,8},{1,9},{2,10},{3,11},{4,12},{5,13},{6,14},{7,15},{8,0},{9,1},... | collective-permute-start | bytes 589832 | tf_op jit(solution)/shard_map/ppermute | solution.py:32
  11.0 30.2 %collective-permute-start.10 = (bf16[6144,384]{1,0:T(8,128)(2,1)S(1)}, bf16[6144,384]{1,0:T(8,128)(2,1)S(1)}, u32[]{:S(2)}, u32[]{:S(2)}) collective-permute-start(bf16[6144,384]{1,0:T(8,128)(2,1)S(1)} %constant_dynamic-slice_fusion.4), channel_id=1, source_target_pairs={{0,1},{1,0},{2,3},{3,2},{4,5},{5,4},{6,7},{7,6},{8,9},{9,8},{10,11... | collective-permute-start | bytes 14155784 | tf_op jit(solution)/shard_map/ppermute | solution.py:32
  13.5 9.3 %collective-permute-start.2 = (bf16[16,6144]{1,0:T(8,128)(2,1)S(1)}, bf16[16,6144]{1,0:T(8,128)(2,1)S(1)}, u32[]{:S(2)}, u32[]{:S(2)}) collective-permute-start(bf16[16,6144]{1,0:T(8,128)(2,1)S(1)} %get-tuple-element.63), channel_id=1, source_target_pairs={{0,2},{1,7},{2,4},{3,1},{4,6},{5,3},{6,0},{7,5},{8,10},{9,15},{10,... | collective-permute-start | bytes 589832 | tf_op jit(solution)/shard_map/ppermute | solution.py:53
  15.2 7.7 %collective-permute-start.3 = (bf16[16,6144]{1,0:T(8,128)(2,1)S(1)}, bf16[16,6144]{1,0:T(8,128)(2,1)S(1)}, u32[]{:S(2)}, u32[]{:S(2)}) collective-permute-start(bf16[16,6144]{1,0:T(8,128)(2,1)S(1)} %get-tuple-element.64), channel_id=1, source_target_pairs={{0,16},{1,49},{2,18},{3,51},{4,20},{5,53},{6,22},{7,55},{8,24},{9,... | collective-permute-start | bytes 589832 | tf_op jit(solution)/shard_map/ppermute | solution.py:53
  17.4 76.7 %collective-permute-start.22 = (bf16[128,3072]{1,0:T(8,128)(2,1)S(1)}, bf16[128,3072]{1,0:T(8,128)(2,1)S(1)}, u32[]{:S(2)}, u32[]{:S(2)}) collective-permute-start(bf16[128,3072]{1,0:T(8,128)(2,1)S(1)} %get-tuple-element.130), channel_id=1, source_target_pairs={{0,1},{1,0},{2,3},{3,2},{4,5},{5,4},{6,7},{7,6},{8,9},{9,8},{10,11... | collective-permute-start | bytes 2359304 | tf_op jit(solution)/shard_map/ppermute | solution.py:32
  19.8 74.3 %collective-permute-start.23 = (bf16[128,3072]{1,0:T(8,128)(2,1)S(1)}, bf16[128,3072]{1,0:T(8,128)(2,1)S(1)}, u32[]{:S(2)}, u32[]{:S(2)}) collective-permute-start(bf16[128,3072]{1,0:T(8,128)(2,1)S(1)} %get-tuple-element.129), channel_id=1, source_target_pairs={{0,8},{1,9},{2,10},{3,11},{4,12},{5,13},{6,14},{7,15},{8,0},{9,1},... | collective-permute-start | bytes 2359304 | tf_op jit(solution)/shard_map/ppermute | solution.py:32
  22.9 6.9 %collective-permute-start.4 = (bf16[16,6144]{1,0:T(8,128)(2,1)S(1)}, bf16[16,6144]{1,0:T(8,128)(2,1)S(1)}, u32[]{:S(2)}, u32[]{:S(2)}) collective-permute-start(bf16[16,6144]{1,0:T(8,128)(2,1)S(1)} %collective-permute-done.2), channel_id=1, source_target_pairs={{0,2},{1,7},{2,4},{3,1},{4,6},{5,3},{6,0},{7,5},{8,10},{9,15},{10,... | collective-permute-start | bytes 589832 | tf_op jit(solution)/shard_map/ppermute | solution.py:53
  24.5 6.9 %collective-permute-start.5 = (bf16[16,6144]{1,0:T(8,128)(2,1)S(1)}, bf16[16,6144]{1,0:T(8,128)(2,1)S(1)}, u32[]{:S(2)}, u32[]{:S(2)}) collective-permute-start(bf16[16,6144]{1,0:T(8,128)(2,1)S(1)} %collective-permute-done.3), channel_id=1, source_target_pairs={{0,16},{1,49},{2,18},{3,51},{4,20},{5,53},{6,22},{7,55},{8,24},{9,... | collective-permute-start | bytes 589832 | tf_op jit(solution)/shard_map/ppermute | solution.py:53
  31.4 6.9 %collective-permute-start.6 = (bf16[16,6144]{1,0:T(8,128)(2,1)S(1)}, bf16[16,6144]{1,0:T(8,128)(2,1)S(1)}, u32[]{:S(2)}, u32[]{:S(2)}) collective-permute-start(bf16[16,6144]{1,0:T(8,128)(2,1)S(1)} %collective-permute-done.4), channel_id=1, source_target_pairs={{0,2},{1,7},{2,4},{3,1},{4,6},{5,3},{6,0},{7,5},{8,10},{9,15},{10,... | collective-permute-start | bytes 589832 | tf_op jit(solution)/shard_map/ppermute | solution.py:53
  32.7 6.9 %collective-permute-start.7 = (bf16[16,6144]{1,0:T(8,128)(2,1)S(1)}, bf16[16,6144]{1,0:T(8,128)(2,1)S(1)}, u32[]{:S(2)}, u32[]{:S(2)}) collective-permute-start(bf16[16,6144]{1,0:T(8,128)(2,1)S(1)} %collective-permute-done.5), channel_id=1, source_target_pairs={{0,16},{1,49},{2,18},{3,51},{4,20},{5,53},{6,22},{7,55},{8,24},{9,... | collective-permute-start | bytes 589832 | tf_op jit(solution)/shard_map/ppermute | solution.py:53
  39.7 13.3 %collective-permute-start.8 = (bf16[64,6144]{1,0:T(8,128)(2,1)S(1)}, bf16[64,6144]{1,0:T(8,128)(2,1)S(1)}, u32[]{:S(2)}, u32[]{:S(2)}) collective-permute-start(bf16[64,6144]{1,0:T(8,128)(2,1)S(1)} %get-tuple-element.75), channel_id=1, source_target_pairs={{0,16},{1,49},{2,18},{3,51},{4,20},{5,53},{6,22},{7,55},{8,24},{9,... | collective-permute-start | bytes 2359304 | tf_op jit(solution)/shard_map/ppermute | solution.py:53
  39.7 13.3 %collective-permute-start.9 = (bf16[64,6144]{1,0:T(8,128)(2,1)S(1)}, bf16[64,6144]{1,0:T(8,128)(2,1)S(1)}, u32[]{:S(2)}, u32[]{:S(2)}) collective-permute-start(bf16[64,6144]{1,0:T(8,128)(2,1)S(1)} %get-tuple-element.76), channel_id=1, source_target_pairs={{0,2},{1,7},{2,4},{3,1},{4,6},{5,3},{6,0},{7,5},{8,10},{9,15},{10,... | collective-permute-start | bytes 2359304 | tf_op jit(solution)/shard_map/ppermute | solution.py:53
  53.1 13.3 %collective-permute-start.11 = (bf16[64,6144]{1,0:T(8,128)(2,1)S(1)}, bf16[64,6144]{1,0:T(8,128)(2,1)S(1)}, u32[]{:S(2)}, u32[]{:S(2)}) collective-permute-start(bf16[64,6144]{1,0:T(8,128)(2,1)S(1)} %collective-permute-done.8), channel_id=1, source_target_pairs={{0,16},{1,49},{2,18},{3,51},{4,20},{5,53},{6,22},{7,55},{8,24},{9,... | collective-permute-start | bytes 2359304 | tf_op jit(solution)/shard_map/ppermute | solution.py:53
  53.2 13.3 %collective-permute-start.12 = (bf16[64,6144]{1,0:T(8,128)(2,1)S(1)}, bf16[64,6144]{1,0:T(8,128)(2,1)S(1)}, u32[]{:S(2)}, u32[]{:S(2)}) collective-permute-start(bf16[64,6144]{1,0:T(8,128)(2,1)S(1)} %collective-permute-done.9), channel_id=1, source_target_pairs={{0,2},{1,7},{2,4},{3,1},{4,6},{5,3},{6,0},{7,5},{8,10},{9,15},{10,... | collective-permute-start | bytes 2359304 | tf_op jit(solution)/shard_map/ppermute | solution.py:53
  66.6 13.3 %collective-permute-start.13 = (bf16[64,6144]{1,0:T(8,128)(2,1)S(1)}, bf16[64,6144]{1,0:T(8,128)(2,1)S(1)}, u32[]{:S(2)}, u32[]{:S(2)}) collective-permute-start(bf16[64,6144]{1,0:T(8,128)(2,1)S(1)} %collective-permute-done.11), channel_id=1, source_target_pairs={{0,16},{1,49},{2,18},{3,51},{4,20},{5,53},{6,22},{7,55},{8,24},{9,... | collective-permute-start | bytes 2359304 | tf_op jit(solution)/shard_map/ppermute | solution.py:53
  67.5 13.2 %collective-permute-start.14 = (bf16[64,6144]{1,0:T(8,128)(2,1)S(1)}, bf16[64,6144]{1,0:T(8,128)(2,1)S(1)}, u32[]{:S(2)}, u32[]{:S(2)}) collective-permute-start(bf16[64,6144]{1,0:T(8,128)(2,1)S(1)} %collective-permute-done.12), channel_id=1, source_target_pairs={{0,2},{1,7},{2,4},{3,1},{4,6},{5,3},{6,0},{7,5},{8,10},{9,15},{10,... | collective-permute-start | bytes 2359304 | tf_op jit(solution)/shard_map/ppermute | solution.py:53
  69.7 24.4 %collective-permute-start.24 = (bf16[128,3072]{1,0:T(8,128)(2,1)S(1)}, bf16[128,3072]{1,0:T(8,128)(2,1)S(1)}, u32[]{:S(2)}, u32[]{:S(2)}) collective-permute-start(bf16[128,3072]{1,0:T(8,128)(2,1)S(1)} %get-tuple-element.128), channel_id=1, source_target_pairs={{0,9},{1,8},{2,11},{3,10},{4,13},{5,12},{6,15},{7,14},{8,1},{9,0},... | collective-permute-start | bytes 2359304 | tf_op jit(solution)/shard_map/ppermute | solution.py:32
  85.7 8.2 %collective-permute-start.20 = (bf16[512,128]{1,0:T(8,128)(2,1)S(1)}, bf16[512,128]{1,0:T(8,128)(2,1)S(1)}, u32[]{:S(2)}, u32[]{:S(2)}) collective-permute-start(bf16[512,128]{1,0:T(8,128)(2,1)S(1)} %convolution_convert_fusion.1), channel_id=1, source_target_pairs={{0,8},{1,9},{2,10},{3,11},{4,12},{5,13},{6,14},{7,15},{8,0},{9,1},... | collective-permute-start | bytes 393224 | tf_op jit(solution)/shard_map/ppermute | solution.py:32
  96.3 9.1 %collective-permute-start.25 = (bf16[64,3072]{1,0:T(8,128)(2,1)S(1)}, bf16[64,3072]{1,0:T(8,128)(2,1)S(1)}, u32[]{:S(2)}, u32[]{:S(2)}) collective-permute-start(bf16[64,3072]{1,0:T(8,128)(2,1)S(1)} %get-tuple-element.95), channel_id=1, source_target_pairs={{0,16},{1,49},{2,18},{3,51},{4,20},{5,53},{6,22},{7,55},{8,24},{9,... | collective-permute-start | bytes 1179656 | tf_op jit(solution)/shard_map/ppermute | solution.py:53
  100.0 9.0 %collective-permute-start.26 = (bf16[64,3072]{1,0:T(8,128)(2,1)S(1)}, bf16[64,3072]{1,0:T(8,128)(2,1)S(1)}, u32[]{:S(2)}, u32[]{:S(2)}) collective-permute-start(bf16[64,3072]{1,0:T(8,128)(2,1)S(1)} %get-tuple-element.96), channel_id=1, source_target_pairs={{0,2},{1,7},{2,4},{3,1},{4,6},{5,3},{6,0},{7,5},{8,10},{9,15},{10,... | collective-permute-start | bytes 1179656 | tf_op jit(solution)/shard_map/ppermute | solution.py:53
  109.1 9.1 %collective-permute-start.27 = (bf16[64,3072]{1,0:T(8,128)(2,1)S(1)}, bf16[64,3072]{1,0:T(8,128)(2,1)S(1)}, u32[]{:S(2)}, u32[]{:S(2)}) collective-permute-start(bf16[64,3072]{1,0:T(8,128)(2,1)S(1)} %get-tuple-element.99), channel_id=1, source_target_pairs={{0,16},{1,49},{2,18},{3,51},{4,20},{5,53},{6,22},{7,55},{8,24},{9,... | collective-permute-start | bytes 1179656 | tf_op jit(solution)/shard_map/ppermute | solution.py:53
  109.5 9.0 %collective-permute-start.28 = (bf16[64,3072]{1,0:T(8,128)(2,1)S(1)}, bf16[64,3072]{1,0:T(8,128)(2,1)S(1)}, u32[]{:S(2)}, u32[]{:S(2)}) collective-permute-start(bf16[64,3072]{1,0:T(8,128)(2,1)S(1)} %get-tuple-element.100), channel_id=1, source_target_pairs={{0,2},{1,7},{2,4},{3,1},{4,6},{5,3},{6,0},{7,5},{8,10},{9,15},{10,... | collective-permute-start | bytes 1179656 | tf_op jit(solution)/shard_map/ppermute | solution.py:53
  118.7 9.1 %collective-permute-start.29 = (bf16[64,3072]{1,0:T(8,128)(2,1)S(1)}, bf16[64,3072]{1,0:T(8,128)(2,1)S(1)}, u32[]{:S(2)}, u32[]{:S(2)}) collective-permute-start(bf16[64,3072]{1,0:T(8,128)(2,1)S(1)} %get-tuple-element.103), channel_id=1, source_target_pairs={{0,16},{1,49},{2,18},{3,51},{4,20},{5,53},{6,22},{7,55},{8,24},{9,... | collective-permute-start | bytes 1179656 | tf_op jit(solution)/shard_map/ppermute | solution.py:53
  118.9 9.2 %collective-permute-start.30 = (bf16[64,3072]{1,0:T(8,128)(2,1)S(1)}, bf16[64,3072]{1,0:T(8,128)(2,1)S(1)}, u32[]{:S(2)}, u32[]{:S(2)}) collective-permute-start(bf16[64,3072]{1,0:T(8,128)(2,1)S(1)} %get-tuple-element.104), channel_id=1, source_target_pairs={{0,2},{1,7},{2,4},{3,1},{4,6},{5,3},{6,0},{7,5},{8,10},{9,15},{10,... | collective-permute-start | bytes 1179656 | tf_op jit(solution)/shard_map/ppermute | solution.py:53
  (21 other events, 169.4 us)

commit v3 on v2

v3 whole, which is shorter than its diff:
```python
import math

import jax
import jax.numpy as jnp
import numpy as np
from jax import lax
from jax.sharding import PartitionSpec as P

RING = 4
AXES = ("pipe", "dp")


def split_place(index):
    core = index % 2
    y = index // 2 % 4
    half_x = index // 8 % 2
    z = index // 16 % 4
    pipe = index // 64
    return pipe, z, half_x, y, core


def join_place(pipe, z, half_x, y, core):
    return (((pipe * 4 + z) * 2 + half_x) * 4 + y) * 2 + core


def send(value, pipe=0, z=0, x=0, y=0, core=0):
    pairs = []
    for source in range(128):
        p0, z0, x0, y0, c0 = split_place(source)
        target = join_place(p0 ^ pipe, (z0 + z) % 4, x0 ^ x, (y0 + y) % 4, c0 ^ core)
        pairs.append((source, target))
    return lax.ppermute(value, AXES, pairs)


def normalize(section_rows, gain_vector):
    values = section_rows.astype(jnp.float32)
    centre = jnp.mean(values, axis=-1, keepdims=True)
    shifted = values - centre
    spread = jnp.mean(shifted * shifted, axis=-1, keepdims=True)
    return (shifted * lax.rsqrt(spread + 1e-05) * gain_vector).astype(jnp.bfloat16)


def swap_pairs(axis, turn):
    pairs = []
    for source in range(128):
        pipe, z, half_x, y, core = split_place(source)
        flip = (1, 3)[turn ^ core]
        if axis == "z":
            z ^= flip
        else:
            y ^= flip
        pairs.append((source, join_place(pipe, z, half_x, y, core)))
    return pairs


def swap_both(first, first_axis, second, second_axis, turn, *beside):
    first, second = lax.optimization_barrier((first, second))
    first = lax.ppermute(first, AXES, swap_pairs(first_axis, turn))
    second = lax.ppermute(second, AXES, swap_pairs(second_axis, turn))
    return lax.optimization_barrier((first, second, *beside))


def near_rows(own, one, two, core):
    size = own.shape[0]
    return jnp.concatenate(
        [
            own,
            jnp.where(core == 0, one, two[:size]),
            jnp.where(core == 0, two[:size], one),
            two[size:],
        ]
    )


def swap_sum(first_far, first_near, second_far, second_near, first_axis, second_axis):
    size = first_far.shape[0] // 2
    first_got, second_got = swap_both(
        first_far.astype(jnp.bfloat16),
        first_axis,
        second_far.astype(jnp.bfloat16),
        second_axis,
        1,
    )
    first_sum = first_near + first_got.astype(jnp.float32)
    second_sum = second_near + second_got.astype(jnp.float32)
    first_got, second_got = swap_both(
        first_sum[size:].astype(jnp.bfloat16),
        first_axis,
        second_sum[size:].astype(jnp.bfloat16),
        second_axis,
        0,
    )
    return (
        first_sum[:size] + first_got.astype(jnp.float32),
        second_sum[:size] + second_got.astype(jnp.float32),
    )


def token_positions(z, y):
    places = np.asarray([0, 1, 3, 2], np.int32)
    far = np.repeat(places, 128)
    side = np.tile(np.repeat(np.asarray([0, 1], np.int32), 64), 4)
    near = np.tile(np.repeat(places, 16), 8)
    low = np.tile(np.arange(16, dtype=np.int32), 32)
    dz = np.where(side == 0, far, near)
    dy = np.where(side == 0, near, far)
    return (((z ^ dz) * 2 + side) * 4 + (y ^ dy)) * 16 + low


def attend(projected, position, head_size):
    queries = projected[:, :head_size]
    keys_part = projected[:, head_size : 2 * head_size]
    values_part = projected[:, 2 * head_size :].astype(jnp.bfloat16)
    scores = jnp.einsum(
        "qd,kd->qk", queries, keys_part, precision=lax.Precision.HIGHEST
    ) / math.sqrt(head_size)
    causal = position[:, None] >= position[None, :]
    scores = jnp.where(causal, scores, -1e30)
    largest = jnp.max(scores, axis=-1, keepdims=True)
    weights = jnp.where(causal, jnp.exp(scores - largest), 0.0)
    totals = jnp.sum(weights, axis=-1, keepdims=True)
    probabilities = (weights / totals).astype(jnp.bfloat16)
    return jnp.dot(probabilities, values_part, preferred_element_type=jnp.float32).astype(
        jnp.bfloat16
    )


def shards(segment_input, norm_gain, head_weights, output_weights):
    head_size = output_weights.shape[1]
    width = segment_input.shape[2]
    half, quarter = width // 2, width // 4
    _, z, half_x, y, core = split_place(lax.axis_index("dp"))

    normed = normalize(segment_input[0], norm_gain[0])
    left, right = normed[:, :half], normed[:, half:]
    kept = jnp.where(core == 0, left, right)
    given = send(jnp.where(core == 0, right, left), core=1)
    block = jnp.where(
        core == 0, jnp.concatenate([kept, given]), jnp.concatenate([given, kept])
    )
    head_block, block = lax.optimization_barrier((head_weights[0, :, 0, :], block))
    other = send(block, x=1)
    first = jnp.where(half_x == 0, block, other)
    second = jnp.where(half_x == 0, other, block)
    own_weights = lax.dynamic_slice_in_dim(head_block, core * half, half, 0)
    swapped_weights = send(
        lax.dynamic_slice_in_dim(head_block, (1 - core) * half, half, 0), core=1
    )

    one = swap_both(first, "y", second, "z", 0)
    two = swap_both(
        jnp.concatenate([first, one[0]]), "y", jnp.concatenate([second, one[1]]), "z", 1
    )
    first_far = [near_rows(first, one[0], two[0], core)]
    second_far = [near_rows(second, one[1], two[1], core)]

    out_rows, _ = lax.optimization_barrier((output_weights[0], two[0]))
    out_parts = []
    for dx, dc in ((0, 0), (0, 1), (1, 0), (1, 1)):
        start = ((half_x ^ dx) * 2 + (core ^ dc)) * quarter
        part = lax.dynamic_slice_in_dim(out_rows, start, quarter, 1)
        out_parts.append(send(part, x=dx, core=dc) if dx or dc else part)
    out_block = jnp.concatenate(out_parts, axis=0)

    def project(k):
        rows = jnp.concatenate([first_far[k], second_far[k]])
        mine = jnp.dot(rows, own_weights, preferred_element_type=jnp.float32)
        theirs = jnp.dot(rows, swapped_weights, preferred_element_type=jnp.float32)
        return mine, theirs

    here = [project(0)]
    for k, (source, turn) in enumerate(((0, 0), (0, 1), (1, 1))):
        got = swap_both(first_far[source], "z", second_far[source], "y", turn, *here[k])
        first_far.append(got[0])
        second_far.append(got[1])
        here[k] = got[2:]
        here.append(project(k + 1))
    by_place = [
        here[0],
        [jnp.where(core == 0, a, b) for a, b in zip(here[1], here[2])],
        [jnp.where(core == 0, b, a) for a, b in zip(here[1], here[2])],
        here[3],
    ]
    projected = jnp.concatenate([mine + send(theirs, core=1) for mine, theirs in by_place])

    attended = attend(projected, token_positions(z, y), head_size)
    across_x = send(attended, x=1)
    across_core = send(attended, core=1)
    across_both = send(across_x, core=1)
    heads = jnp.concatenate([attended, across_core, across_x, across_both], axis=1)

    def turns(blocks):
        middle = jnp.where(core == 0, blocks[2], blocks[1])
        kept = jnp.where(core == 0, blocks[1], blocks[2])
        return [middle, blocks[3]], [blocks[0], kept]

    heads = heads.reshape(4, 2, 64, 4 * head_size)
    first_sent, first_kept = turns(heads[:, 0])
    second_sent, second_kept = turns(heads[:, 1])
    edge = jnp.dot(
        jnp.concatenate(first_sent + second_sent),
        out_block,
        preferred_element_type=jnp.float32,
    ).astype(jnp.bfloat16)
    rest = jnp.dot(
        jnp.concatenate(first_kept + second_kept),
        out_block,
        preferred_element_type=jnp.float32,
    )
    first_sum, second_sum = swap_sum(
        edge[:128], rest[:128], edge[128:], rest[128:], "z", "y"
    )
    first_sent, first_kept = turns(first_sum.reshape(4, 16, quarter))
    second_sent, second_kept = turns(second_sum.reshape(4, 16, quarter))
    first_rows, second_rows = swap_sum(
        jnp.concatenate(first_sent),
        jnp.concatenate(first_kept),
        jnp.concatenate(second_sent),
        jnp.concatenate(second_kept),
        "y",
        "z",
    )
    owners = jnp.stack([first_rows, second_rows]).astype(jnp.bfloat16)
    upper, lower = owners[:, :8], owners[:, 8:]
    stay = jnp.where(core == 0, upper, lower)
    came = send(jnp.where(core == 0, lower, upper), core=1)
    wide = jnp.where(
        core == 0,
        jnp.concatenate([stay, came], axis=2),
        jnp.concatenate([came, stay], axis=2),
    )
    straight = send(jnp.where(half_x == 0, wide[0], wide[1]), pipe=1)
    crossed = send(jnp.where(half_x == 0, wide[1], wide[0]), pipe=1, x=1)
    return jnp.where(
        half_x == 0,
        jnp.concatenate([straight, crossed], axis=1),
        jnp.concatenate([crossed, straight], axis=1),
    )[None]


def solution(mesh):
    placed = (
        P("pipe", "dp", None),
        P("pipe", None),
        P("pipe", None, "dp", None),
        P("pipe", "dp", None),
    )
    return jax.shard_map(
        shards, mesh=mesh, in_specs=placed, out_specs=P("pipe", "dp", None), check_vma=False
    )
```

time: 160 us -> 140 us (0.88)
  waiting for transfers between devices: 98.2 us -> 73.6 us
  matrix products: 12.2 us -> 14.9 us
  starting transfers between devices: 36.8 us -> 38.6 us
  local copies, waits for them, and re-layouts: 3.86 us -> 5.63 us
    ppermute x24 -> x18, waiting for transfers between devices: 85.6 us -> 49.5 us  [the longest x9 41.4 us: swap_both(): first = lax.ppermute(first, AXES, swap_pairs(first_axis, turn))]
    ppermute x17 -> x16, waiting for transfers between devices: 12.6 us -> 24.1 us  [send(): return lax.ppermute(value, AXES, pairs)]
    ppermute x24 -> x18, starting transfers between devices: 16.2 us -> 26.1 us  [the longest x9 14.9 us: swap_both(): second = lax.ppermute(second, AXES, swap_pairs(second_axis, turn))]
    ppermute x17 -> x16, starting transfers between devices: 20.6 us -> 12.5 us  [send(): return lax.ppermute(value, AXES, pairs)]
    dot_general x2, matrix products: 2.25 us -> 5.02 us  [the longest x1 2.59 us: shards(): jnp.dot(jnp.concatenate(first_sent + second_sent), out_block, preferred_e...]
  transfers between devices with their start and end apart: 41 -> 34, of which waited for: 31 -> 23; matrix products, arithmetic and copies ran while one was open for 10% -> 13% of each run, Pallas kernels for 0% -> 0%
where the time goes in v3:
time: 140 us
  waiting for transfers between devices  73.6 us (53%)
  starting transfers between devices  38.6 us (28%)
  matrix products  14.9 us (11%)
  other arithmetic  6.31 us (5%)
  local copies, waits for them, and re-layouts  5.63 us (4%)
    ppermute x9, waiting for transfers between devices, swap_both(): first = lax.ppermute(first, AXES, swap_pairs(first_axis, turn))  41.4 us
    ppermute x16, waiting for transfers between devices, send(): return lax.ppermute(value, AXES, pairs)  24.1 us
    ppermute x9, starting transfers between devices, swap_both(): second = lax.ppermute(second, AXES, swap_pairs(second_axis, turn))  14.9 us
    ppermute x16, starting transfers between devices, send(): return lax.ppermute(value, AXES, pairs)  12.5 us
    ppermute x9, starting transfers between devices, swap_both(): first = lax.ppermute(first, AXES, swap_pairs(first_axis, turn))  11.2 us
    ppermute x9, waiting for transfers between devices, swap_both(): second = lax.ppermute(second, AXES, swap_pairs(second_axis, turn))  8.08 us
    dot_general x4, matrix products, project(): mine = jnp.dot(rows, own_weights, preferred_element_type=jnp.float32)  4.21 us
    dot_general x4, matrix products, project(): theirs = jnp.dot(rows, swapped_weights, preferred_element_type=jnp.float32)  4.18 us
  transfers between devices with their start and end apart: 34, of which 23 were waited for; matrix products, arithmetic and copies ran while one was open for 13% of the time, Pallas kernels for 0%

profile of v3, /device:TPU:0, one launch (start us, length us, event | category | flops | bytes accessed | tf_op | source)
XLA Modules:
  0.0 139.5 jit_solution(11612860738542877142)
XLA Ops:
  5.0 3.2 %collective-permute-start.1 = (bf16[16,6144]{1,0:T(8,128)(2,1)S(1)}, bf16[16,6144]{1,0:T(8,128)(2,1)S(1)}, u32[]{:S(2)}, u32[]{:S(2)}) collective-permute-start(bf16[16,6144]{1,0:T(8,128)(2,1)S(1)} %maximum_select_fusion), channel_id=1, source_target_pairs={{0,8},{1,9},{2,10},{3,11},{4,12},{5,13},{6,14},{7,15},{8,0},{9,1},... | collective-permute-start | bytes 589832 | tf_op jit(solution)/shard_map/ppermute | solution.py:32
  8.2 5.4 %collective-permute-done.1 = bf16[16,6144]{1,0:T(8,128)(2,1)S(1)} collective-permute-done((bf16[16,6144]{1,0:T(8,128)(2,1)S(1)}, bf16[16,6144]{1,0:T(8,128)(2,1)S(1)}, u32[]{:S(2)}, u32[]{:S(2)}) %collective-permute-start.1) | collective-permute-done | bytes 196640 | tf_op jit(solution)/shard_map/ppermute | solution.py:32
  13.6 1.7 %collective-permute-start.2 = (bf16[16,6144]{1,0:T(8,128)(2,1)S(1)}, bf16[16,6144]{1,0:T(8,128)(2,1)S(1)}, u32[]{:S(2)}, u32[]{:S(2)}) collective-permute-start(bf16[16,6144]{1,0:T(8,128)(2,1)S(1)} %get-tuple-element.49), channel_id=1, source_target_pairs={{0,2},{1,7},{2,0},{3,5},{4,6},{5,3},{6,4},{7,1},{8,10},{9,15},{10,... | collective-permute-start | bytes 589832 | tf_op jit(solution)/shard_map/ppermute | solution.py:58
  15.4 1.9 %collective-permute-start.3 = (bf16[16,6144]{1,0:T(8,128)(2,1)S(1)}, bf16[16,6144]{1,0:T(8,128)(2,1)S(1)}, u32[]{:S(2)}, u32[]{:S(2)}) collective-permute-start(bf16[16,6144]{1,0:T(8,128)(2,1)S(1)} %get-tuple-element.50), channel_id=1, source_target_pairs={{0,16},{1,49},{2,18},{3,51},{4,20},{5,53},{6,22},{7,55},{8,24},{9,... | collective-permute-start | bytes 589832 | tf_op jit(solution)/shard_map/ppermute | solution.py:59
  17.3 2.1 %collective-permute-done.2 = bf16[16,6144]{1,0:T(8,128)(2,1)S(1)} collective-permute-done((bf16[16,6144]{1,0:T(8,128)(2,1)S(1)}, bf16[16,6144]{1,0:T(8,128)(2,1)S(1)}, u32[]{:S(2)}, u32[]{:S(2)}) %collective-permute-start.2) | collective-permute-done | bytes 196640 | tf_op jit(solution)/shard_map/ppermute | solution.py:58
  19.4 1.7 %collective-permute-done.3 = bf16[16,6144]{1,0:T(8,128)(2,1)S(1)} collective-permute-done((bf16[16,6144]{1,0:T(8,128)(2,1)S(1)}, bf16[16,6144]{1,0:T(8,128)(2,1)S(1)}, u32[]{:S(2)}, u32[]{:S(2)}) %collective-permute-start.3) | collective-permute-done | bytes 196640 | tf_op jit(solution)/shard_map/ppermute | solution.py:59
  21.1 2.3 %collective-permute-start.4 = (bf16[32,6144]{1,0:T(8,128)(2,1)S(1)}, bf16[32,6144]{1,0:T(8,128)(2,1)S(1)}, u32[]{:S(2)}, u32[]{:S(2)}) collective-permute-start(bf16[32,6144]{1,0:T(8,128)(2,1)S(1)} %pad_maximum_fusion.7), channel_id=1, source_target_pairs={{0,6},{1,3},{2,4},{3,1},{4,2},{5,7},{6,0},{7,5},{8,14},{9,11},{10,... | collective-permute-start | bytes 1179656 | tf_op jit(solution)/shard_map/ppermute | solution.py:58
  23.4 4.0 %collective-permute-start.5 = (bf16[32,6144]{1,0:T(8,128)(2,1)S(1)}, bf16[32,6144]{1,0:T(8,128)(2,1)S(1)}, u32[]{:S(2)}, u32[]{:S(2)}) collective-permute-start(bf16[32,6144]{1,0:T(8,128)(2,1)S(1)} %pad_maximum_fusion.8), channel_id=1, source_target_pairs={{0,48},{1,17},{2,50},{3,19},{4,52},{5,21},{6,54},{7,23},{8,56},{9,... | collective-permute-start | bytes 1179656 | tf_op jit(solution)/shard_map/ppermute | solution.py:59
  27.4 2.8 %constant_dynamic-slice_fusion.4 = bf16[6144,384]{1,0:T(8,128)(2,1)S(1)} fusion(bf16[12288,384]{1,0:T(8,128)(2,1)} %bitcast.56, s32[]{:T(128)S(6)} %select_n.247), kind=kLoop, calls=%fused_computation.126 | loop fusion | bytes 9437188 | tf_op jit(solution)/shard_map/dynamic_slice | solution.py:147
  30.4 2.8 %collective-permute-done.5 = bf16[32,6144]{1,0:T(8,128)(2,1)S(1)} collective-permute-done((bf16[32,6144]{1,0:T(8,128)(2,1)S(1)}, bf16[32,6144]{1,0:T(8,128)(2,1)S(1)}, u32[]{:S(2)}, u32[]{:S(2)}) %collective-permute-start.5) | collective-permute-done | bytes 393248 | tf_op jit(solution)/shard_map/ppermute | solution.py:59
  33.7 3.3 %collective-permute-start.10 = (bf16[64,6144]{1,0:T(8,128)(2,1)S(1)}, bf16[64,6144]{1,0:T(8,128)(2,1)S(1)}, u32[]{:S(2)}, u32[]{:S(2)}) collective-permute-start(bf16[64,6144]{1,0:T(8,128)(2,1)S(1)} %pad_maximum_fusion.1), channel_id=1, source_target_pairs={{0,48},{1,17},{2,50},{3,19},{4,52},{5,21},{6,54},{7,23},{8,56},{9,... | collective-permute-start | bytes 2359304 | tf_op jit(solution)/shard_map/ppermute | solution.py:58
  42.5 10.0 %collective-permute-done.6 = bf16[64,6144]{1,0:T(8,128)(2,1)S(1)} collective-permute-done((bf16[64,6144]{1,0:T(8,128)(2,1)S(1)}, bf16[64,6144]{1,0:T(8,128)(2,1)S(1)}, u32[]{:S(2)}, u32[]{:S(2)}) %collective-permute-start.6) | collective-permute-done | bytes 786464 | tf_op jit(solution)/shard_map/ppermute | solution.py:58
  52.5 3.0 %collective-permute-start.21 = (bf16[128,3072]{1,0:T(8,128)(2,1)S(1)}, bf16[128,3072]{1,0:T(8,128)(2,1)}, u32[]{:S(2)}, u32[]{:S(2)}) collective-permute-start(bf16[128,3072]{1,0:T(8,128)(2,1)S(1)} %get-tuple-element.105), channel_id=1, source_target_pairs={{0,8},{1,9},{2,10},{3,11},{4,12},{5,13},{6,14},{7,15},{8,0},{9,1},... | collective-permute-start | bytes 2359304 | tf_op jit(solution)/shard_map/ppermute | solution.py:32
  63.2 8.0 %collective-permute-done.12 = bf16[64,6144]{1,0:T(8,128)(2,1)S(1)} collective-permute-done((bf16[64,6144]{1,0:T(8,128)(2,1)S(1)}, bf16[64,6144]{1,0:T(8,128)(2,1)S(1)}, u32[]{:S(2)}, u32[]{:S(2)}) %collective-permute-start.12) | collective-permute-done | bytes 786464 | tf_op jit(solution)/shard_map/ppermute | solution.py:58
  79.3 10.0 %collective-permute-done.18 = bf16[512,128]{0,1:T(8,128)(2,1)S(1)} collective-permute-done((bf16[512,128]{0,1:T(8,128)(2,1)S(1)}, bf16[512,128]{0,1:T(8,128)(2,1)S(1)}, u32[]{:S(2)}, u32[]{:S(2)}) %collective-permute-start.18) | collective-permute-done | bytes 131104 | tf_op jit(solution)/shard_map/ppermute | solution.py:32
  91.0 2.6 %convolution_convert_fusion = bf16[256,3072]{1,0:T(8,128)(2,1)S(1)} fusion(bf16[128,3072]{1,0:T(8,128)(2,1)} %collective-permute-done.22, bf16[128,3072]{1,0:T(8,128)(2,1)} %collective-permute-done.21, bf16[128,3072]{1,0:T(8,128)(2,1)} %collective-permute-done.20, bf16[128,3072]{1,0:T(8,128)(2,1)S(1)} %get-tuple-element.103, ...), kind=kOutput, calls=%fused_computation | convolution fusion | flops 819724288 | bytes 4980736 | tf_op jit(solution)/shard_map/dot_general | solution.py:200
  94.9 2.4 %fusion.13 = f32[256,3072]{1,0:T(8,128)S(1)} fusion(bf16[128,3072]{1,0:T(8,128)(2,1)} %collective-permute-done.22, bf16[128,3072]{1,0:T(8,128)(2,1)} %collective-permute-done.21, bf16[128,3072]{1,0:T(8,128)(2,1)} %collective-permute-done.20, bf16[128,3072]{1,0:T(8,128)(2,1)S(1)} %get-tuple-element.103, bf16[64,512]{1,0:T(8,128)(2,1)S(1)} %get-tuple-element.122, ...), kind=kOutput, calls=%fused_computation.26 | convolution fusion | flops 818937856 | bytes 6553600 | tf_op jit(solution)/shard_map/dot_general | solution.py:205
  97.3 9.6 %collective-permute-done.23 = bf16[128,3072]{1,0:T(8,128)(2,1)S(1)} collective-permute-done((bf16[128,3072]{1,0:T(8,128)(2,1)S(1)}, bf16[128,3072]{1,0:T(8,128)(2,1)S(1)}, u32[]{:S(2)}, u32[]{:S(2)}) %collective-permute-start.23) | collective-permute-done | bytes 786464 | tf_op jit(solution)/shard_map/ppermute | solution.py:58
  109.9 6.3 %collective-permute-done.25 = bf16[64,3072]{1,0:T(8,128)(2,1)S(1)} collective-permute-done((bf16[64,3072]{1,0:T(8,128)(2,1)S(1)}, bf16[64,3072]{1,0:T(8,128)(2,1)S(1)}, u32[]{:S(2)}, u32[]{:S(2)}) %collective-permute-start.25) | collective-permute-done | bytes 393248 | tf_op jit(solution)/shard_map/ppermute | solution.py:58
  117.1 3.1 %collective-permute-start.28 = (bf16[32,3072]{1,0:T(8,128)(2,1)S(1)}, bf16[32,3072]{1,0:T(8,128)(2,1)S(1)}, u32[]{:S(2)}, u32[]{:S(2)}) collective-permute-start(bf16[32,3072]{1,0:T(8,128)(2,1)S(1)} %pad_maximum_fusion.10), channel_id=1, source_target_pairs={{0,48},{1,17},{2,50},{3,19},{4,52},{5,21},{6,54},{7,23},{8,56},{9,... | collective-permute-start | bytes 589832 | tf_op jit(solution)/shard_map/ppermute | solution.py:59
  120.3 3.2 %collective-permute-done.27 = bf16[32,3072]{1,0:T(8,128)(2,1)S(1)} collective-permute-done((bf16[32,3072]{1,0:T(8,128)(2,1)S(1)}, bf16[32,3072]{1,0:T(8,128)(2,1)S(1)}, u32[]{:S(2)}, u32[]{:S(2)}) %collective-permute-start.27) | collective-permute-done | bytes 196640 | tf_op jit(solution)/shard_map/ppermute | solution.py:58
  126.6 2.2 %collective-permute-done.29 = bf16[16,3072]{1,0:T(8,128)(2,1)S(1)} collective-permute-done((bf16[16,3072]{1,0:T(8,128)(2,1)S(1)}, bf16[16,3072]{1,0:T(8,128)(2,1)S(1)}, u32[]{:S(2)}, u32[]{:S(2)}) %collective-permute-start.29) | collective-permute-done | bytes 98336 | tf_op jit(solution)/shard_map/ppermute | solution.py:58
  133.0 2.1 %collective-permute-start.33 = (bf16[8,6144]{1,0:T(8,128)(2,1)S(1)}, bf16[8,6144]{1,0:T(8,128)(2,1)S(1)}, u32[]{:S(2)}, u32[]{:S(2)}) collective-permute-start(bf16[8,6144]{1,0:T(8,128)(2,1)S(1)} %get-tuple-element.135), channel_id=1, source_target_pairs={{0,72},{1,73},{2,74},{3,75},{4,76},{5,77},{6,78},{7,79},{8,64},{9,... | collective-permute-start | bytes 294920 | tf_op jit(solution)/shard_map/ppermute | solution.py:32
  136.3 2.5 %collective-permute-done.33 = bf16[8,6144]{1,0:T(8,128)(2,1)S(1)} collective-permute-done((bf16[8,6144]{1,0:T(8,128)(2,1)S(1)}, bf16[8,6144]{1,0:T(8,128)(2,1)S(1)}, u32[]{:S(2)}, u32[]{:S(2)}) %collective-permute-start.33) | collective-permute-done | bytes 98336 | tf_op jit(solution)/shard_map/ppermute | solution.py:32
  (129 shorter events, 42.7 us)
Async XLA Ops:
  5.0 8.5 %collective-permute-start.1 = (bf16[16,6144]{1,0:T(8,128)(2,1)S(1)}, bf16[16,6144]{1,0:T(8,128)(2,1)S(1)}, u32[]{:S(2)}, u32[]{:S(2)}) collective-permute-start(bf16[16,6144]{1,0:T(8,128)(2,1)S(1)} %maximum_select_fusion), channel_id=1, source_target_pairs={{0,8},{1,9},{2,10},{3,11},{4,12},{5,13},{6,14},{7,15},{8,0},{9,1},... | collective-permute-start | bytes 589832 | tf_op jit(solution)/shard_map/ppermute | solution.py:32
  13.6 5.7 %collective-permute-start.2 = (bf16[16,6144]{1,0:T(8,128)(2,1)S(1)}, bf16[16,6144]{1,0:T(8,128)(2,1)S(1)}, u32[]{:S(2)}, u32[]{:S(2)}) collective-permute-start(bf16[16,6144]{1,0:T(8,128)(2,1)S(1)} %get-tuple-element.49), channel_id=1, source_target_pairs={{0,2},{1,7},{2,0},{3,5},{4,6},{5,3},{6,4},{7,1},{8,10},{9,15},{10,... | collective-permute-start | bytes 589832 | tf_op jit(solution)/shard_map/ppermute | solution.py:58
  21.1 9.2 %collective-permute-start.4 = (bf16[32,6144]{1,0:T(8,128)(2,1)S(1)}, bf16[32,6144]{1,0:T(8,128)(2,1)S(1)}, u32[]{:S(2)}, u32[]{:S(2)}) collective-permute-start(bf16[32,6144]{1,0:T(8,128)(2,1)S(1)} %pad_maximum_fusion.7), channel_id=1, source_target_pairs={{0,6},{1,3},{2,4},{3,1},{4,2},{5,7},{6,0},{7,5},{8,14},{9,11},{10,... | collective-permute-start | bytes 1179656 | tf_op jit(solution)/shard_map/ppermute | solution.py:58
  23.4 9.8 %collective-permute-start.5 = (bf16[32,6144]{1,0:T(8,128)(2,1)S(1)}, bf16[32,6144]{1,0:T(8,128)(2,1)S(1)}, u32[]{:S(2)}, u32[]{:S(2)}) collective-permute-start(bf16[32,6144]{1,0:T(8,128)(2,1)S(1)} %pad_maximum_fusion.8), channel_id=1, source_target_pairs={{0,48},{1,17},{2,50},{3,19},{4,52},{5,21},{6,54},{7,23},{8,56},{9,... | collective-permute-start | bytes 1179656 | tf_op jit(solution)/shard_map/ppermute | solution.py:59
  30.2 11.2 %collective-permute-start.8 = (bf16[6144,384]{1,0:T(8,128)(2,1)S(1)}, bf16[6144,384]{1,0:T(8,128)(2,1)S(1)}, u32[]{:S(2)}, u32[]{:S(2)}) collective-permute-start(bf16[6144,384]{1,0:T(8,128)(2,1)S(1)} %constant_dynamic-slice_fusion.4), channel_id=1, source_target_pairs={{0,1},{1,0},{2,3},{3,2},{4,5},{5,4},{6,7},{7,6},{8,9},{9,8},{10,11... | collective-permute-start | bytes 14155784 | tf_op jit(solution)/shard_map/ppermute | solution.py:32
  33.6 18.9 %collective-permute-start.6 = (bf16[64,6144]{1,0:T(8,128)(2,1)S(1)}, bf16[64,6144]{1,0:T(8,128)(2,1)S(1)}, u32[]{:S(2)}, u32[]{:S(2)}) collective-permute-start(bf16[64,6144]{1,0:T(8,128)(2,1)S(1)} %pad_maximum_fusion.1), channel_id=1, source_target_pairs={{0,16},{1,49},{2,18},{3,51},{4,20},{5,53},{6,22},{7,55},{8,24},{9,... | collective-permute-start | bytes 2359304 | tf_op jit(solution)/shard_map/ppermute | solution.py:58
  33.7 24.0 %collective-permute-start.10 = (bf16[64,6144]{1,0:T(8,128)(2,1)S(1)}, bf16[64,6144]{1,0:T(8,128)(2,1)S(1)}, u32[]{:S(2)}, u32[]{:S(2)}) collective-permute-start(bf16[64,6144]{1,0:T(8,128)(2,1)S(1)} %pad_maximum_fusion.1), channel_id=1, source_target_pairs={{0,48},{1,17},{2,50},{3,19},{4,52},{5,21},{6,54},{7,23},{8,56},{9,... | collective-permute-start | bytes 2359304 | tf_op jit(solution)/shard_map/ppermute | solution.py:58
  37.0 18.5 %collective-permute-start.7 = (bf16[64,6144]{1,0:T(8,128)(2,1)S(1)}, bf16[64,6144]{1,0:T(8,128)(2,1)S(1)}, u32[]{:S(2)}, u32[]{:S(2)}) collective-permute-start(bf16[64,6144]{1,0:T(8,128)(2,1)S(1)} %pad_maximum_fusion.2), channel_id=1, source_target_pairs={{0,2},{1,7},{2,0},{3,5},{4,6},{5,3},{6,4},{7,1},{8,10},{9,15},{10,... | collective-permute-start | bytes 2359304 | tf_op jit(solution)/shard_map/ppermute | solution.py:59
  37.7 20.1 %collective-permute-start.11 = (bf16[64,6144]{1,0:T(8,128)(2,1)S(1)}, bf16[64,6144]{1,0:T(8,128)(2,1)S(1)}, u32[]{:S(2)}, u32[]{:S(2)}) collective-permute-start(bf16[64,6144]{1,0:T(8,128)(2,1)S(1)} %pad_maximum_fusion.2), channel_id=1, source_target_pairs={{0,6},{1,3},{2,4},{3,1},{4,2},{5,7},{6,0},{7,5},{8,14},{9,11},{10,... | collective-permute-start | bytes 2359304 | tf_op jit(solution)/shard_map/ppermute | solution.py:59
  41.5 49.5 %collective-permute-start.20 = (bf16[128,3072]{1,0:T(8,128)(2,1)}, bf16[128,3072]{1,0:T(8,128)(2,1)}, u32[]{:S(2)}, u32[]{:S(2)}) collective-permute-start(bf16[128,3072]{1,0:T(8,128)(2,1)} %get-tuple-element.106), channel_id=1, source_target_pairs={{0,1},{1,0},{2,3},{3,2},{4,5},{5,4},{6,7},{7,6},{8,9},{9,8},{10,11... | collective-permute-start | bytes 2359304 | tf_op jit(solution)/shard_map/ppermute | solution.py:32
  52.5 38.5 %collective-permute-start.21 = (bf16[128,3072]{1,0:T(8,128)(2,1)S(1)}, bf16[128,3072]{1,0:T(8,128)(2,1)}, u32[]{:S(2)}, u32[]{:S(2)}) collective-permute-start(bf16[128,3072]{1,0:T(8,128)(2,1)S(1)} %get-tuple-element.105), channel_id=1, source_target_pairs={{0,8},{1,9},{2,10},{3,11},{4,12},{5,13},{6,14},{7,15},{8,0},{9,1},... | collective-permute-start | bytes 2359304 | tf_op jit(solution)/shard_map/ppermute | solution.py:32
  55.5 6.9 %collective-permute-start.9 = (f32[128,384]{1,0:T(8,128)S(1)}, f32[128,384]{1,0:T(8,128)S(1)}, u32[]{:S(2)}, u32[]{:S(2)}) collective-permute-start(f32[128,384]{1,0:T(8,128)S(1)} %fusion.52), channel_id=1, source_target_pairs={{0,1},{1,0},{2,3},{3,2},{4,5},{5,4},{6,7},{7,6},{8,9},{9,8},{10,11... | collective-permute-start | bytes 589832 | tf_op jit(solution)/shard_map/ppermute | solution.py:32
  57.9 13.3 %collective-permute-start.12 = (bf16[64,6144]{1,0:T(8,128)(2,1)S(1)}, bf16[64,6144]{1,0:T(8,128)(2,1)S(1)}, u32[]{:S(2)}, u32[]{:S(2)}) collective-permute-start(bf16[64,6144]{1,0:T(8,128)(2,1)S(1)} %collective-permute-done.6), channel_id=1, source_target_pairs={{0,48},{1,17},{2,50},{3,19},{4,52},{5,21},{6,54},{7,23},{8,56},{9,... | collective-permute-start | bytes 2359304 | tf_op jit(solution)/shard_map/ppermute | solution.py:58
  59.2 13.2 %collective-permute-start.13 = (bf16[64,6144]{1,0:T(8,128)(2,1)S(1)}, bf16[64,6144]{1,0:T(8,128)(2,1)S(1)}, u32[]{:S(2)}, u32[]{:S(2)}) collective-permute-start(bf16[64,6144]{1,0:T(8,128)(2,1)S(1)} %collective-permute-done.7), channel_id=1, source_target_pairs={{0,6},{1,3},{2,4},{3,1},{4,2},{5,7},{6,0},{7,5},{8,14},{9,11},{10,... | collective-permute-start | bytes 2359304 | tf_op jit(solution)/shard_map/ppermute | solution.py:59
  62.5 28.5 %collective-permute-start.22 = (bf16[128,3072]{1,0:T(8,128)(2,1)S(1)}, bf16[128,3072]{1,0:T(8,128)(2,1)}, u32[]{:S(2)}, u32[]{:S(2)}) collective-permute-start(bf16[128,3072]{1,0:T(8,128)(2,1)S(1)} %get-tuple-element.104), channel_id=1, source_target_pairs={{0,9},{1,8},{2,11},{3,10},{4,13},{5,12},{6,15},{7,14},{8,1},{9,0},... | collective-permute-start | bytes 2359304 | tf_op jit(solution)/shard_map/ppermute | solution.py:32
  78.4 10.9 %collective-permute-start.18 = (bf16[512,128]{0,1:T(8,128)(2,1)S(1)}, bf16[512,128]{0,1:T(8,128)(2,1)S(1)}, u32[]{:S(2)}, u32[]{:S(2)}) collective-permute-start(bf16[512,128]{0,1:T(8,128)(2,1)S(1)} %convolution_convert_fusion.1), channel_id=1, source_target_pairs={{0,8},{1,9},{2,10},{3,11},{4,12},{5,13},{6,14},{7,15},{8,0},{9,1},... | collective-permute-start | bytes 393224 | tf_op jit(solution)/shard_map/ppermute | solution.py:32
  79.3 10.0 %collective-permute-start.17 = (bf16[512,128]{0,1:T(8,128)(2,1)S(1)}, bf16[512,128]{0,1:T(8,128)(2,1)S(1)}, u32[]{:S(2)}, u32[]{:S(2)}) collective-permute-start(bf16[512,128]{0,1:T(8,128)(2,1)S(1)} %convolution_convert_fusion.1), channel_id=1, source_target_pairs={{0,1},{1,0},{2,3},{3,2},{4,5},{5,4},{6,7},{7,6},{8,9},{9,8},{10,11... | collective-permute-start | bytes 393224 | tf_op jit(solution)/shard_map/ppermute | solution.py:32
  93.7 13.3 %collective-permute-start.23 = (bf16[128,3072]{1,0:T(8,128)(2,1)S(1)}, bf16[128,3072]{1,0:T(8,128)(2,1)S(1)}, u32[]{:S(2)}, u32[]{:S(2)}) collective-permute-start(bf16[128,3072]{1,0:T(8,128)(2,1)S(1)} %get-tuple-element.75), channel_id=1, source_target_pairs={{0,48},{1,17},{2,50},{3,19},{4,52},{5,21},{6,54},{7,23},{8,56},{9,... | collective-permute-start | bytes 2359304 | tf_op jit(solution)/shard_map/ppermute | solution.py:58
  94.5 13.2 %collective-permute-start.24 = (bf16[128,3072]{1,0:T(8,128)(2,1)S(1)}, bf16[128,3072]{1,0:T(8,128)(2,1)S(1)}, u32[]{:S(2)}, u32[]{:S(2)}) collective-permute-start(bf16[128,3072]{1,0:T(8,128)(2,1)S(1)} %get-tuple-element.76), channel_id=1, source_target_pairs={{0,6},{1,3},{2,4},{3,1},{4,2},{5,7},{6,0},{7,5},{8,14},{9,11},{10,... | collective-permute-start | bytes 2359304 | tf_op jit(solution)/shard_map/ppermute | solution.py:59
  108.3 7.9 %collective-permute-start.25 = (bf16[64,3072]{1,0:T(8,128)(2,1)S(1)}, bf16[64,3072]{1,0:T(8,128)(2,1)S(1)}, u32[]{:S(2)}, u32[]{:S(2)}) collective-permute-start(bf16[64,3072]{1,0:T(8,128)(2,1)S(1)} %slice.321), channel_id=1, source_target_pairs={{0,16},{1,49},{2,18},{3,51},{4,20},{5,53},{6,22},{7,55},{8,24},{9,... | collective-permute-start | bytes 1179656 | tf_op jit(solution)/shard_map/ppermute | solution.py:58
  108.4 7.9 %collective-permute-start.26 = (bf16[64,3072]{1,0:T(8,128)(2,1)S(1)}, bf16[64,3072]{1,0:T(8,128)(2,1)S(1)}, u32[]{:S(2)}, u32[]{:S(2)}) collective-permute-start(bf16[64,3072]{1,0:T(8,128)(2,1)S(1)} %slice.320), channel_id=1, source_target_pairs={{0,2},{1,7},{2,0},{3,5},{4,6},{5,3},{6,4},{7,1},{8,10},{9,15},{10,... | collective-permute-start | bytes 1179656 | tf_op jit(solution)/shard_map/ppermute | solution.py:59
  116.5 7.0 %collective-permute-start.27 = (bf16[32,3072]{1,0:T(8,128)(2,1)S(1)}, bf16[32,3072]{1,0:T(8,128)(2,1)S(1)}, u32[]{:S(2)}, u32[]{:S(2)}) collective-permute-start(bf16[32,3072]{1,0:T(8,128)(2,1)S(1)} %pad_maximum_fusion.9), channel_id=1, source_target_pairs={{0,6},{1,3},{2,4},{3,1},{4,2},{5,7},{6,0},{7,5},{8,14},{9,11},{10,... | collective-permute-start | bytes 589832 | tf_op jit(solution)/shard_map/ppermute | solution.py:58
  117.1 6.9 %collective-permute-start.28 = (bf16[32,3072]{1,0:T(8,128)(2,1)S(1)}, bf16[32,3072]{1,0:T(8,128)(2,1)S(1)}, u32[]{:S(2)}, u32[]{:S(2)}) collective-permute-start(bf16[32,3072]{1,0:T(8,128)(2,1)S(1)} %pad_maximum_fusion.10), channel_id=1, source_target_pairs={{0,48},{1,17},{2,50},{3,19},{4,52},{5,21},{6,54},{7,23},{8,56},{9,... | collective-permute-start | bytes 589832 | tf_op jit(solution)/shard_map/ppermute | solution.py:59
  133.0 5.8 %collective-permute-start.33 = (bf16[8,6144]{1,0:T(8,128)(2,1)S(1)}, bf16[8,6144]{1,0:T(8,128)(2,1)S(1)}, u32[]{:S(2)}, u32[]{:S(2)}) collective-permute-start(bf16[8,6144]{1,0:T(8,128)(2,1)S(1)} %get-tuple-element.135), channel_id=1, source_target_pairs={{0,72},{1,73},{2,74},{3,75},{4,76},{5,77},{6,78},{7,79},{8,64},{9,... | collective-permute-start | bytes 294920 | tf_op jit(solution)/shard_map/ppermute | solution.py:32
  (18 other events, 159.2 us)

commit v4 on v3

--- a/solution.py
+++ b/solution.py
@@ -139,42 +139,72 @@
         core == 0, jnp.concatenate([kept, given]), jnp.concatenate([given, kept])
     )
     head_block, block = lax.optimization_barrier((head_weights[0, :, 0, :], block))
-    other = send(block, x=1)
+    other, their_weights = lax.optimization_barrier(
+        (
+            send(block, x=1),
+            lax.dynamic_slice_in_dim(head_block, (1 - core) * half, half, 0),
+        )
+    )
     first = jnp.where(half_x == 0, block, other)
     second = jnp.where(half_x == 0, other, block)
     own_weights = lax.dynamic_slice_in_dim(head_block, core * half, half, 0)
-    swapped_weights = send(
-        lax.dynamic_slice_in_dim(head_block, (1 - core) * half, half, 0), core=1
-    )
-
-    one = swap_both(first, "y", second, "z", 0)
-    two = swap_both(
-        jnp.concatenate([first, one[0]]), "y", jnp.concatenate([second, one[1]]), "z", 1
-    )
-    first_far = [near_rows(first, one[0], two[0], core)]
-    second_far = [near_rows(second, one[1], two[1], core)]
-
-    out_rows, _ = lax.optimization_barrier((output_weights[0], two[0]))
-    out_parts = []
-    for dx, dc in ((0, 0), (0, 1), (1, 0), (1, 1)):
-        start = ((half_x ^ dx) * 2 + (core ^ dc)) * quarter
-        part = lax.dynamic_slice_in_dim(out_rows, start, quarter, 1)
-        out_parts.append(send(part, x=dx, core=dc) if dx or dc else part)
-    out_block = jnp.concatenate(out_parts, axis=0)
-
-    def project(k):
-        rows = jnp.concatenate([first_far[k], second_far[k]])
+
+    out_rows, _ = lax.optimization_barrier((output_weights[0], block))
+    *one, out_kept, out_given = swap_both(
+        first,
+        "y",
+        second,
+        "z",
+        0,
+        lax.dynamic_slice_in_dim(out_rows, half_x * half, half, 1),
+        lax.dynamic_slice_in_dim(out_rows, (1 - half_x) * half, half, 1),
+    )
+    *two, swapped_weights = swap_both(
+        jnp.concatenate([first, one[0]]),
+        "y",
+        jnp.concatenate([second, one[1]]),
+        "z",
+        1,
+        send(their_weights, core=1),
+    )
+    first_own = near_rows(first, one[0], two[0], core)
+    second_own = near_rows(second, one[1], two[1], core)
+
+    def project(first_rows, second_rows):
+        rows = jnp.concatenate([first_rows, second_rows])
         mine = jnp.dot(rows, own_weights, preferred_element_type=jnp.float32)
         theirs = jnp.dot(rows, swapped_weights, preferred_element_type=jnp.float32)
         return mine, theirs
 
-    here = [project(0)]
-    for k, (source, turn) in enumerate(((0, 0), (0, 1), (1, 1))):
-        got = swap_both(first_far[source], "z", second_far[source], "y", turn, *here[k])
-        first_far.append(got[0])
-        second_far.append(got[1])
-        here[k] = got[2:]
-        here.append(project(k + 1))
+    def swap_far(first_rows, second_rows, turn):
+        return (
+            lax.ppermute(first_rows, AXES, swap_pairs("z", turn)),
+            lax.ppermute(second_rows, AXES, swap_pairs("y", turn)),
+        )
+
+    middle = out_given.shape[0] // 2
+    first_own, second_own, upper, lower = lax.optimization_barrier(
+        (first_own, second_own, out_given[:middle], out_given[middle:])
+    )
+    turn_one = swap_far(first_own, second_own, 0)
+    turn_two = swap_far(first_own, second_own, 1)
+    upper = send(upper, x=1)
+    *turn_one, mine, theirs = lax.optimization_barrier(
+        (*turn_one, *project(first_own, second_own))
+    )
+    here = [(mine, theirs)]
+    *turn_one, upper, lower, mine, theirs, first_rows, second_rows = (
+        lax.optimization_barrier((*turn_one, upper, lower, *project(*turn_one), *turn_two))
+    )
+    here.append((mine, theirs))
+    last = swap_far(*turn_one, 1)
+    here.append(project(first_rows, second_rows))
+    lower, mine, theirs = lax.optimization_barrier((lower, *here[2]))
+    here[2] = mine, theirs
+    lower = send(lower, x=1)
+    *last, mine, theirs = lax.optimization_barrier((*last, *here[2]))
+    here[2] = mine, theirs
+    here.append(project(*last))
     by_place = [
         here[0],
         [jnp.where(core == 0, a, b) for a, b in zip(here[1], here[2])],
@@ -184,10 +214,18 @@
     projected = jnp.concatenate([mine + send(theirs, core=1) for mine, theirs in by_place])
 
     attended = attend(projected, token_positions(z, y), head_size)
-    across_x = send(attended, x=1)
-    across_core = send(attended, core=1)
-    across_both = send(across_x, core=1)
-    heads = jnp.concatenate([attended, across_core, across_x, across_both], axis=1)
+    own_heads = jnp.concatenate([attended, send(attended, x=1)], axis=1)
+    heads = jnp.concatenate([own_heads, send(own_heads, core=1)], axis=1)
+
+    upper, lower, _ = lax.optimization_barrier((upper, lower, attended))
+    out_halves = jnp.concatenate([out_kept, upper, lower])
+    left, right = out_halves[:, :quarter], out_halves[:, quarter:]
+    out_block = jnp.concatenate(
+        [
+            jnp.where(core == 0, left, right),
+            send(jnp.where(core == 0, right, left), core=1),
+        ]
+    )
 
     def turns(blocks):
         middle = jnp.where(core == 0, blocks[2], blocks[1])

time: 140 us -> 143 us (1.021)
  starting transfers between devices: 38.6 us -> 45 us
  waiting for transfers between devices: 73.6 us -> 69.5 us
  other arithmetic: 6.31 us -> 8.18 us
    ppermute x9 -> x6, waiting for transfers between devices: 41.4 us -> 24.3 us  [swap_both(): first = lax.ppermute(first, AXES, swap_pairs(first_axis, turn))]
    ppermute x0 -> x6, waiting for transfers between devices: none -> 16.1 us  [the longest x3 15.1 us: swap_far(): lax.ppermute(first_rows, AXES, swap_pairs('z', turn))]
    ppermute x0 -> x6, starting transfers between devices: none -> 7.66 us  [the longest x3 4.03 us: swap_far(): lax.ppermute(first_rows, AXES, swap_pairs('z', turn))]
    ppermute x16 -> x15, starting transfers between devices: 12.5 us -> 17.1 us  [send(): return lax.ppermute(value, AXES, pairs)]
    ppermute x9 -> x6, starting transfers between devices: 11.2 us -> 7.32 us  [swap_both(): first = lax.ppermute(first, AXES, swap_pairs(first_axis, turn))]
    ppermute x16 -> x15, waiting for transfers between devices: 24.1 us -> 21.2 us  [send(): return lax.ppermute(value, AXES, pairs)]
    ppermute x9 -> x6, starting transfers between devices: 14.9 us -> 12.9 us  [swap_both(): second = lax.ppermute(second, AXES, swap_pairs(second_axis, turn))]
    select_n x0 -> x4, other arithmetic: none -> 1.49 us  [the longest x1 1.38 us: shards(): jnp.where(core == 0, left, right)]
  transfers between devices with their start and end apart: 34 -> 33, of which waited for: 23 -> 26; matrix products, arithmetic and copies ran while one was open for 13% -> 13% of each run, Pallas kernels for 0% -> 0%
where the time goes in v4:
time: 143 us; the launch traced here: 142 us
  waiting for transfers between devices  69.5 us (49%)
  starting transfers between devices  45 us (31%)
  matrix products  14.7 us (10%)
  other arithmetic  8.18 us (6%)
  local copies, waits for them, and re-layouts  4.53 us (3%)
    ppermute x6, waiting for transfers between devices, swap_both(): first = lax.ppermute(first, AXES, swap_pairs(first_axis, turn))  24.3 us
    ppermute x15, waiting for transfers between devices, send(): return lax.ppermute(value, AXES, pairs)  21.2 us
    ppermute x15, starting transfers between devices, send(): return lax.ppermute(value, AXES, pairs)  17.1 us
    ppermute x3, waiting for transfers between devices, swap_far(): lax.ppermute(first_rows, AXES, swap_pairs('z', turn))  15.1 us
    ppermute x6, starting transfers between devices, swap_both(): second = lax.ppermute(second, AXES, swap_pairs(second_axis, turn))  12.9 us
    ppermute x6, waiting for transfers between devices, swap_both(): second = lax.ppermute(second, AXES, swap_pairs(second_axis, turn))  7.92 us
    ppermute x6, starting transfers between devices, swap_both(): first = lax.ppermute(first, AXES, swap_pairs(first_axis, turn))  7.32 us
    dot_general x4, matrix products, project(): theirs = jnp.dot(rows, swapped_weights, preferred_element_type=jnp.float32)  4.25 us
  transfers between devices with their start and end apart: 33, of which 26 were waited for; matrix products, arithmetic and copies ran while one was open for 13% of the time, Pallas kernels for 0%

profile of v4, /device:TPU:0, one launch (start us, length us, event | category | flops | bytes accessed | tf_op | source)
XLA Modules:
  0.0 142.5 jit_solution(10897754188445924455)
XLA Ops:
  4.9 3.2 %collective-permute-start.1 = (bf16[16,6144]{1,0:T(8,128)(2,1)S(1)}, bf16[16,6144]{1,0:T(8,128)(2,1)S(1)}, u32[]{:S(2)}, u32[]{:S(2)}) collective-permute-start(bf16[16,6144]{1,0:T(8,128)(2,1)S(1)} %maximum_select_fusion), channel_id=1, source_target_pairs={{0,8},{1,9},{2,10},{3,11},{4,12},{5,13},{6,14},{7,15},{8,0},{9,1},... | collective-permute-start | bytes 589832 | tf_op jit(solution)/shard_map/ppermute | solution.py:32
  8.1 3.0 %constant_dynamic-slice_fusion.2 = bf16[6144,384]{1,0:T(8,128)(2,1)S(1)} fusion(bf16[12288,384]{1,0:T(8,128)(2,1)} %bitcast.56, s32[]{:T(128)S(6)} %select_n.246), kind=kLoop, calls=%fused_computation.125 | loop fusion | bytes 9437188 | tf_op jit(solution)/shard_map/dynamic_slice | solution.py:145
  11.0 2.4 %collective-permute-done.1 = bf16[16,6144]{1,0:T(8,128)(2,1)S(1)} collective-permute-done((bf16[16,6144]{1,0:T(8,128)(2,1)S(1)}, bf16[16,6144]{1,0:T(8,128)(2,1)S(1)}, u32[]{:S(2)}, u32[]{:S(2)}) %collective-permute-start.1) | collective-permute-done | bytes 196640 | tf_op jit(solution)/shard_map/ppermute | solution.py:32
  23.2 4.0 %collective-permute-start.5 = (bf16[32,6144]{1,0:T(8,128)(2,1)S(1)}, bf16[32,6144]{1,0:T(8,128)(2,1)S(1)}, u32[]{:S(2)}, u32[]{:S(2)}) collective-permute-start(bf16[32,6144]{1,0:T(8,128)(2,1)S(1)} %pad_maximum_fusion.8), channel_id=1, source_target_pairs={{0,48},{1,17},{2,50},{3,19},{4,52},{5,21},{6,54},{7,23},{8,56},{9,... | collective-permute-start | bytes 1179656 | tf_op jit(solution)/shard_map/ppermute | solution.py:59
  27.6 2.5 %collective-permute-done.4 = bf16[32,6144]{1,0:T(8,128)(2,1)S(1)} collective-permute-done((bf16[32,6144]{1,0:T(8,128)(2,1)S(1)}, bf16[32,6144]{1,0:T(8,128)(2,1)S(1)}, u32[]{:S(2)}, u32[]{:S(2)}) %collective-permute-start.4) | collective-permute-done | bytes 393248 | tf_op jit(solution)/shard_map/ppermute | solution.py:58
  30.0 3.0 %collective-permute-done.5 = bf16[32,6144]{1,0:T(8,128)(2,1)S(1)} collective-permute-done((bf16[32,6144]{1,0:T(8,128)(2,1)S(1)}, bf16[32,6144]{1,0:T(8,128)(2,1)S(1)}, u32[]{:S(2)}, u32[]{:S(2)}) %collective-permute-start.5) | collective-permute-done | bytes 393248 | tf_op jit(solution)/shard_map/ppermute | solution.py:59
  33.4 3.3 %collective-permute-start.11 = (bf16[64,6144]{1,0:T(8,128)(2,1)S(1)}, bf16[64,6144]{1,0:T(8,128)(2,1)S(1)}, u32[]{:S(2)}, u32[]{:S(2)}) collective-permute-start(bf16[64,6144]{1,0:T(8,128)(2,1)S(1)} %pad_maximum_fusion.3), channel_id=1, source_target_pairs={{0,48},{1,17},{2,50},{3,19},{4,52},{5,21},{6,54},{7,23},{8,56},{9,... | collective-permute-start | bytes 2359304 | tf_op jit(solution)/shard_map/ppermute | solution.py:181
  38.1 3.1 %collective-permute-start.10 = (bf16[64,6144]{1,0:T(8,128)(2,1)S(1)}, bf16[64,6144]{1,0:T(8,128)(2,1)S(1)}, u32[]{:S(2)}, u32[]{:S(2)}) collective-permute-start(bf16[64,6144]{1,0:T(8,128)(2,1)S(1)} %get-tuple-element.83), channel_id=1, source_target_pairs={{0,8},{1,9},{2,10},{3,11},{4,12},{5,13},{6,14},{7,15},{8,0},{9,1},... | collective-permute-start | bytes 2359304 | tf_op jit(solution)/shard_map/ppermute | solution.py:32
  43.4 10.0 %collective-permute-done.7 = bf16[64,6144]{1,0:T(8,128)(2,1)S(1)} collective-permute-done((bf16[64,6144]{1,0:T(8,128)(2,1)S(1)}, bf16[64,6144]{1,0:T(8,128)(2,1)S(1)}, u32[]{:S(2)}, u32[]{:S(2)}) %collective-permute-start.7) | collective-permute-done | bytes 786464 | tf_op jit(solution)/shard_map/ppermute | solution.py:181
  61.5 3.1 %collective-permute-start.20 = (bf16[64,6144]{1,0:T(8,128)(2,1)S(1)}, bf16[64,6144]{1,0:T(8,128)(2,1)S(1)}, u32[]{:S(2)}, u32[]{:S(2)}) collective-permute-start(bf16[64,6144]{1,0:T(8,128)(2,1)S(1)} %get-tuple-element.100), channel_id=1, source_target_pairs={{0,8},{1,9},{2,10},{3,11},{4,12},{5,13},{6,14},{7,15},{8,0},{9,1},... | collective-permute-start | bytes 2359304 | tf_op jit(solution)/shard_map/ppermute | solution.py:32
  64.6 5.1 %collective-permute-done.13 = bf16[64,6144]{1,0:T(8,128)(2,1)S(1)} collective-permute-done((bf16[64,6144]{1,0:T(8,128)(2,1)S(1)}, bf16[64,6144]{1,0:T(8,128)(2,1)S(1)}, u32[]{:S(2)}, u32[]{:S(2)}) %collective-permute-start.13) | collective-permute-done | bytes 786464 | tf_op jit(solution)/shard_map/ppermute | solution.py:181
  75.9 6.4 %collective-permute-done.20 = bf16[64,6144]{1,0:T(8,128)(2,1)S(1)} collective-permute-done((bf16[64,6144]{1,0:T(8,128)(2,1)S(1)}, bf16[64,6144]{1,0:T(8,128)(2,1)S(1)}, u32[]{:S(2)}, u32[]{:S(2)}) %collective-permute-start.20) | collective-permute-done | bytes 786464 | tf_op jit(solution)/shard_map/ppermute | solution.py:32
  83.8 3.0 %collective-permute-start.18 = (bf16[512,128]{0,1:T(8,128)(2,1)S(1)}, bf16[512,128]{0,1:T(8,128)(2,1)S(1)}, u32[]{:S(2)}, u32[]{:S(2)}) collective-permute-start(bf16[512,128]{0,1:T(8,128)(2,1)S(1)} %convolution_convert_fusion.1), channel_id=1, source_target_pairs={{0,8},{1,9},{2,10},{3,11},{4,12},{5,13},{6,14},{7,15},{8,0},{9,1},... | collective-permute-start | bytes 393224 | tf_op jit(solution)/shard_map/ppermute | solution.py:32
  86.9 4.4 %collective-permute-done.18 = bf16[512,128]{0,1:T(8,128)(2,1)S(1)} collective-permute-done((bf16[512,128]{0,1:T(8,128)(2,1)S(1)}, bf16[512,128]{0,1:T(8,128)(2,1)S(1)}, u32[]{:S(2)}, u32[]{:S(2)}) %collective-permute-start.18) | collective-permute-done | bytes 131104 | tf_op jit(solution)/shard_map/ppermute | solution.py:32
  93.2 2.4 %convolution_convert_fusion = bf16[256,3072]{1,0:T(8,128)(2,1)S(1)} fusion(bf16[256,3072]{1,0:T(8,128)(2,1)} %collective-permute-done.21, bf16[256,3072]{1,0:T(8,128)(2,1)S(1)} %get-tuple-element.121, bf16[64,512]{1,0:T(8,128)(2,1)S(1)} %get-tuple-element.142, bf16[64,512]{1,0:T(8,128)(2,1)S(1)} %get-tuple-element.147, ...), kind=kOutput, calls=%fused_computation | convolution fusion | flops 813432832 | bytes 4980736 | tf_op jit(solution)/shard_map/dot_general | solution.py:238
  96.2 2.4 %collective-permute-start.23 = (bf16[128,3072]{1,0:T(8,128)(2,1)S(1)}, bf16[128,3072]{1,0:T(8,128)(2,1)S(1)}, u32[]{:S(2)}, u32[]{:S(2)}) collective-permute-start(bf16[128,3072]{1,0:T(8,128)(2,1)S(1)} %get-tuple-element.104), channel_id=1, source_target_pairs={{0,6},{1,3},{2,4},{3,1},{4,2},{5,7},{6,0},{7,5},{8,14},{9,11},{10,... | collective-permute-start | bytes 2359304 | tf_op jit(solution)/shard_map/ppermute | solution.py:59
  98.5 2.4 %fusion.8 = f32[256,3072]{1,0:T(8,128)S(1)} fusion(bf16[256,3072]{1,0:T(8,128)(2,1)} %collective-permute-done.21, bf16[256,3072]{1,0:T(8,128)(2,1)S(1)} %get-tuple-element.121, bf16[64,512]{1,0:T(8,128)(2,1)S(1)} %get-tuple-element.146, bf16[64,512]{1,0:T(8,128)(2,1)S(1)} %get-tuple-element.144, bf16[64,512]{1,0:T(8,128)(2,1)S(1)} %get-tuple-element.148, ...), kind=kOutput, calls=%fused_computation.10 | convolution fusion | flops 812646400 | bytes 6553600 | tf_op jit(solution)/shard_map/dot_general | solution.py:243
  100.9 8.1 %collective-permute-done.22 = bf16[128,3072]{1,0:T(8,128)(2,1)S(1)} collective-permute-done((bf16[128,3072]{1,0:T(8,128)(2,1)S(1)}, bf16[128,3072]{1,0:T(8,128)(2,1)S(1)}, u32[]{:S(2)}, u32[]{:S(2)}) %collective-permute-start.22) | collective-permute-done | bytes 786464 | tf_op jit(solution)/shard_map/ppermute | solution.py:58
  110.9 6.9 %collective-permute-done.24 = bf16[64,3072]{1,0:T(8,128)(2,1)S(1)} collective-permute-done((bf16[64,3072]{1,0:T(8,128)(2,1)S(1)}, bf16[64,3072]{1,0:T(8,128)(2,1)S(1)}, u32[]{:S(2)}, u32[]{:S(2)}) %collective-permute-start.24) | collective-permute-done | bytes 393248 | tf_op jit(solution)/shard_map/ppermute | solution.py:58
  118.4 2.4 %collective-permute-start.26 = (bf16[32,3072]{1,0:T(8,128)(2,1)S(1)}, bf16[32,3072]{1,0:T(8,128)(2,1)S(1)}, u32[]{:S(2)}, u32[]{:S(2)}) collective-permute-start(bf16[32,3072]{1,0:T(8,128)(2,1)S(1)} %pad_maximum_fusion.10), channel_id=1, source_target_pairs={{0,6},{1,3},{2,4},{3,1},{4,2},{5,7},{6,0},{7,5},{8,14},{9,11},{10,... | collective-permute-start | bytes 589832 | tf_op jit(solution)/shard_map/ppermute | solution.py:58
  120.9 2.5 %collective-permute-start.27 = (bf16[32,3072]{1,0:T(8,128)(2,1)S(1)}, bf16[32,3072]{1,0:T(8,128)(2,1)S(1)}, u32[]{:S(2)}, u32[]{:S(2)}) collective-permute-start(bf16[32,3072]{1,0:T(8,128)(2,1)S(1)} %pad_maximum_fusion.11), channel_id=1, source_target_pairs={{0,48},{1,17},{2,50},{3,19},{4,52},{5,21},{6,54},{7,23},{8,56},{9,... | collective-permute-start | bytes 589832 | tf_op jit(solution)/shard_map/ppermute | solution.py:59
  125.4 2.5 %collective-permute-done.27 = bf16[32,3072]{1,0:T(8,128)(2,1)S(1)} collective-permute-done((bf16[32,3072]{1,0:T(8,128)(2,1)S(1)}, bf16[32,3072]{1,0:T(8,128)(2,1)S(1)}, u32[]{:S(2)}, u32[]{:S(2)}) %collective-permute-start.27) | collective-permute-done | bytes 196640 | tf_op jit(solution)/shard_map/ppermute | solution.py:59
  129.6 3.1 %collective-permute-done.28 = bf16[16,3072]{1,0:T(8,128)(2,1)S(1)} collective-permute-done((bf16[16,3072]{1,0:T(8,128)(2,1)S(1)}, bf16[16,3072]{1,0:T(8,128)(2,1)S(1)}, u32[]{:S(2)}, u32[]{:S(2)}) %collective-permute-start.28) | collective-permute-done | bytes 98336 | tf_op jit(solution)/shard_map/ppermute | solution.py:58
  139.3 2.5 %collective-permute-done.32 = bf16[8,6144]{1,0:T(8,128)(2,1)S(1)} collective-permute-done((bf16[8,6144]{1,0:T(8,128)(2,1)S(1)}, bf16[8,6144]{1,0:T(8,128)(2,1)S(1)}, u32[]{:S(2)}, u32[]{:S(2)}) %collective-permute-start.32) | collective-permute-done | bytes 98336 | tf_op jit(solution)/shard_map/ppermute | solution.py:32
  (122 shorter events, 50.4 us)
Async XLA Ops:
  4.9 8.5 %collective-permute-start.1 = (bf16[16,6144]{1,0:T(8,128)(2,1)S(1)}, bf16[16,6144]{1,0:T(8,128)(2,1)S(1)}, u32[]{:S(2)}, u32[]{:S(2)}) collective-permute-start(bf16[16,6144]{1,0:T(8,128)(2,1)S(1)} %maximum_select_fusion), channel_id=1, source_target_pairs={{0,8},{1,9},{2,10},{3,11},{4,12},{5,13},{6,14},{7,15},{8,0},{9,1},... | collective-permute-start | bytes 589832 | tf_op jit(solution)/shard_map/ppermute | solution.py:32
  13.4 19.6 %collective-permute-start.6 = (bf16[6144,384]{1,0:T(8,128)(2,1)S(1)}, bf16[6144,384]{1,0:T(8,128)(2,1)S(1)}, u32[]{:S(2)}, u32[]{:S(2)}) collective-permute-start(bf16[6144,384]{1,0:T(8,128)(2,1)S(1)} %constant_dynamic-slice_fusion.2), channel_id=1, source_target_pairs={{0,1},{1,0},{2,3},{3,2},{4,5},{5,4},{6,7},{7,6},{8,9},{9,8},{10,11... | collective-permute-start | bytes 14155784 | tf_op jit(solution)/shard_map/ppermute | solution.py:32
  13.5 5.7 %collective-permute-start.2 = (bf16[16,6144]{1,0:T(8,128)(2,1)S(1)}, bf16[16,6144]{1,0:T(8,128)(2,1)S(1)}, u32[]{:S(2)}, u32[]{:S(2)}) collective-permute-start(bf16[16,6144]{1,0:T(8,128)(2,1)S(1)} %get-tuple-element.65), channel_id=1, source_target_pairs={{0,2},{1,7},{2,0},{3,5},{4,6},{5,3},{6,4},{7,1},{8,10},{9,15},{10,... | collective-permute-start | bytes 589832 | tf_op jit(solution)/shard_map/ppermute | solution.py:58
  15.2 5.7 %collective-permute-start.3 = (bf16[16,6144]{1,0:T(8,128)(2,1)S(1)}, bf16[16,6144]{1,0:T(8,128)(2,1)S(1)}, u32[]{:S(2)}, u32[]{:S(2)}) collective-permute-start(bf16[16,6144]{1,0:T(8,128)(2,1)S(1)} %get-tuple-element.66), channel_id=1, source_target_pairs={{0,16},{1,49},{2,18},{3,51},{4,20},{5,53},{6,22},{7,55},{8,24},{9,... | collective-permute-start | bytes 589832 | tf_op jit(solution)/shard_map/ppermute | solution.py:59
  20.9 9.1 %collective-permute-start.4 = (bf16[32,6144]{1,0:T(8,128)(2,1)S(1)}, bf16[32,6144]{1,0:T(8,128)(2,1)S(1)}, u32[]{:S(2)}, u32[]{:S(2)}) collective-permute-start(bf16[32,6144]{1,0:T(8,128)(2,1)S(1)} %pad_maximum_fusion.7), channel_id=1, source_target_pairs={{0,6},{1,3},{2,4},{3,1},{4,2},{5,7},{6,0},{7,5},{8,14},{9,11},{10,... | collective-permute-start | bytes 1179656 | tf_op jit(solution)/shard_map/ppermute | solution.py:58
  23.2 9.8 %collective-permute-start.5 = (bf16[32,6144]{1,0:T(8,128)(2,1)S(1)}, bf16[32,6144]{1,0:T(8,128)(2,1)S(1)}, u32[]{:S(2)}, u32[]{:S(2)}) collective-permute-start(bf16[32,6144]{1,0:T(8,128)(2,1)S(1)} %pad_maximum_fusion.8), channel_id=1, source_target_pairs={{0,48},{1,17},{2,50},{3,19},{4,52},{5,21},{6,54},{7,23},{8,56},{9,... | collective-permute-start | bytes 1179656 | tf_op jit(solution)/shard_map/ppermute | solution.py:59
  33.3 20.1 %collective-permute-start.7 = (bf16[64,6144]{1,0:T(8,128)(2,1)S(1)}, bf16[64,6144]{1,0:T(8,128)(2,1)S(1)}, u32[]{:S(2)}, u32[]{:S(2)}) collective-permute-start(bf16[64,6144]{1,0:T(8,128)(2,1)S(1)} %pad_maximum_fusion.3), channel_id=1, source_target_pairs={{0,16},{1,49},{2,18},{3,51},{4,20},{5,53},{6,22},{7,55},{8,24},{9,... | collective-permute-start | bytes 2359304 | tf_op jit(solution)/shard_map/ppermute | solution.py:181
  33.4 23.0 %collective-permute-start.11 = (bf16[64,6144]{1,0:T(8,128)(2,1)S(1)}, bf16[64,6144]{1,0:T(8,128)(2,1)S(1)}, u32[]{:S(2)}, u32[]{:S(2)}) collective-permute-start(bf16[64,6144]{1,0:T(8,128)(2,1)S(1)} %pad_maximum_fusion.3), channel_id=1, source_target_pairs={{0,48},{1,17},{2,50},{3,19},{4,52},{5,21},{6,54},{7,23},{8,56},{9,... | collective-permute-start | bytes 2359304 | tf_op jit(solution)/shard_map/ppermute | solution.py:181
  36.7 17.2 %collective-permute-start.8 = (bf16[64,6144]{1,0:T(8,128)(2,1)S(1)}, bf16[64,6144]{1,0:T(8,128)(2,1)S(1)}, u32[]{:S(2)}, u32[]{:S(2)}) collective-permute-start(bf16[64,6144]{1,0:T(8,128)(2,1)S(1)} %pad_maximum_fusion.4), channel_id=1, source_target_pairs={{0,2},{1,7},{2,0},{3,5},{4,6},{5,3},{6,4},{7,1},{8,10},{9,15},{10,... | collective-permute-start | bytes 2359304 | tf_op jit(solution)/shard_map/ppermute | solution.py:182
  37.4 19.0 %collective-permute-start.12 = (bf16[64,6144]{1,0:T(8,128)(2,1)S(1)}, bf16[64,6144]{1,0:T(8,128)(2,1)S(1)}, u32[]{:S(2)}, u32[]{:S(2)}) collective-permute-start(bf16[64,6144]{1,0:T(8,128)(2,1)S(1)} %pad_maximum_fusion.4), channel_id=1, source_target_pairs={{0,6},{1,3},{2,4},{3,1},{4,2},{5,7},{6,0},{7,5},{8,14},{9,11},{10,... | collective-permute-start | bytes 2359304 | tf_op jit(solution)/shard_map/ppermute | solution.py:182
  38.1 18.2 %collective-permute-start.10 = (bf16[64,6144]{1,0:T(8,128)(2,1)S(1)}, bf16[64,6144]{1,0:T(8,128)(2,1)S(1)}, u32[]{:S(2)}, u32[]{:S(2)}) collective-permute-start(bf16[64,6144]{1,0:T(8,128)(2,1)S(1)} %get-tuple-element.83), channel_id=1, source_target_pairs={{0,8},{1,9},{2,10},{3,11},{4,12},{5,13},{6,14},{7,15},{8,0},{9,1},... | collective-permute-start | bytes 2359304 | tf_op jit(solution)/shard_map/ppermute | solution.py:32
  53.9 10.7 %collective-permute-start.9 = (f32[128,384]{1,0:T(8,128)S(1)}, f32[128,384]{1,0:T(8,128)S(1)}, u32[]{:S(2)}, u32[]{:S(2)}) collective-permute-start(f32[128,384]{1,0:T(8,128)S(1)} %fusion.53), channel_id=1, source_target_pairs={{0,1},{1,0},{2,3},{3,2},{4,5},{5,4},{6,7},{7,6},{8,9},{9,8},{10,11... | collective-permute-start | bytes 589832 | tf_op jit(solution)/shard_map/ppermute | solution.py:32
  56.4 13.3 %collective-permute-start.13 = (bf16[64,6144]{1,0:T(8,128)(2,1)S(1)}, bf16[64,6144]{1,0:T(8,128)(2,1)S(1)}, u32[]{:S(2)}, u32[]{:S(2)}) collective-permute-start(bf16[64,6144]{1,0:T(8,128)(2,1)S(1)} %collective-permute-done.7), channel_id=1, source_target_pairs={{0,48},{1,17},{2,50},{3,19},{4,52},{5,21},{6,54},{7,23},{8,56},{9,... | collective-permute-start | bytes 2359304 | tf_op jit(solution)/shard_map/ppermute | solution.py:181
  57.1 13.2 %collective-permute-start.14 = (bf16[64,6144]{1,0:T(8,128)(2,1)S(1)}, bf16[64,6144]{1,0:T(8,128)(2,1)S(1)}, u32[]{:S(2)}, u32[]{:S(2)}) collective-permute-start(bf16[64,6144]{1,0:T(8,128)(2,1)S(1)} %collective-permute-done.8), channel_id=1, source_target_pairs={{0,6},{1,3},{2,4},{3,1},{4,2},{5,7},{6,0},{7,5},{8,14},{9,11},{10,... | collective-permute-start | bytes 2359304 | tf_op jit(solution)/shard_map/ppermute | solution.py:182
  61.5 20.8 %collective-permute-start.20 = (bf16[64,6144]{1,0:T(8,128)(2,1)S(1)}, bf16[64,6144]{1,0:T(8,128)(2,1)S(1)}, u32[]{:S(2)}, u32[]{:S(2)}) collective-permute-start(bf16[64,6144]{1,0:T(8,128)(2,1)S(1)} %get-tuple-element.100), channel_id=1, source_target_pairs={{0,8},{1,9},{2,10},{3,11},{4,12},{5,13},{6,14},{7,15},{8,0},{9,1},... | collective-permute-start | bytes 2359304 | tf_op jit(solution)/shard_map/ppermute | solution.py:32
  83.8 9.4 %collective-permute-start.21 = (bf16[256,3072]{1,0:T(8,128)(2,1)}, bf16[256,3072]{1,0:T(8,128)(2,1)}, u32[]{:S(2)}, u32[]{:S(2)}) collective-permute-start(bf16[256,3072]{1,0:T(8,128)(2,1)} %get-tuple-element.122), channel_id=1, source_target_pairs={{0,1},{1,0},{2,3},{3,2},{4,5},{5,4},{6,7},{7,6},{8,9},{9,8},{10,11... | collective-permute-start | bytes 4718600 | tf_op jit(solution)/shard_map/ppermute | solution.py:32
  83.8 7.4 %collective-permute-start.18 = (bf16[512,128]{0,1:T(8,128)(2,1)S(1)}, bf16[512,128]{0,1:T(8,128)(2,1)S(1)}, u32[]{:S(2)}, u32[]{:S(2)}) collective-permute-start(bf16[512,128]{0,1:T(8,128)(2,1)S(1)} %convolution_convert_fusion.1), channel_id=1, source_target_pairs={{0,8},{1,9},{2,10},{3,11},{4,12},{5,13},{6,14},{7,15},{8,0},{9,1},... | collective-permute-start | bytes 393224 | tf_op jit(solution)/shard_map/ppermute | solution.py:32
  95.7 13.3 %collective-permute-start.22 = (bf16[128,3072]{1,0:T(8,128)(2,1)S(1)}, bf16[128,3072]{1,0:T(8,128)(2,1)S(1)}, u32[]{:S(2)}, u32[]{:S(2)}) collective-permute-start(bf16[128,3072]{1,0:T(8,128)(2,1)S(1)} %get-tuple-element.103), channel_id=1, source_target_pairs={{0,48},{1,17},{2,50},{3,19},{4,52},{5,21},{6,54},{7,23},{8,56},{9,... | collective-permute-start | bytes 2359304 | tf_op jit(solution)/shard_map/ppermute | solution.py:58
  96.2 13.2 %collective-permute-start.23 = (bf16[128,3072]{1,0:T(8,128)(2,1)S(1)}, bf16[128,3072]{1,0:T(8,128)(2,1)S(1)}, u32[]{:S(2)}, u32[]{:S(2)}) collective-permute-start(bf16[128,3072]{1,0:T(8,128)(2,1)S(1)} %get-tuple-element.104), channel_id=1, source_target_pairs={{0,6},{1,3},{2,4},{3,1},{4,2},{5,7},{6,0},{7,5},{8,14},{9,11},{10,... | collective-permute-start | bytes 2359304 | tf_op jit(solution)/shard_map/ppermute | solution.py:59
  110.0 7.9 %collective-permute-start.24 = (bf16[64,3072]{1,0:T(8,128)(2,1)S(1)}, bf16[64,3072]{1,0:T(8,128)(2,1)S(1)}, u32[]{:S(2)}, u32[]{:S(2)}) collective-permute-start(bf16[64,3072]{1,0:T(8,128)(2,1)S(1)} %slice.341), channel_id=1, source_target_pairs={{0,16},{1,49},{2,18},{3,51},{4,20},{5,53},{6,22},{7,55},{8,24},{9,... | collective-permute-start | bytes 1179656 | tf_op jit(solution)/shard_map/ppermute | solution.py:58
  110.3 7.8 %collective-permute-start.25 = (bf16[64,3072]{1,0:T(8,128)(2,1)S(1)}, bf16[64,3072]{1,0:T(8,128)(2,1)S(1)}, u32[]{:S(2)}, u32[]{:S(2)}) collective-permute-start(bf16[64,3072]{1,0:T(8,128)(2,1)S(1)} %slice.340), channel_id=1, source_target_pairs={{0,2},{1,7},{2,0},{3,5},{4,6},{5,3},{6,4},{7,1},{8,10},{9,15},{10,... | collective-permute-start | bytes 1179656 | tf_op jit(solution)/shard_map/ppermute | solution.py:59
  118.4 7.0 %collective-permute-start.26 = (bf16[32,3072]{1,0:T(8,128)(2,1)S(1)}, bf16[32,3072]{1,0:T(8,128)(2,1)S(1)}, u32[]{:S(2)}, u32[]{:S(2)}) collective-permute-start(bf16[32,3072]{1,0:T(8,128)(2,1)S(1)} %pad_maximum_fusion.10), channel_id=1, source_target_pairs={{0,6},{1,3},{2,4},{3,1},{4,2},{5,7},{6,0},{7,5},{8,14},{9,11},{10,... | collective-permute-start | bytes 589832 | tf_op jit(solution)/shard_map/ppermute | solution.py:58
  120.9 7.0 %collective-permute-start.27 = (bf16[32,3072]{1,0:T(8,128)(2,1)S(1)}, bf16[32,3072]{1,0:T(8,128)(2,1)S(1)}, u32[]{:S(2)}, u32[]{:S(2)}) collective-permute-start(bf16[32,3072]{1,0:T(8,128)(2,1)S(1)} %pad_maximum_fusion.11), channel_id=1, source_target_pairs={{0,48},{1,17},{2,50},{3,19},{4,52},{5,21},{6,54},{7,23},{8,56},{9,... | collective-permute-start | bytes 589832 | tf_op jit(solution)/shard_map/ppermute | solution.py:59
  135.9 5.8 %collective-permute-start.32 = (bf16[8,6144]{1,0:T(8,128)(2,1)S(1)}, bf16[8,6144]{1,0:T(8,128)(2,1)S(1)}, u32[]{:S(2)}, u32[]{:S(2)}) collective-permute-start(bf16[8,6144]{1,0:T(8,128)(2,1)S(1)} %get-tuple-element.158), channel_id=1, source_target_pairs={{0,72},{1,73},{2,74},{3,75},{4,76},{5,77},{6,78},{7,79},{8,64},{9,... | collective-permute-start | bytes 294920 | tf_op jit(solution)/shard_map/ppermute | solution.py:32
  (13 other events, 91.8 us)

commit v5 on v3

--- a/solution.py
+++ b/solution.py
@@ -53,11 +53,11 @@
     return pairs
 
 
-def swap_both(first, first_axis, second, second_axis, turn, *beside):
-    first, second = lax.optimization_barrier((first, second))
-    first = lax.ppermute(first, AXES, swap_pairs(first_axis, turn))
-    second = lax.ppermute(second, AXES, swap_pairs(second_axis, turn))
-    return lax.optimization_barrier((first, second, *beside))
+def swap_both(first, first_axis, second, second_axis, turn):
+    return (
+        lax.ppermute(first, AXES, swap_pairs(first_axis, turn)),
+        lax.ppermute(second, AXES, swap_pairs(second_axis, turn)),
+    )
 
 
 def near_rows(own, one, two, core):
@@ -72,28 +72,12 @@
     )
 
 
-def swap_sum(first_far, first_near, second_far, second_near, first_axis, second_axis):
-    size = first_far.shape[0] // 2
-    first_got, second_got = swap_both(
-        first_far.astype(jnp.bfloat16),
-        first_axis,
-        second_far.astype(jnp.bfloat16),
-        second_axis,
-        1,
-    )
-    first_sum = first_near + first_got.astype(jnp.float32)
-    second_sum = second_near + second_got.astype(jnp.float32)
-    first_got, second_got = swap_both(
-        first_sum[size:].astype(jnp.bfloat16),
-        first_axis,
-        second_sum[size:].astype(jnp.bfloat16),
-        second_axis,
-        0,
-    )
-    return (
-        first_sum[:size] + first_got.astype(jnp.float32),
-        second_sum[:size] + second_got.astype(jnp.float32),
-    )
+def swap_sum(far, near, axis):
+    size = near.shape[0] // 2
+    got = lax.ppermute(far.astype(jnp.bfloat16), AXES, swap_pairs(axis, 1))
+    total = near + got.astype(jnp.float32)
+    got = lax.ppermute(total[size:].astype(jnp.bfloat16), AXES, swap_pairs(axis, 0))
+    return total[:size] + got.astype(jnp.float32)
 
 
 def token_positions(z, y):
@@ -139,42 +123,53 @@
         core == 0, jnp.concatenate([kept, given]), jnp.concatenate([given, kept])
     )
     head_block, block = lax.optimization_barrier((head_weights[0, :, 0, :], block))
-    other = send(block, x=1)
+    other, their_weights = lax.optimization_barrier(
+        (
+            send(block, x=1),
+            lax.dynamic_slice_in_dim(head_block, (1 - core) * half, half, 0),
+        )
+    )
     first = jnp.where(half_x == 0, block, other)
     second = jnp.where(half_x == 0, other, block)
     own_weights = lax.dynamic_slice_in_dim(head_block, core * half, half, 0)
-    swapped_weights = send(
-        lax.dynamic_slice_in_dim(head_block, (1 - core) * half, half, 0), core=1
-    )
 
     one = swap_both(first, "y", second, "z", 0)
     two = swap_both(
         jnp.concatenate([first, one[0]]), "y", jnp.concatenate([second, one[1]]), "z", 1
     )
-    first_far = [near_rows(first, one[0], two[0], core)]
-    second_far = [near_rows(second, one[1], two[1], core)]
-
-    out_rows, _ = lax.optimization_barrier((output_weights[0], two[0]))
-    out_parts = []
-    for dx, dc in ((0, 0), (0, 1), (1, 0), (1, 1)):
-        start = ((half_x ^ dx) * 2 + (core ^ dc)) * quarter
-        part = lax.dynamic_slice_in_dim(out_rows, start, quarter, 1)
-        out_parts.append(send(part, x=dx, core=dc) if dx or dc else part)
-    out_block = jnp.concatenate(out_parts, axis=0)
-
-    def project(k):
-        rows = jnp.concatenate([first_far[k], second_far[k]])
+    first_own = near_rows(first, one[0], two[0], core)
+    second_own = near_rows(second, one[1], two[1], core)
+    swapped_weights = send(their_weights, core=1)
+
+    out_rows, _ = lax.optimization_barrier((output_weights[0], block))
+    out_kept = lax.dynamic_slice_in_dim(out_rows, half_x * half, half, 1)
+    out_given = lax.dynamic_slice_in_dim(out_rows, (1 - half_x) * half, half, 1)
+    middle = out_given.shape[0] // 2
+    upper, _ = lax.optimization_barrier((out_given[:middle], one))
+    upper = send(upper, x=1)
+
+    def project(first_rows, second_rows):
+        rows = jnp.concatenate([first_rows, second_rows])
         mine = jnp.dot(rows, own_weights, preferred_element_type=jnp.float32)
         theirs = jnp.dot(rows, swapped_weights, preferred_element_type=jnp.float32)
         return mine, theirs
 
-    here = [project(0)]
-    for k, (source, turn) in enumerate(((0, 0), (0, 1), (1, 1))):
-        got = swap_both(first_far[source], "z", second_far[source], "y", turn, *here[k])
-        first_far.append(got[0])
-        second_far.append(got[1])
-        here[k] = got[2:]
-        here.append(project(k + 1))
+    first_own, second_own = lax.optimization_barrier((first_own, second_own))
+    turn_one = swap_both(first_own, "z", second_own, "y", 0)
+    turn_two = swap_both(first_own, "z", second_own, "y", 1)
+    *turn_one, upper, mine, theirs = lax.optimization_barrier(
+        (*turn_one, upper, *project(first_own, second_own))
+    )
+    here = [(mine, theirs)]
+    lower, _ = lax.optimization_barrier((out_given[middle:], upper))
+    lower = send(lower, x=1)
+    *turn_one, first_rows, second_rows = lax.optimization_barrier((*turn_one, *turn_two))
+    last = swap_both(turn_one[0], "z", turn_one[1], "y", 1)
+    here.append(project(*turn_one))
+    here.append(project(first_rows, second_rows))
+    *last, middle_sums = lax.optimization_barrier((*last, here[1:]))
+    here[1:] = middle_sums
+    here.append(project(*last))
     by_place = [
         here[0],
         [jnp.where(core == 0, a, b) for a, b in zip(here[1], here[2])],
@@ -184,10 +179,23 @@
     projected = jnp.concatenate([mine + send(theirs, core=1) for mine, theirs in by_place])
 
     attended = attend(projected, token_positions(z, y), head_size)
-    across_x = send(attended, x=1)
-    across_core = send(attended, core=1)
-    across_both = send(across_x, core=1)
-    heads = jnp.concatenate([attended, across_core, across_x, across_both], axis=1)
+    own_heads = jnp.concatenate([attended, send(attended, x=1)], axis=1)
+    heads = jnp.concatenate([own_heads, send(own_heads, core=1)], axis=1)
+
+    def swap_quarters(rows):
+        left, right = rows[:, :quarter], rows[:, quarter:]
+        given = send(jnp.where(core == 0, right, left), core=1)
+        return jnp.where(core == 0, left, right), given
+
+    lower, _ = lax.optimization_barrier((lower, attended))
+    out_block = jnp.concatenate(
+        [
+            jnp.concatenate(pieces)
+            for pieces in zip(
+                swap_quarters(jnp.concatenate([out_kept, upper])), swap_quarters(lower)
+            )
+        ]
+    )
 
     def turns(blocks):
         middle = jnp.where(core == 0, blocks[2], blocks[1])
@@ -195,31 +203,19 @@
         return [middle, blocks[3]], [blocks[0], kept]
 
     heads = heads.reshape(4, 2, 64, 4 * head_size)
-    first_sent, first_kept = turns(heads[:, 0])
-    second_sent, second_kept = turns(heads[:, 1])
-    edge = jnp.dot(
-        jnp.concatenate(first_sent + second_sent),
-        out_block,
-        preferred_element_type=jnp.float32,
-    ).astype(jnp.bfloat16)
-    rest = jnp.dot(
-        jnp.concatenate(first_kept + second_kept),
-        out_block,
-        preferred_element_type=jnp.float32,
-    )
-    first_sum, second_sum = swap_sum(
-        edge[:128], rest[:128], edge[128:], rest[128:], "z", "y"
-    )
-    first_sent, first_kept = turns(first_sum.reshape(4, 16, quarter))
-    second_sent, second_kept = turns(second_sum.reshape(4, 16, quarter))
-    first_rows, second_rows = swap_sum(
-        jnp.concatenate(first_sent),
-        jnp.concatenate(first_kept),
-        jnp.concatenate(second_sent),
-        jnp.concatenate(second_kept),
-        "y",
-        "z",
-    )
+
+    def section_rows(side, far_axis, near_axis):
+        sent, kept = turns(heads[:, side])
+        edge = jnp.dot(
+            jnp.concatenate(sent), out_block, preferred_element_type=jnp.float32
+        ).astype(jnp.bfloat16)
+        rest = jnp.dot(jnp.concatenate(kept), out_block, preferred_element_type=jnp.float32)
+        total = swap_sum(edge, lax.optimization_barrier(rest), far_axis)
+        sent, kept = turns(total.reshape(4, 16, quarter))
+        return swap_sum(jnp.concatenate(sent), jnp.concatenate(kept), near_axis)
+
+    first_rows = section_rows(0, "z", "y")
+    second_rows = section_rows(1, "y", "z")
     owners = jnp.stack([first_rows, second_rows]).astype(jnp.bfloat16)
     upper, lower = owners[:, :8], owners[:, 8:]
     stay = jnp.where(core == 0, upper, lower)

time: 140 us -> 136 us (0.971)
  waiting for transfers between devices: 73.6 us -> 58.3 us
  starting transfers between devices: 38.6 us -> 46.6 us
  matrix products: 14.9 us -> 17.9 us
  other arithmetic: 6.31 us -> 8.14 us
    ppermute x18, waiting for transfers between devices: 49.5 us -> 41.7 us  [the longest x4 12.2 us: swap_sum(): lax.ppermute(total[size:].astype(jnp.bfloat16), AXES, swap_pairs(axis, 0))]
    ppermute x16, waiting for transfers between devices: 24.1 us -> 16.6 us  [send(): return lax.ppermute(value, AXES, pairs)]
    ppermute x16, starting transfers between devices: 12.5 us -> 19.9 us  [send(): return lax.ppermute(value, AXES, pairs)]
    dot_general x2 -> x4, matrix products: 5.02 us -> 8.17 us  [the longest x2 4.16 us: section_rows(): jnp.dot(jnp.concatenate(sent), out_block, preferred_element_type=jnp.floa...]
    select_n x0 -> x5, other arithmetic: none -> 1.68 us  [the longest x2 1.57 us: swap_quarters(): return (jnp.where(core == 0, left, right), given)]
  transfers between devices with their start and end apart: 34 -> 34, of which waited for: 23 -> 23; matrix products, arithmetic and copies ran while one was open for 13% -> 17% of each run, Pallas kernels for 0% -> 0%
where the time goes in v5:
time: 136 us
  waiting for transfers between devices  58.3 us (43%)
  starting transfers between devices  46.6 us (34%)
  matrix products  17.9 us (13%)
  other arithmetic  8.14 us (6%)
  local copies, waits for them, and re-layouts  4.27 us (3%)
    ppermute x16, starting transfers between devices, send(): return lax.ppermute(value, AXES, pairs)  19.9 us
    ppermute x16, waiting for transfers between devices, send(): return lax.ppermute(value, AXES, pairs)  16.6 us
    ppermute x4, waiting for transfers between devices, swap_sum(): lax.ppermute(total[size:].astype(jnp.bfloat16), AXES, swap_pairs(axis, 0))  12.2 us
    ppermute x4, waiting for transfers between devices, swap_sum(): got = lax.ppermute(far.astype(jnp.bfloat16), AXES, swap_pairs(axis, 1))  12 us
    ppermute x5, waiting for transfers between devices, swap_both(): lax.ppermute(first, AXES, swap_pairs(first_axis, turn))  10.7 us
    ppermute x5, starting transfers between devices, swap_both(): lax.ppermute(second, AXES, swap_pairs(second_axis, turn))  10.4 us
    ppermute x5, starting transfers between devices, swap_both(): lax.ppermute(first, AXES, swap_pairs(first_axis, turn))  9.15 us
    ppermute x5, waiting for transfers between devices, swap_both(): lax.ppermute(second, AXES, swap_pairs(second_axis, turn))  6.89 us
  transfers between devices with their start and end apart: 34, of which 23 were waited for; matrix products, arithmetic and copies ran while one was open for 17% of the time, Pallas kernels for 0%

profile of v5, /device:TPU:0, one launch (start us, length us, event | category | flops | bytes accessed | tf_op | source)
XLA Modules:
  0.0 135.8 jit_solution(12051239681956431266)
XLA Ops:
  4.9 3.2 %collective-permute-start.1 = (bf16[16,6144]{1,0:T(8,128)(2,1)S(1)}, bf16[16,6144]{1,0:T(8,128)(2,1)S(1)}, u32[]{:S(2)}, u32[]{:S(2)}) collective-permute-start(bf16[16,6144]{1,0:T(8,128)(2,1)S(1)} %maximum_select_fusion), channel_id=1, source_target_pairs={{0,8},{1,9},{2,10},{3,11},{4,12},{5,13},{6,14},{7,15},{8,0},{9,1},... | collective-permute-start | bytes 589832 | tf_op jit(solution)/shard_map/ppermute | solution.py:32
  8.1 3.0 %constant_dynamic-slice_fusion.2 = bf16[6144,384]{1,0:T(8,128)(2,1)S(1)} fusion(bf16[12288,384]{1,0:T(8,128)(2,1)} %bitcast.56, s32[]{:T(128)S(6)} %select_n.258), kind=kLoop, calls=%fused_computation.128 | loop fusion | bytes 9437188 | tf_op jit(solution)/shard_map/dynamic_slice | solution.py:129
  17.3 2.3 %collective-permute-start.9 = (bf16[6144,384]{1,0:T(8,128)(2,1)S(1)}, bf16[6144,384]{1,0:T(8,128)(2,1)S(1)}, u32[]{:S(2)}, u32[]{:S(2)}) collective-permute-start(bf16[6144,384]{1,0:T(8,128)(2,1)S(1)} %constant_dynamic-slice_fusion.2), channel_id=1, source_target_pairs={{0,1},{1,0},{2,3},{3,2},{4,5},{5,4},{6,7},{7,6},{8,9},{9,8},{10,11... | collective-permute-start | bytes 14155784 | tf_op jit(solution)/shard_map/ppermute | solution.py:32
  19.7 3.8 %collective-permute-start.5 = (bf16[32,6144]{1,0:T(8,128)(2,1)S(1)}, bf16[32,6144]{1,0:T(8,128)(2,1)S(1)}, u32[]{:S(2)}, u32[]{:S(2)}) collective-permute-start(bf16[32,6144]{1,0:T(8,128)(2,1)S(1)} %pad_maximum_fusion.7), channel_id=1, source_target_pairs={{0,48},{1,17},{2,50},{3,19},{4,52},{5,21},{6,54},{7,23},{8,56},{9,... | collective-permute-start | bytes 1179656 | tf_op jit(solution)/shard_map/ppermute | solution.py:59
  23.5 3.1 %collective-permute-start.3 = (bf16[32,6144]{1,0:T(8,128)(2,1)S(1)}, bf16[32,6144]{1,0:T(8,128)(2,1)S(1)}, u32[]{:S(2)}, u32[]{:S(2)}) collective-permute-start(bf16[32,6144]{1,0:T(8,128)(2,1)S(1)} %pad_maximum_fusion.6), channel_id=1, source_target_pairs={{0,6},{1,3},{2,4},{3,1},{4,2},{5,7},{6,0},{7,5},{8,14},{9,11},{10,... | collective-permute-start | bytes 1179656 | tf_op jit(solution)/shard_map/ppermute | solution.py:58
  26.6 3.0 %collective-permute-start.8 = (bf16[64,6144]{1,0:T(8,128)(2,1)S(1)}, bf16[64,6144]{1,0:T(8,128)(2,1)S(1)}, u32[]{:S(2)}, u32[]{:S(2)}) collective-permute-start(bf16[64,6144]{1,0:T(8,128)(2,1)S(1)} %get-tuple-element.36), channel_id=1, source_target_pairs={{0,8},{1,9},{2,10},{3,11},{4,12},{5,13},{6,14},{7,15},{8,0},{9,1},... | collective-permute-start | bytes 2359304 | tf_op jit(solution)/shard_map/ppermute | solution.py:32
  29.7 2.8 %collective-permute-done.3 = bf16[32,6144]{1,0:T(8,128)(2,1)S(1)} collective-permute-done((bf16[32,6144]{1,0:T(8,128)(2,1)S(1)}, bf16[32,6144]{1,0:T(8,128)(2,1)S(1)}, u32[]{:S(2)}, u32[]{:S(2)}) %collective-permute-start.3) | collective-permute-done | bytes 393248 | tf_op jit(solution)/shard_map/ppermute | solution.py:58
  35.3 2.7 %collective-permute-start.12 = (bf16[64,6144]{1,0:T(8,128)(2,1)S(1)}, bf16[64,6144]{1,0:T(8,128)(2,1)S(1)}, u32[]{:S(2)}, u32[]{:S(2)}) collective-permute-start(bf16[64,6144]{1,0:T(8,128)(2,1)S(1)} %pad_maximum_fusion.3), channel_id=1, source_target_pairs={{0,6},{1,3},{2,4},{3,1},{4,2},{5,7},{6,0},{7,5},{8,14},{9,11},{10,... | collective-permute-start | bytes 2359304 | tf_op jit(solution)/shard_map/ppermute | solution.py:59
  40.2 3.7 %collective-permute-done.8 = bf16[64,6144]{1,0:T(8,128)(2,1)S(1)} collective-permute-done((bf16[64,6144]{1,0:T(8,128)(2,1)S(1)}, bf16[64,6144]{1,0:T(8,128)(2,1)S(1)}, u32[]{:S(2)}, u32[]{:S(2)}) %collective-permute-start.8) | collective-permute-done | bytes 786464 | tf_op jit(solution)/shard_map/ppermute | solution.py:32
  43.9 5.6 %collective-permute-done.6 = bf16[64,6144]{1,0:T(8,128)(2,1)S(1)} collective-permute-done((bf16[64,6144]{1,0:T(8,128)(2,1)S(1)}, bf16[64,6144]{1,0:T(8,128)(2,1)S(1)}, u32[]{:S(2)}, u32[]{:S(2)}) %collective-permute-start.6) | collective-permute-done | bytes 786464 | tf_op jit(solution)/shard_map/ppermute | solution.py:58
  49.4 3.5 %collective-permute-done.7 = bf16[64,6144]{1,0:T(8,128)(2,1)S(1)} collective-permute-done((bf16[64,6144]{1,0:T(8,128)(2,1)S(1)}, bf16[64,6144]{1,0:T(8,128)(2,1)S(1)}, u32[]{:S(2)}, u32[]{:S(2)}) %collective-permute-start.7) | collective-permute-done | bytes 786464 | tf_op jit(solution)/shard_map/ppermute | solution.py:59
  53.0 2.2 %collective-permute-start.13 = (bf16[64,6144]{1,0:T(8,128)(2,1)S(1)}, bf16[64,6144]{1,0:T(8,128)(2,1)S(1)}, u32[]{:S(2)}, u32[]{:S(2)}) collective-permute-start(bf16[64,6144]{1,0:T(8,128)(2,1)S(1)} %collective-permute-done.6), channel_id=1, source_target_pairs={{0,48},{1,17},{2,50},{3,19},{4,52},{5,21},{6,54},{7,23},{8,56},{9,... | collective-permute-start | bytes 2359304 | tf_op jit(solution)/shard_map/ppermute | solution.py:58
  57.8 3.0 %collective-permute-start.20 = (bf16[64,6144]{1,0:T(8,128)(2,1)S(1)}, bf16[64,6144]{1,0:T(8,128)(2,1)S(1)}, u32[]{:S(2)}, u32[]{:S(2)}) collective-permute-start(bf16[64,6144]{1,0:T(8,128)(2,1)S(1)} %get-tuple-element.53), channel_id=1, source_target_pairs={{0,8},{1,9},{2,10},{3,11},{4,12},{5,13},{6,14},{7,15},{8,0},{9,1},... | collective-permute-start | bytes 2359304 | tf_op jit(solution)/shard_map/ppermute | solution.py:32
  66.3 3.4 %collective-permute-done.14 = bf16[64,6144]{1,0:T(8,128)(2,1)S(1)} collective-permute-done((bf16[64,6144]{1,0:T(8,128)(2,1)S(1)}, bf16[64,6144]{1,0:T(8,128)(2,1)S(1)}, u32[]{:S(2)}, u32[]{:S(2)}) %collective-permute-start.14) | collective-permute-done | bytes 786464 | tf_op jit(solution)/shard_map/ppermute | solution.py:59
  75.2 3.1 %collective-permute-start.18 = (bf16[512,128]{0,1:T(8,128)(2,1)S(1)}, bf16[512,128]{0,1:T(8,128)(2,1)S(1)}, u32[]{:S(2)}, u32[]{:S(2)}) collective-permute-start(bf16[512,128]{0,1:T(8,128)(2,1)S(1)} %convolution_convert_fusion.2), channel_id=1, source_target_pairs={{0,8},{1,9},{2,10},{3,11},{4,12},{5,13},{6,14},{7,15},{8,0},{9,1},... | collective-permute-start | bytes 393224 | tf_op jit(solution)/shard_map/ppermute | solution.py:32
  79.1 3.3 %collective-permute-done.18 = bf16[512,128]{0,1:T(8,128)(2,1)S(1)} collective-permute-done((bf16[512,128]{0,1:T(8,128)(2,1)S(1)}, bf16[512,128]{0,1:T(8,128)(2,1)S(1)}, u32[]{:S(2)}, u32[]{:S(2)}) %collective-permute-start.18) | collective-permute-done | bytes 131104 | tf_op jit(solution)/shard_map/ppermute | solution.py:32
  96.4 4.7 %collective-permute-done.23 = bf16[128,3072]{1,0:T(8,128)(2,1)S(1)} collective-permute-done((bf16[128,3072]{1,0:T(8,128)(2,1)S(1)}, bf16[128,3072]{1,0:T(8,128)(2,1)S(1)}, u32[]{:S(2)}, u32[]{:S(2)}) %collective-permute-start.23) | collective-permute-done | bytes 786464 | tf_op jit(solution)/shard_map/ppermute | solution.py:77
  101.6 2.7 %collective-permute-done.27 = bf16[128,3072]{1,0:T(8,128)(2,1)S(1)} collective-permute-done((bf16[128,3072]{1,0:T(8,128)(2,1)S(1)}, bf16[128,3072]{1,0:T(8,128)(2,1)S(1)}, u32[]{:S(2)}, u32[]{:S(2)}) %collective-permute-start.27) | collective-permute-done | bytes 786464 | tf_op jit(solution)/shard_map/ppermute | solution.py:77
  104.5 4.8 %collective-permute-done.24 = bf16[64,3072]{1,0:T(8,128)(2,1)S(1)} collective-permute-done((bf16[64,3072]{1,0:T(8,128)(2,1)S(1)}, bf16[64,3072]{1,0:T(8,128)(2,1)S(1)}, u32[]{:S(2)}, u32[]{:S(2)}) %collective-permute-start.24) | collective-permute-done | bytes 393248 | tf_op jit(solution)/shard_map/ppermute | solution.py:79
  109.5 2.8 %collective-permute-done.28 = bf16[64,3072]{1,0:T(8,128)(2,1)S(1)} collective-permute-done((bf16[64,3072]{1,0:T(8,128)(2,1)S(1)}, bf16[64,3072]{1,0:T(8,128)(2,1)S(1)}, u32[]{:S(2)}, u32[]{:S(2)}) %collective-permute-start.28) | collective-permute-done | bytes 393248 | tf_op jit(solution)/shard_map/ppermute | solution.py:79
  114.0 2.6 %collective-permute-start.29 = (bf16[32,3072]{1,0:T(8,128)(2,1)S(1)}, bf16[32,3072]{1,0:T(8,128)(2,1)S(1)}, u32[]{:S(2)}, u32[]{:S(2)}) collective-permute-start(bf16[32,3072]{1,0:T(8,128)(2,1)S(1)} %pad_maximum_fusion.10), channel_id=1, source_target_pairs={{0,48},{1,17},{2,50},{3,19},{4,52},{5,21},{6,54},{7,23},{8,56},{9,... | collective-permute-start | bytes 589832 | tf_op jit(solution)/shard_map/ppermute | solution.py:77
  116.5 3.1 %collective-permute-done.25 = bf16[32,3072]{1,0:T(8,128)(2,1)S(1)} collective-permute-done((bf16[32,3072]{1,0:T(8,128)(2,1)S(1)}, bf16[32,3072]{1,0:T(8,128)(2,1)S(1)}, u32[]{:S(2)}, u32[]{:S(2)}) %collective-permute-start.25) | collective-permute-done | bytes 196640 | tf_op jit(solution)/shard_map/ppermute | solution.py:77
  121.5 2.9 %collective-permute-done.26 = bf16[16,3072]{1,0:T(8,128)(2,1)S(1)} collective-permute-done((bf16[16,3072]{1,0:T(8,128)(2,1)S(1)}, bf16[16,3072]{1,0:T(8,128)(2,1)S(1)}, u32[]{:S(2)}, u32[]{:S(2)}) %collective-permute-start.26) | collective-permute-done | bytes 98336 | tf_op jit(solution)/shard_map/ppermute | solution.py:79
  132.6 2.5 %collective-permute-done.33 = bf16[8,6144]{1,0:T(8,128)(2,1)S(1)} collective-permute-done((bf16[8,6144]{1,0:T(8,128)(2,1)S(1)}, bf16[8,6144]{1,0:T(8,128)(2,1)S(1)}, u32[]{:S(2)}, u32[]{:S(2)}) %collective-permute-start.33) | collective-permute-done | bytes 98336 | tf_op jit(solution)/shard_map/ppermute | solution.py:32
  (127 shorter events, 57.3 us)
Async XLA Ops:
  4.9 8.5 %collective-permute-start.1 = (bf16[16,6144]{1,0:T(8,128)(2,1)S(1)}, bf16[16,6144]{1,0:T(8,128)(2,1)S(1)}, u32[]{:S(2)}, u32[]{:S(2)}) collective-permute-start(bf16[16,6144]{1,0:T(8,128)(2,1)S(1)} %maximum_select_fusion), channel_id=1, source_target_pairs={{0,8},{1,9},{2,10},{3,11},{4,12},{5,13},{6,14},{7,15},{8,0},{9,1},... | collective-permute-start | bytes 589832 | tf_op jit(solution)/shard_map/ppermute | solution.py:32
  13.5 6.2 %collective-permute-start.4 = (bf16[16,6144]{1,0:T(8,128)(2,1)S(1)}, bf16[16,6144]{1,0:T(8,128)(2,1)S(1)}, u32[]{:S(2)}, u32[]{:S(2)}) collective-permute-start(bf16[16,6144]{1,0:T(8,128)(2,1)S(1)} %get-tuple-element.86), channel_id=1, source_target_pairs={{0,16},{1,49},{2,18},{3,51},{4,20},{5,53},{6,22},{7,55},{8,24},{9,... | collective-permute-start | bytes 589832 | tf_op jit(solution)/shard_map/ppermute | solution.py:59
  15.6 7.8 %collective-permute-start.2 = (bf16[16,6144]{1,0:T(8,128)(2,1)S(1)}, bf16[16,6144]{1,0:T(8,128)(2,1)S(1)}, u32[]{:S(2)}, u32[]{:S(2)}) collective-permute-start(bf16[16,6144]{1,0:T(8,128)(2,1)S(1)} %get-tuple-element.87), channel_id=1, source_target_pairs={{0,2},{1,7},{2,0},{3,5},{4,6},{5,3},{6,4},{7,1},{8,10},{9,15},{10,... | collective-permute-start | bytes 589832 | tf_op jit(solution)/shard_map/ppermute | solution.py:58
  17.3 17.9 %collective-permute-start.9 = (bf16[6144,384]{1,0:T(8,128)(2,1)S(1)}, bf16[6144,384]{1,0:T(8,128)(2,1)S(1)}, u32[]{:S(2)}, u32[]{:S(2)}) collective-permute-start(bf16[6144,384]{1,0:T(8,128)(2,1)S(1)} %constant_dynamic-slice_fusion.2), channel_id=1, source_target_pairs={{0,1},{1,0},{2,3},{3,2},{4,5},{5,4},{6,7},{7,6},{8,9},{9,8},{10,11... | collective-permute-start | bytes 14155784 | tf_op jit(solution)/shard_map/ppermute | solution.py:32
  19.7 9.9 %collective-permute-start.5 = (bf16[32,6144]{1,0:T(8,128)(2,1)S(1)}, bf16[32,6144]{1,0:T(8,128)(2,1)S(1)}, u32[]{:S(2)}, u32[]{:S(2)}) collective-permute-start(bf16[32,6144]{1,0:T(8,128)(2,1)S(1)} %pad_maximum_fusion.7), channel_id=1, source_target_pairs={{0,48},{1,17},{2,50},{3,19},{4,52},{5,21},{6,54},{7,23},{8,56},{9,... | collective-permute-start | bytes 1179656 | tf_op jit(solution)/shard_map/ppermute | solution.py:59
  23.5 9.1 %collective-permute-start.3 = (bf16[32,6144]{1,0:T(8,128)(2,1)S(1)}, bf16[32,6144]{1,0:T(8,128)(2,1)S(1)}, u32[]{:S(2)}, u32[]{:S(2)}) collective-permute-start(bf16[32,6144]{1,0:T(8,128)(2,1)S(1)} %pad_maximum_fusion.6), channel_id=1, source_target_pairs={{0,6},{1,3},{2,4},{3,1},{4,2},{5,7},{6,0},{7,5},{8,14},{9,11},{10,... | collective-permute-start | bytes 1179656 | tf_op jit(solution)/shard_map/ppermute | solution.py:58
  26.6 17.3 %collective-permute-start.8 = (bf16[64,6144]{1,0:T(8,128)(2,1)S(1)}, bf16[64,6144]{1,0:T(8,128)(2,1)S(1)}, u32[]{:S(2)}, u32[]{:S(2)}) collective-permute-start(bf16[64,6144]{1,0:T(8,128)(2,1)S(1)} %get-tuple-element.36), channel_id=1, source_target_pairs={{0,8},{1,9},{2,10},{3,11},{4,12},{5,13},{6,14},{7,15},{8,0},{9,1},... | collective-permute-start | bytes 2359304 | tf_op jit(solution)/shard_map/ppermute | solution.py:32
  32.7 16.8 %collective-permute-start.6 = (bf16[64,6144]{1,0:T(8,128)(2,1)S(1)}, bf16[64,6144]{1,0:T(8,128)(2,1)S(1)}, u32[]{:S(2)}, u32[]{:S(2)}) collective-permute-start(bf16[64,6144]{1,0:T(8,128)(2,1)S(1)} %pad_maximum_fusion.2), channel_id=1, source_target_pairs={{0,16},{1,49},{2,18},{3,51},{4,20},{5,53},{6,22},{7,55},{8,24},{9,... | collective-permute-start | bytes 2359304 | tf_op jit(solution)/shard_map/ppermute | solution.py:58
  32.8 20.2 %collective-permute-start.11 = (bf16[64,6144]{1,0:T(8,128)(2,1)S(1)}, bf16[64,6144]{1,0:T(8,128)(2,1)S(1)}, u32[]{:S(2)}, u32[]{:S(2)}) collective-permute-start(bf16[64,6144]{1,0:T(8,128)(2,1)S(1)} %pad_maximum_fusion.2), channel_id=1, source_target_pairs={{0,48},{1,17},{2,50},{3,19},{4,52},{5,21},{6,54},{7,23},{8,56},{9,... | collective-permute-start | bytes 2359304 | tf_op jit(solution)/shard_map/ppermute | solution.py:58
  34.8 18.1 %collective-permute-start.7 = (bf16[64,6144]{1,0:T(8,128)(2,1)S(1)}, bf16[64,6144]{1,0:T(8,128)(2,1)S(1)}, u32[]{:S(2)}, u32[]{:S(2)}) collective-permute-start(bf16[64,6144]{1,0:T(8,128)(2,1)S(1)} %pad_maximum_fusion.3), channel_id=1, source_target_pairs={{0,2},{1,7},{2,0},{3,5},{4,6},{5,3},{6,4},{7,1},{8,10},{9,15},{10,... | collective-permute-start | bytes 2359304 | tf_op jit(solution)/shard_map/ppermute | solution.py:59
  35.3 17.7 %collective-permute-start.12 = (bf16[64,6144]{1,0:T(8,128)(2,1)S(1)}, bf16[64,6144]{1,0:T(8,128)(2,1)S(1)}, u32[]{:S(2)}, u32[]{:S(2)}) collective-permute-start(bf16[64,6144]{1,0:T(8,128)(2,1)S(1)} %pad_maximum_fusion.3), channel_id=1, source_target_pairs={{0,6},{1,3},{2,4},{3,1},{4,2},{5,7},{6,0},{7,5},{8,14},{9,11},{10,... | collective-permute-start | bytes 2359304 | tf_op jit(solution)/shard_map/ppermute | solution.py:59
  53.0 13.3 %collective-permute-start.13 = (bf16[64,6144]{1,0:T(8,128)(2,1)S(1)}, bf16[64,6144]{1,0:T(8,128)(2,1)S(1)}, u32[]{:S(2)}, u32[]{:S(2)}) collective-permute-start(bf16[64,6144]{1,0:T(8,128)(2,1)S(1)} %collective-permute-done.6), channel_id=1, source_target_pairs={{0,48},{1,17},{2,50},{3,19},{4,52},{5,21},{6,54},{7,23},{8,56},{9,... | collective-permute-start | bytes 2359304 | tf_op jit(solution)/shard_map/ppermute | solution.py:58
  55.3 8.8 %collective-permute-start.10 = (f32[128,384]{1,0:T(8,128)S(1)}, f32[128,384]{1,0:T(8,128)S(1)}, u32[]{:S(2)}, u32[]{:S(2)}) collective-permute-start(f32[128,384]{1,0:T(8,128)S(1)} %fusion.54), channel_id=1, source_target_pairs={{0,1},{1,0},{2,3},{3,2},{4,5},{5,4},{6,7},{7,6},{8,9},{9,8},{10,11... | collective-permute-start | bytes 589832 | tf_op jit(solution)/shard_map/ppermute | solution.py:32
  56.4 13.3 %collective-permute-start.14 = (bf16[64,6144]{1,0:T(8,128)(2,1)S(1)}, bf16[64,6144]{1,0:T(8,128)(2,1)S(1)}, u32[]{:S(2)}, u32[]{:S(2)}) collective-permute-start(bf16[64,6144]{1,0:T(8,128)(2,1)S(1)} %collective-permute-done.7), channel_id=1, source_target_pairs={{0,6},{1,3},{2,4},{3,1},{4,2},{5,7},{6,0},{7,5},{8,14},{9,11},{10,... | collective-permute-start | bytes 2359304 | tf_op jit(solution)/shard_map/ppermute | solution.py:59
  57.8 21.2 %collective-permute-start.20 = (bf16[64,6144]{1,0:T(8,128)(2,1)S(1)}, bf16[64,6144]{1,0:T(8,128)(2,1)S(1)}, u32[]{:S(2)}, u32[]{:S(2)}) collective-permute-start(bf16[64,6144]{1,0:T(8,128)(2,1)S(1)} %get-tuple-element.53), channel_id=1, source_target_pairs={{0,8},{1,9},{2,10},{3,11},{4,12},{5,13},{6,14},{7,15},{8,0},{9,1},... | collective-permute-start | bytes 2359304 | tf_op jit(solution)/shard_map/ppermute | solution.py:32
  75.2 7.1 %collective-permute-start.18 = (bf16[512,128]{0,1:T(8,128)(2,1)S(1)}, bf16[512,128]{0,1:T(8,128)(2,1)S(1)}, u32[]{:S(2)}, u32[]{:S(2)}) collective-permute-start(bf16[512,128]{0,1:T(8,128)(2,1)S(1)} %convolution_convert_fusion.2), channel_id=1, source_target_pairs={{0,8},{1,9},{2,10},{3,11},{4,12},{5,13},{6,14},{7,15},{8,0},{9,1},... | collective-permute-start | bytes 393224 | tf_op jit(solution)/shard_map/ppermute | solution.py:32
  79.0 5.3 %collective-permute-start.21 = (bf16[192,3072]{1,0:T(8,128)(2,1)S(1)}, bf16[192,3072]{1,0:T(8,128)(2,1)}, u32[]{:S(2)}, u32[]{:S(2)}) collective-permute-start(bf16[192,3072]{1,0:T(8,128)(2,1)S(1)} %get-tuple-element.58), channel_id=1, source_target_pairs={{0,1},{1,0},{2,3},{3,2},{4,5},{5,4},{6,7},{7,6},{8,9},{9,8},{10,11... | collective-permute-start | bytes 3538952 | tf_op jit(solution)/shard_map/ppermute | solution.py:32
  87.8 13.3 %collective-permute-start.23 = (bf16[128,3072]{1,0:T(8,128)(2,1)S(1)}, bf16[128,3072]{1,0:T(8,128)(2,1)S(1)}, u32[]{:S(2)}, u32[]{:S(2)}) collective-permute-start(bf16[128,3072]{1,0:T(8,128)(2,1)S(1)} %convolution_convert_fusion.1), channel_id=1, source_target_pairs={{0,48},{1,17},{2,50},{3,19},{4,52},{5,21},{6,54},{7,23},{8,56},{9,... | collective-permute-start | bytes 2359304 | tf_op jit(solution)/shard_map/ppermute | solution.py:77
  91.0 13.3 %collective-permute-start.27 = (bf16[128,3072]{1,0:T(8,128)(2,1)S(1)}, bf16[128,3072]{1,0:T(8,128)(2,1)S(1)}, u32[]{:S(2)}, u32[]{:S(2)}) collective-permute-start(bf16[128,3072]{1,0:T(8,128)(2,1)S(1)} %convolution_convert_fusion), channel_id=1, source_target_pairs={{0,6},{1,3},{2,4},{3,1},{4,2},{5,7},{6,0},{7,5},{8,14},{9,11},{10,... | collective-permute-start | bytes 2359304 | tf_op jit(solution)/shard_map/ppermute | solution.py:77
  101.3 8.1 %collective-permute-start.24 = (bf16[64,3072]{1,0:T(8,128)(2,1)S(1)}, bf16[64,3072]{1,0:T(8,128)(2,1)S(1)}, u32[]{:S(2)}, u32[]{:S(2)}) collective-permute-start(bf16[64,3072]{1,0:T(8,128)(2,1)S(1)} %slice.345), channel_id=1, source_target_pairs={{0,16},{1,49},{2,18},{3,51},{4,20},{5,53},{6,22},{7,55},{8,24},{9,... | collective-permute-start | bytes 1179656 | tf_op jit(solution)/shard_map/ppermute | solution.py:79
  104.4 7.9 %collective-permute-start.28 = (bf16[64,3072]{1,0:T(8,128)(2,1)S(1)}, bf16[64,3072]{1,0:T(8,128)(2,1)S(1)}, u32[]{:S(2)}, u32[]{:S(2)}) collective-permute-start(bf16[64,3072]{1,0:T(8,128)(2,1)S(1)} %slice.344), channel_id=1, source_target_pairs={{0,2},{1,7},{2,0},{3,5},{4,6},{5,3},{6,4},{7,1},{8,10},{9,15},{10,... | collective-permute-start | bytes 1179656 | tf_op jit(solution)/shard_map/ppermute | solution.py:79
  112.5 7.1 %collective-permute-start.25 = (bf16[32,3072]{1,0:T(8,128)(2,1)S(1)}, bf16[32,3072]{1,0:T(8,128)(2,1)S(1)}, u32[]{:S(2)}, u32[]{:S(2)}) collective-permute-start(bf16[32,3072]{1,0:T(8,128)(2,1)S(1)} %pad_maximum_fusion.9), channel_id=1, source_target_pairs={{0,6},{1,3},{2,4},{3,1},{4,2},{5,7},{6,0},{7,5},{8,14},{9,11},{10,... | collective-permute-start | bytes 589832 | tf_op jit(solution)/shard_map/ppermute | solution.py:77
  114.0 7.4 %collective-permute-start.29 = (bf16[32,3072]{1,0:T(8,128)(2,1)S(1)}, bf16[32,3072]{1,0:T(8,128)(2,1)S(1)}, u32[]{:S(2)}, u32[]{:S(2)}) collective-permute-start(bf16[32,3072]{1,0:T(8,128)(2,1)S(1)} %pad_maximum_fusion.10), channel_id=1, source_target_pairs={{0,48},{1,17},{2,50},{3,19},{4,52},{5,21},{6,54},{7,23},{8,56},{9,... | collective-permute-start | bytes 589832 | tf_op jit(solution)/shard_map/ppermute | solution.py:77
  129.2 5.8 %collective-permute-start.33 = (bf16[8,6144]{1,0:T(8,128)(2,1)S(1)}, bf16[8,6144]{1,0:T(8,128)(2,1)S(1)}, u32[]{:S(2)}, u32[]{:S(2)}) collective-permute-start(bf16[8,6144]{1,0:T(8,128)(2,1)S(1)} %get-tuple-element.90), channel_id=1, source_target_pairs={{0,72},{1,73},{2,74},{3,75},{4,76},{5,77},{6,78},{7,79},{8,64},{9,... | collective-permute-start | bytes 294920 | tf_op jit(solution)/shard_map/ppermute | solution.py:32
  (15 other events, 111.8 us)

commit v6 on v5

--- a/solution.py
+++ b/solution.py
@@ -72,15 +72,18 @@
     )
 
 
-def swap_sum(far, near, axis):
+def swap_sum(far, near, axis, *ready):
     size = near.shape[0] // 2
     got = lax.ppermute(far.astype(jnp.bfloat16), AXES, swap_pairs(axis, 1))
     total = near + got.astype(jnp.float32)
-    got = lax.ppermute(total[size:].astype(jnp.bfloat16), AXES, swap_pairs(axis, 0))
-    return total[:size] + got.astype(jnp.float32)
-
-
-def token_positions(z, y):
+    kept, got = total[:size], lax.ppermute(
+        total[size:].astype(jnp.bfloat16), AXES, swap_pairs(axis, 0)
+    )
+    kept, *_ = lax.optimization_barrier((kept, *ready))
+    return kept + got.astype(jnp.float32)
+
+
+def token_positions(z, half_x, y):
     places = np.asarray([0, 1, 3, 2], np.int32)
     far = np.repeat(places, 128)
     side = np.tile(np.repeat(np.asarray([0, 1], np.int32), 64), 4)
@@ -88,7 +91,7 @@
     low = np.tile(np.arange(16, dtype=np.int32), 32)
     dz = np.where(side == 0, far, near)
     dy = np.where(side == 0, near, far)
-    return (((z ^ dz) * 2 + side) * 4 + (y ^ dy)) * 16 + low
+    return (((z ^ dz) * 2 + (half_x ^ side)) * 4 + (y ^ dy)) * 16 + low
 
 
 def attend(projected, position, head_size):
@@ -123,29 +126,25 @@
         core == 0, jnp.concatenate([kept, given]), jnp.concatenate([given, kept])
     )
     head_block, block = lax.optimization_barrier((head_weights[0, :, 0, :], block))
-    other, their_weights = lax.optimization_barrier(
-        (
-            send(block, x=1),
-            lax.dynamic_slice_in_dim(head_block, (1 - core) * half, half, 0),
-        )
-    )
-    first = jnp.where(half_x == 0, block, other)
-    second = jnp.where(half_x == 0, other, block)
+    first, second = block, send(block, x=1)
+    their_weights = lax.dynamic_slice_in_dim(head_block, (1 - core) * half, half, 0)
+    swapped_weights = send(their_weights, core=1)
     own_weights = lax.dynamic_slice_in_dim(head_block, core * half, half, 0)
 
-    one = swap_both(first, "y", second, "z", 0)
-    two = swap_both(
-        jnp.concatenate([first, one[0]]), "y", jnp.concatenate([second, one[1]]), "z", 1
-    )
-    first_own = near_rows(first, one[0], two[0], core)
-    second_own = near_rows(second, one[1], two[1], core)
-    swapped_weights = send(their_weights, core=1)
+    def near_gather(block, axis):
+        one = lax.ppermute(block, AXES, swap_pairs(axis, 0))
+        two = lax.ppermute(jnp.concatenate([block, one]), AXES, swap_pairs(axis, 1))
+        return lax.optimization_barrier(near_rows(block, one, two, core)), one
+
+    first_own, _ = near_gather(first, "y")
+    second_own, came = near_gather(second, "z")
+    second_own, swapped_weights = lax.optimization_barrier((second_own, swapped_weights))
 
     out_rows, _ = lax.optimization_barrier((output_weights[0], block))
     out_kept = lax.dynamic_slice_in_dim(out_rows, half_x * half, half, 1)
     out_given = lax.dynamic_slice_in_dim(out_rows, (1 - half_x) * half, half, 1)
     middle = out_given.shape[0] // 2
-    upper, _ = lax.optimization_barrier((out_given[:middle], one))
+    upper, _ = lax.optimization_barrier((out_given[:middle], came))
     upper = send(upper, x=1)
 
     def project(first_rows, second_rows):
@@ -154,21 +153,15 @@
         theirs = jnp.dot(rows, swapped_weights, preferred_element_type=jnp.float32)
         return mine, theirs
 
-    first_own, second_own = lax.optimization_barrier((first_own, second_own))
     turn_one = swap_both(first_own, "z", second_own, "y", 0)
     turn_two = swap_both(first_own, "z", second_own, "y", 1)
-    *turn_one, upper, mine, theirs = lax.optimization_barrier(
-        (*turn_one, upper, *project(first_own, second_own))
-    )
-    here = [(mine, theirs)]
+    last = swap_both(turn_one[0], "z", turn_one[1], "y", 1)
+    here = [project(first_own, second_own)]
     lower, _ = lax.optimization_barrier((out_given[middle:], upper))
     lower = send(lower, x=1)
-    *turn_one, first_rows, second_rows = lax.optimization_barrier((*turn_one, *turn_two))
-    last = swap_both(turn_one[0], "z", turn_one[1], "y", 1)
     here.append(project(*turn_one))
-    here.append(project(first_rows, second_rows))
-    *last, middle_sums = lax.optimization_barrier((*last, here[1:]))
-    here[1:] = middle_sums
+    here.append(project(*turn_two))
+    *last, here = lax.optimization_barrier((*last, here))
     here.append(project(*last))
     by_place = [
         here[0],
@@ -178,8 +171,10 @@
     ]
     projected = jnp.concatenate([mine + send(theirs, core=1) for mine, theirs in by_place])
 
-    attended = attend(projected, token_positions(z, y), head_size)
-    own_heads = jnp.concatenate([attended, send(attended, x=1)], axis=1)
+    attended = attend(projected, token_positions(z, half_x, y), head_size)
+    across_x = send(attended, x=1).reshape(4, 2, 4, 16, head_size)
+    across_x = jnp.flip(across_x, 1).transpose(2, 1, 0, 3, 4)
+    own_heads = jnp.concatenate([attended, across_x.reshape(attended.shape)], axis=1)
     heads = jnp.concatenate([own_heads, send(own_heads, core=1)], axis=1)
 
     def swap_quarters(rows):
@@ -204,18 +199,22 @@
 
     heads = heads.reshape(4, 2, 64, 4 * head_size)
 
-    def section_rows(side, far_axis, near_axis):
+    def edge_and_rest(side):
         sent, kept = turns(heads[:, side])
         edge = jnp.dot(
             jnp.concatenate(sent), out_block, preferred_element_type=jnp.float32
         ).astype(jnp.bfloat16)
         rest = jnp.dot(jnp.concatenate(kept), out_block, preferred_element_type=jnp.float32)
-        total = swap_sum(edge, lax.optimization_barrier(rest), far_axis)
-        sent, kept = turns(total.reshape(4, 16, quarter))
-        return swap_sum(jnp.concatenate(sent), jnp.concatenate(kept), near_axis)
-
-    first_rows = section_rows(0, "z", "y")
-    second_rows = section_rows(1, "y", "z")
+        return edge, lax.optimization_barrier(rest)
+
+    def near_chunks(total):
+        sent, kept = turns(lax.optimization_barrier(total).reshape(4, 16, quarter))
+        return jnp.concatenate(sent).astype(jnp.bfloat16), jnp.concatenate(kept)
+
+    first_sent, first_kept = near_chunks(swap_sum(*edge_and_rest(0), "z"))
+    second_sent, second_kept = near_chunks(swap_sum(*edge_and_rest(1), "y", first_sent))
+    first_rows = swap_sum(first_sent, first_kept, "y")
+    second_rows = swap_sum(second_sent, second_kept, "z")
     owners = jnp.stack([first_rows, second_rows]).astype(jnp.bfloat16)
     upper, lower = owners[:, :8], owners[:, 8:]
     stay = jnp.where(core == 0, upper, lower)
@@ -225,8 +224,8 @@
         jnp.concatenate([stay, came], axis=2),
         jnp.concatenate([came, stay], axis=2),
     )
-    straight = send(jnp.where(half_x == 0, wide[0], wide[1]), pipe=1)
-    crossed = send(jnp.where(half_x == 0, wide[1], wide[0]), pipe=1, x=1)
+    straight = send(wide[0], pipe=1)
+    crossed = send(wide[1], pipe=1, x=1)
     return jnp.where(
         half_x == 0,
         jnp.concatenate([straight, crossed], axis=1),

time: 136 us -> 150 us (1.10)
  waiting for transfers between devices: 58.3 us -> 77.2 us
  starting transfers between devices: 46.6 us -> 43.3 us
    ppermute x5 -> x3, waiting for transfers between devices: 6.89 us -> 23.7 us  [swap_both(): lax.ppermute(second, AXES, swap_pairs(second_axis, turn))]
    ppermute x0 -> x4, starting transfers between devices: none -> 10.2 us  [the longest x2 6.6 us: near_gather(): two = lax.ppermute(jnp.concatenate([block, one]), AXES, swap_pairs(axis, 1))]
    ppermute x5 -> x3, waiting for transfers between devices: 10.7 us -> 0.98 us  [swap_both(): lax.ppermute(first, AXES, swap_pairs(first_axis, turn))]
    ppermute x16, waiting for transfers between devices: 16.6 us -> 22.8 us  [send(): return lax.ppermute(value, AXES, pairs)]
    ppermute x5 -> x3, starting transfers between devices: 10.4 us -> 4.4 us  [swap_both(): lax.ppermute(second, AXES, swap_pairs(second_axis, turn))]
    ppermute x16, starting transfers between devices: 19.9 us -> 15.7 us  [send(): return lax.ppermute(value, AXES, pairs)]
    ppermute x5 -> x3, starting transfers between devices: 9.15 us -> 5.35 us  [swap_both(): lax.ppermute(first, AXES, swap_pairs(first_axis, turn))]
    ppermute x0 -> x4, waiting for transfers between devices: none -> 3.53 us  [the longest x2 2.3 us: near_gather(): two = lax.ppermute(jnp.concatenate([block, one]), AXES, swap_pairs(axis, 1))]
  transfers between devices with their start and end apart: 34 -> 34, of which waited for: 23 -> 20; matrix products, arithmetic and copies ran while one was open for 17% -> 15% of each run, Pallas kernels for 0% -> 0%
where the time goes in v6:
time: 150 us; the launch traced here: 149 us
  waiting for transfers between devices  77.2 us (51%)
  starting transfers between devices  43.3 us (29%)
  matrix products  17.2 us (11%)
  other arithmetic  7.21 us (5%)
  local copies, waits for them, and re-layouts  3.85 us (3%)
    ppermute x3, waiting for transfers between devices, swap_both(): lax.ppermute(second, AXES, swap_pairs(second_axis, turn))  23.7 us
    ppermute x16, waiting for transfers between devices, send(): return lax.ppermute(value, AXES, pairs)  22.8 us
    ppermute x16, starting transfers between devices, send(): return lax.ppermute(value, AXES, pairs)  15.7 us
    ppermute x4, waiting for transfers between devices, swap_sum(): got = lax.ppermute(far.astype(jnp.bfloat16), AXES, swap_pairs(axis, 1))  14.1 us
    ppermute x4, waiting for transfers between devices, swap_sum(): lax.ppermute(total[size:].astype(jnp.bfloat16), AXES, swap_pairs(axis, 0))  12 us
    ppermute x4, starting transfers between devices, swap_sum(): got = lax.ppermute(far.astype(jnp.bfloat16), AXES, swap_pairs(axis, 1))  7.31 us
    ppermute x2, starting transfers between devices, near_gather(): two = lax.ppermute(jnp.concatenate([block, one]), AXES, swap_pairs(axis, 1))  6.6 us
    ppermute x3, starting transfers between devices, swap_both(): lax.ppermute(first, AXES, swap_pairs(first_axis, turn))  5.35 us
  transfers between devices with their start and end apart: 34, of which 20 were waited for; matrix products, arithmetic and copies ran while one was open for 15% of the time, Pallas kernels for 0%

profile of v6, /device:TPU:0, one launch (start us, length us, event | category | flops | bytes accessed | tf_op | source)
XLA Modules:
  0.0 149.4 jit_solution(2830523469320930408)
XLA Ops:
  4.9 3.2 %collective-permute-start.5 = (bf16[16,6144]{1,0:T(8,128)(2,1)S(1)}, bf16[16,6144]{1,0:T(8,128)(2,1)S(1)}, u32[]{:S(2)}, u32[]{:S(2)}) collective-permute-start(bf16[16,6144]{1,0:T(8,128)(2,1)S(1)} %maximum_select_fusion), channel_id=1, source_target_pairs={{0,8},{1,9},{2,10},{3,11},{4,12},{5,13},{6,14},{7,15},{8,0},{9,1},... | collective-permute-start | bytes 589832 | tf_op jit(solution)/shard_map/ppermute | solution.py:32
  9.7 3.0 %constant_dynamic-slice_fusion.2 = bf16[6144,384]{1,0:T(8,128)(2,1)S(1)} fusion(bf16[12288,384]{1,0:T(8,128)(2,1)} %bitcast.61, s32[]{:T(128)S(6)} %select_n.234), kind=kLoop, calls=%fused_computation.124 | loop fusion | bytes 9437188 | tf_op jit(solution)/shard_map/dynamic_slice | solution.py:130
  14.0 2.0 %collective-permute-start.6 = (bf16[16,6144]{1,0:T(8,128)(2,1)S(1)}, bf16[16,6144]{1,0:T(8,128)(2,1)S(1)}, u32[]{:S(2)}, u32[]{:S(2)}) collective-permute-start(bf16[16,6144]{1,0:T(8,128)(2,1)S(1)} %collective-permute-done.5), channel_id=1, source_target_pairs={{0,16},{1,49},{2,18},{3,51},{4,20},{5,53},{6,22},{7,55},{8,24},{9,... | collective-permute-start | bytes 589832 | tf_op jit(solution)/shard_map/ppermute | solution.py:135
  16.1 2.5 %collective-permute-start.2 = (bf16[32,6144]{1,0:T(8,128)(2,1)S(1)}, bf16[32,6144]{1,0:T(8,128)(2,1)S(1)}, u32[]{:S(2)}, u32[]{:S(2)}) collective-permute-start(bf16[32,6144]{1,0:T(8,128)(2,1)S(1)} %pad_maximum_fusion.9), channel_id=1, source_target_pairs={{0,6},{1,3},{2,4},{3,1},{4,2},{5,7},{6,0},{7,5},{8,14},{9,11},{10,... | collective-permute-start | bytes 1179656 | tf_op jit(solution)/shard_map/ppermute | solution.py:136
  19.8 4.1 %collective-permute-start.7 = (bf16[32,6144]{1,0:T(8,128)(2,1)S(1)}, bf16[32,6144]{1,0:T(8,128)(2,1)S(1)}, u32[]{:S(2)}, u32[]{:S(2)}) collective-permute-start(bf16[32,6144]{1,0:T(8,128)(2,1)S(1)} %pad_maximum_fusion.10), channel_id=1, source_target_pairs={{0,48},{1,17},{2,50},{3,19},{4,52},{5,21},{6,54},{7,23},{8,56},{9,... | collective-permute-start | bytes 1179656 | tf_op jit(solution)/shard_map/ppermute | solution.py:136
  23.9 2.4 %collective-permute-start.19 = (bf16[64,6144]{1,0:T(8,128)(2,1)S(1)}, bf16[64,6144]{1,0:T(8,128)(2,1)S(1)}, u32[]{:S(2)}, u32[]{:S(2)}) collective-permute-start(bf16[64,6144]{1,0:T(8,128)(2,1)S(1)} %get-tuple-element.35), channel_id=1, source_target_pairs={{0,8},{1,9},{2,10},{3,11},{4,12},{5,13},{6,14},{7,15},{8,0},{9,1},... | collective-permute-start | bytes 2359304 | tf_op jit(solution)/shard_map/ppermute | solution.py:32
  28.9 2.3 %collective-permute-done.7 = bf16[32,6144]{1,0:T(8,128)(2,1)S(1)} collective-permute-done((bf16[32,6144]{1,0:T(8,128)(2,1)S(1)}, bf16[32,6144]{1,0:T(8,128)(2,1)S(1)}, u32[]{:S(2)}, u32[]{:S(2)}) %collective-permute-start.7) | collective-permute-done | bytes 393248 | tf_op jit(solution)/shard_map/ppermute | solution.py:136
  31.3 11.2 %collective-permute-done.19 = bf16[64,6144]{1,0:T(8,128)(2,1)S(1)} collective-permute-done((bf16[64,6144]{1,0:T(8,128)(2,1)S(1)}, bf16[64,6144]{1,0:T(8,128)(2,1)S(1)}, u32[]{:S(2)}, u32[]{:S(2)}) %collective-permute-start.19) | collective-permute-done | bytes 786464 | tf_op jit(solution)/shard_map/ppermute | solution.py:32
  45.0 3.0 %collective-permute-start.4 = (bf16[64,6144]{1,0:T(8,128)(2,1)S(1)}, bf16[64,6144]{1,0:T(8,128)(2,1)S(1)}, u32[]{:S(2)}, u32[]{:S(2)}) collective-permute-start(bf16[64,6144]{1,0:T(8,128)(2,1)S(1)} %collective-permute-done.3), channel_id=1, source_target_pairs={{0,48},{1,17},{2,50},{3,19},{4,52},{5,21},{6,54},{7,23},{8,56},{9,... | collective-permute-start | bytes 2359304 | tf_op jit(solution)/shard_map/ppermute | solution.py:58
  52.3 14.7 %collective-permute-done.12 = bf16[64,6144]{1,0:T(8,128)(2,1)S(1)} collective-permute-done((bf16[64,6144]{1,0:T(8,128)(2,1)S(1)}, bf16[64,6144]{1,0:T(8,128)(2,1)S(1)}, u32[]{:S(2)}, u32[]{:S(2)}) %collective-permute-start.12) | collective-permute-done | bytes 786464 | tf_op jit(solution)/shard_map/ppermute | solution.py:59
  69.1 2.2 %collective-permute-start.10 = (bf16[64,6144]{1,0:T(8,128)(2,1)S(1)}, bf16[64,6144]{1,0:T(8,128)(2,1)S(1)}, u32[]{:S(2)}, u32[]{:S(2)}) collective-permute-start(bf16[64,6144]{1,0:T(8,128)(2,1)S(1)} %collective-permute-done.9), channel_id=1, source_target_pairs={{0,6},{1,3},{2,4},{3,1},{4,2},{5,7},{6,0},{7,5},{8,14},{9,11},{10,... | collective-permute-start | bytes 2359304 | tf_op jit(solution)/shard_map/ppermute | solution.py:59
  73.3 9.1 %collective-permute-done.10 = bf16[64,6144]{1,0:T(8,128)(2,1)S(1)} collective-permute-done((bf16[64,6144]{1,0:T(8,128)(2,1)S(1)}, bf16[64,6144]{1,0:T(8,128)(2,1)S(1)}, u32[]{:S(2)}, u32[]{:S(2)}) %collective-permute-start.10) | collective-permute-done | bytes 786464 | tf_op jit(solution)/shard_map/ppermute | solution.py:59
  88.2 3.1 %collective-permute-start.17 = (bf16[512,128]{1,0:T(8,128)(2,1)S(1)}, bf16[512,128]{1,0:T(8,128)(2,1)S(1)}, u32[]{:S(2)}, u32[]{:S(2)}) collective-permute-start(bf16[512,128]{1,0:T(8,128)(2,1)S(1)} %convolution_convert_fusion.2), channel_id=1, source_target_pairs={{0,8},{1,9},{2,10},{3,11},{4,12},{5,13},{6,14},{7,15},{8,0},{9,1},... | collective-permute-start | bytes 393224 | tf_op jit(solution)/shard_map/ppermute | solution.py:32
  92.1 3.5 %collective-permute-done.17 = bf16[512,128]{1,0:T(8,128)(2,1)S(1)} collective-permute-done((bf16[512,128]{1,0:T(8,128)(2,1)S(1)}, bf16[512,128]{1,0:T(8,128)(2,1)S(1)}, u32[]{:S(2)}, u32[]{:S(2)}) %collective-permute-start.17) | collective-permute-done | bytes 131104 | tf_op jit(solution)/shard_map/ppermute | solution.py:32
  99.7 3.0 %collective-permute-start.23 = (bf16[128,3072]{1,0:T(8,128)(2,1)S(1)}, bf16[128,3072]{1,0:T(8,128)(2,1)S(1)}, u32[]{:S(2)}, u32[]{:S(2)}) collective-permute-start(bf16[128,3072]{1,0:T(8,128)(2,1)S(1)} %convolution_convert_fusion.1), channel_id=1, source_target_pairs={{0,48},{1,17},{2,50},{3,19},{4,52},{5,21},{6,54},{7,23},{8,56},{9,... | collective-permute-start | bytes 2359304 | tf_op jit(solution)/shard_map/ppermute | solution.py:77
  104.6 2.0 %collective-permute-start.27 = (bf16[128,3072]{1,0:T(8,128)(2,1)S(1)}, bf16[128,3072]{1,0:T(8,128)(2,1)S(1)}, u32[]{:S(2)}, u32[]{:S(2)}) collective-permute-start(bf16[128,3072]{1,0:T(8,128)(2,1)S(1)} %convolution_convert_fusion), channel_id=1, source_target_pairs={{0,6},{1,3},{2,4},{3,1},{4,2},{5,7},{6,0},{7,5},{8,14},{9,11},{10,... | collective-permute-start | bytes 2359304 | tf_op jit(solution)/shard_map/ppermute | solution.py:77
  110.4 2.6 %collective-permute-done.23 = bf16[128,3072]{1,0:T(8,128)(2,1)S(1)} collective-permute-done((bf16[128,3072]{1,0:T(8,128)(2,1)S(1)}, bf16[128,3072]{1,0:T(8,128)(2,1)S(1)}, u32[]{:S(2)}, u32[]{:S(2)}) %collective-permute-start.23) | collective-permute-done | bytes 786464 | tf_op jit(solution)/shard_map/ppermute | solution.py:77
  113.5 4.4 %collective-permute-done.27 = bf16[128,3072]{1,0:T(8,128)(2,1)S(1)} collective-permute-done((bf16[128,3072]{1,0:T(8,128)(2,1)S(1)}, bf16[128,3072]{1,0:T(8,128)(2,1)S(1)}, u32[]{:S(2)}, u32[]{:S(2)}) %collective-permute-start.27) | collective-permute-done | bytes 786464 | tf_op jit(solution)/shard_map/ppermute | solution.py:77
  118.3 2.9 %collective-permute-done.24 = bf16[64,3072]{1,0:T(8,128)(2,1)S(1)} collective-permute-done((bf16[64,3072]{1,0:T(8,128)(2,1)S(1)}, bf16[64,3072]{1,0:T(8,128)(2,1)S(1)}, u32[]{:S(2)}, u32[]{:S(2)}) %collective-permute-start.24) | collective-permute-done | bytes 393248 | tf_op jit(solution)/shard_map/ppermute | solution.py:79
  121.3 2.2 %collective-permute-start.25 = (bf16[32,3072]{1,0:T(8,128)(2,1)S(1)}, bf16[32,3072]{1,0:T(8,128)(2,1)S(1)}, u32[]{:S(2)}, u32[]{:S(2)}) collective-permute-start(bf16[32,3072]{1,0:T(8,128)(2,1)S(1)} %pad_maximum_fusion.12), channel_id=1, source_target_pairs={{0,6},{1,3},{2,4},{3,1},{4,2},{5,7},{6,0},{7,5},{8,14},{9,11},{10,... | collective-permute-start | bytes 589832 | tf_op jit(solution)/shard_map/ppermute | solution.py:77
  123.6 4.6 %collective-permute-done.28 = bf16[64,3072]{1,0:T(8,128)(2,1)S(1)} collective-permute-done((bf16[64,3072]{1,0:T(8,128)(2,1)S(1)}, bf16[64,3072]{1,0:T(8,128)(2,1)S(1)}, u32[]{:S(2)}, u32[]{:S(2)}) %collective-permute-start.28) | collective-permute-done | bytes 393248 | tf_op jit(solution)/shard_map/ppermute | solution.py:79
  128.6 7.1 %collective-permute-done.29 = bf16[32,3072]{1,0:T(8,128)(2,1)S(1)} collective-permute-done((bf16[32,3072]{1,0:T(8,128)(2,1)S(1)}, bf16[32,3072]{1,0:T(8,128)(2,1)S(1)}, u32[]{:S(2)}, u32[]{:S(2)}) %collective-permute-start.29) | collective-permute-done | bytes 196640 | tf_op jit(solution)/shard_map/ppermute | solution.py:77
  135.9 4.6 %collective-permute-done.30 = bf16[16,3072]{1,0:T(8,128)(2,1)S(1)} collective-permute-done((bf16[16,3072]{1,0:T(8,128)(2,1)S(1)}, bf16[16,3072]{1,0:T(8,128)(2,1)S(1)}, u32[]{:S(2)}, u32[]{:S(2)}) %collective-permute-start.30) | collective-permute-done | bytes 98336 | tf_op jit(solution)/shard_map/ppermute | solution.py:79
  144.1 2.9 %collective-permute-done.32 = bf16[8,6144]{1,0:T(8,128)(2,1)S(1)} collective-permute-done((bf16[8,6144]{1,0:T(8,128)(2,1)S(1)}, bf16[8,6144]{1,0:T(8,128)(2,1)S(1)}, u32[]{:S(2)}, u32[]{:S(2)}) %collective-permute-start.32) | collective-permute-done | bytes 98336 | tf_op jit(solution)/shard_map/ppermute | solution.py:32
  (128 shorter events, 46.4 us)
Async XLA Ops:
  4.9 9.1 %collective-permute-start.5 = (bf16[16,6144]{1,0:T(8,128)(2,1)S(1)}, bf16[16,6144]{1,0:T(8,128)(2,1)S(1)}, u32[]{:S(2)}, u32[]{:S(2)}) collective-permute-start(bf16[16,6144]{1,0:T(8,128)(2,1)S(1)} %maximum_select_fusion), channel_id=1, source_target_pairs={{0,8},{1,9},{2,10},{3,11},{4,12},{5,13},{6,14},{7,15},{8,0},{9,1},... | collective-permute-start | bytes 589832 | tf_op jit(solution)/shard_map/ppermute | solution.py:32
  8.1 8.0 %collective-permute-start.1 = (bf16[16,6144]{1,0:T(8,128)(2,1)S(1)}, bf16[16,6144]{1,0:T(8,128)(2,1)S(1)}, u32[]{:S(2)}, u32[]{:S(2)}) collective-permute-start(bf16[16,6144]{1,0:T(8,128)(2,1)S(1)} %maximum_select_fusion), channel_id=1, source_target_pairs={{0,2},{1,7},{2,0},{3,5},{4,6},{5,3},{6,4},{7,1},{8,10},{9,15},{10,... | collective-permute-start | bytes 589832 | tf_op jit(solution)/shard_map/ppermute | solution.py:135
  12.6 35.4 %collective-permute-start.8 = (bf16[6144,384]{1,0:T(8,128)(2,1)S(1)}, bf16[6144,384]{1,0:T(8,128)(2,1)S(1)}, u32[]{:S(2)}, u32[]{:S(2)}) collective-permute-start(bf16[6144,384]{1,0:T(8,128)(2,1)S(1)} %constant_dynamic-slice_fusion.2), channel_id=1, source_target_pairs={{0,1},{1,0},{2,3},{3,2},{4,5},{5,4},{6,7},{7,6},{8,9},{9,8},{10,11... | collective-permute-start | bytes 14155784 | tf_op jit(solution)/shard_map/ppermute | solution.py:32
  14.0 5.8 %collective-permute-start.6 = (bf16[16,6144]{1,0:T(8,128)(2,1)S(1)}, bf16[16,6144]{1,0:T(8,128)(2,1)S(1)}, u32[]{:S(2)}, u32[]{:S(2)}) collective-permute-start(bf16[16,6144]{1,0:T(8,128)(2,1)S(1)} %collective-permute-done.5), channel_id=1, source_target_pairs={{0,16},{1,49},{2,18},{3,51},{4,20},{5,53},{6,22},{7,55},{8,24},{9,... | collective-permute-start | bytes 589832 | tf_op jit(solution)/shard_map/ppermute | solution.py:135
  16.1 10.3 %collective-permute-start.2 = (bf16[32,6144]{1,0:T(8,128)(2,1)S(1)}, bf16[32,6144]{1,0:T(8,128)(2,1)S(1)}, u32[]{:S(2)}, u32[]{:S(2)}) collective-permute-start(bf16[32,6144]{1,0:T(8,128)(2,1)S(1)} %pad_maximum_fusion.9), channel_id=1, source_target_pairs={{0,6},{1,3},{2,4},{3,1},{4,2},{5,7},{6,0},{7,5},{8,14},{9,11},{10,... | collective-permute-start | bytes 1179656 | tf_op jit(solution)/shard_map/ppermute | solution.py:136
  19.8 11.3 %collective-permute-start.7 = (bf16[32,6144]{1,0:T(8,128)(2,1)S(1)}, bf16[32,6144]{1,0:T(8,128)(2,1)S(1)}, u32[]{:S(2)}, u32[]{:S(2)}) collective-permute-start(bf16[32,6144]{1,0:T(8,128)(2,1)S(1)} %pad_maximum_fusion.10), channel_id=1, source_target_pairs={{0,48},{1,17},{2,50},{3,19},{4,52},{5,21},{6,54},{7,23},{8,56},{9,... | collective-permute-start | bytes 1179656 | tf_op jit(solution)/shard_map/ppermute | solution.py:136
  23.9 18.5 %collective-permute-start.19 = (bf16[64,6144]{1,0:T(8,128)(2,1)S(1)}, bf16[64,6144]{1,0:T(8,128)(2,1)S(1)}, u32[]{:S(2)}, u32[]{:S(2)}) collective-permute-start(bf16[64,6144]{1,0:T(8,128)(2,1)S(1)} %get-tuple-element.35), channel_id=1, source_target_pairs={{0,8},{1,9},{2,10},{3,11},{4,12},{5,13},{6,14},{7,15},{8,0},{9,1},... | collective-permute-start | bytes 2359304 | tf_op jit(solution)/shard_map/ppermute | solution.py:32
  26.5 23.5 %collective-permute-start.11 = (bf16[64,6144]{1,0:T(8,128)(2,1)S(1)}, bf16[64,6144]{1,0:T(8,128)(2,1)S(1)}, u32[]{:S(2)}, u32[]{:S(2)}) collective-permute-start(bf16[64,6144]{1,0:T(8,128)(2,1)S(1)} %pad_maximum_fusion.5), channel_id=1, source_target_pairs={{0,48},{1,17},{2,50},{3,19},{4,52},{5,21},{6,54},{7,23},{8,56},{9,... | collective-permute-start | bytes 2359304 | tf_op jit(solution)/shard_map/ppermute | solution.py:58
  27.9 17.2 %collective-permute-start.3 = (bf16[64,6144]{1,0:T(8,128)(2,1)S(1)}, bf16[64,6144]{1,0:T(8,128)(2,1)S(1)}, u32[]{:S(2)}, u32[]{:S(2)}) collective-permute-start(bf16[64,6144]{1,0:T(8,128)(2,1)S(1)} %pad_maximum_fusion.5), channel_id=1, source_target_pairs={{0,16},{1,49},{2,18},{3,51},{4,20},{5,53},{6,22},{7,55},{8,24},{9,... | collective-permute-start | bytes 2359304 | tf_op jit(solution)/shard_map/ppermute | solution.py:58
  42.4 49.7 %collective-permute-start.20 = (bf16[64,6144]{1,0:T(8,128)(2,1)S(1)}, bf16[64,6144]{1,0:T(8,128)(2,1)S(1)}, u32[]{:S(2)}, u32[]{:S(2)}) collective-permute-start(bf16[64,6144]{1,0:T(8,128)(2,1)S(1)} %get-tuple-element.36), channel_id=1, source_target_pairs={{0,8},{1,9},{2,10},{3,11},{4,12},{5,13},{6,14},{7,15},{8,0},{9,1},... | collective-permute-start | bytes 2359304 | tf_op jit(solution)/shard_map/ppermute | solution.py:32
  45.0 28.3 %collective-permute-start.4 = (bf16[64,6144]{1,0:T(8,128)(2,1)S(1)}, bf16[64,6144]{1,0:T(8,128)(2,1)S(1)}, u32[]{:S(2)}, u32[]{:S(2)}) collective-permute-start(bf16[64,6144]{1,0:T(8,128)(2,1)S(1)} %collective-permute-done.3), channel_id=1, source_target_pairs={{0,48},{1,17},{2,50},{3,19},{4,52},{5,21},{6,54},{7,23},{8,56},{9,... | collective-permute-start | bytes 2359304 | tf_op jit(solution)/shard_map/ppermute | solution.py:58
  48.1 18.9 %collective-permute-start.12 = (bf16[64,6144]{1,0:T(8,128)(2,1)S(1)}, bf16[64,6144]{1,0:T(8,128)(2,1)S(1)}, u32[]{:S(2)}, u32[]{:S(2)}) collective-permute-start(bf16[64,6144]{1,0:T(8,128)(2,1)S(1)} %pad_maximum_fusion.6), channel_id=1, source_target_pairs={{0,6},{1,3},{2,4},{3,1},{4,2},{5,7},{6,0},{7,5},{8,14},{9,11},{10,... | collective-permute-start | bytes 2359304 | tf_op jit(solution)/shard_map/ppermute | solution.py:59
  50.0 18.0 %collective-permute-start.9 = (bf16[64,6144]{1,0:T(8,128)(2,1)S(1)}, bf16[64,6144]{1,0:T(8,128)(2,1)S(1)}, u32[]{:S(2)}, u32[]{:S(2)}) collective-permute-start(bf16[64,6144]{1,0:T(8,128)(2,1)S(1)} %pad_maximum_fusion.6), channel_id=1, source_target_pairs={{0,2},{1,7},{2,0},{3,5},{4,6},{5,3},{6,4},{7,1},{8,10},{9,15},{10,... | collective-permute-start | bytes 2359304 | tf_op jit(solution)/shard_map/ppermute | solution.py:59
  69.1 13.3 %collective-permute-start.10 = (bf16[64,6144]{1,0:T(8,128)(2,1)S(1)}, bf16[64,6144]{1,0:T(8,128)(2,1)S(1)}, u32[]{:S(2)}, u32[]{:S(2)}) collective-permute-start(bf16[64,6144]{1,0:T(8,128)(2,1)S(1)} %collective-permute-done.9), channel_id=1, source_target_pairs={{0,6},{1,3},{2,4},{3,1},{4,2},{5,7},{6,0},{7,5},{8,14},{9,11},{10,... | collective-permute-start | bytes 2359304 | tf_op jit(solution)/shard_map/ppermute | solution.py:59
  88.2 7.4 %collective-permute-start.17 = (bf16[512,128]{1,0:T(8,128)(2,1)S(1)}, bf16[512,128]{1,0:T(8,128)(2,1)S(1)}, u32[]{:S(2)}, u32[]{:S(2)}) collective-permute-start(bf16[512,128]{1,0:T(8,128)(2,1)S(1)} %convolution_convert_fusion.2), channel_id=1, source_target_pairs={{0,8},{1,9},{2,10},{3,11},{4,12},{5,13},{6,14},{7,15},{8,0},{9,1},... | collective-permute-start | bytes 393224 | tf_op jit(solution)/shard_map/ppermute | solution.py:32
  92.0 5.4 %collective-permute-start.21 = (bf16[192,3072]{1,0:T(8,128)(2,1)S(1)}, bf16[192,3072]{1,0:T(8,128)(2,1)}, u32[]{:S(2)}, u32[]{:S(2)}) collective-permute-start(bf16[192,3072]{1,0:T(8,128)(2,1)S(1)} %get-tuple-element.42), channel_id=1, source_target_pairs={{0,1},{1,0},{2,3},{3,2},{4,5},{5,4},{6,7},{7,6},{8,9},{9,8},{10,11... | collective-permute-start | bytes 3538952 | tf_op jit(solution)/shard_map/ppermute | solution.py:32
  99.7 13.3 %collective-permute-start.23 = (bf16[128,3072]{1,0:T(8,128)(2,1)S(1)}, bf16[128,3072]{1,0:T(8,128)(2,1)S(1)}, u32[]{:S(2)}, u32[]{:S(2)}) collective-permute-start(bf16[128,3072]{1,0:T(8,128)(2,1)S(1)} %convolution_convert_fusion.1), channel_id=1, source_target_pairs={{0,48},{1,17},{2,50},{3,19},{4,52},{5,21},{6,54},{7,23},{8,56},{9,... | collective-permute-start | bytes 2359304 | tf_op jit(solution)/shard_map/ppermute | solution.py:77
  104.6 13.3 %collective-permute-start.27 = (bf16[128,3072]{1,0:T(8,128)(2,1)S(1)}, bf16[128,3072]{1,0:T(8,128)(2,1)S(1)}, u32[]{:S(2)}, u32[]{:S(2)}) collective-permute-start(bf16[128,3072]{1,0:T(8,128)(2,1)S(1)} %convolution_convert_fusion), channel_id=1, source_target_pairs={{0,6},{1,3},{2,4},{3,1},{4,2},{5,7},{6,0},{7,5},{8,14},{9,11},{10,... | collective-permute-start | bytes 2359304 | tf_op jit(solution)/shard_map/ppermute | solution.py:77
  113.3 7.9 %collective-permute-start.24 = (bf16[64,3072]{1,0:T(8,128)(2,1)S(1)}, bf16[64,3072]{1,0:T(8,128)(2,1)S(1)}, u32[]{:S(2)}, u32[]{:S(2)}) collective-permute-start(bf16[64,3072]{1,0:T(8,128)(2,1)S(1)} %slice.329), channel_id=1, source_target_pairs={{0,16},{1,49},{2,18},{3,51},{4,20},{5,53},{6,22},{7,55},{8,24},{9,... | collective-permute-start | bytes 1179656 | tf_op jit(solution)/shard_map/ppermute | solution.py:79
  118.2 10.0 %collective-permute-start.28 = (bf16[64,3072]{1,0:T(8,128)(2,1)S(1)}, bf16[64,3072]{1,0:T(8,128)(2,1)S(1)}, u32[]{:S(2)}, u32[]{:S(2)}) collective-permute-start(bf16[64,3072]{1,0:T(8,128)(2,1)S(1)} %slice.328), channel_id=1, source_target_pairs={{0,2},{1,7},{2,0},{3,5},{4,6},{5,3},{6,4},{7,1},{8,10},{9,15},{10,... | collective-permute-start | bytes 1179656 | tf_op jit(solution)/shard_map/ppermute | solution.py:79
  121.3 7.1 %collective-permute-start.25 = (bf16[32,3072]{1,0:T(8,128)(2,1)S(1)}, bf16[32,3072]{1,0:T(8,128)(2,1)S(1)}, u32[]{:S(2)}, u32[]{:S(2)}) collective-permute-start(bf16[32,3072]{1,0:T(8,128)(2,1)S(1)} %pad_maximum_fusion.12), channel_id=1, source_target_pairs={{0,6},{1,3},{2,4},{3,1},{4,2},{5,7},{6,0},{7,5},{8,14},{9,11},{10,... | collective-permute-start | bytes 589832 | tf_op jit(solution)/shard_map/ppermute | solution.py:77
  128.3 7.4 %collective-permute-start.29 = (bf16[32,3072]{1,0:T(8,128)(2,1)S(1)}, bf16[32,3072]{1,0:T(8,128)(2,1)S(1)}, u32[]{:S(2)}, u32[]{:S(2)}) collective-permute-start(bf16[32,3072]{1,0:T(8,128)(2,1)S(1)} %pad_maximum_fusion.13), channel_id=1, source_target_pairs={{0,48},{1,17},{2,50},{3,19},{4,52},{5,21},{6,54},{7,23},{8,56},{9,... | collective-permute-start | bytes 589832 | tf_op jit(solution)/shard_map/ppermute | solution.py:77
  128.5 7.4 %collective-permute-start.26 = (bf16[16,3072]{1,0:T(8,128)(2,1)S(1)}, bf16[16,3072]{1,0:T(8,128)(2,1)S(1)}, u32[]{:S(2)}, u32[]{:S(2)}) collective-permute-start(bf16[16,3072]{1,0:T(8,128)(2,1)S(1)} %slice.332), channel_id=1, source_target_pairs={{0,2},{1,7},{2,0},{3,5},{4,6},{5,3},{6,4},{7,1},{8,10},{9,15},{10,... | collective-permute-start | bytes 294920 | tf_op jit(solution)/shard_map/ppermute | solution.py:79
  142.9 5.8 %collective-permute-start.33 = (bf16[8,6144]{1,0:T(8,128)(2,1)S(1)}, bf16[8,6144]{1,0:T(8,128)(2,1)S(1)}, u32[]{:S(2)}, u32[]{:S(2)}) collective-permute-start(bf16[8,6144]{1,0:T(8,128)(2,1)S(1)} %get-tuple-element.72), channel_id=1, source_target_pairs={{0,72},{1,73},{2,74},{3,75},{4,76},{5,77},{6,78},{7,79},{8,64},{9,... | collective-permute-start | bytes 294920 | tf_op jit(solution)/shard_map/ppermute | solution.py:32
  (14 other events, 140.7 us)

commit v7 on v5

--- a/solution.py
+++ b/solution.py
@@ -147,29 +147,35 @@
     middle = out_given.shape[0] // 2
     upper, _ = lax.optimization_barrier((out_given[:middle], one))
     upper = send(upper, x=1)
-
-    def project(first_rows, second_rows):
+    first_own, second_own, swapped_weights = lax.optimization_barrier(
+        (first_own, second_own, swapped_weights)
+    )
+
+    def project(first_rows, second_rows, weights):
         rows = jnp.concatenate([first_rows, second_rows])
-        mine = jnp.dot(rows, own_weights, preferred_element_type=jnp.float32)
-        theirs = jnp.dot(rows, swapped_weights, preferred_element_type=jnp.float32)
-        return mine, theirs
-
-    first_own, second_own = lax.optimization_barrier((first_own, second_own))
+        return jnp.dot(rows, weights, preferred_element_type=jnp.float32)
+
     turn_one = swap_both(first_own, "z", second_own, "y", 0)
-    turn_two = swap_both(first_own, "z", second_own, "y", 1)
-    *turn_one, upper, mine, theirs = lax.optimization_barrier(
-        (*turn_one, upper, *project(first_own, second_own))
-    )
-    here = [(mine, theirs)]
-    lower, _ = lax.optimization_barrier((out_given[middle:], upper))
+    mine = [project(first_own, second_own, own_weights)]
+    first_late, second_late, mine[0] = lax.optimization_barrier(
+        (first_own, second_own, mine[0])
+    )
+    turn_two = swap_both(first_late, "z", second_late, "y", 1)
+    theirs = [project(first_own, second_own, swapped_weights)]
+    turn_one, upper, theirs = lax.optimization_barrier((turn_one, upper, theirs))
+    last = swap_both(turn_one[0], "z", turn_one[1], "y", 1)
+    mine.append(project(*turn_one, own_weights))
+    theirs.append(project(*turn_one, swapped_weights))
+    lower, near_block, _ = lax.optimization_barrier(
+        (out_given[middle:], jnp.concatenate([out_kept, upper]), theirs)
+    )
     lower = send(lower, x=1)
-    *turn_one, first_rows, second_rows = lax.optimization_barrier((*turn_one, *turn_two))
-    last = swap_both(turn_one[0], "z", turn_one[1], "y", 1)
-    here.append(project(*turn_one))
-    here.append(project(first_rows, second_rows))
-    *last, middle_sums = lax.optimization_barrier((*last, here[1:]))
-    here[1:] = middle_sums
-    here.append(project(*last))
+    near_crossed = send(near_block, core=1)
+    last, mine, theirs, turn_two = lax.optimization_barrier((last, mine, theirs, turn_two))
+    for rows in (turn_two, last):
+        mine.append(project(*rows, own_weights))
+        theirs.append(project(*rows, swapped_weights))
+    here = list(zip(mine, theirs))
     by_place = [
         here[0],
         [jnp.where(core == 0, a, b) for a, b in zip(here[1], here[2])],
@@ -180,53 +186,42 @@
 
     attended = attend(projected, token_positions(z, y), head_size)
     own_heads = jnp.concatenate([attended, send(attended, x=1)], axis=1)
-    heads = jnp.concatenate([own_heads, send(own_heads, core=1)], axis=1)
-
-    def swap_quarters(rows):
-        left, right = rows[:, :quarter], rows[:, quarter:]
-        given = send(jnp.where(core == 0, right, left), core=1)
-        return jnp.where(core == 0, left, right), given
-
-    lower, _ = lax.optimization_barrier((lower, attended))
-    out_block = jnp.concatenate(
-        [
-            jnp.concatenate(pieces)
-            for pieces in zip(
-                swap_quarters(jnp.concatenate([out_kept, upper])), swap_quarters(lower)
-            )
-        ]
-    )
+    by_core = own_heads.reshape(32, 2, 8, 2 * head_size)
+    upper_rows, lower_rows = by_core[:, 0], by_core[:, 1]
+    kept_heads = jnp.where(core == 0, upper_rows, lower_rows)
+    given_heads = send(jnp.where(core == 0, lower_rows, upper_rows), core=1)
+    heads = jnp.concatenate([kept_heads, given_heads], axis=2)
+
+    lower, near_crossed, _ = lax.optimization_barrier((lower, near_crossed, attended))
+    out_block = jnp.concatenate([near_block, lower, near_crossed, send(lower, core=1)])
 
     def turns(blocks):
         middle = jnp.where(core == 0, blocks[2], blocks[1])
         kept = jnp.where(core == 0, blocks[1], blocks[2])
         return [middle, blocks[3]], [blocks[0], kept]
 
-    heads = heads.reshape(4, 2, 64, 4 * head_size)
+    heads = heads.reshape(4, 2, 32, 4 * head_size)
+
+    def out_rows_of(blocks):
+        return jnp.dot(
+            jnp.concatenate(blocks), out_block, preferred_element_type=jnp.float32
+        )
+
+    first_sent, first_kept = turns(heads[:, 0])
+    second_sent, second_kept = turns(heads[:, 1])
+    edges = out_rows_of(first_sent + second_sent).astype(jnp.bfloat16)
+    rests = lax.optimization_barrier(out_rows_of(first_kept + second_kept))
+    edges, rests = edges.reshape(2, 64, half), rests.reshape(2, 64, half)
 
     def section_rows(side, far_axis, near_axis):
-        sent, kept = turns(heads[:, side])
-        edge = jnp.dot(
-            jnp.concatenate(sent), out_block, preferred_element_type=jnp.float32
-        ).astype(jnp.bfloat16)
-        rest = jnp.dot(jnp.concatenate(kept), out_block, preferred_element_type=jnp.float32)
-        total = swap_sum(edge, lax.optimization_barrier(rest), far_axis)
-        sent, kept = turns(total.reshape(4, 16, quarter))
+        total = swap_sum(edges[side], rests[side], far_axis)
+        sent, kept = turns(total.reshape(4, 8, half))
         return swap_sum(jnp.concatenate(sent), jnp.concatenate(kept), near_axis)
 
-    first_rows = section_rows(0, "z", "y")
-    second_rows = section_rows(1, "y", "z")
-    owners = jnp.stack([first_rows, second_rows]).astype(jnp.bfloat16)
-    upper, lower = owners[:, :8], owners[:, 8:]
-    stay = jnp.where(core == 0, upper, lower)
-    came = send(jnp.where(core == 0, lower, upper), core=1)
-    wide = jnp.where(
-        core == 0,
-        jnp.concatenate([stay, came], axis=2),
-        jnp.concatenate([came, stay], axis=2),
-    )
-    straight = send(jnp.where(half_x == 0, wide[0], wide[1]), pipe=1)
-    crossed = send(jnp.where(half_x == 0, wide[1], wide[0]), pipe=1, x=1)
+    first_rows = section_rows(0, "z", "y").astype(jnp.bfloat16)
+    second_rows = section_rows(1, "y", "z").astype(jnp.bfloat16)
+    straight = send(jnp.where(half_x == 0, first_rows, second_rows), pipe=1)
+    crossed = send(jnp.where(half_x == 0, second_rows, first_rows), pipe=1, x=1)
     return jnp.where(
         half_x == 0,
         jnp.concatenate([straight, crossed], axis=1),

time: 136 us -> 153 us (1.12)
  waiting for transfers between devices: 58.3 us -> 69 us
  starting transfers between devices: 46.6 us -> 55.5 us
  matrix products: 17.9 us -> 11.7 us
  local copies, waits for them, and re-layouts: 4.27 us -> 8.5 us
    ppermute x16 -> x15, waiting for transfers between devices: 16.6 us -> 30.3 us  [send(): return lax.ppermute(value, AXES, pairs)]
    dot_general x12 -> x10, matrix products: 16.4 us -> 10.2 us  [the longest x8 8.21 us: project(): return jnp.dot(rows, weights, preferred_element_type=jnp.float32)]
    ppermute x16 -> x15, starting transfers between devices: 19.9 us -> 15.9 us  [send(): return lax.ppermute(value, AXES, pairs)]
    ppermute x4, starting transfers between devices: 6.56 us -> 10.4 us  [swap_sum(): got = lax.ppermute(far.astype(jnp.bfloat16), AXES, swap_pairs(axis, 1))]
    ppermute x5, starting transfers between devices: 10.4 us -> 13.7 us  [swap_both(): lax.ppermute(second, AXES, swap_pairs(second_axis, turn))]
    unnamed x14 -> x15, local copies, waits for them, and re-layouts: 0.57 us -> 3.79 us
    ppermute x4, starting transfers between devices: 0.56 us -> 3.59 us  [swap_sum(): lax.ppermute(total[size:].astype(jnp.bfloat16), AXES, swap_pairs(axis, 0))]
    ppermute x5, starting transfers between devices: 9.15 us -> 11.9 us  [swap_both(): lax.ppermute(first, AXES, swap_pairs(first_axis, turn))]
  transfers between devices with their start and end apart: 34 -> 33, of which waited for: 23 -> 19; matrix products, arithmetic and copies ran while one was open for 17% -> 14% of each run, Pallas kernels for 0% -> 0%
where the time goes in v7:
time: 153 us; the launch traced here: 152 us
  waiting for transfers between devices  69 us (45%)
  starting transfers between devices  55.5 us (36%)
  matrix products  11.7 us (8%)
  local copies, waits for them, and re-layouts  8.5 us (6%)
  other arithmetic  6.72 us (4%)
    ppermute x15, waiting for transfers between devices, send(): return lax.ppermute(value, AXES, pairs)  30.3 us
    ppermute x15, starting transfers between devices, send(): return lax.ppermute(value, AXES, pairs)  15.9 us
    ppermute x5, starting transfers between devices, swap_both(): lax.ppermute(second, AXES, swap_pairs(second_axis, turn))  13.7 us
    ppermute x4, waiting for transfers between devices, swap_sum(): got = lax.ppermute(far.astype(jnp.bfloat16), AXES, swap_pairs(axis, 1))  13.1 us
    ppermute x5, starting transfers between devices, swap_both(): lax.ppermute(first, AXES, swap_pairs(first_axis, turn))  11.9 us
    ppermute x5, waiting for transfers between devices, swap_both(): lax.ppermute(first, AXES, swap_pairs(first_axis, turn))  11.7 us
    ppermute x4, starting transfers between devices, swap_sum(): got = lax.ppermute(far.astype(jnp.bfloat16), AXES, swap_pairs(axis, 1))  10.4 us
    ppermute x4, waiting for transfers between devices, swap_sum(): lax.ppermute(total[size:].astype(jnp.bfloat16), AXES, swap_pairs(axis, 0))  9.5 us
  transfers between devices with their start and end apart: 33, of which 19 were waited for; matrix products, arithmetic and copies ran while one was open for 14% of the time, Pallas kernels for 0%

profile of v7, /device:TPU:0, one launch (start us, length us, event | category | flops | bytes accessed | tf_op | source)
XLA Modules:
  0.0 151.9 jit_solution(788643798976569679)
XLA Ops:
  4.9 3.2 %collective-permute-start.1 = (bf16[16,6144]{1,0:T(8,128)(2,1)S(1)}, bf16[16,6144]{1,0:T(8,128)(2,1)S(1)}, u32[]{:S(2)}, u32[]{:S(2)}) collective-permute-start(bf16[16,6144]{1,0:T(8,128)(2,1)S(1)} %maximum_select_fusion), channel_id=1, source_target_pairs={{0,8},{1,9},{2,10},{3,11},{4,12},{5,13},{6,14},{7,15},{8,0},{9,1},... | collective-permute-start | bytes 589832 | tf_op jit(solution)/shard_map/ppermute | solution.py:32
  8.1 3.0 %constant_dynamic-slice_fusion.2 = bf16[6144,384]{1,0:T(8,128)(2,1)S(1)} fusion(bf16[12288,384]{1,0:T(8,128)(2,1)} %bitcast.55, s32[]{:T(128)S(6)} %select_n.223), kind=kLoop, calls=%fused_computation.117 | loop fusion | bytes 9437188 | tf_op jit(solution)/shard_map/dynamic_slice | solution.py:129
  19.3 4.1 %collective-permute-start.5 = (bf16[32,6144]{1,0:T(8,128)(2,1)S(1)}, bf16[32,6144]{1,0:T(8,128)(2,1)S(1)}, u32[]{:S(2)}, u32[]{:S(2)}) collective-permute-start(bf16[32,6144]{1,0:T(8,128)(2,1)S(1)} %pad_maximum_fusion.5), channel_id=1, source_target_pairs={{0,48},{1,17},{2,50},{3,19},{4,52},{5,21},{6,54},{7,23},{8,56},{9,... | collective-permute-start | bytes 1179656 | tf_op jit(solution)/shard_map/ppermute | solution.py:59
  23.5 3.1 %collective-permute-start.3 = (bf16[32,6144]{1,0:T(8,128)(2,1)S(1)}, bf16[32,6144]{1,0:T(8,128)(2,1)S(1)}, u32[]{:S(2)}, u32[]{:S(2)}) collective-permute-start(bf16[32,6144]{1,0:T(8,128)(2,1)S(1)} %pad_maximum_fusion.4), channel_id=1, source_target_pairs={{0,6},{1,3},{2,4},{3,1},{4,2},{5,7},{6,0},{7,5},{8,14},{9,11},{10,... | collective-permute-start | bytes 1179656 | tf_op jit(solution)/shard_map/ppermute | solution.py:58
  26.6 3.0 %collective-permute-start.9 = (bf16[64,6144]{1,0:T(8,128)(2,1)S(1)}, bf16[64,6144]{1,0:T(8,128)(2,1)S(1)}, u32[]{:S(2)}, u32[]{:S(2)}) collective-permute-start(bf16[64,6144]{1,0:T(8,128)(2,1)S(1)} %get-tuple-element.40), channel_id=1, source_target_pairs={{0,8},{1,9},{2,10},{3,11},{4,12},{5,13},{6,14},{7,15},{8,0},{9,1},... | collective-permute-start | bytes 2359304 | tf_op jit(solution)/shard_map/ppermute | solution.py:32
  29.7 2.8 %collective-permute-done.3 = bf16[32,6144]{1,0:T(8,128)(2,1)S(1)} collective-permute-done((bf16[32,6144]{1,0:T(8,128)(2,1)S(1)}, bf16[32,6144]{1,0:T(8,128)(2,1)S(1)}, u32[]{:S(2)}, u32[]{:S(2)}) %collective-permute-start.3) | collective-permute-done | bytes 393248 | tf_op jit(solution)/shard_map/ppermute | solution.py:58
  34.4 2.9 %collective-permute-start.12 = (bf16[64,6144]{1,0:T(8,128)(2,1)S(1)}, bf16[64,6144]{1,0:T(8,128)(2,1)S(1)}, u32[]{:S(2)}, u32[]{:S(2)}) collective-permute-start(bf16[64,6144]{1,0:T(8,128)(2,1)S(1)} %pad_maximum_fusion.1), channel_id=1, source_target_pairs={{0,48},{1,17},{2,50},{3,19},{4,52},{5,21},{6,54},{7,23},{8,56},{9,... | collective-permute-start | bytes 2359304 | tf_op jit(solution)/shard_map/ppermute | solution.py:58
  37.3 2.7 %collective-permute-start.13 = (bf16[64,6144]{1,0:T(8,128)(2,1)S(1)}, bf16[64,6144]{1,0:T(8,128)(2,1)S(1)}, u32[]{:S(2)}, u32[]{:S(2)}) collective-permute-start(bf16[64,6144]{1,0:T(8,128)(2,1)S(1)} %pad_maximum_fusion.2), channel_id=1, source_target_pairs={{0,6},{1,3},{2,4},{3,1},{4,2},{5,7},{6,0},{7,5},{8,14},{9,11},{10,... | collective-permute-start | bytes 2359304 | tf_op jit(solution)/shard_map/ppermute | solution.py:59
  41.0 3.9 %collective-permute-done.9 = bf16[64,6144]{1,0:T(8,128)(2,1)S(1)} collective-permute-done((bf16[64,6144]{1,0:T(8,128)(2,1)S(1)}, bf16[64,6144]{1,0:T(8,128)(2,1)S(1)}, u32[]{:S(2)}, u32[]{:S(2)}) %collective-permute-start.9) | collective-permute-done | bytes 786464 | tf_op jit(solution)/shard_map/ppermute | solution.py:32
  44.9 5.8 %collective-permute-done.7 = bf16[64,6144]{1,0:T(8,128)(2,1)S(1)} collective-permute-done((bf16[64,6144]{1,0:T(8,128)(2,1)S(1)}, bf16[64,6144]{1,0:T(8,128)(2,1)S(1)}, u32[]{:S(2)}, u32[]{:S(2)}) %collective-permute-start.7) | collective-permute-done | bytes 786464 | tf_op jit(solution)/shard_map/ppermute | solution.py:58
  50.7 4.2 %collective-permute-start.10 = (bf16[64,6144]{1,0:T(8,128)(2,1)S(1)}, bf16[64,6144]{1,0:T(8,128)(2,1)S(1)}, u32[]{:S(2)}, u32[]{:S(2)}) collective-permute-start(bf16[64,6144]{1,0:T(8,128)(2,1)S(1)} %collective-permute-done.7), channel_id=1, source_target_pairs={{0,48},{1,17},{2,50},{3,19},{4,52},{5,21},{6,54},{7,23},{8,56},{9,... | collective-permute-start | bytes 2359304 | tf_op jit(solution)/shard_map/ppermute | solution.py:58
  54.9 4.4 %collective-permute-start.11 = (bf16[64,6144]{1,0:T(8,128)(2,1)S(1)}, bf16[64,6144]{1,0:T(8,128)(2,1)S(1)}, u32[]{:S(2)}, u32[]{:S(2)}) collective-permute-start(bf16[64,6144]{1,0:T(8,128)(2,1)S(1)} %collective-permute-done.8), channel_id=1, source_target_pairs={{0,6},{1,3},{2,4},{3,1},{4,2},{5,7},{6,0},{7,5},{8,14},{9,11},{10,... | collective-permute-start | bytes 2359304 | tf_op jit(solution)/shard_map/ppermute | solution.py:59
  61.8 3.1 %collective-permute-done.10 = bf16[64,6144]{1,0:T(8,128)(2,1)S(1)} collective-permute-done((bf16[64,6144]{1,0:T(8,128)(2,1)S(1)}, bf16[64,6144]{1,0:T(8,128)(2,1)S(1)}, u32[]{:S(2)}, u32[]{:S(2)}) %collective-permute-start.10) | collective-permute-done | bytes 786464 | tf_op jit(solution)/shard_map/ppermute | solution.py:58
  64.9 4.4 %collective-permute-done.11 = bf16[64,6144]{1,0:T(8,128)(2,1)S(1)} collective-permute-done((bf16[64,6144]{1,0:T(8,128)(2,1)S(1)}, bf16[64,6144]{1,0:T(8,128)(2,1)S(1)}, u32[]{:S(2)}, u32[]{:S(2)}) %collective-permute-start.11) | collective-permute-done | bytes 786464 | tf_op jit(solution)/shard_map/ppermute | solution.py:59
  76.9 3.1 %collective-permute-start.18 = (bf16[512,128]{0,1:T(8,128)(2,1)S(1)}, bf16[512,128]{0,1:T(8,128)(2,1)S(1)}, u32[]{:S(2)}, u32[]{:S(2)}) collective-permute-start(bf16[512,128]{0,1:T(8,128)(2,1)S(1)} %convolution_convert_fusion.1), channel_id=1, source_target_pairs={{0,8},{1,9},{2,10},{3,11},{4,12},{5,13},{6,14},{7,15},{8,0},{9,1},... | collective-permute-start | bytes 393224 | tf_op jit(solution)/shard_map/ppermute | solution.py:32
  80.6 3.6 %collective-permute-done.18 = bf16[512,128]{0,1:T(8,128)(2,1)S(1)} collective-permute-done((bf16[512,128]{0,1:T(8,128)(2,1)S(1)}, bf16[512,128]{0,1:T(8,128)(2,1)S(1)}, u32[]{:S(2)}, u32[]{:S(2)}) %collective-permute-start.18) | collective-permute-done | bytes 131104 | tf_op jit(solution)/shard_map/ppermute | solution.py:32
  85.8 15.4 %collective-permute-done.20 = bf16[64,6144]{1,0:T(8,128)(2,1)} collective-permute-done((bf16[64,6144]{1,0:T(8,128)(2,1)}, bf16[64,6144]{1,0:T(8,128)(2,1)}, u32[]{:S(2)}, u32[]{:S(2)}) %collective-permute-start.20) | collective-permute-done | bytes 786464 | tf_op jit(solution)/shard_map/ppermute | solution.py:32
  105.8 3.2 %collective-permute-start.27 = (bf16[64,6144]{1,0:T(8,128)(2,1)S(1)}, bf16[64,6144]{1,0:T(8,128)(2,1)S(1)}, u32[]{:S(2)}, u32[]{:S(2)}) collective-permute-start(bf16[64,6144]{1,0:T(8,128)(2,1)S(1)} %get-tuple-element.65), channel_id=1, source_target_pairs={{0,6},{1,3},{2,4},{3,1},{4,2},{5,7},{6,0},{7,5},{8,14},{9,11},{10,... | collective-permute-start | bytes 2359304 | tf_op jit(solution)/shard_map/ppermute | solution.py:77
  110.1 8.7 %collective-permute-done.23 = bf16[64,6144]{1,0:T(8,128)(2,1)S(1)} collective-permute-done((bf16[64,6144]{1,0:T(8,128)(2,1)S(1)}, bf16[64,6144]{1,0:T(8,128)(2,1)S(1)}, u32[]{:S(2)}, u32[]{:S(2)}) %collective-permute-start.23) | collective-permute-done | bytes 786464 | tf_op jit(solution)/shard_map/ppermute | solution.py:77
  120.3 6.9 %collective-permute-done.28 = bf16[32,6144]{1,0:T(8,128)(2,1)S(1)} collective-permute-done((bf16[32,6144]{1,0:T(8,128)(2,1)S(1)}, bf16[32,6144]{1,0:T(8,128)(2,1)S(1)}, u32[]{:S(2)}, u32[]{:S(2)}) %collective-permute-start.28) | collective-permute-done | bytes 393248 | tf_op jit(solution)/shard_map/ppermute | solution.py:79
  127.6 3.0 %collective-permute-start.29 = (bf16[16,6144]{1,0:T(8,128)(2,1)S(1)}, bf16[16,6144]{1,0:T(8,128)(2,1)S(1)}, u32[]{:S(2)}, u32[]{:S(2)}) collective-permute-start(bf16[16,6144]{1,0:T(8,128)(2,1)S(1)} %pad_maximum_fusion.9), channel_id=1, source_target_pairs={{0,48},{1,17},{2,50},{3,19},{4,52},{5,21},{6,54},{7,23},{8,56},{9,... | collective-permute-start | bytes 589832 | tf_op jit(solution)/shard_map/ppermute | solution.py:77
  130.7 3.7 %collective-permute-start.25 = (bf16[16,6144]{1,0:T(8,128)(2,1)S(1)}, bf16[16,6144]{1,0:T(8,128)(2,1)S(1)}, u32[]{:S(2)}, u32[]{:S(2)}) collective-permute-start(bf16[16,6144]{1,0:T(8,128)(2,1)S(1)} %pad_maximum_fusion.8), channel_id=1, source_target_pairs={{0,6},{1,3},{2,4},{3,1},{4,2},{5,7},{6,0},{7,5},{8,14},{9,11},{10,... | collective-permute-start | bytes 589832 | tf_op jit(solution)/shard_map/ppermute | solution.py:77
  134.7 3.9 %collective-permute-done.25 = bf16[16,6144]{1,0:T(8,128)(2,1)S(1)} collective-permute-done((bf16[16,6144]{1,0:T(8,128)(2,1)S(1)}, bf16[16,6144]{1,0:T(8,128)(2,1)S(1)}, u32[]{:S(2)}, u32[]{:S(2)}) %collective-permute-start.25) | collective-permute-done | bytes 196640 | tf_op jit(solution)/shard_map/ppermute | solution.py:77
  138.7 2.6 %collective-permute-start.26 = (bf16[8,6144]{1,0:T(8,128)(2,1)S(1)}, bf16[8,6144]{1,0:T(8,128)(2,1)S(1)}, u32[]{:S(2)}, u32[]{:S(2)}) collective-permute-start(bf16[8,6144]{1,0:T(8,128)(2,1)S(1)} %slice.316), channel_id=1, source_target_pairs={{0,2},{1,7},{2,0},{3,5},{4,6},{5,3},{6,4},{7,1},{8,10},{9,15},{10,... | collective-permute-start | bytes 294920 | tf_op jit(solution)/shard_map/ppermute | solution.py:79
  (121 shorter events, 46.5 us)
Async XLA Ops:
  4.9 8.5 %collective-permute-start.1 = (bf16[16,6144]{1,0:T(8,128)(2,1)S(1)}, bf16[16,6144]{1,0:T(8,128)(2,1)S(1)}, u32[]{:S(2)}, u32[]{:S(2)}) collective-permute-start(bf16[16,6144]{1,0:T(8,128)(2,1)S(1)} %maximum_select_fusion), channel_id=1, source_target_pairs={{0,8},{1,9},{2,10},{3,11},{4,12},{5,13},{6,14},{7,15},{8,0},{9,1},... | collective-permute-start | bytes 589832 | tf_op jit(solution)/shard_map/ppermute | solution.py:32
  13.5 5.8 %collective-permute-start.4 = (bf16[16,6144]{1,0:T(8,128)(2,1)S(1)}, bf16[16,6144]{1,0:T(8,128)(2,1)S(1)}, u32[]{:S(2)}, u32[]{:S(2)}) collective-permute-start(bf16[16,6144]{1,0:T(8,128)(2,1)S(1)} %get-tuple-element.86), channel_id=1, source_target_pairs={{0,16},{1,49},{2,18},{3,51},{4,20},{5,53},{6,22},{7,55},{8,24},{9,... | collective-permute-start | bytes 589832 | tf_op jit(solution)/shard_map/ppermute | solution.py:59
  16.5 16.1 %collective-permute-start.6 = (bf16[6144,384]{1,0:T(8,128)(2,1)S(1)}, bf16[6144,384]{1,0:T(8,128)(2,1)S(1)}, u32[]{:S(2)}, u32[]{:S(2)}) collective-permute-start(bf16[6144,384]{1,0:T(8,128)(2,1)S(1)} %constant_dynamic-slice_fusion.2), channel_id=1, source_target_pairs={{0,1},{1,0},{2,3},{3,2},{4,5},{5,4},{6,7},{7,6},{8,9},{9,8},{10,11... | collective-permute-start | bytes 14155784 | tf_op jit(solution)/shard_map/ppermute | solution.py:32
  17.7 5.7 %collective-permute-start.2 = (bf16[16,6144]{1,0:T(8,128)(2,1)S(1)}, bf16[16,6144]{1,0:T(8,128)(2,1)S(1)}, u32[]{:S(2)}, u32[]{:S(2)}) collective-permute-start(bf16[16,6144]{1,0:T(8,128)(2,1)S(1)} %get-tuple-element.87), channel_id=1, source_target_pairs={{0,2},{1,7},{2,0},{3,5},{4,6},{5,3},{6,4},{7,1},{8,10},{9,15},{10,... | collective-permute-start | bytes 589832 | tf_op jit(solution)/shard_map/ppermute | solution.py:58
  19.3 10.3 %collective-permute-start.5 = (bf16[32,6144]{1,0:T(8,128)(2,1)S(1)}, bf16[32,6144]{1,0:T(8,128)(2,1)S(1)}, u32[]{:S(2)}, u32[]{:S(2)}) collective-permute-start(bf16[32,6144]{1,0:T(8,128)(2,1)S(1)} %pad_maximum_fusion.5), channel_id=1, source_target_pairs={{0,48},{1,17},{2,50},{3,19},{4,52},{5,21},{6,54},{7,23},{8,56},{9,... | collective-permute-start | bytes 1179656 | tf_op jit(solution)/shard_map/ppermute | solution.py:59
  23.5 9.1 %collective-permute-start.3 = (bf16[32,6144]{1,0:T(8,128)(2,1)S(1)}, bf16[32,6144]{1,0:T(8,128)(2,1)S(1)}, u32[]{:S(2)}, u32[]{:S(2)}) collective-permute-start(bf16[32,6144]{1,0:T(8,128)(2,1)S(1)} %pad_maximum_fusion.4), channel_id=1, source_target_pairs={{0,6},{1,3},{2,4},{3,1},{4,2},{5,7},{6,0},{7,5},{8,14},{9,11},{10,... | collective-permute-start | bytes 1179656 | tf_op jit(solution)/shard_map/ppermute | solution.py:58
  26.6 18.3 %collective-permute-start.9 = (bf16[64,6144]{1,0:T(8,128)(2,1)S(1)}, bf16[64,6144]{1,0:T(8,128)(2,1)S(1)}, u32[]{:S(2)}, u32[]{:S(2)}) collective-permute-start(bf16[64,6144]{1,0:T(8,128)(2,1)S(1)} %get-tuple-element.40), channel_id=1, source_target_pairs={{0,8},{1,9},{2,10},{3,11},{4,12},{5,13},{6,14},{7,15},{8,0},{9,1},... | collective-permute-start | bytes 2359304 | tf_op jit(solution)/shard_map/ppermute | solution.py:32
  32.7 17.9 %collective-permute-start.7 = (bf16[64,6144]{1,0:T(8,128)(2,1)S(1)}, bf16[64,6144]{1,0:T(8,128)(2,1)S(1)}, u32[]{:S(2)}, u32[]{:S(2)}) collective-permute-start(bf16[64,6144]{1,0:T(8,128)(2,1)S(1)} %pad_maximum_fusion.1), channel_id=1, source_target_pairs={{0,16},{1,49},{2,18},{3,51},{4,20},{5,53},{6,22},{7,55},{8,24},{9,... | collective-permute-start | bytes 2359304 | tf_op jit(solution)/shard_map/ppermute | solution.py:58
  32.8 17.8 %collective-permute-start.8 = (bf16[64,6144]{1,0:T(8,128)(2,1)S(1)}, bf16[64,6144]{1,0:T(8,128)(2,1)S(1)}, u32[]{:S(2)}, u32[]{:S(2)}) collective-permute-start(bf16[64,6144]{1,0:T(8,128)(2,1)S(1)} %pad_maximum_fusion.2), channel_id=1, source_target_pairs={{0,2},{1,7},{2,0},{3,5},{4,6},{5,3},{6,4},{7,1},{8,10},{9,15},{10,... | collective-permute-start | bytes 2359304 | tf_op jit(solution)/shard_map/ppermute | solution.py:59
  34.4 27.4 %collective-permute-start.12 = (bf16[64,6144]{1,0:T(8,128)(2,1)S(1)}, bf16[64,6144]{1,0:T(8,128)(2,1)S(1)}, u32[]{:S(2)}, u32[]{:S(2)}) collective-permute-start(bf16[64,6144]{1,0:T(8,128)(2,1)S(1)} %pad_maximum_fusion.1), channel_id=1, source_target_pairs={{0,48},{1,17},{2,50},{3,19},{4,52},{5,21},{6,54},{7,23},{8,56},{9,... | collective-permute-start | bytes 2359304 | tf_op jit(solution)/shard_map/ppermute | solution.py:58
  37.3 24.5 %collective-permute-start.13 = (bf16[64,6144]{1,0:T(8,128)(2,1)S(1)}, bf16[64,6144]{1,0:T(8,128)(2,1)S(1)}, u32[]{:S(2)}, u32[]{:S(2)}) collective-permute-start(bf16[64,6144]{1,0:T(8,128)(2,1)S(1)} %pad_maximum_fusion.2), channel_id=1, source_target_pairs={{0,6},{1,3},{2,4},{3,1},{4,2},{5,7},{6,0},{7,5},{8,14},{9,11},{10,... | collective-permute-start | bytes 2359304 | tf_op jit(solution)/shard_map/ppermute | solution.py:59
  50.7 14.2 %collective-permute-start.10 = (bf16[64,6144]{1,0:T(8,128)(2,1)S(1)}, bf16[64,6144]{1,0:T(8,128)(2,1)S(1)}, u32[]{:S(2)}, u32[]{:S(2)}) collective-permute-start(bf16[64,6144]{1,0:T(8,128)(2,1)S(1)} %collective-permute-done.7), channel_id=1, source_target_pairs={{0,48},{1,17},{2,50},{3,19},{4,52},{5,21},{6,54},{7,23},{8,56},{9,... | collective-permute-start | bytes 2359304 | tf_op jit(solution)/shard_map/ppermute | solution.py:58
  54.9 14.4 %collective-permute-start.11 = (bf16[64,6144]{1,0:T(8,128)(2,1)S(1)}, bf16[64,6144]{1,0:T(8,128)(2,1)S(1)}, u32[]{:S(2)}, u32[]{:S(2)}) collective-permute-start(bf16[64,6144]{1,0:T(8,128)(2,1)S(1)} %collective-permute-done.8), channel_id=1, source_target_pairs={{0,6},{1,3},{2,4},{3,1},{4,2},{5,7},{6,0},{7,5},{8,14},{9,11},{10,... | collective-permute-start | bytes 2359304 | tf_op jit(solution)/shard_map/ppermute | solution.py:59
  60.6 40.6 %collective-permute-start.21 = (bf16[192,6144]{1,0:T(8,128)(2,1)S(1)}, bf16[192,6144]{1,0:T(8,128)(2,1)}, u32[]{:S(2)}, u32[]{:S(2)}) collective-permute-start(bf16[192,6144]{1,0:T(8,128)(2,1)S(1)} %pad_maximum_fusion), channel_id=1, source_target_pairs={{0,1},{1,0},{2,3},{3,2},{4,5},{5,4},{6,7},{7,6},{8,9},{9,8},{10,11... | collective-permute-start | bytes 7077896 | tf_op jit(solution)/shard_map/ppermute | solution.py:32
  76.9 7.2 %collective-permute-start.18 = (bf16[512,128]{0,1:T(8,128)(2,1)S(1)}, bf16[512,128]{0,1:T(8,128)(2,1)S(1)}, u32[]{:S(2)}, u32[]{:S(2)}) collective-permute-start(bf16[512,128]{0,1:T(8,128)(2,1)S(1)} %convolution_convert_fusion.1), channel_id=1, source_target_pairs={{0,8},{1,9},{2,10},{3,11},{4,12},{5,13},{6,14},{7,15},{8,0},{9,1},... | collective-permute-start | bytes 393224 | tf_op jit(solution)/shard_map/ppermute | solution.py:32
  80.1 21.2 %collective-permute-start.20 = (bf16[64,6144]{1,0:T(8,128)(2,1)}, bf16[64,6144]{1,0:T(8,128)(2,1)}, u32[]{:S(2)}, u32[]{:S(2)}) collective-permute-start(bf16[64,6144]{1,0:T(8,128)(2,1)} %get-tuple-element.58), channel_id=1, source_target_pairs={{0,8},{1,9},{2,10},{3,11},{4,12},{5,13},{6,14},{7,15},{8,0},{9,1},... | collective-permute-start | bytes 2359304 | tf_op jit(solution)/shard_map/ppermute | solution.py:32
  105.5 13.3 %collective-permute-start.23 = (bf16[64,6144]{1,0:T(8,128)(2,1)S(1)}, bf16[64,6144]{1,0:T(8,128)(2,1)S(1)}, u32[]{:S(2)}, u32[]{:S(2)}) collective-permute-start(bf16[64,6144]{1,0:T(8,128)(2,1)S(1)} %get-tuple-element.66), channel_id=1, source_target_pairs={{0,48},{1,17},{2,50},{3,19},{4,52},{5,21},{6,54},{7,23},{8,56},{9,... | collective-permute-start | bytes 2359304 | tf_op jit(solution)/shard_map/ppermute | solution.py:77
  105.8 13.2 %collective-permute-start.27 = (bf16[64,6144]{1,0:T(8,128)(2,1)S(1)}, bf16[64,6144]{1,0:T(8,128)(2,1)S(1)}, u32[]{:S(2)}, u32[]{:S(2)}) collective-permute-start(bf16[64,6144]{1,0:T(8,128)(2,1)S(1)} %get-tuple-element.65), channel_id=1, source_target_pairs={{0,6},{1,3},{2,4},{3,1},{4,2},{5,7},{6,0},{7,5},{8,14},{9,11},{10,... | collective-permute-start | bytes 2359304 | tf_op jit(solution)/shard_map/ppermute | solution.py:77
  119.4 7.9 %collective-permute-start.28 = (bf16[32,6144]{1,0:T(8,128)(2,1)S(1)}, bf16[32,6144]{1,0:T(8,128)(2,1)S(1)}, u32[]{:S(2)}, u32[]{:S(2)}) collective-permute-start(bf16[32,6144]{1,0:T(8,128)(2,1)S(1)} %slice.312), channel_id=1, source_target_pairs={{0,2},{1,7},{2,0},{3,5},{4,6},{5,3},{6,4},{7,1},{8,10},{9,15},{10,... | collective-permute-start | bytes 1179656 | tf_op jit(solution)/shard_map/ppermute | solution.py:79
  119.5 7.9 %collective-permute-start.24 = (bf16[32,6144]{1,0:T(8,128)(2,1)S(1)}, bf16[32,6144]{1,0:T(8,128)(2,1)S(1)}, u32[]{:S(2)}, u32[]{:S(2)}) collective-permute-start(bf16[32,6144]{1,0:T(8,128)(2,1)S(1)} %slice.313), channel_id=1, source_target_pairs={{0,16},{1,49},{2,18},{3,51},{4,20},{5,53},{6,22},{7,55},{8,24},{9,... | collective-permute-start | bytes 1179656 | tf_op jit(solution)/shard_map/ppermute | solution.py:79
  127.6 7.0 %collective-permute-start.29 = (bf16[16,6144]{1,0:T(8,128)(2,1)S(1)}, bf16[16,6144]{1,0:T(8,128)(2,1)S(1)}, u32[]{:S(2)}, u32[]{:S(2)}) collective-permute-start(bf16[16,6144]{1,0:T(8,128)(2,1)S(1)} %pad_maximum_fusion.9), channel_id=1, source_target_pairs={{0,48},{1,17},{2,50},{3,19},{4,52},{5,21},{6,54},{7,23},{8,56},{9,... | collective-permute-start | bytes 589832 | tf_op jit(solution)/shard_map/ppermute | solution.py:77
  130.7 8.0 %collective-permute-start.25 = (bf16[16,6144]{1,0:T(8,128)(2,1)S(1)}, bf16[16,6144]{1,0:T(8,128)(2,1)S(1)}, u32[]{:S(2)}, u32[]{:S(2)}) collective-permute-start(bf16[16,6144]{1,0:T(8,128)(2,1)S(1)} %pad_maximum_fusion.8), channel_id=1, source_target_pairs={{0,6},{1,3},{2,4},{3,1},{4,2},{5,7},{6,0},{7,5},{8,14},{9,11},{10,... | collective-permute-start | bytes 589832 | tf_op jit(solution)/shard_map/ppermute | solution.py:77
  134.6 6.7 %collective-permute-start.30 = (bf16[8,6144]{1,0:T(8,128)(2,1)S(1)}, bf16[8,6144]{1,0:T(8,128)(2,1)S(1)}, u32[]{:S(2)}, u32[]{:S(2)}) collective-permute-start(bf16[8,6144]{1,0:T(8,128)(2,1)S(1)} %slice.314), channel_id=1, source_target_pairs={{0,16},{1,49},{2,18},{3,51},{4,20},{5,53},{6,22},{7,55},{8,24},{9,... | collective-permute-start | bytes 294920 | tf_op jit(solution)/shard_map/ppermute | solution.py:79
  145.4 5.8 %collective-permute-start.32 = (bf16[8,6144]{1,0:T(8,128)(2,1)S(1)}, bf16[8,6144]{1,0:T(8,128)(2,1)S(1)}, u32[]{:S(2)}, u32[]{:S(2)}) collective-permute-start(bf16[8,6144]{1,0:T(8,128)(2,1)S(1)} %get-tuple-element.68), channel_id=1, source_target_pairs={{0,72},{1,73},{2,74},{3,75},{4,76},{5,77},{6,78},{7,79},{8,64},{9,... | collective-permute-start | bytes 294920 | tf_op jit(solution)/shard_map/ppermute | solution.py:32
  (13 other events, 98.3 us)

commit v8 on v7

--- a/solution.py
+++ b/solution.py
@@ -4,6 +4,8 @@
 import jax.numpy as jnp
 import numpy as np
 from jax import lax
+from jax.experimental import pallas as pl
+from jax.experimental.pallas import tpu as pltpu
 from jax.sharding import PartitionSpec as P
 
 RING = 4
@@ -32,12 +34,35 @@
     return lax.ppermute(value, AXES, pairs)
 
 
-def normalize(section_rows, gain_vector):
-    values = section_rows.astype(jnp.float32)
+def normalize_rows(core_ref, rows_ref, gain_ref, kept_ref, given_ref):
+    values = rows_ref[...].astype(jnp.float32)
     centre = jnp.mean(values, axis=-1, keepdims=True)
     shifted = values - centre
     spread = jnp.mean(shifted * shifted, axis=-1, keepdims=True)
-    return (shifted * lax.rsqrt(spread + 1e-05) * gain_vector).astype(jnp.bfloat16)
+    normed = (shifted * lax.rsqrt(spread + 1e-05) * gain_ref[...]).astype(jnp.bfloat16)
+    half = kept_ref.shape[1]
+
+    @pl.when(core_ref[0] == 0)
+    def _():
+        kept_ref[...] = normed[:, :half]
+        given_ref[...] = normed[:, half:]
+
+    @pl.when(core_ref[0] != 0)
+    def _():
+        kept_ref[...] = normed[:, half:]
+        given_ref[...] = normed[:, :half]
+
+
+def normalize(section_rows, gain_vector, core):
+    count, width = section_rows.shape
+    part = jax.ShapeDtypeStruct((count, width // 2), jnp.bfloat16)
+    whole = pl.BlockSpec(memory_space=pltpu.VMEM)
+    return pl.pallas_call(
+        normalize_rows,
+        out_shape=(part, part),
+        in_specs=[pl.BlockSpec(memory_space=pltpu.SMEM), whole, whole],
+        out_specs=(whole, whole),
+    )(jnp.reshape(core, (1,)), section_rows, gain_vector)
 
 
 def swap_pairs(axis, turn):
@@ -72,12 +97,16 @@
     )
 
 
-def swap_sum(far, near, axis):
-    size = near.shape[0] // 2
-    got = lax.ppermute(far.astype(jnp.bfloat16), AXES, swap_pairs(axis, 1))
-    total = near + got.astype(jnp.float32)
-    got = lax.ppermute(total[size:].astype(jnp.bfloat16), AXES, swap_pairs(axis, 0))
-    return total[:size] + got.astype(jnp.float32)
+def swap_sums(fars, nears, axes):
+    size = nears[0].shape[0] // 2
+    fars = lax.optimization_barrier([far.astype(jnp.bfloat16) for far in fars])
+    got = lax.optimization_barrier(swap_both(fars[0], axes[0], fars[1], axes[1], 1))
+    totals = [near + part.astype(jnp.float32) for near, part in zip(nears, got)]
+    sent = lax.optimization_barrier(
+        [total[size:].astype(jnp.bfloat16) for total in totals]
+    )
+    got = lax.optimization_barrier(swap_both(sent[0], axes[0], sent[1], axes[1], 0))
+    return [total[:size] + part.astype(jnp.float32) for total, part in zip(totals, got)]
 
 
 def token_positions(z, y):
@@ -115,10 +144,8 @@
     half, quarter = width // 2, width // 4
     _, z, half_x, y, core = split_place(lax.axis_index("dp"))
 
-    normed = normalize(segment_input[0], norm_gain[0])
-    left, right = normed[:, :half], normed[:, half:]
-    kept = jnp.where(core == 0, left, right)
-    given = send(jnp.where(core == 0, right, left), core=1)
+    kept, given = normalize(segment_input[0], norm_gain, core)
+    given = send(given, core=1)
     block = jnp.where(
         core == 0, jnp.concatenate([kept, given]), jnp.concatenate([given, kept])
     )
@@ -144,38 +171,30 @@
     out_rows, _ = lax.optimization_barrier((output_weights[0], block))
     out_kept = lax.dynamic_slice_in_dim(out_rows, half_x * half, half, 1)
     out_given = lax.dynamic_slice_in_dim(out_rows, (1 - half_x) * half, half, 1)
-    middle = out_given.shape[0] // 2
-    upper, _ = lax.optimization_barrier((out_given[:middle], one))
-    upper = send(upper, x=1)
+    out_given, _ = lax.optimization_barrier((out_given, one))
+    out_across = send(out_given, x=1)
+
+    def project(first_rows, second_rows):
+        rows = jnp.concatenate([first_rows, second_rows])
+        mine = jnp.dot(rows, own_weights, preferred_element_type=jnp.float32)
+        theirs = jnp.dot(rows, swapped_weights, preferred_element_type=jnp.float32)
+        return mine, theirs
+
     first_own, second_own, swapped_weights = lax.optimization_barrier(
         (first_own, second_own, swapped_weights)
     )
-
-    def project(first_rows, second_rows, weights):
-        rows = jnp.concatenate([first_rows, second_rows])
-        return jnp.dot(rows, weights, preferred_element_type=jnp.float32)
-
     turn_one = swap_both(first_own, "z", second_own, "y", 0)
-    mine = [project(first_own, second_own, own_weights)]
-    first_late, second_late, mine[0] = lax.optimization_barrier(
-        (first_own, second_own, mine[0])
-    )
-    turn_two = swap_both(first_late, "z", second_late, "y", 1)
-    theirs = [project(first_own, second_own, swapped_weights)]
-    turn_one, upper, theirs = lax.optimization_barrier((turn_one, upper, theirs))
+    turn_two = swap_both(first_own, "z", second_own, "y", 1)
+    here = [project(first_own, second_own)]
+    turn_one, turn_two, here = lax.optimization_barrier((turn_one, turn_two, here))
     last = swap_both(turn_one[0], "z", turn_one[1], "y", 1)
-    mine.append(project(*turn_one, own_weights))
-    theirs.append(project(*turn_one, swapped_weights))
-    lower, near_block, _ = lax.optimization_barrier(
-        (out_given[middle:], jnp.concatenate([out_kept, upper]), theirs)
-    )
-    lower = send(lower, x=1)
+    here.append(project(*turn_one))
+    here.append(project(*turn_two))
+    out_across, _ = lax.optimization_barrier((out_across, here))
+    near_block = jnp.concatenate([out_kept, out_across])
     near_crossed = send(near_block, core=1)
-    last, mine, theirs, turn_two = lax.optimization_barrier((last, mine, theirs, turn_two))
-    for rows in (turn_two, last):
-        mine.append(project(*rows, own_weights))
-        theirs.append(project(*rows, swapped_weights))
-    here = list(zip(mine, theirs))
+    last, here = lax.optimization_barrier((last, here))
+    here.append(project(*last))
     by_place = [
         here[0],
         [jnp.where(core == 0, a, b) for a, b in zip(here[1], here[2])],
@@ -192,8 +211,7 @@
     given_heads = send(jnp.where(core == 0, lower_rows, upper_rows), core=1)
     heads = jnp.concatenate([kept_heads, given_heads], axis=2)
 
-    lower, near_crossed, _ = lax.optimization_barrier((lower, near_crossed, attended))
-    out_block = jnp.concatenate([near_block, lower, near_crossed, send(lower, core=1)])
+    out_block = jnp.concatenate([near_block, near_crossed])
 
     def turns(blocks):
         middle = jnp.where(core == 0, blocks[2], blocks[1])
@@ -211,15 +229,18 @@
     second_sent, second_kept = turns(heads[:, 1])
     edges = out_rows_of(first_sent + second_sent).astype(jnp.bfloat16)
     rests = lax.optimization_barrier(out_rows_of(first_kept + second_kept))
-    edges, rests = edges.reshape(2, 64, half), rests.reshape(2, 64, half)
-
-    def section_rows(side, far_axis, near_axis):
-        total = swap_sum(edges[side], rests[side], far_axis)
-        sent, kept = turns(total.reshape(4, 8, half))
-        return swap_sum(jnp.concatenate(sent), jnp.concatenate(kept), near_axis)
-
-    first_rows = section_rows(0, "z", "y").astype(jnp.bfloat16)
-    second_rows = section_rows(1, "y", "z").astype(jnp.bfloat16)
+    size = edges.shape[0] // 2
+    totals = swap_sums(
+        (edges[:size], edges[size:]), (rests[:size], rests[size:]), ("z", "y")
+    )
+    chunks = [turns(total.reshape(4, -1, half)) for total in totals]
+    first_rows, second_rows = swap_sums(
+        [jnp.concatenate(sent) for sent, _ in chunks],
+        [jnp.concatenate(kept) for _, kept in chunks],
+        ("y", "z"),
+    )
+    first_rows = first_rows.astype(jnp.bfloat16)
+    second_rows = second_rows.astype(jnp.bfloat16)
     straight = send(jnp.where(half_x == 0, first_rows, second_rows), pipe=1)
     crossed = send(jnp.where(half_x == 0, second_rows, first_rows), pipe=1, x=1)
     return jnp.where(

time: 153 us -> 135 us (0.88)
  waiting for transfers between devices: 69 us -> 57.6 us
  starting transfers between devices: 55.5 us -> 46.2 us
  matrix products: 11.7 us -> 16.2 us
  local copies, waits for them, and re-layouts: 8.5 us -> 4.99 us
  Pallas kernels: 0 us -> 2.03 us
    ppermute x8 -> x0, waiting for transfers between devices: 22.6 us -> none  [the longest x4 13.1 us: swap_sum(): got = lax.ppermute(far.astype(jnp.bfloat16), AXES, swap_pairs(axis, 1))]
    ppermute x15 -> x13, waiting for transfers between devices: 30.3 us -> 13.4 us  [send(): return lax.ppermute(value, AXES, pairs)]
    ppermute x5 -> x9, waiting for transfers between devices: 11.7 us -> 26.3 us  [swap_both(): lax.ppermute(first, AXES, swap_pairs(first_axis, turn))]
    ppermute x8 -> x0, starting transfers between devices: 14 us -> none  [the longest x4 10.4 us: swap_sum(): got = lax.ppermute(far.astype(jnp.bfloat16), AXES, swap_pairs(axis, 1))]
    ppermute x5 -> x9, waiting for transfers between devices: 4.42 us -> 17.8 us  [swap_both(): lax.ppermute(second, AXES, swap_pairs(second_axis, turn))]
    dot_general x2, matrix products: 1.98 us -> 6.25 us  [out_rows_of(): jnp.dot(jnp.concatenate(blocks), out_block, preferred_element_type=jnp.fl...]
    ppermute x5 -> x9, starting transfers between devices: 13.7 us -> 17.5 us  [swap_both(): lax.ppermute(second, AXES, swap_pairs(second_axis, turn))]
    unnamed x15 -> x12, local copies, waits for them, and re-layouts: 3.79 us -> 0.23 us
  transfers between devices with their start and end apart: 33 -> 31, of which waited for: 19 -> 20; matrix products, arithmetic and copies ran while one was open for 14% -> 17% of each run, Pallas kernels for 0% -> 0%
where the time goes in v8:
time: 135 us; the launch traced here: 134 us
  waiting for transfers between devices  57.6 us (43%)
  starting transfers between devices  46.2 us (34%)
  matrix products  16.2 us (12%)
  other arithmetic  6.67 us (5%)
  local copies, waits for them, and re-layouts  4.99 us (4%)
  Pallas kernels  2.03 us (2%)
    ppermute x9, waiting for transfers between devices, swap_both(): lax.ppermute(first, AXES, swap_pairs(first_axis, turn))  26.3 us
    ppermute x9, waiting for transfers between devices, swap_both(): lax.ppermute(second, AXES, swap_pairs(second_axis, turn))  17.8 us
    ppermute x9, starting transfers between devices, swap_both(): lax.ppermute(second, AXES, swap_pairs(second_axis, turn))  17.5 us
    ppermute x13, starting transfers between devices, send(): return lax.ppermute(value, AXES, pairs)  16.6 us
    ppermute x13, waiting for transfers between devices, send(): return lax.ppermute(value, AXES, pairs)  13.4 us
    ppermute x9, starting transfers between devices, swap_both(): lax.ppermute(first, AXES, swap_pairs(first_axis, turn))  12.1 us
    dot_general x2, matrix products, out_rows_of(): jnp.dot(jnp.concatenate(blocks), out_block, preferred_element_type=jnp.fl...  6.25 us
    dot_general x4, matrix products, project(): theirs = jnp.dot(rows, swapped_weights, preferred_element_type=jnp.float32)  4.25 us
  transfers between devices with their start and end apart: 31, of which 20 were waited for; matrix products, arithmetic and copies ran while one was open for 17% of the time, Pallas kernels for 0%

profile of v8, /device:TPU:0, one launch (start us, length us, event | category | flops | bytes accessed | tf_op | source)
XLA Modules:
  0.0 134.1 jit_solution(7437376605896562028)
XLA Ops:
  4.6 3.2 %collective-permute-start.1 = (bf16[16,6144]{1,0:T(8,128)(2,1)S(1)}, bf16[16,6144]{1,0:T(8,128)(2,1)S(1)}, u32[]{:S(2)}, u32[]{:S(2)}) collective-permute-start(bf16[16,6144]{1,0:T(8,128)(2,1)S(1)} %maximum_select_fusion), channel_id=1, source_target_pairs={{0,8},{1,9},{2,10},{3,11},{4,12},{5,13},{6,14},{7,15},{8,0},{9,1},... | collective-permute-start | bytes 589832 | tf_op jit(solution)/shard_map/ppermute | solution.py:34
  7.7 3.0 %constant_dynamic-slice_fusion.2 = bf16[6144,384]{1,0:T(8,128)(2,1)S(1)} fusion(bf16[12288,384]{1,0:T(8,128)(2,1)} %bitcast.40, s32[]{:T(128)S(6)} %select_n.212), kind=kLoop, calls=%fused_computation.104 | loop fusion | bytes 9437188 | tf_op jit(solution)/shard_map/dynamic_slice | solution.py:156
  10.7 2.4 %collective-permute-done.1 = bf16[16,6144]{1,0:T(8,128)(2,1)S(1)} collective-permute-done((bf16[16,6144]{1,0:T(8,128)(2,1)S(1)}, bf16[16,6144]{1,0:T(8,128)(2,1)S(1)}, u32[]{:S(2)}, u32[]{:S(2)}) %collective-permute-start.1) | collective-permute-done | bytes 196640 | tf_op jit(solution)/shard_map/ppermute | solution.py:34
  17.1 2.3 %collective-permute-start.6 = (bf16[6144,384]{1,0:T(8,128)(2,1)S(1)}, bf16[6144,384]{1,0:T(8,128)(2,1)S(1)}, u32[]{:S(2)}, u32[]{:S(2)}) collective-permute-start(bf16[6144,384]{1,0:T(8,128)(2,1)S(1)} %constant_dynamic-slice_fusion.2), channel_id=1, source_target_pairs={{0,1},{1,0},{2,3},{3,2},{4,5},{5,4},{6,7},{7,6},{8,9},{9,8},{10,11... | collective-permute-start | bytes 14155784 | tf_op jit(solution)/shard_map/ppermute | solution.py:34
  19.5 3.6 %collective-permute-start.5 = (bf16[32,6144]{1,0:T(8,128)(2,1)S(1)}, bf16[32,6144]{1,0:T(8,128)(2,1)S(1)}, u32[]{:S(2)}, u32[]{:S(2)}) collective-permute-start(bf16[32,6144]{1,0:T(8,128)(2,1)S(1)} %pad_maximum_fusion.8), channel_id=1, source_target_pairs={{0,48},{1,17},{2,50},{3,19},{4,52},{5,21},{6,54},{7,23},{8,56},{9,... | collective-permute-start | bytes 1179656 | tf_op jit(solution)/shard_map/ppermute | solution.py:84
  23.2 3.1 %collective-permute-start.3 = (bf16[32,6144]{1,0:T(8,128)(2,1)S(1)}, bf16[32,6144]{1,0:T(8,128)(2,1)S(1)}, u32[]{:S(2)}, u32[]{:S(2)}) collective-permute-start(bf16[32,6144]{1,0:T(8,128)(2,1)S(1)} %pad_maximum_fusion.7), channel_id=1, source_target_pairs={{0,6},{1,3},{2,4},{3,1},{4,2},{5,7},{6,0},{7,5},{8,14},{9,11},{10,... | collective-permute-start | bytes 1179656 | tf_op jit(solution)/shard_map/ppermute | solution.py:83
  26.3 3.0 %collective-permute-start.19 = (bf16[128,6144]{1,0:T(8,128)(2,1)S(1)}, bf16[128,6144]{1,0:T(8,128)(2,1)S(1)}, u32[]{:S(2)}, u32[]{:S(2)}) collective-permute-start(bf16[128,6144]{1,0:T(8,128)(2,1)S(1)} %get-tuple-element.71), channel_id=1, source_target_pairs={{0,8},{1,9},{2,10},{3,11},{4,12},{5,13},{6,14},{7,15},{8,0},{9,1},... | collective-permute-start | bytes 4718600 | tf_op jit(solution)/shard_map/ppermute | solution.py:34
  29.4 2.8 %collective-permute-done.3 = bf16[32,6144]{1,0:T(8,128)(2,1)S(1)} collective-permute-done((bf16[32,6144]{1,0:T(8,128)(2,1)S(1)}, bf16[32,6144]{1,0:T(8,128)(2,1)S(1)}, u32[]{:S(2)}, u32[]{:S(2)}) %collective-permute-start.3) | collective-permute-done | bytes 393248 | tf_op jit(solution)/shard_map/ppermute | solution.py:83
  32.5 3.1 %collective-permute-start.10 = (bf16[64,6144]{1,0:T(8,128)(2,1)S(1)}, bf16[64,6144]{1,0:T(8,128)(2,1)S(1)}, u32[]{:S(2)}, u32[]{:S(2)}) collective-permute-start(bf16[64,6144]{1,0:T(8,128)(2,1)S(1)} %pad_maximum_fusion.5), channel_id=1, source_target_pairs={{0,6},{1,3},{2,4},{3,1},{4,2},{5,7},{6,0},{7,5},{8,14},{9,11},{10,... | collective-permute-start | bytes 2359304 | tf_op jit(solution)/shard_map/ppermute | solution.py:84
  35.6 2.2 %collective-permute-start.9 = (bf16[64,6144]{1,0:T(8,128)(2,1)S(1)}, bf16[64,6144]{1,0:T(8,128)(2,1)S(1)}, u32[]{:S(2)}, u32[]{:S(2)}) collective-permute-start(bf16[64,6144]{1,0:T(8,128)(2,1)S(1)} %pad_maximum_fusion.4), channel_id=1, source_target_pairs={{0,48},{1,17},{2,50},{3,19},{4,52},{5,21},{6,54},{7,23},{8,56},{9,... | collective-permute-start | bytes 2359304 | tf_op jit(solution)/shard_map/ppermute | solution.py:83
  40.0 11.5 %collective-permute-done.10 = bf16[64,6144]{1,0:T(8,128)(2,1)S(1)} collective-permute-done((bf16[64,6144]{1,0:T(8,128)(2,1)S(1)}, bf16[64,6144]{1,0:T(8,128)(2,1)S(1)}, u32[]{:S(2)}, u32[]{:S(2)}) %collective-permute-start.10) | collective-permute-done | bytes 786464 | tf_op jit(solution)/shard_map/ppermute | solution.py:84
  54.9 2.9 %collective-permute-start.12 = (bf16[64,6144]{1,0:T(8,128)(2,1)S(1)}, bf16[64,6144]{1,0:T(8,128)(2,1)S(1)}, u32[]{:S(2)}, u32[]{:S(2)}) collective-permute-start(bf16[64,6144]{1,0:T(8,128)(2,1)S(1)} %collective-permute-done.8), channel_id=1, source_target_pairs={{0,6},{1,3},{2,4},{3,1},{4,2},{5,7},{6,0},{7,5},{8,14},{9,11},{10,... | collective-permute-start | bytes 2359304 | tf_op jit(solution)/shard_map/ppermute | solution.py:84
  62.9 2.6 %collective-permute-done.11 = bf16[64,6144]{1,0:T(8,128)(2,1)S(1)} collective-permute-done((bf16[64,6144]{1,0:T(8,128)(2,1)S(1)}, bf16[64,6144]{1,0:T(8,128)(2,1)S(1)}, u32[]{:S(2)}, u32[]{:S(2)}) %collective-permute-start.11) | collective-permute-done | bytes 786464 | tf_op jit(solution)/shard_map/ppermute | solution.py:83
  65.6 2.6 %collective-permute-done.12 = bf16[64,6144]{1,0:T(8,128)(2,1)S(1)} collective-permute-done((bf16[64,6144]{1,0:T(8,128)(2,1)S(1)}, bf16[64,6144]{1,0:T(8,128)(2,1)S(1)}, u32[]{:S(2)}, u32[]{:S(2)}) %collective-permute-start.12) | collective-permute-done | bytes 786464 | tf_op jit(solution)/shard_map/ppermute | solution.py:84
  74.5 3.1 %collective-permute-start.17 = (bf16[512,128]{0,1:T(8,128)(2,1)S(1)}, bf16[512,128]{0,1:T(8,128)(2,1)S(1)}, u32[]{:S(2)}, u32[]{:S(2)}) collective-permute-start(bf16[512,128]{0,1:T(8,128)(2,1)S(1)} %convolution_convert_fusion.1), channel_id=1, source_target_pairs={{0,8},{1,9},{2,10},{3,11},{4,12},{5,13},{6,14},{7,15},{8,0},{9,1},... | collective-permute-start | bytes 393224 | tf_op jit(solution)/shard_map/ppermute | solution.py:34
  77.6 4.2 %collective-permute-done.17 = bf16[512,128]{0,1:T(8,128)(2,1)S(1)} collective-permute-done((bf16[512,128]{0,1:T(8,128)(2,1)S(1)}, bf16[512,128]{0,1:T(8,128)(2,1)S(1)}, u32[]{:S(2)}, u32[]{:S(2)}) %collective-permute-start.17) | collective-permute-done | bytes 131104 | tf_op jit(solution)/shard_map/ppermute | solution.py:34
  85.2 2.9 %convolution_convert_fusion = bf16[128,6144]{1,0:T(8,128)(2,1)S(1)} fusion(bf16[256,6144]{1,0:T(8,128)(2,1)} %collective-permute-done.20, bf16[128,6144]{1,0:T(8,128)(2,1)S(1)} %collective-permute-done.19, bf16[128,6144]{1,0:T(8,128)(2,1)S(1)} %get-tuple-element.91, bf16[32,512]{1,0:T(8,128)(2,1)S(1)} %get-tuple-element.118, ...), kind=kOutput, calls=%fused_computation | convolution fusion | flops 825491456 | bytes 7995392 | tf_op jit(solution)/shard_map/dot_general | solution.py:224
  91.7 3.4 %fusion.8 = f32[128,6144]{1,0:T(8,128)S(1)} fusion(bf16[256,6144]{1,0:T(8,128)(2,1)} %collective-permute-done.20, bf16[128,6144]{1,0:T(8,128)(2,1)S(1)} %collective-permute-done.19, bf16[128,6144]{1,0:T(8,128)(2,1)S(1)} %get-tuple-element.91, bf16[32,512]{1,0:T(8,128)(2,1)S(1)} %get-tuple-element.122, bf16[32,512]{1,0:T(8,128)(2,1)S(1)} %get-tuple-element.120, ...), kind=kOutput, calls=%fused_computation.11 | convolution fusion | flops 824705024 | bytes 9568256 | tf_op jit(solution)/shard_map/dot_general | solution.py:224
  95.0 6.5 %collective-permute-done.21 = bf16[64,6144]{1,0:T(8,128)(2,1)S(1)} collective-permute-done((bf16[64,6144]{1,0:T(8,128)(2,1)S(1)}, bf16[64,6144]{1,0:T(8,128)(2,1)S(1)}, u32[]{:S(2)}, u32[]{:S(2)}) %collective-permute-start.21) | collective-permute-done | bytes 786464 | tf_op jit(solution)/shard_map/ppermute | solution.py:83
  104.1 7.7 %collective-permute-done.23 = bf16[32,6144]{1,0:T(8,128)(2,1)S(1)} collective-permute-done((bf16[32,6144]{1,0:T(8,128)(2,1)S(1)}, bf16[32,6144]{1,0:T(8,128)(2,1)S(1)}, u32[]{:S(2)}, u32[]{:S(2)}) %collective-permute-start.23) | collective-permute-done | bytes 393248 | tf_op jit(solution)/shard_map/ppermute | solution.py:83
  113.7 2.7 %collective-permute-start.26 = (bf16[16,6144]{1,0:T(8,128)(2,1)S(1)}, bf16[16,6144]{1,0:T(8,128)(2,1)S(1)}, u32[]{:S(2)}, u32[]{:S(2)}) collective-permute-start(bf16[16,6144]{1,0:T(8,128)(2,1)S(1)} %pad_maximum_fusion.12), channel_id=1, source_target_pairs={{0,48},{1,17},{2,50},{3,19},{4,52},{5,21},{6,54},{7,23},{8,56},{9,... | collective-permute-start | bytes 589832 | tf_op jit(solution)/shard_map/ppermute | solution.py:84
  116.5 2.9 %collective-permute-done.25 = bf16[16,6144]{1,0:T(8,128)(2,1)S(1)} collective-permute-done((bf16[16,6144]{1,0:T(8,128)(2,1)S(1)}, bf16[16,6144]{1,0:T(8,128)(2,1)S(1)}, u32[]{:S(2)}, u32[]{:S(2)}) %collective-permute-start.25) | collective-permute-done | bytes 196640 | tf_op jit(solution)/shard_map/ppermute | solution.py:83
  122.7 3.1 %collective-permute-done.27 = bf16[8,6144]{1,0:T(8,128)(2,1)S(1)} collective-permute-done((bf16[8,6144]{1,0:T(8,128)(2,1)S(1)}, bf16[8,6144]{1,0:T(8,128)(2,1)S(1)}, u32[]{:S(2)}, u32[]{:S(2)}) %collective-permute-start.27) | collective-permute-done | bytes 98336 | tf_op jit(solution)/shard_map/ppermute | solution.py:83
  130.7 2.7 %collective-permute-done.30 = bf16[8,6144]{1,0:T(8,128)(2,1)S(1)} collective-permute-done((bf16[8,6144]{1,0:T(8,128)(2,1)S(1)}, bf16[8,6144]{1,0:T(8,128)(2,1)S(1)}, u32[]{:S(2)}, u32[]{:S(2)}) %collective-permute-start.30) | collective-permute-done | bytes 98336 | tf_op jit(solution)/shard_map/ppermute | solution.py:34
  (106 shorter events, 46.1 us)
Async XLA Ops:
  4.6 8.5 %collective-permute-start.1 = (bf16[16,6144]{1,0:T(8,128)(2,1)S(1)}, bf16[16,6144]{1,0:T(8,128)(2,1)S(1)}, u32[]{:S(2)}, u32[]{:S(2)}) collective-permute-start(bf16[16,6144]{1,0:T(8,128)(2,1)S(1)} %maximum_select_fusion), channel_id=1, source_target_pairs={{0,8},{1,9},{2,10},{3,11},{4,12},{5,13},{6,14},{7,15},{8,0},{9,1},... | collective-permute-start | bytes 589832 | tf_op jit(solution)/shard_map/ppermute | solution.py:34
  13.1 6.3 %collective-permute-start.4 = (bf16[16,6144]{1,0:T(8,128)(2,1)S(1)}, bf16[16,6144]{1,0:T(8,128)(2,1)S(1)}, u32[]{:S(2)}, u32[]{:S(2)}) collective-permute-start(bf16[16,6144]{1,0:T(8,128)(2,1)S(1)} %get-tuple-element.115), channel_id=1, source_target_pairs={{0,16},{1,49},{2,18},{3,51},{4,20},{5,53},{6,22},{7,55},{8,24},{9,... | collective-permute-start | bytes 589832 | tf_op jit(solution)/shard_map/ppermute | solution.py:84
  15.5 7.6 %collective-permute-start.2 = (bf16[16,6144]{1,0:T(8,128)(2,1)S(1)}, bf16[16,6144]{1,0:T(8,128)(2,1)S(1)}, u32[]{:S(2)}, u32[]{:S(2)}) collective-permute-start(bf16[16,6144]{1,0:T(8,128)(2,1)S(1)} %get-tuple-element.116), channel_id=1, source_target_pairs={{0,2},{1,7},{2,0},{3,5},{4,6},{5,3},{6,4},{7,1},{8,10},{9,15},{10,... | collective-permute-start | bytes 589832 | tf_op jit(solution)/shard_map/ppermute | solution.py:83
  17.1 15.2 %collective-permute-start.6 = (bf16[6144,384]{1,0:T(8,128)(2,1)S(1)}, bf16[6144,384]{1,0:T(8,128)(2,1)S(1)}, u32[]{:S(2)}, u32[]{:S(2)}) collective-permute-start(bf16[6144,384]{1,0:T(8,128)(2,1)S(1)} %constant_dynamic-slice_fusion.2), channel_id=1, source_target_pairs={{0,1},{1,0},{2,3},{3,2},{4,5},{5,4},{6,7},{7,6},{8,9},{9,8},{10,11... | collective-permute-start | bytes 14155784 | tf_op jit(solution)/shard_map/ppermute | solution.py:34
  19.5 9.8 %collective-permute-start.5 = (bf16[32,6144]{1,0:T(8,128)(2,1)S(1)}, bf16[32,6144]{1,0:T(8,128)(2,1)S(1)}, u32[]{:S(2)}, u32[]{:S(2)}) collective-permute-start(bf16[32,6144]{1,0:T(8,128)(2,1)S(1)} %pad_maximum_fusion.8), channel_id=1, source_target_pairs={{0,48},{1,17},{2,50},{3,19},{4,52},{5,21},{6,54},{7,23},{8,56},{9,... | collective-permute-start | bytes 1179656 | tf_op jit(solution)/shard_map/ppermute | solution.py:84
  23.2 9.1 %collective-permute-start.3 = (bf16[32,6144]{1,0:T(8,128)(2,1)S(1)}, bf16[32,6144]{1,0:T(8,128)(2,1)S(1)}, u32[]{:S(2)}, u32[]{:S(2)}) collective-permute-start(bf16[32,6144]{1,0:T(8,128)(2,1)S(1)} %pad_maximum_fusion.7), channel_id=1, source_target_pairs={{0,6},{1,3},{2,4},{3,1},{4,2},{5,7},{6,0},{7,5},{8,14},{9,11},{10,... | collective-permute-start | bytes 1179656 | tf_op jit(solution)/shard_map/ppermute | solution.py:83
  26.3 34.8 %collective-permute-start.19 = (bf16[128,6144]{1,0:T(8,128)(2,1)S(1)}, bf16[128,6144]{1,0:T(8,128)(2,1)S(1)}, u32[]{:S(2)}, u32[]{:S(2)}) collective-permute-start(bf16[128,6144]{1,0:T(8,128)(2,1)S(1)} %get-tuple-element.71), channel_id=1, source_target_pairs={{0,8},{1,9},{2,10},{3,11},{4,12},{5,13},{6,14},{7,15},{8,0},{9,1},... | collective-permute-start | bytes 4718600 | tf_op jit(solution)/shard_map/ppermute | solution.py:34
  32.4 19.8 %collective-permute-start.7 = (bf16[64,6144]{1,0:T(8,128)(2,1)S(1)}, bf16[64,6144]{1,0:T(8,128)(2,1)S(1)}, u32[]{:S(2)}, u32[]{:S(2)}) collective-permute-start(bf16[64,6144]{1,0:T(8,128)(2,1)S(1)} %pad_maximum_fusion.4), channel_id=1, source_target_pairs={{0,16},{1,49},{2,18},{3,51},{4,20},{5,53},{6,22},{7,55},{8,24},{9,... | collective-permute-start | bytes 2359304 | tf_op jit(solution)/shard_map/ppermute | solution.py:83
  32.5 19.0 %collective-permute-start.10 = (bf16[64,6144]{1,0:T(8,128)(2,1)S(1)}, bf16[64,6144]{1,0:T(8,128)(2,1)S(1)}, u32[]{:S(2)}, u32[]{:S(2)}) collective-permute-start(bf16[64,6144]{1,0:T(8,128)(2,1)S(1)} %pad_maximum_fusion.5), channel_id=1, source_target_pairs={{0,6},{1,3},{2,4},{3,1},{4,2},{5,7},{6,0},{7,5},{8,14},{9,11},{10,... | collective-permute-start | bytes 2359304 | tf_op jit(solution)/shard_map/ppermute | solution.py:84
  35.6 16.6 %collective-permute-start.8 = (bf16[64,6144]{1,0:T(8,128)(2,1)S(1)}, bf16[64,6144]{1,0:T(8,128)(2,1)S(1)}, u32[]{:S(2)}, u32[]{:S(2)}) collective-permute-start(bf16[64,6144]{1,0:T(8,128)(2,1)S(1)} %pad_maximum_fusion.5), channel_id=1, source_target_pairs={{0,2},{1,7},{2,0},{3,5},{4,6},{5,3},{6,4},{7,1},{8,10},{9,15},{10,... | collective-permute-start | bytes 2359304 | tf_op jit(solution)/shard_map/ppermute | solution.py:84
  35.6 16.6 %collective-permute-start.9 = (bf16[64,6144]{1,0:T(8,128)(2,1)S(1)}, bf16[64,6144]{1,0:T(8,128)(2,1)S(1)}, u32[]{:S(2)}, u32[]{:S(2)}) collective-permute-start(bf16[64,6144]{1,0:T(8,128)(2,1)S(1)} %pad_maximum_fusion.4), channel_id=1, source_target_pairs={{0,48},{1,17},{2,50},{3,19},{4,52},{5,21},{6,54},{7,23},{8,56},{9,... | collective-permute-start | bytes 2359304 | tf_op jit(solution)/shard_map/ppermute | solution.py:83
  52.3 13.3 %collective-permute-start.11 = (bf16[64,6144]{1,0:T(8,128)(2,1)S(1)}, bf16[64,6144]{1,0:T(8,128)(2,1)S(1)}, u32[]{:S(2)}, u32[]{:S(2)}) collective-permute-start(bf16[64,6144]{1,0:T(8,128)(2,1)S(1)} %collective-permute-done.7), channel_id=1, source_target_pairs={{0,48},{1,17},{2,50},{3,19},{4,52},{5,21},{6,54},{7,23},{8,56},{9,... | collective-permute-start | bytes 2359304 | tf_op jit(solution)/shard_map/ppermute | solution.py:83
  54.9 13.3 %collective-permute-start.12 = (bf16[64,6144]{1,0:T(8,128)(2,1)S(1)}, bf16[64,6144]{1,0:T(8,128)(2,1)S(1)}, u32[]{:S(2)}, u32[]{:S(2)}) collective-permute-start(bf16[64,6144]{1,0:T(8,128)(2,1)S(1)} %collective-permute-done.8), channel_id=1, source_target_pairs={{0,6},{1,3},{2,4},{3,1},{4,2},{5,7},{6,0},{7,5},{8,14},{9,11},{10,... | collective-permute-start | bytes 2359304 | tf_op jit(solution)/shard_map/ppermute | solution.py:84
  62.9 22.3 %collective-permute-start.20 = (bf16[256,6144]{1,0:T(8,128)(2,1)}, bf16[256,6144]{1,0:T(8,128)(2,1)}, u32[]{:S(2)}, u32[]{:S(2)}) collective-permute-start(bf16[256,6144]{1,0:T(8,128)(2,1)} %pad_maximum_fusion.1), channel_id=1, source_target_pairs={{0,1},{1,0},{2,3},{3,2},{4,5},{5,4},{6,7},{7,6},{8,9},{9,8},{10,11... | collective-permute-start | bytes 9437192 | tf_op jit(solution)/shard_map/ppermute | solution.py:34
  74.5 7.4 %collective-permute-start.17 = (bf16[512,128]{0,1:T(8,128)(2,1)S(1)}, bf16[512,128]{0,1:T(8,128)(2,1)S(1)}, u32[]{:S(2)}, u32[]{:S(2)}) collective-permute-start(bf16[512,128]{0,1:T(8,128)(2,1)S(1)} %convolution_convert_fusion.1), channel_id=1, source_target_pairs={{0,8},{1,9},{2,10},{3,11},{4,12},{5,13},{6,14},{7,15},{8,0},{9,1},... | collective-permute-start | bytes 393224 | tf_op jit(solution)/shard_map/ppermute | solution.py:34
  88.2 13.3 %collective-permute-start.21 = (bf16[64,6144]{1,0:T(8,128)(2,1)S(1)}, bf16[64,6144]{1,0:T(8,128)(2,1)S(1)}, u32[]{:S(2)}, u32[]{:S(2)}) collective-permute-start(bf16[64,6144]{1,0:T(8,128)(2,1)S(1)} %get-tuple-element.73), channel_id=1, source_target_pairs={{0,48},{1,17},{2,50},{3,19},{4,52},{5,21},{6,54},{7,23},{8,56},{9,... | collective-permute-start | bytes 2359304 | tf_op jit(solution)/shard_map/ppermute | solution.py:83
  90.2 13.2 %collective-permute-start.22 = (bf16[64,6144]{1,0:T(8,128)(2,1)S(1)}, bf16[64,6144]{1,0:T(8,128)(2,1)S(1)}, u32[]{:S(2)}, u32[]{:S(2)}) collective-permute-start(bf16[64,6144]{1,0:T(8,128)(2,1)S(1)} %get-tuple-element.74), channel_id=1, source_target_pairs={{0,6},{1,3},{2,4},{3,1},{4,2},{5,7},{6,0},{7,5},{8,14},{9,11},{10,... | collective-permute-start | bytes 2359304 | tf_op jit(solution)/shard_map/ppermute | solution.py:84
  103.9 7.9 %collective-permute-start.23 = (bf16[32,6144]{1,0:T(8,128)(2,1)S(1)}, bf16[32,6144]{1,0:T(8,128)(2,1)S(1)}, u32[]{:S(2)}, u32[]{:S(2)}) collective-permute-start(bf16[32,6144]{1,0:T(8,128)(2,1)S(1)} %slice.287), channel_id=1, source_target_pairs={{0,16},{1,49},{2,18},{3,51},{4,20},{5,53},{6,22},{7,55},{8,24},{9,... | collective-permute-start | bytes 1179656 | tf_op jit(solution)/shard_map/ppermute | solution.py:83
  104.0 7.9 %collective-permute-start.24 = (bf16[32,6144]{1,0:T(8,128)(2,1)S(1)}, bf16[32,6144]{1,0:T(8,128)(2,1)S(1)}, u32[]{:S(2)}, u32[]{:S(2)}) collective-permute-start(bf16[32,6144]{1,0:T(8,128)(2,1)S(1)} %slice.286), channel_id=1, source_target_pairs={{0,2},{1,7},{2,0},{3,5},{4,6},{5,3},{6,4},{7,1},{8,10},{9,15},{10,... | collective-permute-start | bytes 1179656 | tf_op jit(solution)/shard_map/ppermute | solution.py:84
  112.1 7.3 %collective-permute-start.25 = (bf16[16,6144]{1,0:T(8,128)(2,1)S(1)}, bf16[16,6144]{1,0:T(8,128)(2,1)S(1)}, u32[]{:S(2)}, u32[]{:S(2)}) collective-permute-start(bf16[16,6144]{1,0:T(8,128)(2,1)S(1)} %pad_maximum_fusion.11), channel_id=1, source_target_pairs={{0,6},{1,3},{2,4},{3,1},{4,2},{5,7},{6,0},{7,5},{8,14},{9,11},{10,... | collective-permute-start | bytes 589832 | tf_op jit(solution)/shard_map/ppermute | solution.py:83
  113.7 7.3 %collective-permute-start.26 = (bf16[16,6144]{1,0:T(8,128)(2,1)S(1)}, bf16[16,6144]{1,0:T(8,128)(2,1)S(1)}, u32[]{:S(2)}, u32[]{:S(2)}) collective-permute-start(bf16[16,6144]{1,0:T(8,128)(2,1)S(1)} %pad_maximum_fusion.12), channel_id=1, source_target_pairs={{0,48},{1,17},{2,50},{3,19},{4,52},{5,21},{6,54},{7,23},{8,56},{9,... | collective-permute-start | bytes 589832 | tf_op jit(solution)/shard_map/ppermute | solution.py:84
  121.1 4.7 %collective-permute-start.27 = (bf16[8,6144]{1,0:T(8,128)(2,1)S(1)}, bf16[8,6144]{1,0:T(8,128)(2,1)S(1)}, u32[]{:S(2)}, u32[]{:S(2)}) collective-permute-start(bf16[8,6144]{1,0:T(8,128)(2,1)S(1)} %slice.289), channel_id=1, source_target_pairs={{0,2},{1,7},{2,0},{3,5},{4,6},{5,3},{6,4},{7,1},{8,10},{9,15},{10,... | collective-permute-start | bytes 294920 | tf_op jit(solution)/shard_map/ppermute | solution.py:83
  121.2 4.7 %collective-permute-start.28 = (bf16[8,6144]{1,0:T(8,128)(2,1)S(1)}, bf16[8,6144]{1,0:T(8,128)(2,1)S(1)}, u32[]{:S(2)}, u32[]{:S(2)}) collective-permute-start(bf16[8,6144]{1,0:T(8,128)(2,1)S(1)} %slice.288), channel_id=1, source_target_pairs={{0,16},{1,49},{2,18},{3,51},{4,20},{5,53},{6,22},{7,55},{8,24},{9,... | collective-permute-start | bytes 294920 | tf_op jit(solution)/shard_map/ppermute | solution.py:84
  127.6 5.8 %collective-permute-start.30 = (bf16[8,6144]{1,0:T(8,128)(2,1)S(1)}, bf16[8,6144]{1,0:T(8,128)(2,1)S(1)}, u32[]{:S(2)}, u32[]{:S(2)}) collective-permute-start(bf16[8,6144]{1,0:T(8,128)(2,1)S(1)} %get-tuple-element.96), channel_id=1, source_target_pairs={{0,72},{1,73},{2,74},{3,75},{4,76},{5,77},{6,78},{7,79},{8,64},{9,... | collective-permute-start | bytes 294920 | tf_op jit(solution)/shard_map/ppermute | solution.py:34
  (11 other events, 101.8 us)

commit v9 on v8

--- a/solution.py
+++ b/solution.py
@@ -5,6 +5,7 @@
 import numpy as np
 from jax import lax
 from jax.experimental import pallas as pl
+from jax.experimental.layout import Layout, with_layout_constraint
 from jax.experimental.pallas import tpu as pltpu
 from jax.sharding import PartitionSpec as P
 
@@ -55,7 +56,7 @@
 
 def normalize(section_rows, gain_vector, core):
     count, width = section_rows.shape
-    part = jax.ShapeDtypeStruct((count, width // 2), jnp.bfloat16)
+    part = pltpu.VMEM((count, width // 2), jnp.bfloat16)
     whole = pl.BlockSpec(memory_space=pltpu.VMEM)
     return pl.pallas_call(
         normalize_rows,
@@ -203,15 +204,25 @@
     ]
     projected = jnp.concatenate([mine + send(theirs, core=1) for mine, theirs in by_place])
 
-    attended = attend(projected, token_positions(z, y), head_size)
-    own_heads = jnp.concatenate([attended, send(attended, x=1)], axis=1)
-    by_core = own_heads.reshape(32, 2, 8, 2 * head_size)
-    upper_rows, lower_rows = by_core[:, 0], by_core[:, 1]
-    kept_heads = jnp.where(core == 0, upper_rows, lower_rows)
-    given_heads = send(jnp.where(core == 0, lower_rows, upper_rows), core=1)
-    heads = jnp.concatenate([kept_heads, given_heads], axis=2)
-
-    out_block = jnp.concatenate([near_block, near_crossed])
+    attended = with_layout_constraint(
+        attend(projected, token_positions(z, y), head_size), Layout(major_to_minor=(0, 1))
+    )
+    across = send(attended, x=1)
+    out_block, across = lax.optimization_barrier(
+        (jnp.concatenate([near_block, near_crossed]), across)
+    )
+
+    def of_core(rows, place):
+        by_core = rows.reshape(32, 2, 8, head_size)
+        return jnp.where(place == 0, by_core[:, 0], by_core[:, 1])
+
+    given_heads = send(
+        jnp.concatenate([of_core(attended, 1 - core), of_core(across, 1 - core)], axis=2),
+        core=1,
+    )
+    heads = jnp.concatenate(
+        [of_core(attended, core), of_core(across, core), given_heads], axis=2
+    )
 
     def turns(blocks):
         middle = jnp.where(core == 0, blocks[2], blocks[1])

time: 135 us -> 129 us (0.956)
  matrix products: 16.2 us -> 12 us
  waiting for transfers between devices: 57.6 us -> 60.5 us
  other arithmetic: 6.67 us -> 3.85 us
    dot_general x2, matrix products: 6.25 us -> 1.98 us  [out_rows_of(): jnp.dot(jnp.concatenate(blocks), out_block, preferred_element_type=jnp.fl...]
    ppermute x9, waiting for transfers between devices: 26.3 us -> 30.1 us  [swap_both(): lax.ppermute(first, AXES, swap_pairs(first_axis, turn))]
    concatenate x1, other arithmetic: 1.85 us -> 0.32 us  [shards(): near_block = jnp.concatenate([out_kept, out_across])]
  transfers between devices with their start and end apart: 31 -> 31, of which waited for: 20 -> 20; matrix products, arithmetic and copies ran while one was open for 17% -> 13% of each run, Pallas kernels for 0% -> 0%
where the time goes in v9:
time: 129 us
  waiting for transfers between devices  60.5 us (47%)
  starting transfers between devices  46.5 us (36%)
  matrix products  12 us (9%)
  local copies, waits for them, and re-layouts  3.86 us (3%)
  other arithmetic  3.85 us (3%)
  Pallas kernels  1.36 us (1%)
    ppermute x9, waiting for transfers between devices, swap_both(): lax.ppermute(first, AXES, swap_pairs(first_axis, turn))  30.1 us
    ppermute x9, waiting for transfers between devices, swap_both(): lax.ppermute(second, AXES, swap_pairs(second_axis, turn))  17.9 us
    ppermute x9, starting transfers between devices, swap_both(): lax.ppermute(second, AXES, swap_pairs(second_axis, turn))  17.4 us
    ppermute x13, starting transfers between devices, send(): return lax.ppermute(value, AXES, pairs)  16.9 us
    ppermute x13, waiting for transfers between devices, send(): return lax.ppermute(value, AXES, pairs)  12.6 us
    ppermute x9, starting transfers between devices, swap_both(): lax.ppermute(first, AXES, swap_pairs(first_axis, turn))  12.1 us
    dot_general x4, matrix products, project(): theirs = jnp.dot(rows, swapped_weights, preferred_element_type=jnp.float32)  4.25 us
    dot_general x4, matrix products, project(): mine = jnp.dot(rows, own_weights, preferred_element_type=jnp.float32)  4.19 us
  transfers between devices with their start and end apart: 31, of which 20 were waited for; matrix products, arithmetic and copies ran while one was open for 13% of the time, Pallas kernels for 0%

profile of v9, /device:TPU:0, one launch (start us, length us, event | category | flops | bytes accessed | tf_op | source)
XLA Modules:
  0.0 128.6 jit_solution(13907103575253892208)
XLA Ops:
  2.8 3.2 %collective-permute-start.1 = (bf16[16,6144]{1,0:T(8,128)(2,1)S(1)}, bf16[16,6144]{1,0:T(8,128)(2,1)S(1)}, u32[]{:S(2)}, u32[]{:S(2)}) collective-permute-start(bf16[16,6144]{1,0:T(8,128)(2,1)S(1)} %maximum_select_fusion), channel_id=1, source_target_pairs={{0,8},{1,9},{2,10},{3,11},{4,12},{5,13},{6,14},{7,15},{8,0},{9,1},... | collective-permute-start | bytes 589832 | tf_op jit(solution)/shard_map/ppermute | solution.py:35
  6.0 3.0 %constant_dynamic-slice_fusion.2 = bf16[6144,384]{1,0:T(8,128)(2,1)S(1)} fusion(bf16[12288,384]{1,0:T(8,128)(2,1)} %bitcast.71, s32[]{:T(128)S(6)} %select_n.228), kind=kLoop, calls=%fused_computation.110 | loop fusion | bytes 9437188 | tf_op jit(solution)/shard_map/dynamic_slice | solution.py:157
  8.9 2.4 %collective-permute-done.1 = bf16[16,6144]{1,0:T(8,128)(2,1)S(1)} collective-permute-done((bf16[16,6144]{1,0:T(8,128)(2,1)S(1)}, bf16[16,6144]{1,0:T(8,128)(2,1)S(1)}, u32[]{:S(2)}, u32[]{:S(2)}) %collective-permute-start.1) | collective-permute-done | bytes 196640 | tf_op jit(solution)/shard_map/ppermute | solution.py:35
  11.4 2.1 %collective-permute-start.4 = (bf16[16,6144]{1,0:T(8,128)(2,1)S(1)}, bf16[16,6144]{1,0:T(8,128)(2,1)S(1)}, u32[]{:S(2)}, u32[]{:S(2)}) collective-permute-start(bf16[16,6144]{1,0:T(8,128)(2,1)S(1)} %get-tuple-element.119), channel_id=1, source_target_pairs={{0,16},{1,49},{2,18},{3,51},{4,20},{5,53},{6,22},{7,55},{8,24},{9,... | collective-permute-start | bytes 589832 | tf_op jit(solution)/shard_map/ppermute | solution.py:85
  15.4 2.3 %collective-permute-start.6 = (bf16[6144,384]{1,0:T(8,128)(2,1)S(1)}, bf16[6144,384]{1,0:T(8,128)(2,1)S(1)}, u32[]{:S(2)}, u32[]{:S(2)}) collective-permute-start(bf16[6144,384]{1,0:T(8,128)(2,1)S(1)} %constant_dynamic-slice_fusion.2), channel_id=1, source_target_pairs={{0,1},{1,0},{2,3},{3,2},{4,5},{5,4},{6,7},{7,6},{8,9},{9,8},{10,11... | collective-permute-start | bytes 14155784 | tf_op jit(solution)/shard_map/ppermute | solution.py:35
  17.7 3.6 %collective-permute-start.5 = (bf16[32,6144]{1,0:T(8,128)(2,1)S(1)}, bf16[32,6144]{1,0:T(8,128)(2,1)S(1)}, u32[]{:S(2)}, u32[]{:S(2)}) collective-permute-start(bf16[32,6144]{1,0:T(8,128)(2,1)S(1)} %pad_maximum_fusion.6), channel_id=1, source_target_pairs={{0,48},{1,17},{2,50},{3,19},{4,52},{5,21},{6,54},{7,23},{8,56},{9,... | collective-permute-start | bytes 1179656 | tf_op jit(solution)/shard_map/ppermute | solution.py:85
  21.4 3.1 %collective-permute-start.3 = (bf16[32,6144]{1,0:T(8,128)(2,1)S(1)}, bf16[32,6144]{1,0:T(8,128)(2,1)S(1)}, u32[]{:S(2)}, u32[]{:S(2)}) collective-permute-start(bf16[32,6144]{1,0:T(8,128)(2,1)S(1)} %pad_maximum_fusion.5), channel_id=1, source_target_pairs={{0,6},{1,3},{2,4},{3,1},{4,2},{5,7},{6,0},{7,5},{8,14},{9,11},{10,... | collective-permute-start | bytes 1179656 | tf_op jit(solution)/shard_map/ppermute | solution.py:84
  24.5 3.0 %collective-permute-start.17 = (bf16[128,6144]{1,0:T(8,128)(2,1)S(1)}, bf16[128,6144]{1,0:T(8,128)(2,1)S(1)}, u32[]{:S(2)}, u32[]{:S(2)}) collective-permute-start(bf16[128,6144]{1,0:T(8,128)(2,1)S(1)} %get-tuple-element.73), channel_id=1, source_target_pairs={{0,8},{1,9},{2,10},{3,11},{4,12},{5,13},{6,14},{7,15},{8,0},{9,1},... | collective-permute-start | bytes 4718600 | tf_op jit(solution)/shard_map/ppermute | solution.py:35
  27.6 2.8 %collective-permute-done.3 = bf16[32,6144]{1,0:T(8,128)(2,1)S(1)} collective-permute-done((bf16[32,6144]{1,0:T(8,128)(2,1)S(1)}, bf16[32,6144]{1,0:T(8,128)(2,1)S(1)}, u32[]{:S(2)}, u32[]{:S(2)}) %collective-permute-start.3) | collective-permute-done | bytes 393248 | tf_op jit(solution)/shard_map/ppermute | solution.py:84
  30.7 3.1 %collective-permute-start.10 = (bf16[64,6144]{1,0:T(8,128)(2,1)S(1)}, bf16[64,6144]{1,0:T(8,128)(2,1)S(1)}, u32[]{:S(2)}, u32[]{:S(2)}) collective-permute-start(bf16[64,6144]{1,0:T(8,128)(2,1)S(1)} %pad_maximum_fusion.3), channel_id=1, source_target_pairs={{0,6},{1,3},{2,4},{3,1},{4,2},{5,7},{6,0},{7,5},{8,14},{9,11},{10,... | collective-permute-start | bytes 2359304 | tf_op jit(solution)/shard_map/ppermute | solution.py:85
  33.8 2.1 %collective-permute-start.9 = (bf16[64,6144]{1,0:T(8,128)(2,1)S(1)}, bf16[64,6144]{1,0:T(8,128)(2,1)S(1)}, u32[]{:S(2)}, u32[]{:S(2)}) collective-permute-start(bf16[64,6144]{1,0:T(8,128)(2,1)S(1)} %pad_maximum_fusion.2), channel_id=1, source_target_pairs={{0,48},{1,17},{2,50},{3,19},{4,52},{5,21},{6,54},{7,23},{8,56},{9,... | collective-permute-start | bytes 2359304 | tf_op jit(solution)/shard_map/ppermute | solution.py:84
  38.2 11.5 %collective-permute-done.10 = bf16[64,6144]{1,0:T(8,128)(2,1)S(1)} collective-permute-done((bf16[64,6144]{1,0:T(8,128)(2,1)S(1)}, bf16[64,6144]{1,0:T(8,128)(2,1)S(1)}, u32[]{:S(2)}, u32[]{:S(2)}) %collective-permute-start.10) | collective-permute-done | bytes 786464 | tf_op jit(solution)/shard_map/ppermute | solution.py:85
  53.1 2.9 %collective-permute-start.12 = (bf16[64,6144]{1,0:T(8,128)(2,1)S(1)}, bf16[64,6144]{1,0:T(8,128)(2,1)S(1)}, u32[]{:S(2)}, u32[]{:S(2)}) collective-permute-start(bf16[64,6144]{1,0:T(8,128)(2,1)S(1)} %collective-permute-done.8), channel_id=1, source_target_pairs={{0,6},{1,3},{2,4},{3,1},{4,2},{5,7},{6,0},{7,5},{8,14},{9,11},{10,... | collective-permute-start | bytes 2359304 | tf_op jit(solution)/shard_map/ppermute | solution.py:85
  59.9 3.9 %collective-permute-done.11 = bf16[64,6144]{1,0:T(8,128)(2,1)S(1)} collective-permute-done((bf16[64,6144]{1,0:T(8,128)(2,1)S(1)}, bf16[64,6144]{1,0:T(8,128)(2,1)S(1)}, u32[]{:S(2)}, u32[]{:S(2)}) %collective-permute-start.11) | collective-permute-done | bytes 786464 | tf_op jit(solution)/shard_map/ppermute | solution.py:84
  63.8 2.6 %collective-permute-done.12 = bf16[64,6144]{1,0:T(8,128)(2,1)S(1)} collective-permute-done((bf16[64,6144]{1,0:T(8,128)(2,1)S(1)}, bf16[64,6144]{1,0:T(8,128)(2,1)S(1)}, u32[]{:S(2)}, u32[]{:S(2)}) %collective-permute-start.12) | collective-permute-done | bytes 786464 | tf_op jit(solution)/shard_map/ppermute | solution.py:85
  72.8 3.1 %collective-permute-start.19 = (bf16[512,128]{1,0:T(8,128)(2,1)S(1)}, bf16[512,128]{1,0:T(8,128)(2,1)S(1)}, u32[]{:S(2)}, u32[]{:S(2)}) collective-permute-start(bf16[512,128]{1,0:T(8,128)(2,1)S(1)} %convolution_convert_fusion.1), channel_id=1, source_target_pairs={{0,8},{1,9},{2,10},{3,11},{4,12},{5,13},{6,14},{7,15},{8,0},{9,1},... | collective-permute-start | bytes 393224 | tf_op jit(solution)/shard_map/ppermute | solution.py:35
  76.4 3.7 %collective-permute-done.19 = bf16[512,128]{1,0:T(8,128)(2,1)S(1)} collective-permute-done((bf16[512,128]{1,0:T(8,128)(2,1)S(1)}, bf16[512,128]{1,0:T(8,128)(2,1)S(1)}, u32[]{:S(2)}, u32[]{:S(2)}) %collective-permute-start.19) | collective-permute-done | bytes 131104 | tf_op jit(solution)/shard_map/ppermute | solution.py:35
  87.3 8.8 %collective-permute-done.21 = bf16[64,6144]{1,0:T(8,128)(2,1)S(1)} collective-permute-done((bf16[64,6144]{1,0:T(8,128)(2,1)S(1)}, bf16[64,6144]{1,0:T(8,128)(2,1)S(1)}, u32[]{:S(2)}, u32[]{:S(2)}) %collective-permute-start.21) | collective-permute-done | bytes 786464 | tf_op jit(solution)/shard_map/ppermute | solution.py:84
  98.6 7.7 %collective-permute-done.23 = bf16[32,6144]{1,0:T(8,128)(2,1)S(1)} collective-permute-done((bf16[32,6144]{1,0:T(8,128)(2,1)S(1)}, bf16[32,6144]{1,0:T(8,128)(2,1)S(1)}, u32[]{:S(2)}, u32[]{:S(2)}) %collective-permute-start.23) | collective-permute-done | bytes 393248 | tf_op jit(solution)/shard_map/ppermute | solution.py:84
  108.2 2.7 %collective-permute-start.26 = (bf16[16,6144]{1,0:T(8,128)(2,1)S(1)}, bf16[16,6144]{1,0:T(8,128)(2,1)S(1)}, u32[]{:S(2)}, u32[]{:S(2)}) collective-permute-start(bf16[16,6144]{1,0:T(8,128)(2,1)S(1)} %pad_maximum_fusion.9), channel_id=1, source_target_pairs={{0,48},{1,17},{2,50},{3,19},{4,52},{5,21},{6,54},{7,23},{8,56},{9,... | collective-permute-start | bytes 589832 | tf_op jit(solution)/shard_map/ppermute | solution.py:85
  111.0 3.0 %collective-permute-done.25 = bf16[16,6144]{1,0:T(8,128)(2,1)S(1)} collective-permute-done((bf16[16,6144]{1,0:T(8,128)(2,1)S(1)}, bf16[16,6144]{1,0:T(8,128)(2,1)S(1)}, u32[]{:S(2)}, u32[]{:S(2)}) %collective-permute-start.25) | collective-permute-done | bytes 196640 | tf_op jit(solution)/shard_map/ppermute | solution.py:84
  117.2 3.2 %collective-permute-done.27 = bf16[8,6144]{1,0:T(8,128)(2,1)S(1)} collective-permute-done((bf16[8,6144]{1,0:T(8,128)(2,1)S(1)}, bf16[8,6144]{1,0:T(8,128)(2,1)S(1)}, u32[]{:S(2)}, u32[]{:S(2)}) %collective-permute-start.27) | collective-permute-done | bytes 98336 | tf_op jit(solution)/shard_map/ppermute | solution.py:84
  122.1 2.1 %collective-permute-start.30 = (bf16[8,6144]{1,0:T(8,128)(2,1)S(1)}, bf16[8,6144]{1,0:T(8,128)(2,1)S(1)}, u32[]{:S(2)}, u32[]{:S(2)}) collective-permute-start(bf16[8,6144]{1,0:T(8,128)(2,1)S(1)} %get-tuple-element.100), channel_id=1, source_target_pairs={{0,72},{1,73},{2,74},{3,75},{4,76},{5,77},{6,78},{7,79},{8,64},{9,... | collective-permute-start | bytes 294920 | tf_op jit(solution)/shard_map/ppermute | solution.py:35
  125.2 2.7 %collective-permute-done.30 = bf16[8,6144]{1,0:T(8,128)(2,1)S(1)} collective-permute-done((bf16[8,6144]{1,0:T(8,128)(2,1)S(1)}, bf16[8,6144]{1,0:T(8,128)(2,1)S(1)}, u32[]{:S(2)}, u32[]{:S(2)}) %collective-permute-start.30) | collective-permute-done | bytes 98336 | tf_op jit(solution)/shard_map/ppermute | solution.py:35
  (108 shorter events, 39.4 us)
Async XLA Ops:
  2.8 8.5 %collective-permute-start.1 = (bf16[16,6144]{1,0:T(8,128)(2,1)S(1)}, bf16[16,6144]{1,0:T(8,128)(2,1)S(1)}, u32[]{:S(2)}, u32[]{:S(2)}) collective-permute-start(bf16[16,6144]{1,0:T(8,128)(2,1)S(1)} %maximum_select_fusion), channel_id=1, source_target_pairs={{0,8},{1,9},{2,10},{3,11},{4,12},{5,13},{6,14},{7,15},{8,0},{9,1},... | collective-permute-start | bytes 589832 | tf_op jit(solution)/shard_map/ppermute | solution.py:35
  11.4 6.3 %collective-permute-start.4 = (bf16[16,6144]{1,0:T(8,128)(2,1)S(1)}, bf16[16,6144]{1,0:T(8,128)(2,1)S(1)}, u32[]{:S(2)}, u32[]{:S(2)}) collective-permute-start(bf16[16,6144]{1,0:T(8,128)(2,1)S(1)} %get-tuple-element.119), channel_id=1, source_target_pairs={{0,16},{1,49},{2,18},{3,51},{4,20},{5,53},{6,22},{7,55},{8,24},{9,... | collective-permute-start | bytes 589832 | tf_op jit(solution)/shard_map/ppermute | solution.py:85
  13.7 7.7 %collective-permute-start.2 = (bf16[16,6144]{1,0:T(8,128)(2,1)S(1)}, bf16[16,6144]{1,0:T(8,128)(2,1)S(1)}, u32[]{:S(2)}, u32[]{:S(2)}) collective-permute-start(bf16[16,6144]{1,0:T(8,128)(2,1)S(1)} %get-tuple-element.120), channel_id=1, source_target_pairs={{0,2},{1,7},{2,0},{3,5},{4,6},{5,3},{6,4},{7,1},{8,10},{9,15},{10,... | collective-permute-start | bytes 589832 | tf_op jit(solution)/shard_map/ppermute | solution.py:84
  15.4 15.2 %collective-permute-start.6 = (bf16[6144,384]{1,0:T(8,128)(2,1)S(1)}, bf16[6144,384]{1,0:T(8,128)(2,1)S(1)}, u32[]{:S(2)}, u32[]{:S(2)}) collective-permute-start(bf16[6144,384]{1,0:T(8,128)(2,1)S(1)} %constant_dynamic-slice_fusion.2), channel_id=1, source_target_pairs={{0,1},{1,0},{2,3},{3,2},{4,5},{5,4},{6,7},{7,6},{8,9},{9,8},{10,11... | collective-permute-start | bytes 14155784 | tf_op jit(solution)/shard_map/ppermute | solution.py:35
  17.7 9.8 %collective-permute-start.5 = (bf16[32,6144]{1,0:T(8,128)(2,1)S(1)}, bf16[32,6144]{1,0:T(8,128)(2,1)S(1)}, u32[]{:S(2)}, u32[]{:S(2)}) collective-permute-start(bf16[32,6144]{1,0:T(8,128)(2,1)S(1)} %pad_maximum_fusion.6), channel_id=1, source_target_pairs={{0,48},{1,17},{2,50},{3,19},{4,52},{5,21},{6,54},{7,23},{8,56},{9,... | collective-permute-start | bytes 1179656 | tf_op jit(solution)/shard_map/ppermute | solution.py:85
  21.4 9.1 %collective-permute-start.3 = (bf16[32,6144]{1,0:T(8,128)(2,1)S(1)}, bf16[32,6144]{1,0:T(8,128)(2,1)S(1)}, u32[]{:S(2)}, u32[]{:S(2)}) collective-permute-start(bf16[32,6144]{1,0:T(8,128)(2,1)S(1)} %pad_maximum_fusion.5), channel_id=1, source_target_pairs={{0,6},{1,3},{2,4},{3,1},{4,2},{5,7},{6,0},{7,5},{8,14},{9,11},{10,... | collective-permute-start | bytes 1179656 | tf_op jit(solution)/shard_map/ppermute | solution.py:84
  24.5 34.8 %collective-permute-start.17 = (bf16[128,6144]{1,0:T(8,128)(2,1)S(1)}, bf16[128,6144]{1,0:T(8,128)(2,1)S(1)}, u32[]{:S(2)}, u32[]{:S(2)}) collective-permute-start(bf16[128,6144]{1,0:T(8,128)(2,1)S(1)} %get-tuple-element.73), channel_id=1, source_target_pairs={{0,8},{1,9},{2,10},{3,11},{4,12},{5,13},{6,14},{7,15},{8,0},{9,1},... | collective-permute-start | bytes 4718600 | tf_op jit(solution)/shard_map/ppermute | solution.py:35
  30.6 19.8 %collective-permute-start.7 = (bf16[64,6144]{1,0:T(8,128)(2,1)S(1)}, bf16[64,6144]{1,0:T(8,128)(2,1)S(1)}, u32[]{:S(2)}, u32[]{:S(2)}) collective-permute-start(bf16[64,6144]{1,0:T(8,128)(2,1)S(1)} %pad_maximum_fusion.2), channel_id=1, source_target_pairs={{0,16},{1,49},{2,18},{3,51},{4,20},{5,53},{6,22},{7,55},{8,24},{9,... | collective-permute-start | bytes 2359304 | tf_op jit(solution)/shard_map/ppermute | solution.py:84
  30.7 19.0 %collective-permute-start.10 = (bf16[64,6144]{1,0:T(8,128)(2,1)S(1)}, bf16[64,6144]{1,0:T(8,128)(2,1)S(1)}, u32[]{:S(2)}, u32[]{:S(2)}) collective-permute-start(bf16[64,6144]{1,0:T(8,128)(2,1)S(1)} %pad_maximum_fusion.3), channel_id=1, source_target_pairs={{0,6},{1,3},{2,4},{3,1},{4,2},{5,7},{6,0},{7,5},{8,14},{9,11},{10,... | collective-permute-start | bytes 2359304 | tf_op jit(solution)/shard_map/ppermute | solution.py:85
  33.8 16.6 %collective-permute-start.8 = (bf16[64,6144]{1,0:T(8,128)(2,1)S(1)}, bf16[64,6144]{1,0:T(8,128)(2,1)S(1)}, u32[]{:S(2)}, u32[]{:S(2)}) collective-permute-start(bf16[64,6144]{1,0:T(8,128)(2,1)S(1)} %pad_maximum_fusion.3), channel_id=1, source_target_pairs={{0,2},{1,7},{2,0},{3,5},{4,6},{5,3},{6,4},{7,1},{8,10},{9,15},{10,... | collective-permute-start | bytes 2359304 | tf_op jit(solution)/shard_map/ppermute | solution.py:85
  33.8 16.6 %collective-permute-start.9 = (bf16[64,6144]{1,0:T(8,128)(2,1)S(1)}, bf16[64,6144]{1,0:T(8,128)(2,1)S(1)}, u32[]{:S(2)}, u32[]{:S(2)}) collective-permute-start(bf16[64,6144]{1,0:T(8,128)(2,1)S(1)} %pad_maximum_fusion.2), channel_id=1, source_target_pairs={{0,48},{1,17},{2,50},{3,19},{4,52},{5,21},{6,54},{7,23},{8,56},{9,... | collective-permute-start | bytes 2359304 | tf_op jit(solution)/shard_map/ppermute | solution.py:84
  50.5 13.3 %collective-permute-start.11 = (bf16[64,6144]{1,0:T(8,128)(2,1)S(1)}, bf16[64,6144]{1,0:T(8,128)(2,1)S(1)}, u32[]{:S(2)}, u32[]{:S(2)}) collective-permute-start(bf16[64,6144]{1,0:T(8,128)(2,1)S(1)} %collective-permute-done.7), channel_id=1, source_target_pairs={{0,48},{1,17},{2,50},{3,19},{4,52},{5,21},{6,54},{7,23},{8,56},{9,... | collective-permute-start | bytes 2359304 | tf_op jit(solution)/shard_map/ppermute | solution.py:84
  53.1 13.3 %collective-permute-start.12 = (bf16[64,6144]{1,0:T(8,128)(2,1)S(1)}, bf16[64,6144]{1,0:T(8,128)(2,1)S(1)}, u32[]{:S(2)}, u32[]{:S(2)}) collective-permute-start(bf16[64,6144]{1,0:T(8,128)(2,1)S(1)} %collective-permute-done.8), channel_id=1, source_target_pairs={{0,6},{1,3},{2,4},{3,1},{4,2},{5,7},{6,0},{7,5},{8,14},{9,11},{10,... | collective-permute-start | bytes 2359304 | tf_op jit(solution)/shard_map/ppermute | solution.py:85
  59.6 16.3 %collective-permute-start.18 = (bf16[256,6144]{1,0:T(8,128)(2,1)S(1)}, bf16[256,6144]{1,0:T(8,128)(2,1)S(1)}, u32[]{:S(2)}, u32[]{:S(2)}) collective-permute-start(bf16[256,6144]{1,0:T(8,128)(2,1)S(1)} %pad_maximum_fusion.1), channel_id=1, source_target_pairs={{0,1},{1,0},{2,3},{3,2},{4,5},{5,4},{6,7},{7,6},{8,9},{9,8},{10,11... | collective-permute-start | bytes 9437192 | tf_op jit(solution)/shard_map/ppermute | solution.py:35
  72.8 7.4 %collective-permute-start.19 = (bf16[512,128]{1,0:T(8,128)(2,1)S(1)}, bf16[512,128]{1,0:T(8,128)(2,1)S(1)}, u32[]{:S(2)}, u32[]{:S(2)}) collective-permute-start(bf16[512,128]{1,0:T(8,128)(2,1)S(1)} %convolution_convert_fusion.1), channel_id=1, source_target_pairs={{0,8},{1,9},{2,10},{3,11},{4,12},{5,13},{6,14},{7,15},{8,0},{9,1},... | collective-permute-start | bytes 393224 | tf_op jit(solution)/shard_map/ppermute | solution.py:35
  82.8 13.3 %collective-permute-start.21 = (bf16[64,6144]{1,0:T(8,128)(2,1)S(1)}, bf16[64,6144]{1,0:T(8,128)(2,1)S(1)}, u32[]{:S(2)}, u32[]{:S(2)}) collective-permute-start(bf16[64,6144]{1,0:T(8,128)(2,1)S(1)} %get-tuple-element.77), channel_id=1, source_target_pairs={{0,48},{1,17},{2,50},{3,19},{4,52},{5,21},{6,54},{7,23},{8,56},{9,... | collective-permute-start | bytes 2359304 | tf_op jit(solution)/shard_map/ppermute | solution.py:84
  84.8 13.2 %collective-permute-start.22 = (bf16[64,6144]{1,0:T(8,128)(2,1)S(1)}, bf16[64,6144]{1,0:T(8,128)(2,1)S(1)}, u32[]{:S(2)}, u32[]{:S(2)}) collective-permute-start(bf16[64,6144]{1,0:T(8,128)(2,1)S(1)} %get-tuple-element.78), channel_id=1, source_target_pairs={{0,6},{1,3},{2,4},{3,1},{4,2},{5,7},{6,0},{7,5},{8,14},{9,11},{10,... | collective-permute-start | bytes 2359304 | tf_op jit(solution)/shard_map/ppermute | solution.py:85
  98.4 7.9 %collective-permute-start.23 = (bf16[32,6144]{1,0:T(8,128)(2,1)S(1)}, bf16[32,6144]{1,0:T(8,128)(2,1)S(1)}, u32[]{:S(2)}, u32[]{:S(2)}) collective-permute-start(bf16[32,6144]{1,0:T(8,128)(2,1)S(1)} %slice.311), channel_id=1, source_target_pairs={{0,16},{1,49},{2,18},{3,51},{4,20},{5,53},{6,22},{7,55},{8,24},{9,... | collective-permute-start | bytes 1179656 | tf_op jit(solution)/shard_map/ppermute | solution.py:84
  98.5 7.9 %collective-permute-start.24 = (bf16[32,6144]{1,0:T(8,128)(2,1)S(1)}, bf16[32,6144]{1,0:T(8,128)(2,1)S(1)}, u32[]{:S(2)}, u32[]{:S(2)}) collective-permute-start(bf16[32,6144]{1,0:T(8,128)(2,1)S(1)} %slice.310), channel_id=1, source_target_pairs={{0,2},{1,7},{2,0},{3,5},{4,6},{5,3},{6,4},{7,1},{8,10},{9,15},{10,... | collective-permute-start | bytes 1179656 | tf_op jit(solution)/shard_map/ppermute | solution.py:85
  106.6 7.3 %collective-permute-start.25 = (bf16[16,6144]{1,0:T(8,128)(2,1)S(1)}, bf16[16,6144]{1,0:T(8,128)(2,1)S(1)}, u32[]{:S(2)}, u32[]{:S(2)}) collective-permute-start(bf16[16,6144]{1,0:T(8,128)(2,1)S(1)} %pad_maximum_fusion.8), channel_id=1, source_target_pairs={{0,6},{1,3},{2,4},{3,1},{4,2},{5,7},{6,0},{7,5},{8,14},{9,11},{10,... | collective-permute-start | bytes 589832 | tf_op jit(solution)/shard_map/ppermute | solution.py:84
  108.2 7.4 %collective-permute-start.26 = (bf16[16,6144]{1,0:T(8,128)(2,1)S(1)}, bf16[16,6144]{1,0:T(8,128)(2,1)S(1)}, u32[]{:S(2)}, u32[]{:S(2)}) collective-permute-start(bf16[16,6144]{1,0:T(8,128)(2,1)S(1)} %pad_maximum_fusion.9), channel_id=1, source_target_pairs={{0,48},{1,17},{2,50},{3,19},{4,52},{5,21},{6,54},{7,23},{8,56},{9,... | collective-permute-start | bytes 589832 | tf_op jit(solution)/shard_map/ppermute | solution.py:85
  115.7 4.7 %collective-permute-start.27 = (bf16[8,6144]{1,0:T(8,128)(2,1)S(1)}, bf16[8,6144]{1,0:T(8,128)(2,1)S(1)}, u32[]{:S(2)}, u32[]{:S(2)}) collective-permute-start(bf16[8,6144]{1,0:T(8,128)(2,1)S(1)} %slice.313), channel_id=1, source_target_pairs={{0,2},{1,7},{2,0},{3,5},{4,6},{5,3},{6,4},{7,1},{8,10},{9,15},{10,... | collective-permute-start | bytes 294920 | tf_op jit(solution)/shard_map/ppermute | solution.py:84
  115.8 4.7 %collective-permute-start.28 = (bf16[8,6144]{1,0:T(8,128)(2,1)S(1)}, bf16[8,6144]{1,0:T(8,128)(2,1)S(1)}, u32[]{:S(2)}, u32[]{:S(2)}) collective-permute-start(bf16[8,6144]{1,0:T(8,128)(2,1)S(1)} %slice.312), channel_id=1, source_target_pairs={{0,16},{1,49},{2,18},{3,51},{4,20},{5,53},{6,22},{7,55},{8,24},{9,... | collective-permute-start | bytes 294920 | tf_op jit(solution)/shard_map/ppermute | solution.py:85
  122.1 5.8 %collective-permute-start.30 = (bf16[8,6144]{1,0:T(8,128)(2,1)S(1)}, bf16[8,6144]{1,0:T(8,128)(2,1)S(1)}, u32[]{:S(2)}, u32[]{:S(2)}) collective-permute-start(bf16[8,6144]{1,0:T(8,128)(2,1)S(1)} %get-tuple-element.100), channel_id=1, source_target_pairs={{0,72},{1,73},{2,74},{3,75},{4,76},{5,77},{6,78},{7,79},{8,64},{9,... | collective-permute-start | bytes 294920 | tf_op jit(solution)/shard_map/ppermute | solution.py:35
  (11 other events, 101.6 us)

commit v10 on v9

--- a/solution.py
+++ b/solution.py
@@ -151,12 +151,9 @@
         core == 0, jnp.concatenate([kept, given]), jnp.concatenate([given, kept])
     )
     head_block, block = lax.optimization_barrier((head_weights[0, :, 0, :], block))
-    other, their_weights = lax.optimization_barrier(
-        (
-            send(block, x=1),
-            lax.dynamic_slice_in_dim(head_block, (1 - core) * half, half, 0),
-        )
-    )
+    other = send(block, x=1)
+    their_weights = lax.dynamic_slice_in_dim(head_block, (1 - core) * half, half, 0)
+    swapped_weights = send(their_weights, core=1)
     first = jnp.where(half_x == 0, block, other)
     second = jnp.where(half_x == 0, other, block)
     own_weights = lax.dynamic_slice_in_dim(head_block, core * half, half, 0)
@@ -167,7 +164,6 @@
     )
     first_own = near_rows(first, one[0], two[0], core)
     second_own = near_rows(second, one[1], two[1], core)
-    swapped_weights = send(their_weights, core=1)
 
     out_rows, _ = lax.optimization_barrier((output_weights[0], block))
     out_kept = lax.dynamic_slice_in_dim(out_rows, half_x * half, half, 1)
@@ -194,15 +190,18 @@
     out_across, _ = lax.optimization_barrier((out_across, here))
     near_block = jnp.concatenate([out_kept, out_across])
     near_crossed = send(near_block, core=1)
-    last, here = lax.optimization_barrier((last, here))
-    here.append(project(*last))
-    by_place = [
-        here[0],
-        [jnp.where(core == 0, a, b) for a, b in zip(here[1], here[2])],
-        [jnp.where(core == 0, b, a) for a, b in zip(here[1], here[2])],
-        here[3],
+    sums = [
+        mine + send(theirs, core=1)
+        for mine, theirs in (
+            here[0],
+            [jnp.where(core == 0, a, b) for a, b in zip(here[1], here[2])],
+            [jnp.where(core == 0, b, a) for a, b in zip(here[1], here[2])],
+        )
     ]
-    projected = jnp.concatenate([mine + send(theirs, core=1) for mine, theirs in by_place])
+    last, sums = lax.optimization_barrier((last, sums))
+    mine, theirs = project(*last)
+    sums.append(lax.optimization_barrier(mine) + send(theirs, core=1))
+    projected = jnp.concatenate(sums)
 
     attended = with_layout_constraint(
         attend(projected, token_positions(z, y), head_size), Layout(major_to_minor=(0, 1))

time: 129 us -> 126 us (0.977)
  starting transfers between devices: 46.5 us -> 44.9 us
  waiting for transfers between devices: 60.5 us -> 59 us
    ppermute x13, starting transfers between devices: 16.9 us -> 14.8 us  [send(): return lax.ppermute(value, AXES, pairs)]
  transfers between devices with their start and end apart: 31 -> 31, of which waited for: 20 -> 21; matrix products, arithmetic and copies ran while one was open for 13% -> 13% of each run, Pallas kernels for 0% -> 0%
where the time goes in v10:
time: 126 us; the launch traced here: 125 us
  waiting for transfers between devices  59 us (47%)
  starting transfers between devices  44.9 us (36%)
  matrix products  12 us (10%)
  local copies, waits for them, and re-layouts  3.86 us (3%)
  other arithmetic  3.8 us (3%)
  Pallas kernels  1.36 us (1%)
    ppermute x9, waiting for transfers between devices, swap_both(): lax.ppermute(first, AXES, swap_pairs(first_axis, turn))  28.8 us
    ppermute x9, waiting for transfers between devices, swap_both(): lax.ppermute(second, AXES, swap_pairs(second_axis, turn))  18.5 us
    ppermute x9, starting transfers between devices, swap_both(): lax.ppermute(second, AXES, swap_pairs(second_axis, turn))  18 us
    ppermute x13, starting transfers between devices, send(): return lax.ppermute(value, AXES, pairs)  14.8 us
    ppermute x9, starting transfers between devices, swap_both(): lax.ppermute(first, AXES, swap_pairs(first_axis, turn))  12.1 us
    ppermute x13, waiting for transfers between devices, send(): return lax.ppermute(value, AXES, pairs)  11.7 us
    dot_general x4, matrix products, project(): theirs = jnp.dot(rows, swapped_weights, preferred_element_type=jnp.float32)  4.25 us
    dot_general x4, matrix products, project(): mine = jnp.dot(rows, own_weights, preferred_element_type=jnp.float32)  4.19 us
  transfers between devices with their start and end apart: 31, of which 21 were waited for; matrix products, arithmetic and copies ran while one was open for 13% of the time, Pallas kernels for 0%

profile of v10, /device:TPU:0, one launch (start us, length us, event | category | flops | bytes accessed | tf_op | source)
XLA Modules:
  0.0 125.5 jit_solution(8057130724441850789)
XLA Ops:
  2.8 3.2 %collective-permute-start.1 = (bf16[16,6144]{1,0:T(8,128)(2,1)S(1)}, bf16[16,6144]{1,0:T(8,128)(2,1)S(1)}, u32[]{:S(2)}, u32[]{:S(2)}) collective-permute-start(bf16[16,6144]{1,0:T(8,128)(2,1)S(1)} %maximum_select_fusion), channel_id=1, source_target_pairs={{0,8},{1,9},{2,10},{3,11},{4,12},{5,13},{6,14},{7,15},{8,0},{9,1},... | collective-permute-start | bytes 589832 | tf_op jit(solution)/shard_map/ppermute | solution.py:35
  6.0 3.0 %constant_dynamic-slice_fusion.2 = bf16[6144,384]{1,0:T(8,128)(2,1)S(1)} fusion(bf16[12288,384]{1,0:T(8,128)(2,1)} %bitcast.71, s32[]{:T(128)S(6)} %select_n.234), kind=kLoop, calls=%fused_computation.109 | loop fusion | bytes 9437188 | tf_op jit(solution)/shard_map/dynamic_slice | solution.py:155
  9.0 2.3 %collective-permute-done.1 = bf16[16,6144]{1,0:T(8,128)(2,1)S(1)} collective-permute-done((bf16[16,6144]{1,0:T(8,128)(2,1)S(1)}, bf16[16,6144]{1,0:T(8,128)(2,1)S(1)}, u32[]{:S(2)}, u32[]{:S(2)}) %collective-permute-start.1) | collective-permute-done | bytes 196640 | tf_op jit(solution)/shard_map/ppermute | solution.py:35
  11.4 2.1 %collective-permute-start.4 = (bf16[16,6144]{1,0:T(8,128)(2,1)S(1)}, bf16[16,6144]{1,0:T(8,128)(2,1)S(1)}, u32[]{:S(2)}, u32[]{:S(2)}) collective-permute-start(bf16[16,6144]{1,0:T(8,128)(2,1)S(1)} %get-tuple-element.109), channel_id=1, source_target_pairs={{0,16},{1,49},{2,18},{3,51},{4,20},{5,53},{6,22},{7,55},{8,24},{9,... | collective-permute-start | bytes 589832 | tf_op jit(solution)/shard_map/ppermute | solution.py:85
  17.2 4.2 %collective-permute-start.5 = (bf16[32,6144]{1,0:T(8,128)(2,1)S(1)}, bf16[32,6144]{1,0:T(8,128)(2,1)S(1)}, u32[]{:S(2)}, u32[]{:S(2)}) collective-permute-start(bf16[32,6144]{1,0:T(8,128)(2,1)S(1)} %pad_maximum_fusion.6), channel_id=1, source_target_pairs={{0,48},{1,17},{2,50},{3,19},{4,52},{5,21},{6,54},{7,23},{8,56},{9,... | collective-permute-start | bytes 1179656 | tf_op jit(solution)/shard_map/ppermute | solution.py:85
  21.4 3.1 %collective-permute-start.3 = (bf16[32,6144]{1,0:T(8,128)(2,1)S(1)}, bf16[32,6144]{1,0:T(8,128)(2,1)S(1)}, u32[]{:S(2)}, u32[]{:S(2)}) collective-permute-start(bf16[32,6144]{1,0:T(8,128)(2,1)S(1)} %pad_maximum_fusion.5), channel_id=1, source_target_pairs={{0,6},{1,3},{2,4},{3,1},{4,2},{5,7},{6,0},{7,5},{8,14},{9,11},{10,... | collective-permute-start | bytes 1179656 | tf_op jit(solution)/shard_map/ppermute | solution.py:84
  24.5 3.0 %collective-permute-start.17 = (bf16[128,6144]{1,0:T(8,128)(2,1)S(1)}, bf16[128,6144]{1,0:T(8,128)(2,1)S(1)}, u32[]{:S(2)}, u32[]{:S(2)}) collective-permute-start(bf16[128,6144]{1,0:T(8,128)(2,1)S(1)} %get-tuple-element.63), channel_id=1, source_target_pairs={{0,8},{1,9},{2,10},{3,11},{4,12},{5,13},{6,14},{7,15},{8,0},{9,1},... | collective-permute-start | bytes 4718600 | tf_op jit(solution)/shard_map/ppermute | solution.py:35
  27.6 2.8 %collective-permute-done.3 = bf16[32,6144]{1,0:T(8,128)(2,1)S(1)} collective-permute-done((bf16[32,6144]{1,0:T(8,128)(2,1)S(1)}, bf16[32,6144]{1,0:T(8,128)(2,1)S(1)}, u32[]{:S(2)}, u32[]{:S(2)}) %collective-permute-start.3) | collective-permute-done | bytes 393248 | tf_op jit(solution)/shard_map/ppermute | solution.py:84
  30.7 3.1 %collective-permute-start.10 = (bf16[64,6144]{1,0:T(8,128)(2,1)S(1)}, bf16[64,6144]{1,0:T(8,128)(2,1)S(1)}, u32[]{:S(2)}, u32[]{:S(2)}) collective-permute-start(bf16[64,6144]{1,0:T(8,128)(2,1)S(1)} %pad_maximum_fusion.3), channel_id=1, source_target_pairs={{0,6},{1,3},{2,4},{3,1},{4,2},{5,7},{6,0},{7,5},{8,14},{9,11},{10,... | collective-permute-start | bytes 2359304 | tf_op jit(solution)/shard_map/ppermute | solution.py:85
  33.8 2.1 %collective-permute-start.9 = (bf16[64,6144]{1,0:T(8,128)(2,1)S(1)}, bf16[64,6144]{1,0:T(8,128)(2,1)S(1)}, u32[]{:S(2)}, u32[]{:S(2)}) collective-permute-start(bf16[64,6144]{1,0:T(8,128)(2,1)S(1)} %pad_maximum_fusion.2), channel_id=1, source_target_pairs={{0,48},{1,17},{2,50},{3,19},{4,52},{5,21},{6,54},{7,23},{8,56},{9,... | collective-permute-start | bytes 2359304 | tf_op jit(solution)/shard_map/ppermute | solution.py:84
  38.2 11.5 %collective-permute-done.10 = bf16[64,6144]{1,0:T(8,128)(2,1)S(1)} collective-permute-done((bf16[64,6144]{1,0:T(8,128)(2,1)S(1)}, bf16[64,6144]{1,0:T(8,128)(2,1)S(1)}, u32[]{:S(2)}, u32[]{:S(2)}) %collective-permute-start.10) | collective-permute-done | bytes 786464 | tf_op jit(solution)/shard_map/ppermute | solution.py:85
  52.0 2.9 %collective-permute-start.12 = (bf16[64,6144]{1,0:T(8,128)(2,1)S(1)}, bf16[64,6144]{1,0:T(8,128)(2,1)S(1)}, u32[]{:S(2)}, u32[]{:S(2)}) collective-permute-start(bf16[64,6144]{1,0:T(8,128)(2,1)S(1)} %collective-permute-done.8), channel_id=1, source_target_pairs={{0,6},{1,3},{2,4},{3,1},{4,2},{5,7},{6,0},{7,5},{8,14},{9,11},{10,... | collective-permute-start | bytes 2359304 | tf_op jit(solution)/shard_map/ppermute | solution.py:85
  61.1 2.7 %collective-permute-done.11 = bf16[64,6144]{1,0:T(8,128)(2,1)S(1)} collective-permute-done((bf16[64,6144]{1,0:T(8,128)(2,1)S(1)}, bf16[64,6144]{1,0:T(8,128)(2,1)S(1)}, u32[]{:S(2)}, u32[]{:S(2)}) %collective-permute-start.11) | collective-permute-done | bytes 786464 | tf_op jit(solution)/shard_map/ppermute | solution.py:84
  69.9 3.1 %collective-permute-start.19 = (bf16[512,128]{1,0:T(8,128)(2,1)S(1)}, bf16[512,128]{1,0:T(8,128)(2,1)S(1)}, u32[]{:S(2)}, u32[]{:S(2)}) collective-permute-start(bf16[512,128]{1,0:T(8,128)(2,1)S(1)} %convolution_convert_fusion.1), channel_id=1, source_target_pairs={{0,8},{1,9},{2,10},{3,11},{4,12},{5,13},{6,14},{7,15},{8,0},{9,1},... | collective-permute-start | bytes 393224 | tf_op jit(solution)/shard_map/ppermute | solution.py:35
  73.5 3.5 %collective-permute-done.19 = bf16[512,128]{1,0:T(8,128)(2,1)S(1)} collective-permute-done((bf16[512,128]{1,0:T(8,128)(2,1)S(1)}, bf16[512,128]{1,0:T(8,128)(2,1)S(1)}, u32[]{:S(2)}, u32[]{:S(2)}) %collective-permute-start.19) | collective-permute-done | bytes 131104 | tf_op jit(solution)/shard_map/ppermute | solution.py:35
  79.6 2.0 %collective-permute-start.21 = (bf16[64,6144]{1,0:T(8,128)(2,1)S(1)}, bf16[64,6144]{1,0:T(8,128)(2,1)S(1)}, u32[]{:S(2)}, u32[]{:S(2)}) collective-permute-start(bf16[64,6144]{1,0:T(8,128)(2,1)S(1)} %get-tuple-element.67), channel_id=1, source_target_pairs={{0,48},{1,17},{2,50},{3,19},{4,52},{5,21},{6,54},{7,23},{8,56},{9,... | collective-permute-start | bytes 2359304 | tf_op jit(solution)/shard_map/ppermute | solution.py:84
  84.1 8.8 %collective-permute-done.21 = bf16[64,6144]{1,0:T(8,128)(2,1)S(1)} collective-permute-done((bf16[64,6144]{1,0:T(8,128)(2,1)S(1)}, bf16[64,6144]{1,0:T(8,128)(2,1)S(1)}, u32[]{:S(2)}, u32[]{:S(2)}) %collective-permute-start.21) | collective-permute-done | bytes 786464 | tf_op jit(solution)/shard_map/ppermute | solution.py:84
  92.9 1.9 %collective-permute-done.22 = bf16[64,6144]{1,0:T(8,128)(2,1)S(1)} collective-permute-done((bf16[64,6144]{1,0:T(8,128)(2,1)S(1)}, bf16[64,6144]{1,0:T(8,128)(2,1)S(1)}, u32[]{:S(2)}, u32[]{:S(2)}) %collective-permute-start.22) | collective-permute-done | bytes 786464 | tf_op jit(solution)/shard_map/ppermute | solution.py:85
  95.4 7.7 %collective-permute-done.23 = bf16[32,6144]{1,0:T(8,128)(2,1)S(1)} collective-permute-done((bf16[32,6144]{1,0:T(8,128)(2,1)S(1)}, bf16[32,6144]{1,0:T(8,128)(2,1)S(1)}, u32[]{:S(2)}, u32[]{:S(2)}) %collective-permute-start.23) | collective-permute-done | bytes 393248 | tf_op jit(solution)/shard_map/ppermute | solution.py:84
  105.1 2.7 %collective-permute-start.26 = (bf16[16,6144]{1,0:T(8,128)(2,1)S(1)}, bf16[16,6144]{1,0:T(8,128)(2,1)S(1)}, u32[]{:S(2)}, u32[]{:S(2)}) collective-permute-start(bf16[16,6144]{1,0:T(8,128)(2,1)S(1)} %pad_maximum_fusion.9), channel_id=1, source_target_pairs={{0,48},{1,17},{2,50},{3,19},{4,52},{5,21},{6,54},{7,23},{8,56},{9,... | collective-permute-start | bytes 589832 | tf_op jit(solution)/shard_map/ppermute | solution.py:85
  107.8 3.0 %collective-permute-done.25 = bf16[16,6144]{1,0:T(8,128)(2,1)S(1)} collective-permute-done((bf16[16,6144]{1,0:T(8,128)(2,1)S(1)}, bf16[16,6144]{1,0:T(8,128)(2,1)S(1)}, u32[]{:S(2)}, u32[]{:S(2)}) %collective-permute-start.25) | collective-permute-done | bytes 196640 | tf_op jit(solution)/shard_map/ppermute | solution.py:84
  114.1 3.1 %collective-permute-done.27 = bf16[8,6144]{1,0:T(8,128)(2,1)S(1)} collective-permute-done((bf16[8,6144]{1,0:T(8,128)(2,1)S(1)}, bf16[8,6144]{1,0:T(8,128)(2,1)S(1)}, u32[]{:S(2)}, u32[]{:S(2)}) %collective-permute-start.27) | collective-permute-done | bytes 98336 | tf_op jit(solution)/shard_map/ppermute | solution.py:84
  118.9 2.1 %collective-permute-start.30 = (bf16[8,6144]{1,0:T(8,128)(2,1)S(1)}, bf16[8,6144]{1,0:T(8,128)(2,1)S(1)}, u32[]{:S(2)}, u32[]{:S(2)}) collective-permute-start(bf16[8,6144]{1,0:T(8,128)(2,1)S(1)} %get-tuple-element.90), channel_id=1, source_target_pairs={{0,72},{1,73},{2,74},{3,75},{4,76},{5,77},{6,78},{7,79},{8,64},{9,... | collective-permute-start | bytes 294920 | tf_op jit(solution)/shard_map/ppermute | solution.py:35
  122.1 2.7 %collective-permute-done.30 = bf16[8,6144]{1,0:T(8,128)(2,1)S(1)} collective-permute-done((bf16[8,6144]{1,0:T(8,128)(2,1)S(1)}, bf16[8,6144]{1,0:T(8,128)(2,1)S(1)}, u32[]{:S(2)}, u32[]{:S(2)}) %collective-permute-start.30) | collective-permute-done | bytes 98336 | tf_op jit(solution)/shard_map/ppermute | solution.py:35
  (107 shorter events, 38.3 us)
Async XLA Ops:
  2.8 8.5 %collective-permute-start.1 = (bf16[16,6144]{1,0:T(8,128)(2,1)S(1)}, bf16[16,6144]{1,0:T(8,128)(2,1)S(1)}, u32[]{:S(2)}, u32[]{:S(2)}) collective-permute-start(bf16[16,6144]{1,0:T(8,128)(2,1)S(1)} %maximum_select_fusion), channel_id=1, source_target_pairs={{0,8},{1,9},{2,10},{3,11},{4,12},{5,13},{6,14},{7,15},{8,0},{9,1},... | collective-permute-start | bytes 589832 | tf_op jit(solution)/shard_map/ppermute | solution.py:35
  8.9 21.6 %collective-permute-start.6 = (bf16[6144,384]{1,0:T(8,128)(2,1)S(1)}, bf16[6144,384]{1,0:T(8,128)(2,1)S(1)}, u32[]{:S(2)}, u32[]{:S(2)}) collective-permute-start(bf16[6144,384]{1,0:T(8,128)(2,1)S(1)} %constant_dynamic-slice_fusion.2), channel_id=1, source_target_pairs={{0,1},{1,0},{2,3},{3,2},{4,5},{5,4},{6,7},{7,6},{8,9},{9,8},{10,11... | collective-permute-start | bytes 14155784 | tf_op jit(solution)/shard_map/ppermute | solution.py:35
  11.4 5.8 %collective-permute-start.4 = (bf16[16,6144]{1,0:T(8,128)(2,1)S(1)}, bf16[16,6144]{1,0:T(8,128)(2,1)S(1)}, u32[]{:S(2)}, u32[]{:S(2)}) collective-permute-start(bf16[16,6144]{1,0:T(8,128)(2,1)S(1)} %get-tuple-element.109), channel_id=1, source_target_pairs={{0,16},{1,49},{2,18},{3,51},{4,20},{5,53},{6,22},{7,55},{8,24},{9,... | collective-permute-start | bytes 589832 | tf_op jit(solution)/shard_map/ppermute | solution.py:85
  13.7 7.7 %collective-permute-start.2 = (bf16[16,6144]{1,0:T(8,128)(2,1)S(1)}, bf16[16,6144]{1,0:T(8,128)(2,1)S(1)}, u32[]{:S(2)}, u32[]{:S(2)}) collective-permute-start(bf16[16,6144]{1,0:T(8,128)(2,1)S(1)} %get-tuple-element.110), channel_id=1, source_target_pairs={{0,2},{1,7},{2,0},{3,5},{4,6},{5,3},{6,4},{7,1},{8,10},{9,15},{10,... | collective-permute-start | bytes 589832 | tf_op jit(solution)/shard_map/ppermute | solution.py:84
  17.2 10.4 %collective-permute-start.5 = (bf16[32,6144]{1,0:T(8,128)(2,1)S(1)}, bf16[32,6144]{1,0:T(8,128)(2,1)S(1)}, u32[]{:S(2)}, u32[]{:S(2)}) collective-permute-start(bf16[32,6144]{1,0:T(8,128)(2,1)S(1)} %pad_maximum_fusion.6), channel_id=1, source_target_pairs={{0,48},{1,17},{2,50},{3,19},{4,52},{5,21},{6,54},{7,23},{8,56},{9,... | collective-permute-start | bytes 1179656 | tf_op jit(solution)/shard_map/ppermute | solution.py:85
  21.4 9.1 %collective-permute-start.3 = (bf16[32,6144]{1,0:T(8,128)(2,1)S(1)}, bf16[32,6144]{1,0:T(8,128)(2,1)S(1)}, u32[]{:S(2)}, u32[]{:S(2)}) collective-permute-start(bf16[32,6144]{1,0:T(8,128)(2,1)S(1)} %pad_maximum_fusion.5), channel_id=1, source_target_pairs={{0,6},{1,3},{2,4},{3,1},{4,2},{5,7},{6,0},{7,5},{8,14},{9,11},{10,... | collective-permute-start | bytes 1179656 | tf_op jit(solution)/shard_map/ppermute | solution.py:84
  24.5 35.7 %collective-permute-start.17 = (bf16[128,6144]{1,0:T(8,128)(2,1)S(1)}, bf16[128,6144]{1,0:T(8,128)(2,1)S(1)}, u32[]{:S(2)}, u32[]{:S(2)}) collective-permute-start(bf16[128,6144]{1,0:T(8,128)(2,1)S(1)} %get-tuple-element.63), channel_id=1, source_target_pairs={{0,8},{1,9},{2,10},{3,11},{4,12},{5,13},{6,14},{7,15},{8,0},{9,1},... | collective-permute-start | bytes 4718600 | tf_op jit(solution)/shard_map/ppermute | solution.py:35
  30.6 19.8 %collective-permute-start.7 = (bf16[64,6144]{1,0:T(8,128)(2,1)S(1)}, bf16[64,6144]{1,0:T(8,128)(2,1)S(1)}, u32[]{:S(2)}, u32[]{:S(2)}) collective-permute-start(bf16[64,6144]{1,0:T(8,128)(2,1)S(1)} %pad_maximum_fusion.2), channel_id=1, source_target_pairs={{0,16},{1,49},{2,18},{3,51},{4,20},{5,53},{6,22},{7,55},{8,24},{9,... | collective-permute-start | bytes 2359304 | tf_op jit(solution)/shard_map/ppermute | solution.py:84
  30.7 19.0 %collective-permute-start.10 = (bf16[64,6144]{1,0:T(8,128)(2,1)S(1)}, bf16[64,6144]{1,0:T(8,128)(2,1)S(1)}, u32[]{:S(2)}, u32[]{:S(2)}) collective-permute-start(bf16[64,6144]{1,0:T(8,128)(2,1)S(1)} %pad_maximum_fusion.3), channel_id=1, source_target_pairs={{0,6},{1,3},{2,4},{3,1},{4,2},{5,7},{6,0},{7,5},{8,14},{9,11},{10,... | collective-permute-start | bytes 2359304 | tf_op jit(solution)/shard_map/ppermute | solution.py:85
  33.8 16.6 %collective-permute-start.8 = (bf16[64,6144]{1,0:T(8,128)(2,1)S(1)}, bf16[64,6144]{1,0:T(8,128)(2,1)S(1)}, u32[]{:S(2)}, u32[]{:S(2)}) collective-permute-start(bf16[64,6144]{1,0:T(8,128)(2,1)S(1)} %pad_maximum_fusion.3), channel_id=1, source_target_pairs={{0,2},{1,7},{2,0},{3,5},{4,6},{5,3},{6,4},{7,1},{8,10},{9,15},{10,... | collective-permute-start | bytes 2359304 | tf_op jit(solution)/shard_map/ppermute | solution.py:85
  33.8 16.6 %collective-permute-start.9 = (bf16[64,6144]{1,0:T(8,128)(2,1)S(1)}, bf16[64,6144]{1,0:T(8,128)(2,1)S(1)}, u32[]{:S(2)}, u32[]{:S(2)}) collective-permute-start(bf16[64,6144]{1,0:T(8,128)(2,1)S(1)} %pad_maximum_fusion.2), channel_id=1, source_target_pairs={{0,48},{1,17},{2,50},{3,19},{4,52},{5,21},{6,54},{7,23},{8,56},{9,... | collective-permute-start | bytes 2359304 | tf_op jit(solution)/shard_map/ppermute | solution.py:84
  50.5 13.3 %collective-permute-start.11 = (bf16[64,6144]{1,0:T(8,128)(2,1)S(1)}, bf16[64,6144]{1,0:T(8,128)(2,1)S(1)}, u32[]{:S(2)}, u32[]{:S(2)}) collective-permute-start(bf16[64,6144]{1,0:T(8,128)(2,1)S(1)} %collective-permute-done.7), channel_id=1, source_target_pairs={{0,48},{1,17},{2,50},{3,19},{4,52},{5,21},{6,54},{7,23},{8,56},{9,... | collective-permute-start | bytes 2359304 | tf_op jit(solution)/shard_map/ppermute | solution.py:84
  52.0 13.3 %collective-permute-start.12 = (bf16[64,6144]{1,0:T(8,128)(2,1)S(1)}, bf16[64,6144]{1,0:T(8,128)(2,1)S(1)}, u32[]{:S(2)}, u32[]{:S(2)}) collective-permute-start(bf16[64,6144]{1,0:T(8,128)(2,1)S(1)} %collective-permute-done.8), channel_id=1, source_target_pairs={{0,6},{1,3},{2,4},{3,1},{4,2},{5,7},{6,0},{7,5},{8,14},{9,11},{10,... | collective-permute-start | bytes 2359304 | tf_op jit(solution)/shard_map/ppermute | solution.py:85
  60.6 12.4 %collective-permute-start.18 = (bf16[256,6144]{1,0:T(8,128)(2,1)S(1)}, bf16[256,6144]{1,0:T(8,128)(2,1)S(1)}, u32[]{:S(2)}, u32[]{:S(2)}) collective-permute-start(bf16[256,6144]{1,0:T(8,128)(2,1)S(1)} %pad_maximum_fusion.1), channel_id=1, source_target_pairs={{0,1},{1,0},{2,3},{3,2},{4,5},{5,4},{6,7},{7,6},{8,9},{9,8},{10,11... | collective-permute-start | bytes 9437192 | tf_op jit(solution)/shard_map/ppermute | solution.py:35
  69.9 7.1 %collective-permute-start.19 = (bf16[512,128]{1,0:T(8,128)(2,1)S(1)}, bf16[512,128]{1,0:T(8,128)(2,1)S(1)}, u32[]{:S(2)}, u32[]{:S(2)}) collective-permute-start(bf16[512,128]{1,0:T(8,128)(2,1)S(1)} %convolution_convert_fusion.1), channel_id=1, source_target_pairs={{0,8},{1,9},{2,10},{3,11},{4,12},{5,13},{6,14},{7,15},{8,0},{9,1},... | collective-permute-start | bytes 393224 | tf_op jit(solution)/shard_map/ppermute | solution.py:35
  79.6 13.3 %collective-permute-start.21 = (bf16[64,6144]{1,0:T(8,128)(2,1)S(1)}, bf16[64,6144]{1,0:T(8,128)(2,1)S(1)}, u32[]{:S(2)}, u32[]{:S(2)}) collective-permute-start(bf16[64,6144]{1,0:T(8,128)(2,1)S(1)} %get-tuple-element.67), channel_id=1, source_target_pairs={{0,48},{1,17},{2,50},{3,19},{4,52},{5,21},{6,54},{7,23},{8,56},{9,... | collective-permute-start | bytes 2359304 | tf_op jit(solution)/shard_map/ppermute | solution.py:84
  81.6 13.2 %collective-permute-start.22 = (bf16[64,6144]{1,0:T(8,128)(2,1)S(1)}, bf16[64,6144]{1,0:T(8,128)(2,1)S(1)}, u32[]{:S(2)}, u32[]{:S(2)}) collective-permute-start(bf16[64,6144]{1,0:T(8,128)(2,1)S(1)} %get-tuple-element.68), channel_id=1, source_target_pairs={{0,6},{1,3},{2,4},{3,1},{4,2},{5,7},{6,0},{7,5},{8,14},{9,11},{10,... | collective-permute-start | bytes 2359304 | tf_op jit(solution)/shard_map/ppermute | solution.py:85
  95.2 7.9 %collective-permute-start.23 = (bf16[32,6144]{1,0:T(8,128)(2,1)S(1)}, bf16[32,6144]{1,0:T(8,128)(2,1)S(1)}, u32[]{:S(2)}, u32[]{:S(2)}) collective-permute-start(bf16[32,6144]{1,0:T(8,128)(2,1)S(1)} %slice.311), channel_id=1, source_target_pairs={{0,16},{1,49},{2,18},{3,51},{4,20},{5,53},{6,22},{7,55},{8,24},{9,... | collective-permute-start | bytes 1179656 | tf_op jit(solution)/shard_map/ppermute | solution.py:84
  95.3 7.9 %collective-permute-start.24 = (bf16[32,6144]{1,0:T(8,128)(2,1)S(1)}, bf16[32,6144]{1,0:T(8,128)(2,1)S(1)}, u32[]{:S(2)}, u32[]{:S(2)}) collective-permute-start(bf16[32,6144]{1,0:T(8,128)(2,1)S(1)} %slice.310), channel_id=1, source_target_pairs={{0,2},{1,7},{2,0},{3,5},{4,6},{5,3},{6,4},{7,1},{8,10},{9,15},{10,... | collective-permute-start | bytes 1179656 | tf_op jit(solution)/shard_map/ppermute | solution.py:85
  103.5 7.3 %collective-permute-start.25 = (bf16[16,6144]{1,0:T(8,128)(2,1)S(1)}, bf16[16,6144]{1,0:T(8,128)(2,1)S(1)}, u32[]{:S(2)}, u32[]{:S(2)}) collective-permute-start(bf16[16,6144]{1,0:T(8,128)(2,1)S(1)} %pad_maximum_fusion.8), channel_id=1, source_target_pairs={{0,6},{1,3},{2,4},{3,1},{4,2},{5,7},{6,0},{7,5},{8,14},{9,11},{10,... | collective-permute-start | bytes 589832 | tf_op jit(solution)/shard_map/ppermute | solution.py:84
  105.1 7.3 %collective-permute-start.26 = (bf16[16,6144]{1,0:T(8,128)(2,1)S(1)}, bf16[16,6144]{1,0:T(8,128)(2,1)S(1)}, u32[]{:S(2)}, u32[]{:S(2)}) collective-permute-start(bf16[16,6144]{1,0:T(8,128)(2,1)S(1)} %pad_maximum_fusion.9), channel_id=1, source_target_pairs={{0,48},{1,17},{2,50},{3,19},{4,52},{5,21},{6,54},{7,23},{8,56},{9,... | collective-permute-start | bytes 589832 | tf_op jit(solution)/shard_map/ppermute | solution.py:85
  112.5 4.7 %collective-permute-start.27 = (bf16[8,6144]{1,0:T(8,128)(2,1)S(1)}, bf16[8,6144]{1,0:T(8,128)(2,1)S(1)}, u32[]{:S(2)}, u32[]{:S(2)}) collective-permute-start(bf16[8,6144]{1,0:T(8,128)(2,1)S(1)} %slice.313), channel_id=1, source_target_pairs={{0,2},{1,7},{2,0},{3,5},{4,6},{5,3},{6,4},{7,1},{8,10},{9,15},{10,... | collective-permute-start | bytes 294920 | tf_op jit(solution)/shard_map/ppermute | solution.py:84
  112.6 4.7 %collective-permute-start.28 = (bf16[8,6144]{1,0:T(8,128)(2,1)S(1)}, bf16[8,6144]{1,0:T(8,128)(2,1)S(1)}, u32[]{:S(2)}, u32[]{:S(2)}) collective-permute-start(bf16[8,6144]{1,0:T(8,128)(2,1)S(1)} %slice.312), channel_id=1, source_target_pairs={{0,16},{1,49},{2,18},{3,51},{4,20},{5,53},{6,22},{7,55},{8,24},{9,... | collective-permute-start | bytes 294920 | tf_op jit(solution)/shard_map/ppermute | solution.py:85
  118.9 5.8 %collective-permute-start.30 = (bf16[8,6144]{1,0:T(8,128)(2,1)S(1)}, bf16[8,6144]{1,0:T(8,128)(2,1)S(1)}, u32[]{:S(2)}, u32[]{:S(2)}) collective-permute-start(bf16[8,6144]{1,0:T(8,128)(2,1)S(1)} %get-tuple-element.90), channel_id=1, source_target_pairs={{0,72},{1,73},{2,74},{3,75},{4,76},{5,77},{6,78},{7,79},{8,64},{9,... | collective-permute-start | bytes 294920 | tf_op jit(solution)/shard_map/ppermute | solution.py:35
  (11 other events, 101.4 us)

commit v11 on v10

--- a/solution.py
+++ b/solution.py
@@ -98,16 +98,24 @@
     )
 
 
-def swap_sums(fars, nears, axes):
-    size = nears[0].shape[0] // 2
+def halve_sums(fars, nears, axes, turn):
     fars = lax.optimization_barrier([far.astype(jnp.bfloat16) for far in fars])
-    got = lax.optimization_barrier(swap_both(fars[0], axes[0], fars[1], axes[1], 1))
-    totals = [near + part.astype(jnp.float32) for near, part in zip(nears, got)]
-    sent = lax.optimization_barrier(
-        [total[size:].astype(jnp.bfloat16) for total in totals]
-    )
-    got = lax.optimization_barrier(swap_both(sent[0], axes[0], sent[1], axes[1], 0))
-    return [total[:size] + part.astype(jnp.float32) for total, part in zip(totals, got)]
+    got = lax.optimization_barrier(swap_both(fars[0], axes[0], fars[1], axes[1], turn))
+    return [near + part.astype(jnp.float32) for near, part in zip(nears, got)]
+
+
+def owner_pairs(crossed, near):
+    pairs = []
+    for source in range(128):
+        pipe, z, half_x, y, core = split_place(source)
+        half_x ^= crossed
+        flip = (1, 3)[core] if near else 0
+        if half_x:
+            z ^= flip
+        else:
+            y ^= flip
+        pairs.append((source, join_place(1 - pipe, z, half_x, y, core)))
+    return pairs
 
 
 def token_positions(z, y):
@@ -240,19 +248,32 @@
     edges = out_rows_of(first_sent + second_sent).astype(jnp.bfloat16)
     rests = lax.optimization_barrier(out_rows_of(first_kept + second_kept))
     size = edges.shape[0] // 2
-    totals = swap_sums(
-        (edges[:size], edges[size:]), (rests[:size], rests[size:]), ("z", "y")
+    totals = halve_sums(
+        (edges[:size], edges[size:]), (rests[:size], rests[size:]), ("z", "y"), 1
+    )
+    middle = size // 2
+    totals = halve_sums(
+        [total[middle:] for total in totals], [total[:middle] for total in totals], ("z", "y"), 0
     )
     chunks = [turns(total.reshape(4, -1, half)) for total in totals]
-    first_rows, second_rows = swap_sums(
+    totals = halve_sums(
         [jnp.concatenate(sent) for sent, _ in chunks],
         [jnp.concatenate(kept) for _, kept in chunks],
         ("y", "z"),
-    )
-    first_rows = first_rows.astype(jnp.bfloat16)
-    second_rows = second_rows.astype(jnp.bfloat16)
-    straight = send(jnp.where(half_x == 0, first_rows, second_rows), pipe=1)
-    crossed = send(jnp.where(half_x == 0, second_rows, first_rows), pipe=1, x=1)
+        1,
+    )
+    first, second = lax.optimization_barrier(
+        [total.astype(jnp.bfloat16).reshape(2, -1, half) for total in totals]
+    )
+    pairs_of = jnp.where(half_x == 0, first, second), jnp.where(half_x == 0, second, first)
+    halves = []
+    for crossed, rows in enumerate(pairs_of):
+        own, near = (
+            lax.ppermute(rows[k], AXES, owner_pairs(crossed, k)).astype(jnp.float32)
+            for k in (0, 1)
+        )
+        halves.append((own + near).astype(jnp.bfloat16))
+    straight, crossed = halves
     return jnp.where(
         half_x == 0,
         jnp.concatenate([straight, crossed], axis=1),

time: 126 us -> 126 us (level)
  starting transfers between devices: 44.9 us -> 46.7 us
  waiting for transfers between devices: 59 us -> 57.5 us
    ppermute x0 -> x4, starting transfers between devices: none -> 6.98 us  [shards(): lax.ppermute(rows[k], AXES, owner_pairs(crossed, k)).astype(jnp.float32)]
    ppermute x0 -> x4, waiting for transfers between devices: none -> 5.93 us  [shards(): lax.ppermute(rows[k], AXES, owner_pairs(crossed, k)).astype(jnp.float32)]
    ppermute x13 -> x11, waiting for transfers between devices: 11.7 us -> 8.01 us  [send(): return lax.ppermute(value, AXES, pairs)]
    ppermute x13 -> x11, starting transfers between devices: 14.8 us -> 11.1 us  [send(): return lax.ppermute(value, AXES, pairs)]
    ppermute x9 -> x8, waiting for transfers between devices: 28.8 us -> 25.3 us  [swap_both(): lax.ppermute(first, AXES, swap_pairs(first_axis, turn))]
    ppermute x9 -> x8, starting transfers between devices: 18 us -> 16.6 us  [swap_both(): lax.ppermute(second, AXES, swap_pairs(second_axis, turn))]
    ppermute x9 -> x8, waiting for transfers between devices: 18.5 us -> 18.3 us  [swap_both(): lax.ppermute(second, AXES, swap_pairs(second_axis, turn))]
    ppermute x9 -> x8, starting transfers between devices: 12.1 us -> 12 us  [swap_both(): lax.ppermute(first, AXES, swap_pairs(first_axis, turn))]
  transfers between devices with their start and end apart: 31 -> 31, of which waited for: 21 -> 20; matrix products, arithmetic and copies ran while one was open for 13% -> 13% of each run, Pallas kernels for 0% -> 0%
where the time goes in v11:
time: 126 us
  waiting for transfers between devices  57.5 us (46%)
  starting transfers between devices  46.7 us (37%)
  matrix products  12 us (10%)
  local copies, waits for them, and re-layouts  3.86 us (3%)
  other arithmetic  3.84 us (3%)
  Pallas kernels  1.36 us (1%)
    ppermute x8, waiting for transfers between devices, swap_both(): lax.ppermute(first, AXES, swap_pairs(first_axis, turn))  25.3 us
    ppermute x8, waiting for transfers between devices, swap_both(): lax.ppermute(second, AXES, swap_pairs(second_axis, turn))  18.3 us
    ppermute x8, starting transfers between devices, swap_both(): lax.ppermute(second, AXES, swap_pairs(second_axis, turn))  16.6 us
    ppermute x8, starting transfers between devices, swap_both(): lax.ppermute(first, AXES, swap_pairs(first_axis, turn))  12 us
    ppermute x11, starting transfers between devices, send(): return lax.ppermute(value, AXES, pairs)  11.1 us
    ppermute x11, waiting for transfers between devices, send(): return lax.ppermute(value, AXES, pairs)  8.01 us
    ppermute x4, starting transfers between devices, shards(): lax.ppermute(rows[k], AXES, owner_pairs(crossed, k)).astype(jnp.float32)  6.98 us
    ppermute x4, waiting for transfers between devices, shards(): lax.ppermute(rows[k], AXES, owner_pairs(crossed, k)).astype(jnp.float32)  5.93 us
  transfers between devices with their start and end apart: 31, of which 20 were waited for; matrix products, arithmetic and copies ran while one was open for 13% of the time, Pallas kernels for 0%

profile of v11, /device:TPU:0, one launch (start us, length us, event | category | flops | bytes accessed | tf_op | source)
XLA Modules:
  0.0 125.8 jit_solution(17925899381684901313)
XLA Ops:
  2.8 3.2 %collective-permute-start.1 = (bf16[16,6144]{1,0:T(8,128)(2,1)S(1)}, bf16[16,6144]{1,0:T(8,128)(2,1)S(1)}, u32[]{:S(2)}, u32[]{:S(2)}) collective-permute-start(bf16[16,6144]{1,0:T(8,128)(2,1)S(1)} %maximum_select_fusion), channel_id=1, source_target_pairs={{0,8},{1,9},{2,10},{3,11},{4,12},{5,13},{6,14},{7,15},{8,0},{9,1},... | collective-permute-start | bytes 589832 | tf_op jit(solution)/shard_map/ppermute | solution.py:35
  6.0 3.0 %constant_dynamic-slice_fusion.2 = bf16[6144,384]{1,0:T(8,128)(2,1)S(1)} fusion(bf16[12288,384]{1,0:T(8,128)(2,1)} %bitcast.85, s32[]{:T(128)S(6)} %select_n.234), kind=kLoop, calls=%fused_computation.115 | loop fusion | bytes 9437188 | tf_op jit(solution)/shard_map/dynamic_slice | solution.py:163
  9.0 2.3 %collective-permute-done.1 = bf16[16,6144]{1,0:T(8,128)(2,1)S(1)} collective-permute-done((bf16[16,6144]{1,0:T(8,128)(2,1)S(1)}, bf16[16,6144]{1,0:T(8,128)(2,1)S(1)}, u32[]{:S(2)}, u32[]{:S(2)}) %collective-permute-start.1) | collective-permute-done | bytes 196640 | tf_op jit(solution)/shard_map/ppermute | solution.py:35
  11.4 2.1 %collective-permute-start.4 = (bf16[16,6144]{1,0:T(8,128)(2,1)S(1)}, bf16[16,6144]{1,0:T(8,128)(2,1)S(1)}, u32[]{:S(2)}, u32[]{:S(2)}) collective-permute-start(bf16[16,6144]{1,0:T(8,128)(2,1)S(1)} %get-tuple-element.105), channel_id=1, source_target_pairs={{0,16},{1,49},{2,18},{3,51},{4,20},{5,53},{6,22},{7,55},{8,24},{9,... | collective-permute-start | bytes 589832 | tf_op jit(solution)/shard_map/ppermute | solution.py:85
  15.4 1.8 %collective-permute-done.4 = bf16[16,6144]{1,0:T(8,128)(2,1)S(1)} collective-permute-done((bf16[16,6144]{1,0:T(8,128)(2,1)S(1)}, bf16[16,6144]{1,0:T(8,128)(2,1)S(1)}, u32[]{:S(2)}, u32[]{:S(2)}) %collective-permute-start.4) | collective-permute-done | bytes 196640 | tf_op jit(solution)/shard_map/ppermute | solution.py:85
  17.2 4.2 %collective-permute-start.5 = (bf16[32,6144]{1,0:T(8,128)(2,1)S(1)}, bf16[32,6144]{1,0:T(8,128)(2,1)S(1)}, u32[]{:S(2)}, u32[]{:S(2)}) collective-permute-start(bf16[32,6144]{1,0:T(8,128)(2,1)S(1)} %pad_maximum_fusion.6), channel_id=1, source_target_pairs={{0,48},{1,17},{2,50},{3,19},{4,52},{5,21},{6,54},{7,23},{8,56},{9,... | collective-permute-start | bytes 1179656 | tf_op jit(solution)/shard_map/ppermute | solution.py:85
  21.4 3.1 %collective-permute-start.3 = (bf16[32,6144]{1,0:T(8,128)(2,1)S(1)}, bf16[32,6144]{1,0:T(8,128)(2,1)S(1)}, u32[]{:S(2)}, u32[]{:S(2)}) collective-permute-start(bf16[32,6144]{1,0:T(8,128)(2,1)S(1)} %pad_maximum_fusion.5), channel_id=1, source_target_pairs={{0,6},{1,3},{2,4},{3,1},{4,2},{5,7},{6,0},{7,5},{8,14},{9,11},{10,... | collective-permute-start | bytes 1179656 | tf_op jit(solution)/shard_map/ppermute | solution.py:84
  24.5 3.0 %collective-permute-start.17 = (bf16[128,6144]{1,0:T(8,128)(2,1)S(1)}, bf16[128,6144]{1,0:T(8,128)(2,1)S(1)}, u32[]{:S(2)}, u32[]{:S(2)}) collective-permute-start(bf16[128,6144]{1,0:T(8,128)(2,1)S(1)} %get-tuple-element.61), channel_id=1, source_target_pairs={{0,8},{1,9},{2,10},{3,11},{4,12},{5,13},{6,14},{7,15},{8,0},{9,1},... | collective-permute-start | bytes 4718600 | tf_op jit(solution)/shard_map/ppermute | solution.py:35
  27.6 2.8 %collective-permute-done.3 = bf16[32,6144]{1,0:T(8,128)(2,1)S(1)} collective-permute-done((bf16[32,6144]{1,0:T(8,128)(2,1)S(1)}, bf16[32,6144]{1,0:T(8,128)(2,1)S(1)}, u32[]{:S(2)}, u32[]{:S(2)}) %collective-permute-start.3) | collective-permute-done | bytes 393248 | tf_op jit(solution)/shard_map/ppermute | solution.py:84
  30.7 3.1 %collective-permute-start.10 = (bf16[64,6144]{1,0:T(8,128)(2,1)S(1)}, bf16[64,6144]{1,0:T(8,128)(2,1)S(1)}, u32[]{:S(2)}, u32[]{:S(2)}) collective-permute-start(bf16[64,6144]{1,0:T(8,128)(2,1)S(1)} %pad_maximum_fusion.3), channel_id=1, source_target_pairs={{0,6},{1,3},{2,4},{3,1},{4,2},{5,7},{6,0},{7,5},{8,14},{9,11},{10,... | collective-permute-start | bytes 2359304 | tf_op jit(solution)/shard_map/ppermute | solution.py:85
  33.8 2.1 %collective-permute-start.9 = (bf16[64,6144]{1,0:T(8,128)(2,1)S(1)}, bf16[64,6144]{1,0:T(8,128)(2,1)S(1)}, u32[]{:S(2)}, u32[]{:S(2)}) collective-permute-start(bf16[64,6144]{1,0:T(8,128)(2,1)S(1)} %pad_maximum_fusion.2), channel_id=1, source_target_pairs={{0,48},{1,17},{2,50},{3,19},{4,52},{5,21},{6,54},{7,23},{8,56},{9,... | collective-permute-start | bytes 2359304 | tf_op jit(solution)/shard_map/ppermute | solution.py:84
  38.2 11.5 %collective-permute-done.10 = bf16[64,6144]{1,0:T(8,128)(2,1)S(1)} collective-permute-done((bf16[64,6144]{1,0:T(8,128)(2,1)S(1)}, bf16[64,6144]{1,0:T(8,128)(2,1)S(1)}, u32[]{:S(2)}, u32[]{:S(2)}) %collective-permute-start.10) | collective-permute-done | bytes 786464 | tf_op jit(solution)/shard_map/ppermute | solution.py:85
  52.0 2.9 %collective-permute-start.12 = (bf16[64,6144]{1,0:T(8,128)(2,1)S(1)}, bf16[64,6144]{1,0:T(8,128)(2,1)S(1)}, u32[]{:S(2)}, u32[]{:S(2)}) collective-permute-start(bf16[64,6144]{1,0:T(8,128)(2,1)S(1)} %collective-permute-done.8), channel_id=1, source_target_pairs={{0,6},{1,3},{2,4},{3,1},{4,2},{5,7},{6,0},{7,5},{8,14},{9,11},{10,... | collective-permute-start | bytes 2359304 | tf_op jit(solution)/shard_map/ppermute | solution.py:85
  61.1 2.7 %collective-permute-done.11 = bf16[64,6144]{1,0:T(8,128)(2,1)S(1)} collective-permute-done((bf16[64,6144]{1,0:T(8,128)(2,1)S(1)}, bf16[64,6144]{1,0:T(8,128)(2,1)S(1)}, u32[]{:S(2)}, u32[]{:S(2)}) %collective-permute-start.11) | collective-permute-done | bytes 786464 | tf_op jit(solution)/shard_map/ppermute | solution.py:84
  69.9 3.1 %collective-permute-start.19 = (bf16[512,128]{1,0:T(8,128)(2,1)S(1)}, bf16[512,128]{1,0:T(8,128)(2,1)S(1)}, u32[]{:S(2)}, u32[]{:S(2)}) collective-permute-start(bf16[512,128]{1,0:T(8,128)(2,1)S(1)} %convolution_convert_fusion.1), channel_id=1, source_target_pairs={{0,8},{1,9},{2,10},{3,11},{4,12},{5,13},{6,14},{7,15},{8,0},{9,1},... | collective-permute-start | bytes 393224 | tf_op jit(solution)/shard_map/ppermute | solution.py:35
  73.5 3.5 %collective-permute-done.19 = bf16[512,128]{1,0:T(8,128)(2,1)S(1)} collective-permute-done((bf16[512,128]{1,0:T(8,128)(2,1)S(1)}, bf16[512,128]{1,0:T(8,128)(2,1)S(1)}, u32[]{:S(2)}, u32[]{:S(2)}) %collective-permute-start.19) | collective-permute-done | bytes 131104 | tf_op jit(solution)/shard_map/ppermute | solution.py:35
  79.6 2.0 %collective-permute-start.21 = (bf16[64,6144]{1,0:T(8,128)(2,1)S(1)}, bf16[64,6144]{1,0:T(8,128)(2,1)S(1)}, u32[]{:S(2)}, u32[]{:S(2)}) collective-permute-start(bf16[64,6144]{1,0:T(8,128)(2,1)S(1)} %get-tuple-element.65), channel_id=1, source_target_pairs={{0,48},{1,17},{2,50},{3,19},{4,52},{5,21},{6,54},{7,23},{8,56},{9,... | collective-permute-start | bytes 2359304 | tf_op jit(solution)/shard_map/ppermute | solution.py:84
  84.1 8.8 %collective-permute-done.21 = bf16[64,6144]{1,0:T(8,128)(2,1)S(1)} collective-permute-done((bf16[64,6144]{1,0:T(8,128)(2,1)S(1)}, bf16[64,6144]{1,0:T(8,128)(2,1)S(1)}, u32[]{:S(2)}, u32[]{:S(2)}) %collective-permute-start.21) | collective-permute-done | bytes 786464 | tf_op jit(solution)/shard_map/ppermute | solution.py:84
  92.9 1.9 %collective-permute-done.22 = bf16[64,6144]{1,0:T(8,128)(2,1)S(1)} collective-permute-done((bf16[64,6144]{1,0:T(8,128)(2,1)S(1)}, bf16[64,6144]{1,0:T(8,128)(2,1)S(1)}, u32[]{:S(2)}, u32[]{:S(2)}) %collective-permute-start.22) | collective-permute-done | bytes 786464 | tf_op jit(solution)/shard_map/ppermute | solution.py:85
  95.4 7.7 %collective-permute-done.23 = bf16[32,6144]{1,0:T(8,128)(2,1)S(1)} collective-permute-done((bf16[32,6144]{1,0:T(8,128)(2,1)S(1)}, bf16[32,6144]{1,0:T(8,128)(2,1)S(1)}, u32[]{:S(2)}, u32[]{:S(2)}) %collective-permute-start.23) | collective-permute-done | bytes 393248 | tf_op jit(solution)/shard_map/ppermute | solution.py:84
  105.1 2.7 %collective-permute-start.26 = (bf16[16,6144]{1,0:T(8,128)(2,1)S(1)}, bf16[16,6144]{1,0:T(8,128)(2,1)S(1)}, u32[]{:S(2)}, u32[]{:S(2)}) collective-permute-start(bf16[16,6144]{1,0:T(8,128)(2,1)S(1)} %pad_maximum_fusion.9), channel_id=1, source_target_pairs={{0,48},{1,17},{2,50},{3,19},{4,52},{5,21},{6,54},{7,23},{8,56},{9,... | collective-permute-start | bytes 589832 | tf_op jit(solution)/shard_map/ppermute | solution.py:85
  107.8 2.6 %collective-permute-done.25 = bf16[16,6144]{1,0:T(8,128)(2,1)S(1)} collective-permute-done((bf16[16,6144]{1,0:T(8,128)(2,1)S(1)}, bf16[16,6144]{1,0:T(8,128)(2,1)S(1)}, u32[]{:S(2)}, u32[]{:S(2)}) %collective-permute-start.25) | collective-permute-done | bytes 196640 | tf_op jit(solution)/shard_map/ppermute | solution.py:84
  113.7 4.6 %collective-permute-start.29 = (bf16[8,6144]{1,0:T(8,128)(2,1)S(1)}, bf16[8,6144]{1,0:T(8,128)(2,1)S(1)}, u32[]{:S(2)}, u32[]{:S(2)}) collective-permute-start(bf16[8,6144]{1,0:T(8,128)(2,1)S(1)} %get-tuple-element.117), channel_id=1, source_target_pairs={{0,72},{1,73},{2,74},{3,75},{4,76},{5,77},{6,78},{7,79},{8,64},{9,... | collective-permute-start | bytes 294920 | tf_op jit(solution)/shard_map/ppermute | solution.py:272
  120.9 4.1 %collective-permute-done.30 = bf16[8,6144]{1,0:T(8,128)(2,1)S(1)} collective-permute-done((bf16[8,6144]{1,0:T(8,128)(2,1)S(1)}, bf16[8,6144]{1,0:T(8,128)(2,1)S(1)}, u32[]{:S(2)}, u32[]{:S(2)}) %collective-permute-start.30) | collective-permute-done | bytes 98336 | tf_op jit(solution)/shard_map/ppermute | solution.py:272
  (109 shorter events, 36.4 us)
Async XLA Ops:
  2.8 8.5 %collective-permute-start.1 = (bf16[16,6144]{1,0:T(8,128)(2,1)S(1)}, bf16[16,6144]{1,0:T(8,128)(2,1)S(1)}, u32[]{:S(2)}, u32[]{:S(2)}) collective-permute-start(bf16[16,6144]{1,0:T(8,128)(2,1)S(1)} %maximum_select_fusion), channel_id=1, source_target_pairs={{0,8},{1,9},{2,10},{3,11},{4,12},{5,13},{6,14},{7,15},{8,0},{9,1},... | collective-permute-start | bytes 589832 | tf_op jit(solution)/shard_map/ppermute | solution.py:35
  8.9 21.6 %collective-permute-start.6 = (bf16[6144,384]{1,0:T(8,128)(2,1)S(1)}, bf16[6144,384]{1,0:T(8,128)(2,1)S(1)}, u32[]{:S(2)}, u32[]{:S(2)}) collective-permute-start(bf16[6144,384]{1,0:T(8,128)(2,1)S(1)} %constant_dynamic-slice_fusion.2), channel_id=1, source_target_pairs={{0,1},{1,0},{2,3},{3,2},{4,5},{5,4},{6,7},{7,6},{8,9},{9,8},{10,11... | collective-permute-start | bytes 14155784 | tf_op jit(solution)/shard_map/ppermute | solution.py:35
  11.4 5.8 %collective-permute-start.4 = (bf16[16,6144]{1,0:T(8,128)(2,1)S(1)}, bf16[16,6144]{1,0:T(8,128)(2,1)S(1)}, u32[]{:S(2)}, u32[]{:S(2)}) collective-permute-start(bf16[16,6144]{1,0:T(8,128)(2,1)S(1)} %get-tuple-element.105), channel_id=1, source_target_pairs={{0,16},{1,49},{2,18},{3,51},{4,20},{5,53},{6,22},{7,55},{8,24},{9,... | collective-permute-start | bytes 589832 | tf_op jit(solution)/shard_map/ppermute | solution.py:85
  13.7 7.7 %collective-permute-start.2 = (bf16[16,6144]{1,0:T(8,128)(2,1)S(1)}, bf16[16,6144]{1,0:T(8,128)(2,1)S(1)}, u32[]{:S(2)}, u32[]{:S(2)}) collective-permute-start(bf16[16,6144]{1,0:T(8,128)(2,1)S(1)} %get-tuple-element.106), channel_id=1, source_target_pairs={{0,2},{1,7},{2,0},{3,5},{4,6},{5,3},{6,4},{7,1},{8,10},{9,15},{10,... | collective-permute-start | bytes 589832 | tf_op jit(solution)/shard_map/ppermute | solution.py:84
  17.2 10.4 %collective-permute-start.5 = (bf16[32,6144]{1,0:T(8,128)(2,1)S(1)}, bf16[32,6144]{1,0:T(8,128)(2,1)S(1)}, u32[]{:S(2)}, u32[]{:S(2)}) collective-permute-start(bf16[32,6144]{1,0:T(8,128)(2,1)S(1)} %pad_maximum_fusion.6), channel_id=1, source_target_pairs={{0,48},{1,17},{2,50},{3,19},{4,52},{5,21},{6,54},{7,23},{8,56},{9,... | collective-permute-start | bytes 1179656 | tf_op jit(solution)/shard_map/ppermute | solution.py:85
  21.4 9.1 %collective-permute-start.3 = (bf16[32,6144]{1,0:T(8,128)(2,1)S(1)}, bf16[32,6144]{1,0:T(8,128)(2,1)S(1)}, u32[]{:S(2)}, u32[]{:S(2)}) collective-permute-start(bf16[32,6144]{1,0:T(8,128)(2,1)S(1)} %pad_maximum_fusion.5), channel_id=1, source_target_pairs={{0,6},{1,3},{2,4},{3,1},{4,2},{5,7},{6,0},{7,5},{8,14},{9,11},{10,... | collective-permute-start | bytes 1179656 | tf_op jit(solution)/shard_map/ppermute | solution.py:84
  24.5 35.7 %collective-permute-start.17 = (bf16[128,6144]{1,0:T(8,128)(2,1)S(1)}, bf16[128,6144]{1,0:T(8,128)(2,1)S(1)}, u32[]{:S(2)}, u32[]{:S(2)}) collective-permute-start(bf16[128,6144]{1,0:T(8,128)(2,1)S(1)} %get-tuple-element.61), channel_id=1, source_target_pairs={{0,8},{1,9},{2,10},{3,11},{4,12},{5,13},{6,14},{7,15},{8,0},{9,1},... | collective-permute-start | bytes 4718600 | tf_op jit(solution)/shard_map/ppermute | solution.py:35
  30.6 19.8 %collective-permute-start.7 = (bf16[64,6144]{1,0:T(8,128)(2,1)S(1)}, bf16[64,6144]{1,0:T(8,128)(2,1)S(1)}, u32[]{:S(2)}, u32[]{:S(2)}) collective-permute-start(bf16[64,6144]{1,0:T(8,128)(2,1)S(1)} %pad_maximum_fusion.2), channel_id=1, source_target_pairs={{0,16},{1,49},{2,18},{3,51},{4,20},{5,53},{6,22},{7,55},{8,24},{9,... | collective-permute-start | bytes 2359304 | tf_op jit(solution)/shard_map/ppermute | solution.py:84
  30.7 19.0 %collective-permute-start.10 = (bf16[64,6144]{1,0:T(8,128)(2,1)S(1)}, bf16[64,6144]{1,0:T(8,128)(2,1)S(1)}, u32[]{:S(2)}, u32[]{:S(2)}) collective-permute-start(bf16[64,6144]{1,0:T(8,128)(2,1)S(1)} %pad_maximum_fusion.3), channel_id=1, source_target_pairs={{0,6},{1,3},{2,4},{3,1},{4,2},{5,7},{6,0},{7,5},{8,14},{9,11},{10,... | collective-permute-start | bytes 2359304 | tf_op jit(solution)/shard_map/ppermute | solution.py:85
  33.8 16.6 %collective-permute-start.8 = (bf16[64,6144]{1,0:T(8,128)(2,1)S(1)}, bf16[64,6144]{1,0:T(8,128)(2,1)S(1)}, u32[]{:S(2)}, u32[]{:S(2)}) collective-permute-start(bf16[64,6144]{1,0:T(8,128)(2,1)S(1)} %pad_maximum_fusion.3), channel_id=1, source_target_pairs={{0,2},{1,7},{2,0},{3,5},{4,6},{5,3},{6,4},{7,1},{8,10},{9,15},{10,... | collective-permute-start | bytes 2359304 | tf_op jit(solution)/shard_map/ppermute | solution.py:85
  33.8 16.6 %collective-permute-start.9 = (bf16[64,6144]{1,0:T(8,128)(2,1)S(1)}, bf16[64,6144]{1,0:T(8,128)(2,1)S(1)}, u32[]{:S(2)}, u32[]{:S(2)}) collective-permute-start(bf16[64,6144]{1,0:T(8,128)(2,1)S(1)} %pad_maximum_fusion.2), channel_id=1, source_target_pairs={{0,48},{1,17},{2,50},{3,19},{4,52},{5,21},{6,54},{7,23},{8,56},{9,... | collective-permute-start | bytes 2359304 | tf_op jit(solution)/shard_map/ppermute | solution.py:84
  50.5 13.3 %collective-permute-start.11 = (bf16[64,6144]{1,0:T(8,128)(2,1)S(1)}, bf16[64,6144]{1,0:T(8,128)(2,1)S(1)}, u32[]{:S(2)}, u32[]{:S(2)}) collective-permute-start(bf16[64,6144]{1,0:T(8,128)(2,1)S(1)} %collective-permute-done.7), channel_id=1, source_target_pairs={{0,48},{1,17},{2,50},{3,19},{4,52},{5,21},{6,54},{7,23},{8,56},{9,... | collective-permute-start | bytes 2359304 | tf_op jit(solution)/shard_map/ppermute | solution.py:84
  52.0 13.3 %collective-permute-start.12 = (bf16[64,6144]{1,0:T(8,128)(2,1)S(1)}, bf16[64,6144]{1,0:T(8,128)(2,1)S(1)}, u32[]{:S(2)}, u32[]{:S(2)}) collective-permute-start(bf16[64,6144]{1,0:T(8,128)(2,1)S(1)} %collective-permute-done.8), channel_id=1, source_target_pairs={{0,6},{1,3},{2,4},{3,1},{4,2},{5,7},{6,0},{7,5},{8,14},{9,11},{10,... | collective-permute-start | bytes 2359304 | tf_op jit(solution)/shard_map/ppermute | solution.py:85
  60.6 12.4 %collective-permute-start.18 = (bf16[256,6144]{1,0:T(8,128)(2,1)S(1)}, bf16[256,6144]{1,0:T(8,128)(2,1)S(1)}, u32[]{:S(2)}, u32[]{:S(2)}) collective-permute-start(bf16[256,6144]{1,0:T(8,128)(2,1)S(1)} %pad_maximum_fusion.1), channel_id=1, source_target_pairs={{0,1},{1,0},{2,3},{3,2},{4,5},{5,4},{6,7},{7,6},{8,9},{9,8},{10,11... | collective-permute-start | bytes 9437192 | tf_op jit(solution)/shard_map/ppermute | solution.py:35
  69.9 7.1 %collective-permute-start.19 = (bf16[512,128]{1,0:T(8,128)(2,1)S(1)}, bf16[512,128]{1,0:T(8,128)(2,1)S(1)}, u32[]{:S(2)}, u32[]{:S(2)}) collective-permute-start(bf16[512,128]{1,0:T(8,128)(2,1)S(1)} %convolution_convert_fusion.1), channel_id=1, source_target_pairs={{0,8},{1,9},{2,10},{3,11},{4,12},{5,13},{6,14},{7,15},{8,0},{9,1},... | collective-permute-start | bytes 393224 | tf_op jit(solution)/shard_map/ppermute | solution.py:35
  79.6 13.3 %collective-permute-start.21 = (bf16[64,6144]{1,0:T(8,128)(2,1)S(1)}, bf16[64,6144]{1,0:T(8,128)(2,1)S(1)}, u32[]{:S(2)}, u32[]{:S(2)}) collective-permute-start(bf16[64,6144]{1,0:T(8,128)(2,1)S(1)} %get-tuple-element.65), channel_id=1, source_target_pairs={{0,48},{1,17},{2,50},{3,19},{4,52},{5,21},{6,54},{7,23},{8,56},{9,... | collective-permute-start | bytes 2359304 | tf_op jit(solution)/shard_map/ppermute | solution.py:84
  81.6 13.2 %collective-permute-start.22 = (bf16[64,6144]{1,0:T(8,128)(2,1)S(1)}, bf16[64,6144]{1,0:T(8,128)(2,1)S(1)}, u32[]{:S(2)}, u32[]{:S(2)}) collective-permute-start(bf16[64,6144]{1,0:T(8,128)(2,1)S(1)} %get-tuple-element.66), channel_id=1, source_target_pairs={{0,6},{1,3},{2,4},{3,1},{4,2},{5,7},{6,0},{7,5},{8,14},{9,11},{10,... | collective-permute-start | bytes 2359304 | tf_op jit(solution)/shard_map/ppermute | solution.py:85
  95.2 7.9 %collective-permute-start.23 = (bf16[32,6144]{1,0:T(8,128)(2,1)S(1)}, bf16[32,6144]{1,0:T(8,128)(2,1)S(1)}, u32[]{:S(2)}, u32[]{:S(2)}) collective-permute-start(bf16[32,6144]{1,0:T(8,128)(2,1)S(1)} %slice.297), channel_id=1, source_target_pairs={{0,16},{1,49},{2,18},{3,51},{4,20},{5,53},{6,22},{7,55},{8,24},{9,... | collective-permute-start | bytes 1179656 | tf_op jit(solution)/shard_map/ppermute | solution.py:84
  95.3 7.9 %collective-permute-start.24 = (bf16[32,6144]{1,0:T(8,128)(2,1)S(1)}, bf16[32,6144]{1,0:T(8,128)(2,1)S(1)}, u32[]{:S(2)}, u32[]{:S(2)}) collective-permute-start(bf16[32,6144]{1,0:T(8,128)(2,1)S(1)} %slice.296), channel_id=1, source_target_pairs={{0,2},{1,7},{2,0},{3,5},{4,6},{5,3},{6,4},{7,1},{8,10},{9,15},{10,... | collective-permute-start | bytes 1179656 | tf_op jit(solution)/shard_map/ppermute | solution.py:85
  103.5 7.0 %collective-permute-start.25 = (bf16[16,6144]{1,0:T(8,128)(2,1)S(1)}, bf16[16,6144]{1,0:T(8,128)(2,1)S(1)}, u32[]{:S(2)}, u32[]{:S(2)}) collective-permute-start(bf16[16,6144]{1,0:T(8,128)(2,1)S(1)} %pad_maximum_fusion.8), channel_id=1, source_target_pairs={{0,6},{1,3},{2,4},{3,1},{4,2},{5,7},{6,0},{7,5},{8,14},{9,11},{10,... | collective-permute-start | bytes 589832 | tf_op jit(solution)/shard_map/ppermute | solution.py:84
  105.1 6.9 %collective-permute-start.26 = (bf16[16,6144]{1,0:T(8,128)(2,1)S(1)}, bf16[16,6144]{1,0:T(8,128)(2,1)S(1)}, u32[]{:S(2)}, u32[]{:S(2)}) collective-permute-start(bf16[16,6144]{1,0:T(8,128)(2,1)S(1)} %pad_maximum_fusion.9), channel_id=1, source_target_pairs={{0,48},{1,17},{2,50},{3,19},{4,52},{5,21},{6,54},{7,23},{8,56},{9,... | collective-permute-start | bytes 589832 | tf_op jit(solution)/shard_map/ppermute | solution.py:85
  112.1 7.0 %collective-permute-start.27 = (bf16[8,6144]{1,0:T(8,128)(2,1)S(1)}, bf16[8,6144]{1,0:T(8,128)(2,1)S(1)}, u32[]{:S(2)}, u32[]{:S(2)}) collective-permute-start(bf16[8,6144]{1,0:T(8,128)(2,1)S(1)} %get-tuple-element.115), channel_id=1, source_target_pairs={{0,64},{1,65},{2,66},{3,67},{4,68},{5,69},{6,70},{7,71},{8,72},{9,... | collective-permute-start | bytes 294920 | tf_op jit(solution)/shard_map/ppermute | solution.py:272
  113.7 7.2 %collective-permute-start.29 = (bf16[8,6144]{1,0:T(8,128)(2,1)S(1)}, bf16[8,6144]{1,0:T(8,128)(2,1)S(1)}, u32[]{:S(2)}, u32[]{:S(2)}) collective-permute-start(bf16[8,6144]{1,0:T(8,128)(2,1)S(1)} %get-tuple-element.117), channel_id=1, source_target_pairs={{0,72},{1,73},{2,74},{3,75},{4,76},{5,77},{6,78},{7,79},{8,64},{9,... | collective-permute-start | bytes 294920 | tf_op jit(solution)/shard_map/ppermute | solution.py:272
  118.3 6.7 %collective-permute-start.30 = (bf16[8,6144]{1,0:T(8,128)(2,1)S(1)}, bf16[8,6144]{1,0:T(8,128)(2,1)S(1)}, u32[]{:S(2)}, u32[]{:S(2)}) collective-permute-start(bf16[8,6144]{1,0:T(8,128)(2,1)S(1)} %get-tuple-element.118), channel_id=1, source_target_pairs={{0,88},{1,121},{2,90},{3,123},{4,92},{5,125},{6,94},{7,127},{8,66}... | collective-permute-start | bytes 294920 | tf_op jit(solution)/shard_map/ppermute | solution.py:272
  (11 other events, 102.2 us)

commit v12 on v11

--- a/solution.py
+++ b/solution.py
@@ -22,6 +22,10 @@
     return pipe, z, half_x, y, core
 
 
+def role_of(z, y, core):
+    return (core + z + y) % 2
+
+
 def join_place(pipe, z, half_x, y, core):
     return (((pipe * 4 + z) * 2 + half_x) * 4 + y) * 2 + core
 
@@ -35,7 +39,7 @@
     return lax.ppermute(value, AXES, pairs)
 
 
-def normalize_rows(core_ref, rows_ref, gain_ref, kept_ref, given_ref):
+def normalize_rows(role_ref, rows_ref, gain_ref, kept_ref, given_ref):
     values = rows_ref[...].astype(jnp.float32)
     centre = jnp.mean(values, axis=-1, keepdims=True)
     shifted = values - centre
@@ -43,18 +47,18 @@
     normed = (shifted * lax.rsqrt(spread + 1e-05) * gain_ref[...]).astype(jnp.bfloat16)
     half = kept_ref.shape[1]
 
-    @pl.when(core_ref[0] == 0)
+    @pl.when(role_ref[0] == 0)
     def _():
         kept_ref[...] = normed[:, :half]
         given_ref[...] = normed[:, half:]
 
-    @pl.when(core_ref[0] != 0)
+    @pl.when(role_ref[0] != 0)
     def _():
         kept_ref[...] = normed[:, half:]
         given_ref[...] = normed[:, :half]
 
 
-def normalize(section_rows, gain_vector, core):
+def normalize(section_rows, gain_vector, role):
     count, width = section_rows.shape
     part = pltpu.VMEM((count, width // 2), jnp.bfloat16)
     whole = pl.BlockSpec(memory_space=pltpu.VMEM)
@@ -63,19 +67,19 @@
         out_shape=(part, part),
         in_specs=[pl.BlockSpec(memory_space=pltpu.SMEM), whole, whole],
         out_specs=(whole, whole),
-    )(jnp.reshape(core, (1,)), section_rows, gain_vector)
+    )(jnp.reshape(role, (1,)), section_rows, gain_vector)
 
 
 def swap_pairs(axis, turn):
     pairs = []
     for source in range(128):
         pipe, z, half_x, y, core = split_place(source)
-        flip = (1, 3)[turn ^ core]
+        flip = (1, 3)[turn ^ role_of(z, y, core)]
         if axis == "z":
             z ^= flip
         else:
             y ^= flip
-        pairs.append((source, join_place(pipe, z, half_x, y, core)))
+        pairs.append((source, join_place(pipe, z, half_x, y, 1 - core)))
     return pairs
 
 
@@ -86,13 +90,13 @@
     )
 
 
-def near_rows(own, one, two, core):
+def near_rows(own, one, two, role):
     size = own.shape[0]
     return jnp.concatenate(
         [
             own,
-            jnp.where(core == 0, one, two[:size]),
-            jnp.where(core == 0, two[:size], one),
+            jnp.where(role == 0, one, two[:size]),
+            jnp.where(role == 0, two[:size], one),
             two[size:],
         ]
     )
@@ -109,12 +113,12 @@
     for source in range(128):
         pipe, z, half_x, y, core = split_place(source)
         half_x ^= crossed
-        flip = (1, 3)[core] if near else 0
+        flip = (1, 3)[role_of(z, y, core)] if near else 0
         if half_x:
             z ^= flip
         else:
             y ^= flip
-        pairs.append((source, join_place(1 - pipe, z, half_x, y, core)))
+        pairs.append((source, join_place(1 - pipe, z, half_x, y, core ^ near)))
     return pairs
 
 
@@ -152,26 +156,27 @@
     width = segment_input.shape[2]
     half, quarter = width // 2, width // 4
     _, z, half_x, y, core = split_place(lax.axis_index("dp"))
-
-    kept, given = normalize(segment_input[0], norm_gain, core)
+    role = role_of(z, y, core)
+
+    kept, given = normalize(segment_input[0], norm_gain, role)
     given = send(given, core=1)
     block = jnp.where(
         core == 0, jnp.concatenate([kept, given]), jnp.concatenate([given, kept])
     )
     head_block, block = lax.optimization_barrier((head_weights[0, :, 0, :], block))
     other = send(block, x=1)
-    their_weights = lax.dynamic_slice_in_dim(head_block, (1 - core) * half, half, 0)
+    their_weights = lax.dynamic_slice_in_dim(head_block, (1 - role) * half, half, 0)
     swapped_weights = send(their_weights, core=1)
     first = jnp.where(half_x == 0, block, other)
     second = jnp.where(half_x == 0, other, block)
-    own_weights = lax.dynamic_slice_in_dim(head_block, core * half, half, 0)
+    own_weights = lax.dynamic_slice_in_dim(head_block, role * half, half, 0)
 
     one = swap_both(first, "y", second, "z", 0)
     two = swap_both(
         jnp.concatenate([first, one[0]]), "y", jnp.concatenate([second, one[1]]), "z", 1
     )
-    first_own = near_rows(first, one[0], two[0], core)
-    second_own = near_rows(second, one[1], two[1], core)
+    first_own = near_rows(first, one[0], two[0], role)
+    second_own = near_rows(second, one[1], two[1], role)
 
     out_rows, _ = lax.optimization_barrier((output_weights[0], block))
     out_kept = lax.dynamic_slice_in_dim(out_rows, half_x * half, half, 1)
@@ -202,8 +207,8 @@
         mine + send(theirs, core=1)
         for mine, theirs in (
             here[0],
-            [jnp.where(core == 0, a, b) for a, b in zip(here[1], here[2])],
-            [jnp.where(core == 0, b, a) for a, b in zip(here[1], here[2])],
+            [jnp.where(role == 0, a, b) for a, b in zip(here[1], here[2])],
+            [jnp.where(role == 0, b, a) for a, b in zip(here[1], here[2])],
         )
     ]
     last, sums = lax.optimization_barrier((last, sums))
@@ -219,9 +224,13 @@
         (jnp.concatenate([near_block, near_crossed]), across)
     )
 
+    odd = np.asarray([0, 1, 1, 0])
+    odd = (odd[:, None, None] ^ odd[None, None, :]) ^ np.zeros((1, 2, 1), np.int64)
+    odd = odd.astype(np.int32).reshape(32, 1, 1)
+
     def of_core(rows, place):
         by_core = rows.reshape(32, 2, 8, head_size)
-        return jnp.where(place == 0, by_core[:, 0], by_core[:, 1])
+        return jnp.where((odd ^ place) == 0, by_core[:, 0], by_core[:, 1])
 
     given_heads = send(
         jnp.concatenate([of_core(attended, 1 - core), of_core(across, 1 - core)], axis=2),
@@ -232,8 +241,8 @@
     )
 
     def turns(blocks):
-        middle = jnp.where(core == 0, blocks[2], blocks[1])
-        kept = jnp.where(core == 0, blocks[1], blocks[2])
+        middle = jnp.where(role == 0, blocks[2], blocks[1])
+        kept = jnp.where(role == 0, blocks[1], blocks[2])
         return [middle, blocks[3]], [blocks[0], kept]
 
     heads = heads.reshape(4, 2, 32, 4 * head_size)

time: 126 us -> 124 us (0.984)
  starting transfers between devices: 46.7 us -> 41.9 us
  waiting for transfers between devices: 57.5 us -> 59.8 us
    ppermute x8, starting transfers between devices: 16.6 us -> 11.9 us  [swap_both(): lax.ppermute(second, AXES, swap_pairs(second_axis, turn))]
    ppermute x8, waiting for transfers between devices: 18.3 us -> 20.9 us  [swap_both(): lax.ppermute(second, AXES, swap_pairs(second_axis, turn))]
    ppermute x8, starting transfers between devices: 12 us -> 13.7 us  [swap_both(): lax.ppermute(first, AXES, swap_pairs(first_axis, turn))]
    ppermute x4, starting transfers between devices: 6.98 us -> 5.64 us  [shards(): lax.ppermute(rows[k], AXES, owner_pairs(crossed, k)).astype(jnp.float32)]
  transfers between devices with their start and end apart: 31 -> 31, of which waited for: 20 -> 22; matrix products, arithmetic and copies ran while one was open for 13% -> 14% of each run, Pallas kernels for 0% -> 0%
where the time goes in v12:
time: 124 us
  waiting for transfers between devices  59.8 us (48%)
  starting transfers between devices  41.9 us (34%)
  matrix products  12 us (10%)
  local copies, waits for them, and re-layouts  4.1 us (3%)
  other arithmetic  3.92 us (3%)
  Pallas kernels  1.36 us (1%)
    ppermute x8, waiting for transfers between devices, swap_both(): lax.ppermute(first, AXES, swap_pairs(first_axis, turn))  24.7 us
    ppermute x8, waiting for transfers between devices, swap_both(): lax.ppermute(second, AXES, swap_pairs(second_axis, turn))  20.9 us
    ppermute x8, starting transfers between devices, swap_both(): lax.ppermute(first, AXES, swap_pairs(first_axis, turn))  13.7 us
    ppermute x8, starting transfers between devices, swap_both(): lax.ppermute(second, AXES, swap_pairs(second_axis, turn))  11.9 us
    ppermute x11, starting transfers between devices, send(): return lax.ppermute(value, AXES, pairs)  10.7 us
    ppermute x11, waiting for transfers between devices, send(): return lax.ppermute(value, AXES, pairs)  8.91 us
    ppermute x4, starting transfers between devices, shards(): lax.ppermute(rows[k], AXES, owner_pairs(crossed, k)).astype(jnp.float32)  5.64 us
    ppermute x4, waiting for transfers between devices, shards(): lax.ppermute(rows[k], AXES, owner_pairs(crossed, k)).astype(jnp.float32)  5.26 us
  transfers between devices with their start and end apart: 31, of which 22 were waited for; matrix products, arithmetic and copies ran while one was open for 14% of the time, Pallas kernels for 0%

profile of v12, /device:TPU:0, one launch (start us, length us, event | category | flops | bytes accessed | tf_op | source)
XLA Modules:
  0.0 123.6 jit_solution(8886621778937121543)
XLA Ops:
  2.8 3.2 %collective-permute-start.1 = (bf16[16,6144]{1,0:T(8,128)(2,1)S(1)}, bf16[16,6144]{1,0:T(8,128)(2,1)S(1)}, u32[]{:S(2)}, u32[]{:S(2)}) collective-permute-start(bf16[16,6144]{1,0:T(8,128)(2,1)S(1)} %maximum_select_fusion), channel_id=1, source_target_pairs={{0,8},{1,9},{2,10},{3,11},{4,12},{5,13},{6,14},{7,15},{8,0},{9,1},... | collective-permute-start | bytes 589832 | tf_op jit(solution)/shard_map/ppermute | solution.py:39
  6.0 3.0 %constant_dynamic-slice_fusion.2 = bf16[6144,384]{1,0:T(8,128)(2,1)S(1)} fusion(bf16[12288,384]{1,0:T(8,128)(2,1)} %bitcast.87, s32[]{:T(128)S(6)} %select_n.220), kind=kLoop, calls=%fused_computation.117 | loop fusion | bytes 9437188 | tf_op jit(solution)/shard_map/dynamic_slice | solution.py:168
  9.0 2.3 %collective-permute-done.1 = bf16[16,6144]{1,0:T(8,128)(2,1)S(1)} collective-permute-done((bf16[16,6144]{1,0:T(8,128)(2,1)S(1)}, bf16[16,6144]{1,0:T(8,128)(2,1)S(1)}, u32[]{:S(2)}, u32[]{:S(2)}) %collective-permute-start.1) | collective-permute-done | bytes 196640 | tf_op jit(solution)/shard_map/ppermute | solution.py:39
  12.6 2.4 %collective-permute-start.2 = (bf16[16,6144]{1,0:T(8,128)(2,1)S(1)}, bf16[16,6144]{1,0:T(8,128)(2,1)S(1)}, u32[]{:S(2)}, u32[]{:S(2)}) collective-permute-start(bf16[16,6144]{1,0:T(8,128)(2,1)S(1)} %get-tuple-element.106), channel_id=1, source_target_pairs={{0,3},{1,6},{2,5},{3,0},{4,7},{5,2},{6,1},{7,4},{8,11},{9,14},{10,... | collective-permute-start | bytes 589832 | tf_op jit(solution)/shard_map/ppermute | solution.py:88
  16.6 3.4 %collective-permute-start.5 = (bf16[32,6144]{1,0:T(8,128)(2,1)S(1)}, bf16[32,6144]{1,0:T(8,128)(2,1)S(1)}, u32[]{:S(2)}, u32[]{:S(2)}) collective-permute-start(bf16[32,6144]{1,0:T(8,128)(2,1)S(1)} %pad_maximum_fusion.6), channel_id=1, source_target_pairs={{0,49},{1,16},{2,19},{3,50},{4,53},{5,20},{6,23},{7,54},{8,57},{9,... | collective-permute-start | bytes 1179656 | tf_op jit(solution)/shard_map/ppermute | solution.py:89
  20.0 3.6 %collective-permute-start.3 = (bf16[32,6144]{1,0:T(8,128)(2,1)S(1)}, bf16[32,6144]{1,0:T(8,128)(2,1)S(1)}, u32[]{:S(2)}, u32[]{:S(2)}) collective-permute-start(bf16[32,6144]{1,0:T(8,128)(2,1)S(1)} %pad_maximum_fusion.5), channel_id=1, source_target_pairs={{0,7},{1,2},{2,1},{3,4},{4,3},{5,6},{6,5},{7,0},{8,15},{9,10},{10,... | collective-permute-start | bytes 1179656 | tf_op jit(solution)/shard_map/ppermute | solution.py:88
  23.6 3.0 %collective-permute-start.17 = (bf16[128,6144]{1,0:T(8,128)(2,1)S(1)}, bf16[128,6144]{1,0:T(8,128)(2,1)S(1)}, u32[]{:S(2)}, u32[]{:S(2)}) collective-permute-start(bf16[128,6144]{1,0:T(8,128)(2,1)S(1)} %get-tuple-element.61), channel_id=1, source_target_pairs={{0,8},{1,9},{2,10},{3,11},{4,12},{5,13},{6,14},{7,15},{8,0},{9,1},... | collective-permute-start | bytes 4718600 | tf_op jit(solution)/shard_map/ppermute | solution.py:39
  26.8 2.3 %collective-permute-done.3 = bf16[32,6144]{1,0:T(8,128)(2,1)S(1)} collective-permute-done((bf16[32,6144]{1,0:T(8,128)(2,1)S(1)}, bf16[32,6144]{1,0:T(8,128)(2,1)S(1)}, u32[]{:S(2)}, u32[]{:S(2)}) %collective-permute-start.3) | collective-permute-done | bytes 393248 | tf_op jit(solution)/shard_map/ppermute | solution.py:88
  29.4 3.3 %collective-permute-start.10 = (bf16[64,6144]{1,0:T(8,128)(2,1)S(1)}, bf16[64,6144]{1,0:T(8,128)(2,1)S(1)}, u32[]{:S(2)}, u32[]{:S(2)}) collective-permute-start(bf16[64,6144]{1,0:T(8,128)(2,1)S(1)} %pad_maximum_fusion.3), channel_id=1, source_target_pairs={{0,7},{1,2},{2,1},{3,4},{4,3},{5,6},{6,5},{7,0},{8,15},{9,10},{10,... | collective-permute-start | bytes 2359304 | tf_op jit(solution)/shard_map/ppermute | solution.py:89
  32.7 1.9 %collective-permute-start.9 = (bf16[64,6144]{1,0:T(8,128)(2,1)S(1)}, bf16[64,6144]{1,0:T(8,128)(2,1)S(1)}, u32[]{:S(2)}, u32[]{:S(2)}) collective-permute-start(bf16[64,6144]{1,0:T(8,128)(2,1)S(1)} %pad_maximum_fusion.2), channel_id=1, source_target_pairs={{0,49},{1,16},{2,19},{3,50},{4,53},{5,20},{6,23},{7,54},{8,57},{9,... | collective-permute-start | bytes 2359304 | tf_op jit(solution)/shard_map/ppermute | solution.py:88
  36.8 13.7 %collective-permute-done.10 = bf16[64,6144]{1,0:T(8,128)(2,1)S(1)} collective-permute-done((bf16[64,6144]{1,0:T(8,128)(2,1)S(1)}, bf16[64,6144]{1,0:T(8,128)(2,1)S(1)}, u32[]{:S(2)}, u32[]{:S(2)}) %collective-permute-start.10) | collective-permute-done | bytes 786464 | tf_op jit(solution)/shard_map/ppermute | solution.py:89
  61.3 3.2 %collective-permute-done.11 = bf16[64,6144]{1,0:T(8,128)(2,1)S(1)} collective-permute-done((bf16[64,6144]{1,0:T(8,128)(2,1)S(1)}, bf16[64,6144]{1,0:T(8,128)(2,1)S(1)}, u32[]{:S(2)}, u32[]{:S(2)}) %collective-permute-start.11) | collective-permute-done | bytes 786464 | tf_op jit(solution)/shard_map/ppermute | solution.py:88
  70.4 3.1 %collective-permute-start.19 = (bf16[512,128]{1,0:T(8,128)(2,1)S(1)}, bf16[512,128]{1,0:T(8,128)(2,1)S(1)}, u32[]{:S(2)}, u32[]{:S(2)}) collective-permute-start(bf16[512,128]{1,0:T(8,128)(2,1)S(1)} %convolution_convert_fusion.1), channel_id=1, source_target_pairs={{0,8},{1,9},{2,10},{3,11},{4,12},{5,13},{6,14},{7,15},{8,0},{9,1},... | collective-permute-start | bytes 393224 | tf_op jit(solution)/shard_map/ppermute | solution.py:39
  74.0 3.6 %collective-permute-done.19 = bf16[512,128]{1,0:T(8,128)(2,1)S(1)} collective-permute-done((bf16[512,128]{1,0:T(8,128)(2,1)S(1)}, bf16[512,128]{1,0:T(8,128)(2,1)S(1)}, u32[]{:S(2)}, u32[]{:S(2)}) %collective-permute-start.19) | collective-permute-done | bytes 131104 | tf_op jit(solution)/shard_map/ppermute | solution.py:39
  80.3 1.9 %collective-permute-start.21 = (bf16[64,6144]{1,0:T(8,128)(2,1)S(1)}, bf16[64,6144]{1,0:T(8,128)(2,1)S(1)}, u32[]{:S(2)}, u32[]{:S(2)}) collective-permute-start(bf16[64,6144]{1,0:T(8,128)(2,1)S(1)} %get-tuple-element.65), channel_id=1, source_target_pairs={{0,49},{1,16},{2,19},{3,50},{4,53},{5,20},{6,23},{7,54},{8,57},{9,... | collective-permute-start | bytes 2359304 | tf_op jit(solution)/shard_map/ppermute | solution.py:88
  82.2 2.1 %collective-permute-start.22 = (bf16[64,6144]{1,0:T(8,128)(2,1)S(1)}, bf16[64,6144]{1,0:T(8,128)(2,1)S(1)}, u32[]{:S(2)}, u32[]{:S(2)}) collective-permute-start(bf16[64,6144]{1,0:T(8,128)(2,1)S(1)} %get-tuple-element.66), channel_id=1, source_target_pairs={{0,7},{1,2},{2,1},{3,4},{4,3},{5,6},{6,5},{7,0},{8,15},{9,10},{10,... | collective-permute-start | bytes 2359304 | tf_op jit(solution)/shard_map/ppermute | solution.py:89
  85.3 7.7 %collective-permute-done.21 = bf16[64,6144]{1,0:T(8,128)(2,1)S(1)} collective-permute-done((bf16[64,6144]{1,0:T(8,128)(2,1)S(1)}, bf16[64,6144]{1,0:T(8,128)(2,1)S(1)}, u32[]{:S(2)}, u32[]{:S(2)}) %collective-permute-start.21) | collective-permute-done | bytes 786464 | tf_op jit(solution)/shard_map/ppermute | solution.py:88
  93.0 1.8 %collective-permute-done.22 = bf16[64,6144]{1,0:T(8,128)(2,1)S(1)} collective-permute-done((bf16[64,6144]{1,0:T(8,128)(2,1)S(1)}, bf16[64,6144]{1,0:T(8,128)(2,1)S(1)}, u32[]{:S(2)}, u32[]{:S(2)}) %collective-permute-start.22) | collective-permute-done | bytes 786464 | tf_op jit(solution)/shard_map/ppermute | solution.py:89
  95.4 7.1 %collective-permute-done.23 = bf16[32,6144]{1,0:T(8,128)(2,1)S(1)} collective-permute-done((bf16[32,6144]{1,0:T(8,128)(2,1)S(1)}, bf16[32,6144]{1,0:T(8,128)(2,1)S(1)}, u32[]{:S(2)}, u32[]{:S(2)}) %collective-permute-start.23) | collective-permute-done | bytes 393248 | tf_op jit(solution)/shard_map/ppermute | solution.py:88
  102.9 2.5 %collective-permute-start.25 = (bf16[16,6144]{1,0:T(8,128)(2,1)S(1)}, bf16[16,6144]{1,0:T(8,128)(2,1)S(1)}, u32[]{:S(2)}, u32[]{:S(2)}) collective-permute-start(bf16[16,6144]{1,0:T(8,128)(2,1)S(1)} %pad_maximum_fusion.8), channel_id=1, source_target_pairs={{0,7},{1,2},{2,1},{3,4},{4,3},{5,6},{6,5},{7,0},{8,15},{9,10},{10,... | collective-permute-start | bytes 589832 | tf_op jit(solution)/shard_map/ppermute | solution.py:88
  106.0 3.3 %collective-permute-done.25 = bf16[16,6144]{1,0:T(8,128)(2,1)S(1)} collective-permute-done((bf16[16,6144]{1,0:T(8,128)(2,1)S(1)}, bf16[16,6144]{1,0:T(8,128)(2,1)S(1)}, u32[]{:S(2)}, u32[]{:S(2)}) %collective-permute-start.25) | collective-permute-done | bytes 196640 | tf_op jit(solution)/shard_map/ppermute | solution.py:88
  109.3 2.4 %collective-permute-done.26 = bf16[16,6144]{1,0:T(8,128)(2,1)S(1)} collective-permute-done((bf16[16,6144]{1,0:T(8,128)(2,1)S(1)}, bf16[16,6144]{1,0:T(8,128)(2,1)S(1)}, u32[]{:S(2)}, u32[]{:S(2)}) %collective-permute-start.26) | collective-permute-done | bytes 196640 | tf_op jit(solution)/shard_map/ppermute | solution.py:89
  113.4 2.7 %collective-permute-start.29 = (bf16[8,6144]{1,0:T(8,128)(2,1)S(1)}, bf16[8,6144]{1,0:T(8,128)(2,1)S(1)}, u32[]{:S(2)}, u32[]{:S(2)}) collective-permute-start(bf16[8,6144]{1,0:T(8,128)(2,1)S(1)} %get-tuple-element.117), channel_id=1, source_target_pairs={{0,72},{1,73},{2,74},{3,75},{4,76},{5,77},{6,78},{7,79},{8,64},{9,... | collective-permute-start | bytes 294920 | tf_op jit(solution)/shard_map/ppermute | solution.py:281
  119.3 3.5 %collective-permute-done.30 = bf16[8,6144]{1,0:T(8,128)(2,1)S(1)} collective-permute-done((bf16[8,6144]{1,0:T(8,128)(2,1)S(1)}, bf16[8,6144]{1,0:T(8,128)(2,1)S(1)}, u32[]{:S(2)}, u32[]{:S(2)}) %collective-permute-start.30) | collective-permute-done | bytes 98336 | tf_op jit(solution)/shard_map/ppermute | solution.py:281
  (110 shorter events, 36.1 us)
Async XLA Ops:
  2.8 8.5 %collective-permute-start.1 = (bf16[16,6144]{1,0:T(8,128)(2,1)S(1)}, bf16[16,6144]{1,0:T(8,128)(2,1)S(1)}, u32[]{:S(2)}, u32[]{:S(2)}) collective-permute-start(bf16[16,6144]{1,0:T(8,128)(2,1)S(1)} %maximum_select_fusion), channel_id=1, source_target_pairs={{0,8},{1,9},{2,10},{3,11},{4,12},{5,13},{6,14},{7,15},{8,0},{9,1},... | collective-permute-start | bytes 589832 | tf_op jit(solution)/shard_map/ppermute | solution.py:39
  8.9 20.3 %collective-permute-start.6 = (bf16[6144,384]{1,0:T(8,128)(2,1)S(1)}, bf16[6144,384]{1,0:T(8,128)(2,1)S(1)}, u32[]{:S(2)}, u32[]{:S(2)}) collective-permute-start(bf16[6144,384]{1,0:T(8,128)(2,1)S(1)} %constant_dynamic-slice_fusion.2), channel_id=1, source_target_pairs={{0,1},{1,0},{2,3},{3,2},{4,5},{5,4},{6,7},{7,6},{8,9},{9,8},{10,11... | collective-permute-start | bytes 14155784 | tf_op jit(solution)/shard_map/ppermute | solution.py:39
  11.4 5.2 %collective-permute-start.4 = (bf16[16,6144]{1,0:T(8,128)(2,1)S(1)}, bf16[16,6144]{1,0:T(8,128)(2,1)S(1)}, u32[]{:S(2)}, u32[]{:S(2)}) collective-permute-start(bf16[16,6144]{1,0:T(8,128)(2,1)S(1)} %get-tuple-element.105), channel_id=1, source_target_pairs={{0,17},{1,48},{2,51},{3,18},{4,21},{5,52},{6,55},{7,22},{8,25},{9,... | collective-permute-start | bytes 589832 | tf_op jit(solution)/shard_map/ppermute | solution.py:89
  12.6 7.4 %collective-permute-start.2 = (bf16[16,6144]{1,0:T(8,128)(2,1)S(1)}, bf16[16,6144]{1,0:T(8,128)(2,1)S(1)}, u32[]{:S(2)}, u32[]{:S(2)}) collective-permute-start(bf16[16,6144]{1,0:T(8,128)(2,1)S(1)} %get-tuple-element.106), channel_id=1, source_target_pairs={{0,3},{1,6},{2,5},{3,0},{4,7},{5,2},{6,1},{7,4},{8,11},{9,14},{10,... | collective-permute-start | bytes 589832 | tf_op jit(solution)/shard_map/ppermute | solution.py:88
  16.6 10.1 %collective-permute-start.5 = (bf16[32,6144]{1,0:T(8,128)(2,1)S(1)}, bf16[32,6144]{1,0:T(8,128)(2,1)S(1)}, u32[]{:S(2)}, u32[]{:S(2)}) collective-permute-start(bf16[32,6144]{1,0:T(8,128)(2,1)S(1)} %pad_maximum_fusion.6), channel_id=1, source_target_pairs={{0,49},{1,16},{2,19},{3,50},{4,53},{5,20},{6,23},{7,54},{8,57},{9,... | collective-permute-start | bytes 1179656 | tf_op jit(solution)/shard_map/ppermute | solution.py:89
  20.0 9.1 %collective-permute-start.3 = (bf16[32,6144]{1,0:T(8,128)(2,1)S(1)}, bf16[32,6144]{1,0:T(8,128)(2,1)S(1)}, u32[]{:S(2)}, u32[]{:S(2)}) collective-permute-start(bf16[32,6144]{1,0:T(8,128)(2,1)S(1)} %pad_maximum_fusion.5), channel_id=1, source_target_pairs={{0,7},{1,2},{2,1},{3,4},{4,3},{5,6},{6,5},{7,0},{8,15},{9,10},{10,... | collective-permute-start | bytes 1179656 | tf_op jit(solution)/shard_map/ppermute | solution.py:88
  23.6 37.0 %collective-permute-start.17 = (bf16[128,6144]{1,0:T(8,128)(2,1)S(1)}, bf16[128,6144]{1,0:T(8,128)(2,1)S(1)}, u32[]{:S(2)}, u32[]{:S(2)}) collective-permute-start(bf16[128,6144]{1,0:T(8,128)(2,1)S(1)} %get-tuple-element.61), channel_id=1, source_target_pairs={{0,8},{1,9},{2,10},{3,11},{4,12},{5,13},{6,14},{7,15},{8,0},{9,1},... | collective-permute-start | bytes 4718600 | tf_op jit(solution)/shard_map/ppermute | solution.py:39
  29.3 21.2 %collective-permute-start.7 = (bf16[64,6144]{1,0:T(8,128)(2,1)S(1)}, bf16[64,6144]{1,0:T(8,128)(2,1)S(1)}, u32[]{:S(2)}, u32[]{:S(2)}) collective-permute-start(bf16[64,6144]{1,0:T(8,128)(2,1)S(1)} %pad_maximum_fusion.2), channel_id=1, source_target_pairs={{0,17},{1,48},{2,51},{3,18},{4,21},{5,52},{6,55},{7,22},{8,25},{9,... | collective-permute-start | bytes 2359304 | tf_op jit(solution)/shard_map/ppermute | solution.py:88
  29.4 21.0 %collective-permute-start.10 = (bf16[64,6144]{1,0:T(8,128)(2,1)S(1)}, bf16[64,6144]{1,0:T(8,128)(2,1)S(1)}, u32[]{:S(2)}, u32[]{:S(2)}) collective-permute-start(bf16[64,6144]{1,0:T(8,128)(2,1)S(1)} %pad_maximum_fusion.3), channel_id=1, source_target_pairs={{0,7},{1,2},{2,1},{3,4},{4,3},{5,6},{6,5},{7,0},{8,15},{9,10},{10,... | collective-permute-start | bytes 2359304 | tf_op jit(solution)/shard_map/ppermute | solution.py:89
  32.7 17.9 %collective-permute-start.8 = (bf16[64,6144]{1,0:T(8,128)(2,1)S(1)}, bf16[64,6144]{1,0:T(8,128)(2,1)S(1)}, u32[]{:S(2)}, u32[]{:S(2)}) collective-permute-start(bf16[64,6144]{1,0:T(8,128)(2,1)S(1)} %pad_maximum_fusion.3), channel_id=1, source_target_pairs={{0,3},{1,6},{2,5},{3,0},{4,7},{5,2},{6,1},{7,4},{8,11},{9,14},{10,... | collective-permute-start | bytes 2359304 | tf_op jit(solution)/shard_map/ppermute | solution.py:89
  32.7 19.0 %collective-permute-start.9 = (bf16[64,6144]{1,0:T(8,128)(2,1)S(1)}, bf16[64,6144]{1,0:T(8,128)(2,1)S(1)}, u32[]{:S(2)}, u32[]{:S(2)}) collective-permute-start(bf16[64,6144]{1,0:T(8,128)(2,1)S(1)} %pad_maximum_fusion.2), channel_id=1, source_target_pairs={{0,49},{1,16},{2,19},{3,50},{4,53},{5,20},{6,23},{7,54},{8,57},{9,... | collective-permute-start | bytes 2359304 | tf_op jit(solution)/shard_map/ppermute | solution.py:88
  51.8 12.7 %collective-permute-start.11 = (bf16[64,6144]{1,0:T(8,128)(2,1)S(1)}, bf16[64,6144]{1,0:T(8,128)(2,1)S(1)}, u32[]{:S(2)}, u32[]{:S(2)}) collective-permute-start(bf16[64,6144]{1,0:T(8,128)(2,1)S(1)} %collective-permute-done.7), channel_id=1, source_target_pairs={{0,49},{1,16},{2,19},{3,50},{4,53},{5,20},{6,23},{7,54},{8,57},{9,... | collective-permute-start | bytes 2359304 | tf_op jit(solution)/shard_map/ppermute | solution.py:88
  53.1 12.7 %collective-permute-start.12 = (bf16[64,6144]{1,0:T(8,128)(2,1)S(1)}, bf16[64,6144]{1,0:T(8,128)(2,1)S(1)}, u32[]{:S(2)}, u32[]{:S(2)}) collective-permute-start(bf16[64,6144]{1,0:T(8,128)(2,1)S(1)} %collective-permute-done.8), channel_id=1, source_target_pairs={{0,7},{1,2},{2,1},{3,4},{4,3},{5,6},{6,5},{7,0},{8,15},{9,10},{10,... | collective-permute-start | bytes 2359304 | tf_op jit(solution)/shard_map/ppermute | solution.py:89
  61.0 12.6 %collective-permute-start.18 = (bf16[256,6144]{1,0:T(8,128)(2,1)S(1)}, bf16[256,6144]{1,0:T(8,128)(2,1)S(1)}, u32[]{:S(2)}, u32[]{:S(2)}) collective-permute-start(bf16[256,6144]{1,0:T(8,128)(2,1)S(1)} %pad_maximum_fusion.1), channel_id=1, source_target_pairs={{0,1},{1,0},{2,3},{3,2},{4,5},{5,4},{6,7},{7,6},{8,9},{9,8},{10,11... | collective-permute-start | bytes 9437192 | tf_op jit(solution)/shard_map/ppermute | solution.py:39
  70.4 7.1 %collective-permute-start.19 = (bf16[512,128]{1,0:T(8,128)(2,1)S(1)}, bf16[512,128]{1,0:T(8,128)(2,1)S(1)}, u32[]{:S(2)}, u32[]{:S(2)}) collective-permute-start(bf16[512,128]{1,0:T(8,128)(2,1)S(1)} %convolution_convert_fusion.1), channel_id=1, source_target_pairs={{0,8},{1,9},{2,10},{3,11},{4,12},{5,13},{6,14},{7,15},{8,0},{9,1},... | collective-permute-start | bytes 393224 | tf_op jit(solution)/shard_map/ppermute | solution.py:39
  80.3 12.7 %collective-permute-start.21 = (bf16[64,6144]{1,0:T(8,128)(2,1)S(1)}, bf16[64,6144]{1,0:T(8,128)(2,1)S(1)}, u32[]{:S(2)}, u32[]{:S(2)}) collective-permute-start(bf16[64,6144]{1,0:T(8,128)(2,1)S(1)} %get-tuple-element.65), channel_id=1, source_target_pairs={{0,49},{1,16},{2,19},{3,50},{4,53},{5,20},{6,23},{7,54},{8,57},{9,... | collective-permute-start | bytes 2359304 | tf_op jit(solution)/shard_map/ppermute | solution.py:88
  82.2 12.6 %collective-permute-start.22 = (bf16[64,6144]{1,0:T(8,128)(2,1)S(1)}, bf16[64,6144]{1,0:T(8,128)(2,1)S(1)}, u32[]{:S(2)}, u32[]{:S(2)}) collective-permute-start(bf16[64,6144]{1,0:T(8,128)(2,1)S(1)} %get-tuple-element.66), channel_id=1, source_target_pairs={{0,7},{1,2},{2,1},{3,4},{4,3},{5,6},{6,5},{7,0},{8,15},{9,10},{10,... | collective-permute-start | bytes 2359304 | tf_op jit(solution)/shard_map/ppermute | solution.py:89
  95.2 7.3 %collective-permute-start.23 = (bf16[32,6144]{1,0:T(8,128)(2,1)S(1)}, bf16[32,6144]{1,0:T(8,128)(2,1)S(1)}, u32[]{:S(2)}, u32[]{:S(2)}) collective-permute-start(bf16[32,6144]{1,0:T(8,128)(2,1)S(1)} %slice.303), channel_id=1, source_target_pairs={{0,17},{1,48},{2,51},{3,18},{4,21},{5,52},{6,55},{7,22},{8,25},{9,... | collective-permute-start | bytes 1179656 | tf_op jit(solution)/shard_map/ppermute | solution.py:88
  95.3 7.3 %collective-permute-start.24 = (bf16[32,6144]{1,0:T(8,128)(2,1)S(1)}, bf16[32,6144]{1,0:T(8,128)(2,1)S(1)}, u32[]{:S(2)}, u32[]{:S(2)}) collective-permute-start(bf16[32,6144]{1,0:T(8,128)(2,1)S(1)} %slice.302), channel_id=1, source_target_pairs={{0,3},{1,6},{2,5},{3,0},{4,7},{5,2},{6,1},{7,4},{8,11},{9,14},{10,... | collective-permute-start | bytes 1179656 | tf_op jit(solution)/shard_map/ppermute | solution.py:89
  102.9 6.4 %collective-permute-start.25 = (bf16[16,6144]{1,0:T(8,128)(2,1)S(1)}, bf16[16,6144]{1,0:T(8,128)(2,1)S(1)}, u32[]{:S(2)}, u32[]{:S(2)}) collective-permute-start(bf16[16,6144]{1,0:T(8,128)(2,1)S(1)} %pad_maximum_fusion.8), channel_id=1, source_target_pairs={{0,7},{1,2},{2,1},{3,4},{4,3},{5,6},{6,5},{7,0},{8,15},{9,10},{10,... | collective-permute-start | bytes 589832 | tf_op jit(solution)/shard_map/ppermute | solution.py:88
  105.4 6.3 %collective-permute-start.26 = (bf16[16,6144]{1,0:T(8,128)(2,1)S(1)}, bf16[16,6144]{1,0:T(8,128)(2,1)S(1)}, u32[]{:S(2)}, u32[]{:S(2)}) collective-permute-start(bf16[16,6144]{1,0:T(8,128)(2,1)S(1)} %pad_maximum_fusion.9), channel_id=1, source_target_pairs={{0,49},{1,16},{2,19},{3,50},{4,53},{5,20},{6,23},{7,54},{8,57},{9,... | collective-permute-start | bytes 589832 | tf_op jit(solution)/shard_map/ppermute | solution.py:89
  111.9 5.7 %collective-permute-start.27 = (bf16[8,6144]{1,0:T(8,128)(2,1)S(1)}, bf16[8,6144]{1,0:T(8,128)(2,1)S(1)}, u32[]{:S(2)}, u32[]{:S(2)}) collective-permute-start(bf16[8,6144]{1,0:T(8,128)(2,1)S(1)} %get-tuple-element.115), channel_id=1, source_target_pairs={{0,64},{1,65},{2,66},{3,67},{4,68},{5,69},{6,70},{7,71},{8,72},{9,... | collective-permute-start | bytes 294920 | tf_op jit(solution)/shard_map/ppermute | solution.py:281
  113.4 5.9 %collective-permute-start.29 = (bf16[8,6144]{1,0:T(8,128)(2,1)S(1)}, bf16[8,6144]{1,0:T(8,128)(2,1)S(1)}, u32[]{:S(2)}, u32[]{:S(2)}) collective-permute-start(bf16[8,6144]{1,0:T(8,128)(2,1)S(1)} %get-tuple-element.117), channel_id=1, source_target_pairs={{0,72},{1,73},{2,74},{3,75},{4,76},{5,77},{6,78},{7,79},{8,64},{9,... | collective-permute-start | bytes 294920 | tf_op jit(solution)/shard_map/ppermute | solution.py:281
  116.1 6.7 %collective-permute-start.30 = (bf16[8,6144]{1,0:T(8,128)(2,1)S(1)}, bf16[8,6144]{1,0:T(8,128)(2,1)S(1)}, u32[]{:S(2)}, u32[]{:S(2)}) collective-permute-start(bf16[8,6144]{1,0:T(8,128)(2,1)S(1)} %get-tuple-element.118), channel_id=1, source_target_pairs={{0,89},{1,120},{2,123},{3,90},{4,93},{5,124},{6,127},{7,94},{8,67}... | collective-permute-start | bytes 294920 | tf_op jit(solution)/shard_map/ppermute | solution.py:281
  (12 other events, 98.1 us)

commit v13 on v12

--- a/solution.py
+++ b/solution.py
@@ -159,13 +159,19 @@
     role = role_of(z, y, core)
 
     kept, given = normalize(segment_input[0], norm_gain, role)
-    given = send(given, core=1)
-    block = jnp.where(
-        core == 0, jnp.concatenate([kept, given]), jnp.concatenate([given, kept])
-    )
-    head_block, block = lax.optimization_barrier((head_weights[0, :, 0, :], block))
-    other = send(block, x=1)
+    kept, given = lax.optimization_barrier((kept, given))
+    across, across_other = send(kept, x=1), send(given, x=1, core=1)
+    beside = send(given, core=1)
+
+    def in_core_order(mine, others):
+        return jnp.where(
+            core == 0, jnp.concatenate([mine, others]), jnp.concatenate([others, mine])
+        )
+
+    head_block, beside = lax.optimization_barrier((head_weights[0, :, 0, :], beside))
     their_weights = lax.dynamic_slice_in_dim(head_block, (1 - role) * half, half, 0)
+    across, _ = lax.optimization_barrier((across, their_weights))
+    block, other = in_core_order(kept, beside), in_core_order(across, across_other)
     swapped_weights = send(their_weights, core=1)
     first = jnp.where(half_x == 0, block, other)
     second = jnp.where(half_x == 0, other, block)
@@ -275,14 +281,16 @@
         [total.astype(jnp.bfloat16).reshape(2, -1, half) for total in totals]
     )
     pairs_of = jnp.where(half_x == 0, first, second), jnp.where(half_x == 0, second, first)
-    halves = []
-    for crossed, rows in enumerate(pairs_of):
-        own, near = (
-            lax.ppermute(rows[k], AXES, owner_pairs(crossed, k)).astype(jnp.float32)
-            for k in (0, 1)
-        )
-        halves.append((own + near).astype(jnp.bfloat16))
-    straight, crossed = halves
+    parts = {
+        (crossed, near): lax.ppermute(
+            pairs_of[crossed][near], AXES, owner_pairs(crossed, near)
+        ).astype(jnp.float32)
+        for near in (1, 0)
+        for crossed in (1, 0)
+    }
+    straight, crossed = (
+        (parts[k, 0] + parts[k, 1]).astype(jnp.bfloat16) for k in (0, 1)
+    )
     return jnp.where(
         half_x == 0,
         jnp.concatenate([straight, crossed], axis=1),

time: 124 us -> 125 us (level)
  waiting for transfers between devices: 59.8 us -> 55.4 us
  matrix products: 12 us -> 14.3 us
  starting transfers between devices: 41.9 us -> 43.6 us
  local copies, waits for them, and re-layouts: 4.1 us -> 5.6 us
    ppermute x8, waiting for transfers between devices: 20.9 us -> 9.01 us  [swap_both(): lax.ppermute(second, AXES, swap_pairs(second_axis, turn))]
    ppermute x8, waiting for transfers between devices: 24.7 us -> 34 us  [swap_both(): lax.ppermute(first, AXES, swap_pairs(first_axis, turn))]
    ppermute x11 -> x12, starting transfers between devices: 10.7 us -> 13.7 us  [send(): return lax.ppermute(value, AXES, pairs)]
    ppermute x8, starting transfers between devices: 13.7 us -> 11 us  [swap_both(): lax.ppermute(first, AXES, swap_pairs(first_axis, turn))]
    dot_general x4, matrix products: 4.19 us -> 6.54 us  [project(): mine = jnp.dot(rows, own_weights, preferred_element_type=jnp.float32)]
    ppermute x8, starting transfers between devices: 11.9 us -> 13.9 us  [swap_both(): lax.ppermute(second, AXES, swap_pairs(second_axis, turn))]
    ppermute x11 -> x12, waiting for transfers between devices: 8.91 us -> 6.9 us  [send(): return lax.ppermute(value, AXES, pairs)]
    dynamic_slice x1, local copies, waits for them, and re-layouts: 0.25 us -> 2.08 us  [shards(): out_kept = lax.dynamic_slice_in_dim(out_rows, half_x * half, half, 1)]
  transfers between devices with their start and end apart: 31 -> 32, of which waited for: 22 -> 21; matrix products, arithmetic and copies ran while one was open for 14% -> 16% of each run, Pallas kernels for 0% -> 0%
where the time goes in v13:
time: 125 us
  waiting for transfers between devices  55.4 us (44%)
  starting transfers between devices  43.6 us (35%)
  matrix products  14.3 us (11%)
  local copies, waits for them, and re-layouts  5.6 us (4%)
  other arithmetic  4.15 us (3%)
  Pallas kernels  1.36 us (1%)
    ppermute x8, waiting for transfers between devices, swap_both(): lax.ppermute(first, AXES, swap_pairs(first_axis, turn))  34 us
    ppermute x8, starting transfers between devices, swap_both(): lax.ppermute(second, AXES, swap_pairs(second_axis, turn))  13.9 us
    ppermute x12, starting transfers between devices, send(): return lax.ppermute(value, AXES, pairs)  13.7 us
    ppermute x8, starting transfers between devices, swap_both(): lax.ppermute(first, AXES, swap_pairs(first_axis, turn))  11 us
    ppermute x8, waiting for transfers between devices, swap_both(): lax.ppermute(second, AXES, swap_pairs(second_axis, turn))  9.01 us
    ppermute x12, waiting for transfers between devices, send(): return lax.ppermute(value, AXES, pairs)  6.9 us
    dot_general x4, matrix products, project(): mine = jnp.dot(rows, own_weights, preferred_element_type=jnp.float32)  6.54 us
    ppermute x4, waiting for transfers between devices, shards(): lax.ppermute(pairs_of[crossed][near], AXES, owner_pairs(crossed, near))  5.57 us
  transfers between devices with their start and end apart: 32, of which 21 were waited for; matrix products, arithmetic and copies ran while one was open for 16% of the time, Pallas kernels for 0%

profile of v13, /device:TPU:0, one launch (start us, length us, event | category | flops | bytes accessed | tf_op | source)
XLA Modules:
  0.0 125.0 jit_solution(5351336082840120798)
XLA Ops:
  1.5 3.2 %collective-permute-start.2 = (bf16[8,6144]{1,0:T(8,128)(2,1)S(1)}, bf16[8,6144]{1,0:T(8,128)(2,1)S(1)}, u32[]{:S(2)}, u32[]{:S(2)}) collective-permute-start(bf16[8,6144]{1,0:T(8,128)(2,1)S(1)} %get-tuple-element.44), channel_id=1, source_target_pairs={{0,9},{1,8},{2,11},{3,10},{4,13},{5,12},{6,15},{7,14},{8,1},{9,0},... | collective-permute-start | bytes 294920 | tf_op jit(solution)/shard_map/ppermute | solution.py:39
  5.1 2.1 %constant_dynamic-slice_fusion.1 = (bf16[128,6144]{1,0:T(8,128)(2,1)S(1)}, bf16[128,6144]{1,0:T(8,128)(2,1)S(1)}) fusion(bf16[128,12288]{1,0:T(8,128)(2,1)} %bitcast.94, s32[]{:T(128)S(6)} %select_n.235, s32[]{:T(128)S(6)} %select_n.236), kind=kLoop, calls=%fused_computation.116 | loop fusion | bytes 6291464 | tf_op jit(solution)/shard_map/dynamic_slice | solution.py:188
  7.3 2.8 %constant_dynamic-slice_fusion.2 = bf16[6144,384]{1,0:T(8,128)(2,1)S(1)} fusion(bf16[12288,384]{1,0:T(8,128)(2,1)} %bitcast.87, s32[]{:T(128)S(6)} %select_n.217), kind=kLoop, calls=%fused_computation.118 | loop fusion | bytes 9437188 | tf_op jit(solution)/shard_map/dynamic_slice | solution.py:172
  13.0 3.5 %collective-permute-start.7 = (bf16[6144,384]{1,0:T(8,128)(2,1)S(1)}, bf16[6144,384]{1,0:T(8,128)(2,1)S(1)}, u32[]{:S(2)}, u32[]{:S(2)}) collective-permute-start(bf16[6144,384]{1,0:T(8,128)(2,1)S(1)} %constant_dynamic-slice_fusion.2), channel_id=1, source_target_pairs={{0,1},{1,0},{2,3},{3,2},{4,5},{5,4},{6,7},{7,6},{8,9},{9,8},{10,11... | collective-permute-start | bytes 14155784 | tf_op jit(solution)/shard_map/ppermute | solution.py:39
  17.4 3.3 %collective-permute-start.6 = (bf16[32,6144]{1,0:T(8,128)(2,1)S(1)}, bf16[32,6144]{1,0:T(8,128)(2,1)S(1)}, u32[]{:S(2)}, u32[]{:S(2)}) collective-permute-start(bf16[32,6144]{1,0:T(8,128)(2,1)S(1)} %pad_maximum_fusion.6), channel_id=1, source_target_pairs={{0,49},{1,16},{2,19},{3,50},{4,53},{5,20},{6,23},{7,54},{8,57},{9,... | collective-permute-start | bytes 1179656 | tf_op jit(solution)/shard_map/ppermute | solution.py:89
  21.6 2.7 %collective-permute-start.4 = (bf16[32,6144]{1,0:T(8,128)(2,1)S(1)}, bf16[32,6144]{1,0:T(8,128)(2,1)S(1)}, u32[]{:S(2)}, u32[]{:S(2)}) collective-permute-start(bf16[32,6144]{1,0:T(8,128)(2,1)S(1)} %pad_maximum_fusion.5), channel_id=1, source_target_pairs={{0,7},{1,2},{2,1},{3,4},{4,3},{5,6},{6,5},{7,0},{8,15},{9,10},{10,... | collective-permute-start | bytes 1179656 | tf_op jit(solution)/shard_map/ppermute | solution.py:88
  24.3 2.4 %collective-permute-start.18 = (bf16[128,6144]{1,0:T(8,128)(2,1)S(1)}, bf16[128,6144]{1,0:T(8,128)(2,1)S(1)}, u32[]{:S(2)}, u32[]{:S(2)}) collective-permute-start(bf16[128,6144]{1,0:T(8,128)(2,1)S(1)} %get-tuple-element.63), channel_id=1, source_target_pairs={{0,8},{1,9},{2,10},{3,11},{4,12},{5,13},{6,14},{7,15},{8,0},{9,1},... | collective-permute-start | bytes 4718600 | tf_op jit(solution)/shard_map/ppermute | solution.py:39
  26.8 3.3 %collective-permute-done.4 = bf16[32,6144]{1,0:T(8,128)(2,1)S(1)} collective-permute-done((bf16[32,6144]{1,0:T(8,128)(2,1)S(1)}, bf16[32,6144]{1,0:T(8,128)(2,1)S(1)}, u32[]{:S(2)}, u32[]{:S(2)}) %collective-permute-start.4) | collective-permute-done | bytes 393248 | tf_op jit(solution)/shard_map/ppermute | solution.py:88
  31.6 3.2 %collective-permute-start.11 = (bf16[64,6144]{1,0:T(8,128)(2,1)S(1)}, bf16[64,6144]{1,0:T(8,128)(2,1)S(1)}, u32[]{:S(2)}, u32[]{:S(2)}) collective-permute-start(bf16[64,6144]{1,0:T(8,128)(2,1)S(1)} %pad_maximum_fusion.3), channel_id=1, source_target_pairs={{0,7},{1,2},{2,1},{3,4},{4,3},{5,6},{6,5},{7,0},{8,15},{9,10},{10,... | collective-permute-start | bytes 2359304 | tf_op jit(solution)/shard_map/ppermute | solution.py:89
  34.9 3.4 %fusion.6 = f32[128,384]{1,0:T(8,128)S(1)} fusion(bf16[128,6144]{1,0:T(8,128)(2,1)S(1)} %constant_dynamic-update-slice_fusion, bf16[12288,384]{1,0:T(8,128)(2,1)} %bitcast.88, s32[]{:T(128)S(6)} %select_n.226), kind=kOutput, calls=%fused_computation.9 | convolution fusion | flops 603979776 | bytes 6488068 | tf_op jit(solution)/shard_map/dot_general | solution.py:195
  39.3 11.1 %collective-permute-done.10 = bf16[64,6144]{1,0:T(8,128)(2,1)S(1)} collective-permute-done((bf16[64,6144]{1,0:T(8,128)(2,1)S(1)}, bf16[64,6144]{1,0:T(8,128)(2,1)S(1)}, u32[]{:S(2)}, u32[]{:S(2)}) %collective-permute-start.10) | collective-permute-done | bytes 786464 | tf_op jit(solution)/shard_map/ppermute | solution.py:88
  52.7 2.1 %collective-permute-start.12 = (bf16[64,6144]{1,0:T(8,128)(2,1)S(1)}, bf16[64,6144]{1,0:T(8,128)(2,1)S(1)}, u32[]{:S(2)}, u32[]{:S(2)}) collective-permute-start(bf16[64,6144]{1,0:T(8,128)(2,1)S(1)} %collective-permute-done.8), channel_id=1, source_target_pairs={{0,49},{1,16},{2,19},{3,50},{4,53},{5,20},{6,23},{7,54},{8,57},{9,... | collective-permute-start | bytes 2359304 | tf_op jit(solution)/shard_map/ppermute | solution.py:88
  54.8 2.5 %collective-permute-start.13 = (bf16[64,6144]{1,0:T(8,128)(2,1)S(1)}, bf16[64,6144]{1,0:T(8,128)(2,1)S(1)}, u32[]{:S(2)}, u32[]{:S(2)}) collective-permute-start(bf16[64,6144]{1,0:T(8,128)(2,1)S(1)} %collective-permute-done.9), channel_id=1, source_target_pairs={{0,7},{1,2},{2,1},{3,4},{4,3},{5,6},{6,5},{7,0},{8,15},{9,10},{10,... | collective-permute-start | bytes 2359304 | tf_op jit(solution)/shard_map/ppermute | solution.py:89
  65.4 2.1 %collective-permute-done.13 = bf16[64,6144]{1,0:T(8,128)(2,1)S(1)} collective-permute-done((bf16[64,6144]{1,0:T(8,128)(2,1)S(1)}, bf16[64,6144]{1,0:T(8,128)(2,1)S(1)}, u32[]{:S(2)}, u32[]{:S(2)}) %collective-permute-start.13) | collective-permute-done | bytes 786464 | tf_op jit(solution)/shard_map/ppermute | solution.py:89
  72.1 2.5 %collective-permute-start.20 = (bf16[512,128]{1,0:T(8,128)(2,1)S(1)}, bf16[512,128]{1,0:T(8,128)(2,1)S(1)}, u32[]{:S(2)}, u32[]{:S(2)}) collective-permute-start(bf16[512,128]{1,0:T(8,128)(2,1)S(1)} %convolution_convert_fusion.1), channel_id=1, source_target_pairs={{0,8},{1,9},{2,10},{3,11},{4,12},{5,13},{6,14},{7,15},{8,0},{9,1},... | collective-permute-start | bytes 393224 | tf_op jit(solution)/shard_map/ppermute | solution.py:39
  75.1 4.2 %collective-permute-done.20 = bf16[512,128]{1,0:T(8,128)(2,1)S(1)} collective-permute-done((bf16[512,128]{1,0:T(8,128)(2,1)S(1)}, bf16[512,128]{1,0:T(8,128)(2,1)S(1)}, u32[]{:S(2)}, u32[]{:S(2)}) %collective-permute-start.20) | collective-permute-done | bytes 131104 | tf_op jit(solution)/shard_map/ppermute | solution.py:39
  83.4 2.9 %collective-permute-start.23 = (bf16[64,6144]{1,0:T(8,128)(2,1)S(1)}, bf16[64,6144]{1,0:T(8,128)(2,1)S(1)}, u32[]{:S(2)}, u32[]{:S(2)}) collective-permute-start(bf16[64,6144]{1,0:T(8,128)(2,1)S(1)} %get-tuple-element.68), channel_id=1, source_target_pairs={{0,7},{1,2},{2,1},{3,4},{4,3},{5,6},{6,5},{7,0},{8,15},{9,10},{10,... | collective-permute-start | bytes 2359304 | tf_op jit(solution)/shard_map/ppermute | solution.py:89
  87.3 7.4 %collective-permute-done.22 = bf16[64,6144]{1,0:T(8,128)(2,1)S(1)} collective-permute-done((bf16[64,6144]{1,0:T(8,128)(2,1)S(1)}, bf16[64,6144]{1,0:T(8,128)(2,1)S(1)}, u32[]{:S(2)}, u32[]{:S(2)}) %collective-permute-start.22) | collective-permute-done | bytes 786464 | tf_op jit(solution)/shard_map/ppermute | solution.py:88
  96.6 7.1 %collective-permute-done.24 = bf16[32,6144]{1,0:T(8,128)(2,1)S(1)} collective-permute-done((bf16[32,6144]{1,0:T(8,128)(2,1)S(1)}, bf16[32,6144]{1,0:T(8,128)(2,1)S(1)}, u32[]{:S(2)}, u32[]{:S(2)}) %collective-permute-start.24) | collective-permute-done | bytes 393248 | tf_op jit(solution)/shard_map/ppermute | solution.py:88
  104.1 3.1 %collective-permute-start.26 = (bf16[16,6144]{1,0:T(8,128)(2,1)S(1)}, bf16[16,6144]{1,0:T(8,128)(2,1)S(1)}, u32[]{:S(2)}, u32[]{:S(2)}) collective-permute-start(bf16[16,6144]{1,0:T(8,128)(2,1)S(1)} %pad_maximum_fusion.8), channel_id=1, source_target_pairs={{0,7},{1,2},{2,1},{3,4},{4,3},{5,6},{6,5},{7,0},{8,15},{9,10},{10,... | collective-permute-start | bytes 589832 | tf_op jit(solution)/shard_map/ppermute | solution.py:88
  108.4 2.2 %collective-permute-done.26 = bf16[16,6144]{1,0:T(8,128)(2,1)S(1)} collective-permute-done((bf16[16,6144]{1,0:T(8,128)(2,1)S(1)}, bf16[16,6144]{1,0:T(8,128)(2,1)S(1)}, u32[]{:S(2)}, u32[]{:S(2)}) %collective-permute-start.26) | collective-permute-done | bytes 196640 | tf_op jit(solution)/shard_map/ppermute | solution.py:88
  110.6 3.0 %collective-permute-done.27 = bf16[16,6144]{1,0:T(8,128)(2,1)S(1)} collective-permute-done((bf16[16,6144]{1,0:T(8,128)(2,1)S(1)}, bf16[16,6144]{1,0:T(8,128)(2,1)S(1)}, u32[]{:S(2)}, u32[]{:S(2)}) %collective-permute-start.27) | collective-permute-done | bytes 196640 | tf_op jit(solution)/shard_map/ppermute | solution.py:89
  114.3 3.2 %collective-permute-start.30 = (bf16[8,6144]{1,0:T(8,128)(2,1)S(1)}, bf16[8,6144]{1,0:T(8,128)(2,1)S(1)}, u32[]{:S(2)}, u32[]{:S(2)}) collective-permute-start(bf16[8,6144]{1,0:T(8,128)(2,1)S(1)} %get-tuple-element.119), channel_id=1, source_target_pairs={{0,72},{1,73},{2,74},{3,75},{4,76},{5,77},{6,78},{7,79},{8,64},{9,... | collective-permute-start | bytes 294920 | tf_op jit(solution)/shard_map/ppermute | solution.py:285
  120.5 3.8 %collective-permute-done.31 = bf16[8,6144]{1,0:T(8,128)(2,1)S(1)} collective-permute-done((bf16[8,6144]{1,0:T(8,128)(2,1)S(1)}, bf16[8,6144]{1,0:T(8,128)(2,1)S(1)}, u32[]{:S(2)}, u32[]{:S(2)}) %collective-permute-start.31) | collective-permute-done | bytes 98336 | tf_op jit(solution)/shard_map/ppermute | solution.py:285
  (117 shorter events, 37.5 us)
Async XLA Ops:
  1.4 5.9 %collective-permute-start = (bf16[8,6144]{1,0:T(8,128)(2,1)S(1)}, bf16[8,6144]{1,0:T(8,128)(2,1)S(1)}, u32[]{:S(2)}, u32[]{:S(2)}) collective-permute-start(bf16[8,6144]{1,0:T(8,128)(2,1)S(1)} %get-tuple-element.44), channel_id=1, source_target_pairs={{0,1},{1,0},{2,3},{3,2},{4,5},{5,4},{6,7},{7,6},{8,9},{9,8},{10,11... | collective-permute-start | bytes 294920 | tf_op jit(solution)/shard_map/ppermute | solution.py:39
  1.5 9.6 %collective-permute-start.2 = (bf16[8,6144]{1,0:T(8,128)(2,1)S(1)}, bf16[8,6144]{1,0:T(8,128)(2,1)S(1)}, u32[]{:S(2)}, u32[]{:S(2)}) collective-permute-start(bf16[8,6144]{1,0:T(8,128)(2,1)S(1)} %get-tuple-element.44), channel_id=1, source_target_pairs={{0,9},{1,8},{2,11},{3,10},{4,13},{5,12},{6,15},{7,14},{8,1},{9,0},... | collective-permute-start | bytes 294920 | tf_op jit(solution)/shard_map/ppermute | solution.py:39
  4.7 6.4 %collective-permute-start.1 = (bf16[8,6144]{1,0:T(8,128)(2,1)S(1)}, bf16[8,6144]{1,0:T(8,128)(2,1)}, u32[]{:S(2)}, u32[]{:S(2)}) collective-permute-start(bf16[8,6144]{1,0:T(8,128)(2,1)S(1)} %get-tuple-element.43), channel_id=1, source_target_pairs={{0,8},{1,9},{2,10},{3,11},{4,12},{5,13},{6,14},{7,15},{8,0},{9,1},... | collective-permute-start | bytes 294920 | tf_op jit(solution)/shard_map/ppermute | solution.py:39
  12.1 5.2 %collective-permute-start.5 = (bf16[16,6144]{1,0:T(8,128)(2,1)S(1)}, bf16[16,6144]{1,0:T(8,128)(2,1)S(1)}, u32[]{:S(2)}, u32[]{:S(2)}) collective-permute-start(bf16[16,6144]{1,0:T(8,128)(2,1)S(1)} %get-tuple-element.107), channel_id=1, source_target_pairs={{0,17},{1,48},{2,51},{3,18},{4,21},{5,52},{6,55},{7,22},{8,25},{9,... | collective-permute-start | bytes 589832 | tf_op jit(solution)/shard_map/ppermute | solution.py:89
  13.0 17.2 %collective-permute-start.7 = (bf16[6144,384]{1,0:T(8,128)(2,1)S(1)}, bf16[6144,384]{1,0:T(8,128)(2,1)S(1)}, u32[]{:S(2)}, u32[]{:S(2)}) collective-permute-start(bf16[6144,384]{1,0:T(8,128)(2,1)S(1)} %constant_dynamic-slice_fusion.2), channel_id=1, source_target_pairs={{0,1},{1,0},{2,3},{3,2},{4,5},{5,4},{6,7},{7,6},{8,9},{9,8},{10,11... | collective-permute-start | bytes 14155784 | tf_op jit(solution)/shard_map/ppermute | solution.py:39
  17.4 9.4 %collective-permute-start.6 = (bf16[32,6144]{1,0:T(8,128)(2,1)S(1)}, bf16[32,6144]{1,0:T(8,128)(2,1)S(1)}, u32[]{:S(2)}, u32[]{:S(2)}) collective-permute-start(bf16[32,6144]{1,0:T(8,128)(2,1)S(1)} %pad_maximum_fusion.6), channel_id=1, source_target_pairs={{0,49},{1,16},{2,19},{3,50},{4,53},{5,20},{6,23},{7,54},{8,57},{9,... | collective-permute-start | bytes 1179656 | tf_op jit(solution)/shard_map/ppermute | solution.py:89
  21.6 8.5 %collective-permute-start.4 = (bf16[32,6144]{1,0:T(8,128)(2,1)S(1)}, bf16[32,6144]{1,0:T(8,128)(2,1)S(1)}, u32[]{:S(2)}, u32[]{:S(2)}) collective-permute-start(bf16[32,6144]{1,0:T(8,128)(2,1)S(1)} %pad_maximum_fusion.5), channel_id=1, source_target_pairs={{0,7},{1,2},{2,1},{3,4},{4,3},{5,6},{6,5},{7,0},{8,15},{9,10},{10,... | collective-permute-start | bytes 1179656 | tf_op jit(solution)/shard_map/ppermute | solution.py:88
  24.3 38.3 %collective-permute-start.18 = (bf16[128,6144]{1,0:T(8,128)(2,1)S(1)}, bf16[128,6144]{1,0:T(8,128)(2,1)S(1)}, u32[]{:S(2)}, u32[]{:S(2)}) collective-permute-start(bf16[128,6144]{1,0:T(8,128)(2,1)S(1)} %get-tuple-element.63), channel_id=1, source_target_pairs={{0,8},{1,9},{2,10},{3,11},{4,12},{5,13},{6,14},{7,15},{8,0},{9,1},... | collective-permute-start | bytes 4718600 | tf_op jit(solution)/shard_map/ppermute | solution.py:39
  30.3 20.2 %collective-permute-start.10 = (bf16[64,6144]{1,0:T(8,128)(2,1)S(1)}, bf16[64,6144]{1,0:T(8,128)(2,1)S(1)}, u32[]{:S(2)}, u32[]{:S(2)}) collective-permute-start(bf16[64,6144]{1,0:T(8,128)(2,1)S(1)} %pad_maximum_fusion.2), channel_id=1, source_target_pairs={{0,49},{1,16},{2,19},{3,50},{4,53},{5,20},{6,23},{7,54},{8,57},{9,... | collective-permute-start | bytes 2359304 | tf_op jit(solution)/shard_map/ppermute | solution.py:88
  31.1 21.4 %collective-permute-start.8 = (bf16[64,6144]{1,0:T(8,128)(2,1)S(1)}, bf16[64,6144]{1,0:T(8,128)(2,1)S(1)}, u32[]{:S(2)}, u32[]{:S(2)}) collective-permute-start(bf16[64,6144]{1,0:T(8,128)(2,1)S(1)} %pad_maximum_fusion.2), channel_id=1, source_target_pairs={{0,17},{1,48},{2,51},{3,18},{4,21},{5,52},{6,55},{7,22},{8,25},{9,... | collective-permute-start | bytes 2359304 | tf_op jit(solution)/shard_map/ppermute | solution.py:88
  31.6 20.9 %collective-permute-start.11 = (bf16[64,6144]{1,0:T(8,128)(2,1)S(1)}, bf16[64,6144]{1,0:T(8,128)(2,1)S(1)}, u32[]{:S(2)}, u32[]{:S(2)}) collective-permute-start(bf16[64,6144]{1,0:T(8,128)(2,1)S(1)} %pad_maximum_fusion.3), channel_id=1, source_target_pairs={{0,7},{1,2},{2,1},{3,4},{4,3},{5,6},{6,5},{7,0},{8,15},{9,10},{10,... | collective-permute-start | bytes 2359304 | tf_op jit(solution)/shard_map/ppermute | solution.py:89
  34.8 17.8 %collective-permute-start.9 = (bf16[64,6144]{1,0:T(8,128)(2,1)S(1)}, bf16[64,6144]{1,0:T(8,128)(2,1)S(1)}, u32[]{:S(2)}, u32[]{:S(2)}) collective-permute-start(bf16[64,6144]{1,0:T(8,128)(2,1)S(1)} %pad_maximum_fusion.3), channel_id=1, source_target_pairs={{0,3},{1,6},{2,5},{3,0},{4,7},{5,2},{6,1},{7,4},{8,11},{9,14},{10,... | collective-permute-start | bytes 2359304 | tf_op jit(solution)/shard_map/ppermute | solution.py:89
  52.7 12.7 %collective-permute-start.12 = (bf16[64,6144]{1,0:T(8,128)(2,1)S(1)}, bf16[64,6144]{1,0:T(8,128)(2,1)S(1)}, u32[]{:S(2)}, u32[]{:S(2)}) collective-permute-start(bf16[64,6144]{1,0:T(8,128)(2,1)S(1)} %collective-permute-done.8), channel_id=1, source_target_pairs={{0,49},{1,16},{2,19},{3,50},{4,53},{5,20},{6,23},{7,54},{8,57},{9,... | collective-permute-start | bytes 2359304 | tf_op jit(solution)/shard_map/ppermute | solution.py:88
  54.8 12.7 %collective-permute-start.13 = (bf16[64,6144]{1,0:T(8,128)(2,1)S(1)}, bf16[64,6144]{1,0:T(8,128)(2,1)S(1)}, u32[]{:S(2)}, u32[]{:S(2)}) collective-permute-start(bf16[64,6144]{1,0:T(8,128)(2,1)S(1)} %collective-permute-done.9), channel_id=1, source_target_pairs={{0,7},{1,2},{2,1},{3,4},{4,3},{5,6},{6,5},{7,0},{8,15},{9,10},{10,... | collective-permute-start | bytes 2359304 | tf_op jit(solution)/shard_map/ppermute | solution.py:89
  63.0 11.6 %collective-permute-start.19 = (bf16[256,6144]{1,0:T(8,128)(2,1)S(1)}, bf16[256,6144]{1,0:T(8,128)(2,1)S(1)}, u32[]{:S(2)}, u32[]{:S(2)}) collective-permute-start(bf16[256,6144]{1,0:T(8,128)(2,1)S(1)} %pad_maximum_fusion.1), channel_id=1, source_target_pairs={{0,1},{1,0},{2,3},{3,2},{4,5},{5,4},{6,7},{7,6},{8,9},{9,8},{10,11... | collective-permute-start | bytes 9437192 | tf_op jit(solution)/shard_map/ppermute | solution.py:39
  72.1 7.1 %collective-permute-start.20 = (bf16[512,128]{1,0:T(8,128)(2,1)S(1)}, bf16[512,128]{1,0:T(8,128)(2,1)S(1)}, u32[]{:S(2)}, u32[]{:S(2)}) collective-permute-start(bf16[512,128]{1,0:T(8,128)(2,1)S(1)} %convolution_convert_fusion.1), channel_id=1, source_target_pairs={{0,8},{1,9},{2,10},{3,11},{4,12},{5,13},{6,14},{7,15},{8,0},{9,1},... | collective-permute-start | bytes 393224 | tf_op jit(solution)/shard_map/ppermute | solution.py:39
  82.0 12.7 %collective-permute-start.22 = (bf16[64,6144]{1,0:T(8,128)(2,1)S(1)}, bf16[64,6144]{1,0:T(8,128)(2,1)S(1)}, u32[]{:S(2)}, u32[]{:S(2)}) collective-permute-start(bf16[64,6144]{1,0:T(8,128)(2,1)S(1)} %get-tuple-element.67), channel_id=1, source_target_pairs={{0,49},{1,16},{2,19},{3,50},{4,53},{5,20},{6,23},{7,54},{8,57},{9,... | collective-permute-start | bytes 2359304 | tf_op jit(solution)/shard_map/ppermute | solution.py:88
  83.4 12.6 %collective-permute-start.23 = (bf16[64,6144]{1,0:T(8,128)(2,1)S(1)}, bf16[64,6144]{1,0:T(8,128)(2,1)S(1)}, u32[]{:S(2)}, u32[]{:S(2)}) collective-permute-start(bf16[64,6144]{1,0:T(8,128)(2,1)S(1)} %get-tuple-element.68), channel_id=1, source_target_pairs={{0,7},{1,2},{2,1},{3,4},{4,3},{5,6},{6,5},{7,0},{8,15},{9,10},{10,... | collective-permute-start | bytes 2359304 | tf_op jit(solution)/shard_map/ppermute | solution.py:89
  96.4 7.3 %collective-permute-start.24 = (bf16[32,6144]{1,0:T(8,128)(2,1)S(1)}, bf16[32,6144]{1,0:T(8,128)(2,1)S(1)}, u32[]{:S(2)}, u32[]{:S(2)}) collective-permute-start(bf16[32,6144]{1,0:T(8,128)(2,1)S(1)} %slice.303), channel_id=1, source_target_pairs={{0,17},{1,48},{2,51},{3,18},{4,21},{5,52},{6,55},{7,22},{8,25},{9,... | collective-permute-start | bytes 1179656 | tf_op jit(solution)/shard_map/ppermute | solution.py:88
  96.5 7.3 %collective-permute-start.25 = (bf16[32,6144]{1,0:T(8,128)(2,1)S(1)}, bf16[32,6144]{1,0:T(8,128)(2,1)S(1)}, u32[]{:S(2)}, u32[]{:S(2)}) collective-permute-start(bf16[32,6144]{1,0:T(8,128)(2,1)S(1)} %slice.302), channel_id=1, source_target_pairs={{0,3},{1,6},{2,5},{3,0},{4,7},{5,2},{6,1},{7,4},{8,11},{9,14},{10,... | collective-permute-start | bytes 1179656 | tf_op jit(solution)/shard_map/ppermute | solution.py:89
  104.1 6.4 %collective-permute-start.26 = (bf16[16,6144]{1,0:T(8,128)(2,1)S(1)}, bf16[16,6144]{1,0:T(8,128)(2,1)S(1)}, u32[]{:S(2)}, u32[]{:S(2)}) collective-permute-start(bf16[16,6144]{1,0:T(8,128)(2,1)S(1)} %pad_maximum_fusion.8), channel_id=1, source_target_pairs={{0,7},{1,2},{2,1},{3,4},{4,3},{5,6},{6,5},{7,0},{8,15},{9,10},{10,... | collective-permute-start | bytes 589832 | tf_op jit(solution)/shard_map/ppermute | solution.py:88
  107.2 6.3 %collective-permute-start.27 = (bf16[16,6144]{1,0:T(8,128)(2,1)S(1)}, bf16[16,6144]{1,0:T(8,128)(2,1)S(1)}, u32[]{:S(2)}, u32[]{:S(2)}) collective-permute-start(bf16[16,6144]{1,0:T(8,128)(2,1)S(1)} %pad_maximum_fusion.9), channel_id=1, source_target_pairs={{0,49},{1,16},{2,19},{3,50},{4,53},{5,20},{6,23},{7,54},{8,57},{9,... | collective-permute-start | bytes 589832 | tf_op jit(solution)/shard_map/ppermute | solution.py:89
  114.3 6.2 %collective-permute-start.30 = (bf16[8,6144]{1,0:T(8,128)(2,1)S(1)}, bf16[8,6144]{1,0:T(8,128)(2,1)S(1)}, u32[]{:S(2)}, u32[]{:S(2)}) collective-permute-start(bf16[8,6144]{1,0:T(8,128)(2,1)S(1)} %get-tuple-element.119), channel_id=1, source_target_pairs={{0,72},{1,73},{2,74},{3,75},{4,76},{5,77},{6,78},{7,79},{8,64},{9,... | collective-permute-start | bytes 294920 | tf_op jit(solution)/shard_map/ppermute | solution.py:285
  117.5 6.7 %collective-permute-start.31 = (bf16[8,6144]{1,0:T(8,128)(2,1)S(1)}, bf16[8,6144]{1,0:T(8,128)(2,1)S(1)}, u32[]{:S(2)}, u32[]{:S(2)}) collective-permute-start(bf16[8,6144]{1,0:T(8,128)(2,1)S(1)} %get-tuple-element.120), channel_id=1, source_target_pairs={{0,89},{1,120},{2,123},{3,90},{4,93},{5,124},{6,127},{7,94},{8,67}... | collective-permute-start | bytes 294920 | tf_op jit(solution)/shard_map/ppermute | solution.py:285
  (16 other events, 79.7 us)

commit v14 on v13

--- a/solution.py
+++ b/solution.py
@@ -184,7 +184,7 @@
     first_own = near_rows(first, one[0], two[0], role)
     second_own = near_rows(second, one[1], two[1], role)
 
-    out_rows, _ = lax.optimization_barrier((output_weights[0], block))
+    out_rows, _ = lax.optimization_barrier((output_weights[0], first))
     out_kept = lax.dynamic_slice_in_dim(out_rows, half_x * half, half, 1)
     out_given = lax.dynamic_slice_in_dim(out_rows, (1 - half_x) * half, half, 1)
     out_given, _ = lax.optimization_barrier((out_given, one))

time: 125 us -> 124 us (level)
  waiting for transfers between devices: 55.4 us -> 58.1 us
  matrix products: 14.3 us -> 12 us
  local copies, waits for them, and re-layouts: 5.6 us -> 3.88 us
    ppermute x12, starting transfers between devices: 13.7 us -> 10.2 us  [send(): return lax.ppermute(value, AXES, pairs)]
    dot_general x4, matrix products: 6.54 us -> 4.19 us  [project(): mine = jnp.dot(rows, own_weights, preferred_element_type=jnp.float32)]
    ppermute x8, starting transfers between devices: 11 us -> 13.2 us  [swap_both(): lax.ppermute(first, AXES, swap_pairs(first_axis, turn))]
    dynamic_slice x1, local copies, waits for them, and re-layouts: 2.08 us -> 0.25 us  [shards(): out_kept = lax.dynamic_slice_in_dim(out_rows, half_x * half, half, 1)]
  transfers between devices with their start and end apart: 32 -> 32, of which waited for: 21 -> 20; matrix products, arithmetic and copies ran while one was open for 16% -> 14% of each run, Pallas kernels for 0% -> 0%
where the time goes in v14:
time: 124 us; the launch traced here: 123 us
  waiting for transfers between devices  58.1 us (47%)
  starting transfers between devices  43.1 us (35%)
  matrix products  12 us (10%)
  other arithmetic  3.93 us (3%)
  local copies, waits for them, and re-layouts  3.88 us (3%)
  Pallas kernels  1.36 us (1%)
    ppermute x8, waiting for transfers between devices, swap_both(): lax.ppermute(first, AXES, swap_pairs(first_axis, turn))  34.8 us
    ppermute x8, starting transfers between devices, swap_both(): lax.ppermute(second, AXES, swap_pairs(second_axis, turn))  14.7 us
    ppermute x8, starting transfers between devices, swap_both(): lax.ppermute(first, AXES, swap_pairs(first_axis, turn))  13.2 us
    ppermute x12, starting transfers between devices, send(): return lax.ppermute(value, AXES, pairs)  10.2 us
    ppermute x8, waiting for transfers between devices, swap_both(): lax.ppermute(second, AXES, swap_pairs(second_axis, turn))  9.86 us
    ppermute x12, waiting for transfers between devices, send(): return lax.ppermute(value, AXES, pairs)  8.07 us
    ppermute x4, waiting for transfers between devices, shards(): lax.ppermute(pairs_of[crossed][near], AXES, owner_pairs(crossed, near))  5.34 us
    ppermute x4, starting transfers between devices, shards(): lax.ppermute(pairs_of[crossed][near], AXES, owner_pairs(crossed, near))  5.01 us
  transfers between devices with their start and end apart: 32, of which 20 were waited for; matrix products, arithmetic and copies ran while one was open for 14% of the time, Pallas kernels for 0%

profile of v14, /device:TPU:0, one launch (start us, length us, event | category | flops | bytes accessed | tf_op | source)
XLA Modules:
  0.0 122.9 jit_solution(2821216380430316155)
XLA Ops:
  1.5 3.2 %collective-permute-start.2 = (bf16[8,6144]{1,0:T(8,128)(2,1)S(1)}, bf16[8,6144]{1,0:T(8,128)(2,1)S(1)}, u32[]{:S(2)}, u32[]{:S(2)}) collective-permute-start(bf16[8,6144]{1,0:T(8,128)(2,1)S(1)} %get-tuple-element.44), channel_id=1, source_target_pairs={{0,9},{1,8},{2,11},{3,10},{4,13},{5,12},{6,15},{7,14},{8,1},{9,0},... | collective-permute-start | bytes 294920 | tf_op jit(solution)/shard_map/ppermute | solution.py:39
  5.9 3.0 %constant_dynamic-slice_fusion.2 = bf16[6144,384]{1,0:T(8,128)(2,1)S(1)} fusion(bf16[12288,384]{1,0:T(8,128)(2,1)} %bitcast.87, s32[]{:T(128)S(6)} %select_n.217), kind=kLoop, calls=%fused_computation.118 | loop fusion | bytes 9437188 | tf_op jit(solution)/shard_map/dynamic_slice | solution.py:172
  8.9 2.0 %collective-permute-done.1 = bf16[8,6144]{1,0:T(8,128)(2,1)S(1)} collective-permute-done((bf16[8,6144]{1,0:T(8,128)(2,1)S(1)}, bf16[8,6144]{1,0:T(8,128)(2,1)S(1)}, u32[]{:S(2)}, u32[]{:S(2)}) %collective-permute-start.1) | collective-permute-done | bytes 98336 | tf_op jit(solution)/shard_map/ppermute | solution.py:39
  11.9 2.5 %collective-permute-start.3 = (bf16[16,6144]{1,0:T(8,128)(2,1)S(1)}, bf16[16,6144]{1,0:T(8,128)(2,1)S(1)}, u32[]{:S(2)}, u32[]{:S(2)}) collective-permute-start(bf16[16,6144]{1,0:T(8,128)(2,1)S(1)} %get-tuple-element.108), channel_id=1, source_target_pairs={{0,3},{1,6},{2,5},{3,0},{4,7},{5,2},{6,1},{7,4},{8,11},{9,14},{10,... | collective-permute-start | bytes 589832 | tf_op jit(solution)/shard_map/ppermute | solution.py:88
  14.6 1.6 %collective-permute-done.5 = bf16[16,6144]{1,0:T(8,128)(2,1)S(1)} collective-permute-done((bf16[16,6144]{1,0:T(8,128)(2,1)S(1)}, bf16[16,6144]{1,0:T(8,128)(2,1)S(1)}, u32[]{:S(2)}, u32[]{:S(2)}) %collective-permute-start.5) | collective-permute-done | bytes 196640 | tf_op jit(solution)/shard_map/ppermute | solution.py:89
  16.3 3.3 %collective-permute-start.6 = (bf16[32,6144]{1,0:T(8,128)(2,1)S(1)}, bf16[32,6144]{1,0:T(8,128)(2,1)S(1)}, u32[]{:S(2)}, u32[]{:S(2)}) collective-permute-start(bf16[32,6144]{1,0:T(8,128)(2,1)S(1)} %pad_maximum_fusion.6), channel_id=1, source_target_pairs={{0,49},{1,16},{2,19},{3,50},{4,53},{5,20},{6,23},{7,54},{8,57},{9,... | collective-permute-start | bytes 1179656 | tf_op jit(solution)/shard_map/ppermute | solution.py:89
  19.6 3.7 %collective-permute-start.4 = (bf16[32,6144]{1,0:T(8,128)(2,1)S(1)}, bf16[32,6144]{1,0:T(8,128)(2,1)S(1)}, u32[]{:S(2)}, u32[]{:S(2)}) collective-permute-start(bf16[32,6144]{1,0:T(8,128)(2,1)S(1)} %pad_maximum_fusion.5), channel_id=1, source_target_pairs={{0,7},{1,2},{2,1},{3,4},{4,3},{5,6},{6,5},{7,0},{8,15},{9,10},{10,... | collective-permute-start | bytes 1179656 | tf_op jit(solution)/shard_map/ppermute | solution.py:88
  23.3 2.4 %collective-permute-start.18 = (bf16[128,6144]{1,0:T(8,128)(2,1)S(1)}, bf16[128,6144]{1,0:T(8,128)(2,1)S(1)}, u32[]{:S(2)}, u32[]{:S(2)}) collective-permute-start(bf16[128,6144]{1,0:T(8,128)(2,1)S(1)} %get-tuple-element.63), channel_id=1, source_target_pairs={{0,8},{1,9},{2,10},{3,11},{4,12},{5,13},{6,14},{7,15},{8,0},{9,1},... | collective-permute-start | bytes 4718600 | tf_op jit(solution)/shard_map/ppermute | solution.py:39
  25.8 3.0 %collective-permute-done.4 = bf16[32,6144]{1,0:T(8,128)(2,1)S(1)} collective-permute-done((bf16[32,6144]{1,0:T(8,128)(2,1)S(1)}, bf16[32,6144]{1,0:T(8,128)(2,1)S(1)}, u32[]{:S(2)}, u32[]{:S(2)}) %collective-permute-start.4) | collective-permute-done | bytes 393248 | tf_op jit(solution)/shard_map/ppermute | solution.py:88
  30.0 3.2 %collective-permute-start.11 = (bf16[64,6144]{1,0:T(8,128)(2,1)S(1)}, bf16[64,6144]{1,0:T(8,128)(2,1)S(1)}, u32[]{:S(2)}, u32[]{:S(2)}) collective-permute-start(bf16[64,6144]{1,0:T(8,128)(2,1)S(1)} %pad_maximum_fusion.3), channel_id=1, source_target_pairs={{0,7},{1,2},{2,1},{3,4},{4,3},{5,6},{6,5},{7,0},{8,15},{9,10},{10,... | collective-permute-start | bytes 2359304 | tf_op jit(solution)/shard_map/ppermute | solution.py:89
  35.4 13.5 %collective-permute-done.10 = bf16[64,6144]{1,0:T(8,128)(2,1)S(1)} collective-permute-done((bf16[64,6144]{1,0:T(8,128)(2,1)S(1)}, bf16[64,6144]{1,0:T(8,128)(2,1)S(1)}, u32[]{:S(2)}, u32[]{:S(2)}) %collective-permute-start.10) | collective-permute-done | bytes 786464 | tf_op jit(solution)/shard_map/ppermute | solution.py:88
  51.4 2.2 %collective-permute-start.12 = (bf16[64,6144]{1,0:T(8,128)(2,1)S(1)}, bf16[64,6144]{1,0:T(8,128)(2,1)S(1)}, u32[]{:S(2)}, u32[]{:S(2)}) collective-permute-start(bf16[64,6144]{1,0:T(8,128)(2,1)S(1)} %collective-permute-done.8), channel_id=1, source_target_pairs={{0,49},{1,16},{2,19},{3,50},{4,53},{5,20},{6,23},{7,54},{8,57},{9,... | collective-permute-start | bytes 2359304 | tf_op jit(solution)/shard_map/ppermute | solution.py:88
  53.7 2.8 %collective-permute-start.13 = (bf16[64,6144]{1,0:T(8,128)(2,1)S(1)}, bf16[64,6144]{1,0:T(8,128)(2,1)S(1)}, u32[]{:S(2)}, u32[]{:S(2)}) collective-permute-start(bf16[64,6144]{1,0:T(8,128)(2,1)S(1)} %collective-permute-done.9), channel_id=1, source_target_pairs={{0,7},{1,2},{2,1},{3,4},{4,3},{5,6},{6,5},{7,0},{8,15},{9,10},{10,... | collective-permute-start | bytes 2359304 | tf_op jit(solution)/shard_map/ppermute | solution.py:89
  64.1 2.3 %collective-permute-done.13 = bf16[64,6144]{1,0:T(8,128)(2,1)S(1)} collective-permute-done((bf16[64,6144]{1,0:T(8,128)(2,1)S(1)}, bf16[64,6144]{1,0:T(8,128)(2,1)S(1)}, u32[]{:S(2)}, u32[]{:S(2)}) %collective-permute-start.13) | collective-permute-done | bytes 786464 | tf_op jit(solution)/shard_map/ppermute | solution.py:89
  71.0 2.3 %collective-permute-start.20 = (bf16[512,128]{1,0:T(8,128)(2,1)S(1)}, bf16[512,128]{1,0:T(8,128)(2,1)S(1)}, u32[]{:S(2)}, u32[]{:S(2)}) collective-permute-start(bf16[512,128]{1,0:T(8,128)(2,1)S(1)} %convolution_convert_fusion.1), channel_id=1, source_target_pairs={{0,8},{1,9},{2,10},{3,11},{4,12},{5,13},{6,14},{7,15},{8,0},{9,1},... | collective-permute-start | bytes 393224 | tf_op jit(solution)/shard_map/ppermute | solution.py:39
  73.8 4.3 %collective-permute-done.20 = bf16[512,128]{1,0:T(8,128)(2,1)S(1)} collective-permute-done((bf16[512,128]{1,0:T(8,128)(2,1)S(1)}, bf16[512,128]{1,0:T(8,128)(2,1)S(1)}, u32[]{:S(2)}, u32[]{:S(2)}) %collective-permute-start.20) | collective-permute-done | bytes 131104 | tf_op jit(solution)/shard_map/ppermute | solution.py:39
  81.8 2.3 %collective-permute-start.23 = (bf16[64,6144]{1,0:T(8,128)(2,1)S(1)}, bf16[64,6144]{1,0:T(8,128)(2,1)S(1)}, u32[]{:S(2)}, u32[]{:S(2)}) collective-permute-start(bf16[64,6144]{1,0:T(8,128)(2,1)S(1)} %get-tuple-element.68), channel_id=1, source_target_pairs={{0,7},{1,2},{2,1},{3,4},{4,3},{5,6},{6,5},{7,0},{8,15},{9,10},{10,... | collective-permute-start | bytes 2359304 | tf_op jit(solution)/shard_map/ppermute | solution.py:89
  85.1 8.4 %collective-permute-done.22 = bf16[64,6144]{1,0:T(8,128)(2,1)S(1)} collective-permute-done((bf16[64,6144]{1,0:T(8,128)(2,1)S(1)}, bf16[64,6144]{1,0:T(8,128)(2,1)S(1)}, u32[]{:S(2)}, u32[]{:S(2)}) %collective-permute-start.22) | collective-permute-done | bytes 786464 | tf_op jit(solution)/shard_map/ppermute | solution.py:88
  95.1 7.1 %collective-permute-done.24 = bf16[32,6144]{1,0:T(8,128)(2,1)S(1)} collective-permute-done((bf16[32,6144]{1,0:T(8,128)(2,1)S(1)}, bf16[32,6144]{1,0:T(8,128)(2,1)S(1)}, u32[]{:S(2)}, u32[]{:S(2)}) %collective-permute-start.24) | collective-permute-done | bytes 393248 | tf_op jit(solution)/shard_map/ppermute | solution.py:88
  102.5 2.7 %collective-permute-start.26 = (bf16[16,6144]{1,0:T(8,128)(2,1)S(1)}, bf16[16,6144]{1,0:T(8,128)(2,1)S(1)}, u32[]{:S(2)}, u32[]{:S(2)}) collective-permute-start(bf16[16,6144]{1,0:T(8,128)(2,1)S(1)} %pad_maximum_fusion.8), channel_id=1, source_target_pairs={{0,7},{1,2},{2,1},{3,4},{4,3},{5,6},{6,5},{7,0},{8,15},{9,10},{10,... | collective-permute-start | bytes 589832 | tf_op jit(solution)/shard_map/ppermute | solution.py:88
  105.2 2.2 %collective-permute-start.27 = (bf16[16,6144]{1,0:T(8,128)(2,1)S(1)}, bf16[16,6144]{1,0:T(8,128)(2,1)S(1)}, u32[]{:S(2)}, u32[]{:S(2)}) collective-permute-start(bf16[16,6144]{1,0:T(8,128)(2,1)S(1)} %pad_maximum_fusion.9), channel_id=1, source_target_pairs={{0,49},{1,16},{2,19},{3,50},{4,53},{5,20},{6,23},{7,54},{8,57},{9,... | collective-permute-start | bytes 589832 | tf_op jit(solution)/shard_map/ppermute | solution.py:89
  108.9 2.6 %collective-permute-done.27 = bf16[16,6144]{1,0:T(8,128)(2,1)S(1)} collective-permute-done((bf16[16,6144]{1,0:T(8,128)(2,1)S(1)}, bf16[16,6144]{1,0:T(8,128)(2,1)S(1)}, u32[]{:S(2)}, u32[]{:S(2)}) %collective-permute-start.27) | collective-permute-done | bytes 196640 | tf_op jit(solution)/shard_map/ppermute | solution.py:89
  112.3 3.2 %collective-permute-start.30 = (bf16[8,6144]{1,0:T(8,128)(2,1)S(1)}, bf16[8,6144]{1,0:T(8,128)(2,1)S(1)}, u32[]{:S(2)}, u32[]{:S(2)}) collective-permute-start(bf16[8,6144]{1,0:T(8,128)(2,1)S(1)} %get-tuple-element.119), channel_id=1, source_target_pairs={{0,72},{1,73},{2,74},{3,75},{4,76},{5,77},{6,78},{7,79},{8,64},{9,... | collective-permute-start | bytes 294920 | tf_op jit(solution)/shard_map/ppermute | solution.py:285
  118.9 3.2 %collective-permute-done.31 = bf16[8,6144]{1,0:T(8,128)(2,1)S(1)} collective-permute-done((bf16[8,6144]{1,0:T(8,128)(2,1)S(1)}, bf16[8,6144]{1,0:T(8,128)(2,1)S(1)}, u32[]{:S(2)}, u32[]{:S(2)}) %collective-permute-start.31) | collective-permute-done | bytes 98336 | tf_op jit(solution)/shard_map/ppermute | solution.py:285
  (111 shorter events, 35.3 us)
Async XLA Ops:
  1.5 9.5 %collective-permute-start.2 = (bf16[8,6144]{1,0:T(8,128)(2,1)S(1)}, bf16[8,6144]{1,0:T(8,128)(2,1)S(1)}, u32[]{:S(2)}, u32[]{:S(2)}) collective-permute-start(bf16[8,6144]{1,0:T(8,128)(2,1)S(1)} %get-tuple-element.44), channel_id=1, source_target_pairs={{0,9},{1,8},{2,11},{3,10},{4,13},{5,12},{6,15},{7,14},{8,1},{9,0},... | collective-permute-start | bytes 294920 | tf_op jit(solution)/shard_map/ppermute | solution.py:39
  4.7 6.3 %collective-permute-start.1 = (bf16[8,6144]{1,0:T(8,128)(2,1)S(1)}, bf16[8,6144]{1,0:T(8,128)(2,1)S(1)}, u32[]{:S(2)}, u32[]{:S(2)}) collective-permute-start(bf16[8,6144]{1,0:T(8,128)(2,1)S(1)} %get-tuple-element.43), channel_id=1, source_target_pairs={{0,8},{1,9},{2,10},{3,11},{4,12},{5,13},{6,14},{7,15},{8,0},{9,1},... | collective-permute-start | bytes 294920 | tf_op jit(solution)/shard_map/ppermute | solution.py:39
  8.9 20.0 %collective-permute-start.7 = (bf16[6144,384]{1,0:T(8,128)(2,1)S(1)}, bf16[6144,384]{1,0:T(8,128)(2,1)S(1)}, u32[]{:S(2)}, u32[]{:S(2)}) collective-permute-start(bf16[6144,384]{1,0:T(8,128)(2,1)S(1)} %constant_dynamic-slice_fusion.2), channel_id=1, source_target_pairs={{0,1},{1,0},{2,3},{3,2},{4,5},{5,4},{6,7},{7,6},{8,9},{9,8},{10,11... | collective-permute-start | bytes 14155784 | tf_op jit(solution)/shard_map/ppermute | solution.py:39
  11.1 5.2 %collective-permute-start.5 = (bf16[16,6144]{1,0:T(8,128)(2,1)S(1)}, bf16[16,6144]{1,0:T(8,128)(2,1)S(1)}, u32[]{:S(2)}, u32[]{:S(2)}) collective-permute-start(bf16[16,6144]{1,0:T(8,128)(2,1)S(1)} %get-tuple-element.107), channel_id=1, source_target_pairs={{0,17},{1,48},{2,51},{3,18},{4,21},{5,52},{6,55},{7,22},{8,25},{9,... | collective-permute-start | bytes 589832 | tf_op jit(solution)/shard_map/ppermute | solution.py:89
  11.9 7.6 %collective-permute-start.3 = (bf16[16,6144]{1,0:T(8,128)(2,1)S(1)}, bf16[16,6144]{1,0:T(8,128)(2,1)S(1)}, u32[]{:S(2)}, u32[]{:S(2)}) collective-permute-start(bf16[16,6144]{1,0:T(8,128)(2,1)S(1)} %get-tuple-element.108), channel_id=1, source_target_pairs={{0,3},{1,6},{2,5},{3,0},{4,7},{5,2},{6,1},{7,4},{8,11},{9,14},{10,... | collective-permute-start | bytes 589832 | tf_op jit(solution)/shard_map/ppermute | solution.py:88
  16.3 9.4 %collective-permute-start.6 = (bf16[32,6144]{1,0:T(8,128)(2,1)S(1)}, bf16[32,6144]{1,0:T(8,128)(2,1)S(1)}, u32[]{:S(2)}, u32[]{:S(2)}) collective-permute-start(bf16[32,6144]{1,0:T(8,128)(2,1)S(1)} %pad_maximum_fusion.6), channel_id=1, source_target_pairs={{0,49},{1,16},{2,19},{3,50},{4,53},{5,20},{6,23},{7,54},{8,57},{9,... | collective-permute-start | bytes 1179656 | tf_op jit(solution)/shard_map/ppermute | solution.py:89
  19.6 9.1 %collective-permute-start.4 = (bf16[32,6144]{1,0:T(8,128)(2,1)S(1)}, bf16[32,6144]{1,0:T(8,128)(2,1)S(1)}, u32[]{:S(2)}, u32[]{:S(2)}) collective-permute-start(bf16[32,6144]{1,0:T(8,128)(2,1)S(1)} %pad_maximum_fusion.5), channel_id=1, source_target_pairs={{0,7},{1,2},{2,1},{3,4},{4,3},{5,6},{6,5},{7,0},{8,15},{9,10},{10,... | collective-permute-start | bytes 1179656 | tf_op jit(solution)/shard_map/ppermute | solution.py:88
  23.3 38.6 %collective-permute-start.18 = (bf16[128,6144]{1,0:T(8,128)(2,1)S(1)}, bf16[128,6144]{1,0:T(8,128)(2,1)S(1)}, u32[]{:S(2)}, u32[]{:S(2)}) collective-permute-start(bf16[128,6144]{1,0:T(8,128)(2,1)S(1)} %get-tuple-element.63), channel_id=1, source_target_pairs={{0,8},{1,9},{2,10},{3,11},{4,12},{5,13},{6,14},{7,15},{8,0},{9,1},... | collective-permute-start | bytes 4718600 | tf_op jit(solution)/shard_map/ppermute | solution.py:39
  28.9 20.1 %collective-permute-start.10 = (bf16[64,6144]{1,0:T(8,128)(2,1)S(1)}, bf16[64,6144]{1,0:T(8,128)(2,1)S(1)}, u32[]{:S(2)}, u32[]{:S(2)}) collective-permute-start(bf16[64,6144]{1,0:T(8,128)(2,1)S(1)} %pad_maximum_fusion.2), channel_id=1, source_target_pairs={{0,49},{1,16},{2,19},{3,50},{4,53},{5,20},{6,23},{7,54},{8,57},{9,... | collective-permute-start | bytes 2359304 | tf_op jit(solution)/shard_map/ppermute | solution.py:88
  29.8 20.5 %collective-permute-start.8 = (bf16[64,6144]{1,0:T(8,128)(2,1)S(1)}, bf16[64,6144]{1,0:T(8,128)(2,1)S(1)}, u32[]{:S(2)}, u32[]{:S(2)}) collective-permute-start(bf16[64,6144]{1,0:T(8,128)(2,1)S(1)} %pad_maximum_fusion.2), channel_id=1, source_target_pairs={{0,17},{1,48},{2,51},{3,18},{4,21},{5,52},{6,55},{7,22},{8,25},{9,... | collective-permute-start | bytes 2359304 | tf_op jit(solution)/shard_map/ppermute | solution.py:88
  30.0 20.3 %collective-permute-start.11 = (bf16[64,6144]{1,0:T(8,128)(2,1)S(1)}, bf16[64,6144]{1,0:T(8,128)(2,1)S(1)}, u32[]{:S(2)}, u32[]{:S(2)}) collective-permute-start(bf16[64,6144]{1,0:T(8,128)(2,1)S(1)} %pad_maximum_fusion.3), channel_id=1, source_target_pairs={{0,7},{1,2},{2,1},{3,4},{4,3},{5,6},{6,5},{7,0},{8,15},{9,10},{10,... | collective-permute-start | bytes 2359304 | tf_op jit(solution)/shard_map/ppermute | solution.py:89
  33.2 18.1 %collective-permute-start.9 = (bf16[64,6144]{1,0:T(8,128)(2,1)S(1)}, bf16[64,6144]{1,0:T(8,128)(2,1)S(1)}, u32[]{:S(2)}, u32[]{:S(2)}) collective-permute-start(bf16[64,6144]{1,0:T(8,128)(2,1)S(1)} %pad_maximum_fusion.3), channel_id=1, source_target_pairs={{0,3},{1,6},{2,5},{3,0},{4,7},{5,2},{6,1},{7,4},{8,11},{9,14},{10,... | collective-permute-start | bytes 2359304 | tf_op jit(solution)/shard_map/ppermute | solution.py:89
  51.4 12.7 %collective-permute-start.12 = (bf16[64,6144]{1,0:T(8,128)(2,1)S(1)}, bf16[64,6144]{1,0:T(8,128)(2,1)S(1)}, u32[]{:S(2)}, u32[]{:S(2)}) collective-permute-start(bf16[64,6144]{1,0:T(8,128)(2,1)S(1)} %collective-permute-done.8), channel_id=1, source_target_pairs={{0,49},{1,16},{2,19},{3,50},{4,53},{5,20},{6,23},{7,54},{8,57},{9,... | collective-permute-start | bytes 2359304 | tf_op jit(solution)/shard_map/ppermute | solution.py:88
  53.7 12.7 %collective-permute-start.13 = (bf16[64,6144]{1,0:T(8,128)(2,1)S(1)}, bf16[64,6144]{1,0:T(8,128)(2,1)S(1)}, u32[]{:S(2)}, u32[]{:S(2)}) collective-permute-start(bf16[64,6144]{1,0:T(8,128)(2,1)S(1)} %collective-permute-done.9), channel_id=1, source_target_pairs={{0,7},{1,2},{2,1},{3,4},{4,3},{5,6},{6,5},{7,0},{8,15},{9,10},{10,... | collective-permute-start | bytes 2359304 | tf_op jit(solution)/shard_map/ppermute | solution.py:89
  62.2 11.2 %collective-permute-start.19 = (bf16[256,6144]{1,0:T(8,128)(2,1)S(1)}, bf16[256,6144]{1,0:T(8,128)(2,1)S(1)}, u32[]{:S(2)}, u32[]{:S(2)}) collective-permute-start(bf16[256,6144]{1,0:T(8,128)(2,1)S(1)} %pad_maximum_fusion.1), channel_id=1, source_target_pairs={{0,1},{1,0},{2,3},{3,2},{4,5},{5,4},{6,7},{7,6},{8,9},{9,8},{10,11... | collective-permute-start | bytes 9437192 | tf_op jit(solution)/shard_map/ppermute | solution.py:39
  71.0 7.1 %collective-permute-start.20 = (bf16[512,128]{1,0:T(8,128)(2,1)S(1)}, bf16[512,128]{1,0:T(8,128)(2,1)S(1)}, u32[]{:S(2)}, u32[]{:S(2)}) collective-permute-start(bf16[512,128]{1,0:T(8,128)(2,1)S(1)} %convolution_convert_fusion.1), channel_id=1, source_target_pairs={{0,8},{1,9},{2,10},{3,11},{4,12},{5,13},{6,14},{7,15},{8,0},{9,1},... | collective-permute-start | bytes 393224 | tf_op jit(solution)/shard_map/ppermute | solution.py:39
  80.9 12.7 %collective-permute-start.22 = (bf16[64,6144]{1,0:T(8,128)(2,1)S(1)}, bf16[64,6144]{1,0:T(8,128)(2,1)S(1)}, u32[]{:S(2)}, u32[]{:S(2)}) collective-permute-start(bf16[64,6144]{1,0:T(8,128)(2,1)S(1)} %get-tuple-element.67), channel_id=1, source_target_pairs={{0,49},{1,16},{2,19},{3,50},{4,53},{5,20},{6,23},{7,54},{8,57},{9,... | collective-permute-start | bytes 2359304 | tf_op jit(solution)/shard_map/ppermute | solution.py:88
  81.8 12.6 %collective-permute-start.23 = (bf16[64,6144]{1,0:T(8,128)(2,1)S(1)}, bf16[64,6144]{1,0:T(8,128)(2,1)S(1)}, u32[]{:S(2)}, u32[]{:S(2)}) collective-permute-start(bf16[64,6144]{1,0:T(8,128)(2,1)S(1)} %get-tuple-element.68), channel_id=1, source_target_pairs={{0,7},{1,2},{2,1},{3,4},{4,3},{5,6},{6,5},{7,0},{8,15},{9,10},{10,... | collective-permute-start | bytes 2359304 | tf_op jit(solution)/shard_map/ppermute | solution.py:89
  94.9 7.3 %collective-permute-start.24 = (bf16[32,6144]{1,0:T(8,128)(2,1)S(1)}, bf16[32,6144]{1,0:T(8,128)(2,1)S(1)}, u32[]{:S(2)}, u32[]{:S(2)}) collective-permute-start(bf16[32,6144]{1,0:T(8,128)(2,1)S(1)} %slice.303), channel_id=1, source_target_pairs={{0,17},{1,48},{2,51},{3,18},{4,21},{5,52},{6,55},{7,22},{8,25},{9,... | collective-permute-start | bytes 1179656 | tf_op jit(solution)/shard_map/ppermute | solution.py:88
  95.0 7.2 %collective-permute-start.25 = (bf16[32,6144]{1,0:T(8,128)(2,1)S(1)}, bf16[32,6144]{1,0:T(8,128)(2,1)S(1)}, u32[]{:S(2)}, u32[]{:S(2)}) collective-permute-start(bf16[32,6144]{1,0:T(8,128)(2,1)S(1)} %slice.302), channel_id=1, source_target_pairs={{0,3},{1,6},{2,5},{3,0},{4,7},{5,2},{6,1},{7,4},{8,11},{9,14},{10,... | collective-permute-start | bytes 1179656 | tf_op jit(solution)/shard_map/ppermute | solution.py:89
  102.5 6.4 %collective-permute-start.26 = (bf16[16,6144]{1,0:T(8,128)(2,1)S(1)}, bf16[16,6144]{1,0:T(8,128)(2,1)S(1)}, u32[]{:S(2)}, u32[]{:S(2)}) collective-permute-start(bf16[16,6144]{1,0:T(8,128)(2,1)S(1)} %pad_maximum_fusion.8), channel_id=1, source_target_pairs={{0,7},{1,2},{2,1},{3,4},{4,3},{5,6},{6,5},{7,0},{8,15},{9,10},{10,... | collective-permute-start | bytes 589832 | tf_op jit(solution)/shard_map/ppermute | solution.py:88
  105.2 6.3 %collective-permute-start.27 = (bf16[16,6144]{1,0:T(8,128)(2,1)S(1)}, bf16[16,6144]{1,0:T(8,128)(2,1)S(1)}, u32[]{:S(2)}, u32[]{:S(2)}) collective-permute-start(bf16[16,6144]{1,0:T(8,128)(2,1)S(1)} %pad_maximum_fusion.9), channel_id=1, source_target_pairs={{0,49},{1,16},{2,19},{3,50},{4,53},{5,20},{6,23},{7,54},{8,57},{9,... | collective-permute-start | bytes 589832 | tf_op jit(solution)/shard_map/ppermute | solution.py:89
  112.3 6.5 %collective-permute-start.30 = (bf16[8,6144]{1,0:T(8,128)(2,1)S(1)}, bf16[8,6144]{1,0:T(8,128)(2,1)S(1)}, u32[]{:S(2)}, u32[]{:S(2)}) collective-permute-start(bf16[8,6144]{1,0:T(8,128)(2,1)S(1)} %get-tuple-element.119), channel_id=1, source_target_pairs={{0,72},{1,73},{2,74},{3,75},{4,76},{5,77},{6,78},{7,79},{8,64},{9,... | collective-permute-start | bytes 294920 | tf_op jit(solution)/shard_map/ppermute | solution.py:285
  115.5 6.6 %collective-permute-start.31 = (bf16[8,6144]{1,0:T(8,128)(2,1)S(1)}, bf16[8,6144]{1,0:T(8,128)(2,1)S(1)}, u32[]{:S(2)}, u32[]{:S(2)}) collective-permute-start(bf16[8,6144]{1,0:T(8,128)(2,1)S(1)} %get-tuple-element.120), channel_id=1, source_target_pairs={{0,89},{1,120},{2,123},{3,90},{4,93},{5,124},{6,127},{7,94},{8,67}... | collective-permute-start | bytes 294920 | tf_op jit(solution)/shard_map/ppermute | solution.py:285
  (13 other events, 104.7 us)
